TPU v7x, 32 devices: a whole 2x2x4 slice. The times are simulated.
32 devices in a mesh: dp: 8 (over y, x, core), tensor: 4 (over z).
Axes of the slice: x: 2, y: 2, z: 4, core: 2. Of those that a mesh axis runs over, the one named last changes fastest.
Arguments:
- tokens: bfloat16 [8192, 1024], P('dp', 'tensor'), may hold values from -6 to 6
- doc_lengths: int32 [8, 6], P('dp'), may hold values from 1 to 512, 1024 in all within a row
- grad_out: bfloat16 [8192, 1024], P('dp', 'tensor'), may hold values from -6 to 6
- norm_gains: float32 [4, 1024], replicated, may hold values from 0.1 to 1.9
- head_gains: float32 [2, 64], replicated, may hold values from 0.1 to 1.9
- conv_in: bfloat16 [1024, 3, 1024], P(None, None, 'tensor'), may hold values from -0.1875 to 0.1875
- conv_kernel: float32 [3, 1024], P(None, 'tensor'), may hold values from -3 to 3
- conv_out: bfloat16 [1024, 1024], P('tensor'), may hold values from -0.1875 to 0.1875
- query_w: bfloat16 [1024, 1024], P(None, 'tensor'), may hold values from -0.1875 to 0.1875
- kv_w: bfloat16 [1024, 2, 512], P(None, None, 'tensor'), may hold values from -0.1875 to 0.1875
- out_w: bfloat16 [1024, 1024], P('tensor'), may hold values from -1.75 to 1.75
- gate_up: bfloat16 [2, 1024, 2, 4608], P(None, 'dp', None, 'tensor'), may hold values from -0.1875 to 0.1875
- down: bfloat16 [2, 4608, 1024], P(None, 'tensor', 'dp'), may hold values from -0.09375 to 0.09375
Outputs:
- output: bfloat16 [8192, 1024], P('dp', 'tensor')
- grad_tokens: float32 [8192, 1024], P('dp', 'tensor')
- grad_norm_gains: float32 [4, 1024], replicated
- grad_head_gains: float32 [2, 64], replicated
- grad_conv_in: float32 [1024, 3, 1024], P('dp', None, 'tensor')
- grad_conv_kernel: float32 [3, 1024], replicated
- grad_conv_out: float32 [1024, 1024], P('tensor', 'dp')
- grad_query_w: float32 [1024, 1024], P('dp', 'tensor')
- grad_kv_w: float32 [1024, 2, 512], P('dp', None, 'tensor')
- grad_out_w: float32 [1024, 1024], P('tensor', 'dp')
- grad_gate_up: float32 [2, 1024, 2, 4608], P(None, 'dp', None, 'tensor')
- grad_down: float32 [2, 4608, 1024], P(None, 'tensor', 'dp')
Inputs may be any that keep to these rules, and one draw needn't show every extreme that they name: `doc_lengths`: in each row the 6 document lengths sum to 1024, and the longest is 512.
All inputs are finite; a program needn't handle non-finite values.
Results may differ from a plain program's by a relative error of at most 0.024.
Values may be sent and summed in bfloat16 or wider, within the bound.
A program may use at most 192 MiB of HBM per device.

v0:
```python
import jax
import jax.numpy as jnp
from jax import lax
from jax.sharding import PartitionSpec as P

epsilon = 1e-05
rope_base = 1000000.0


def doc_layout(lengths_row, length):
    doc_ends = jnp.cumsum(lengths_row)
    places = jnp.arange(length, dtype=jnp.int32)
    passed = places[:, None] >= doc_ends[None, :]
    segment = jnp.sum(passed.astype(jnp.int32), axis=1)
    doc_start = jnp.max(jnp.where(passed, doc_ends[None, :], 0), axis=1)
    return (segment, places - doc_start)


def rope_tables(position, head_dim):
    half_dim = head_dim // 2
    inverse = rope_base ** (-2.0 * jnp.arange(half_dim, dtype=jnp.float32) / head_dim)
    angles = position.astype(jnp.float32)[:, None] * inverse[None, :]
    return (jnp.cos(angles)[:, None, :], jnp.sin(angles)[:, None, :])


def rotate(values, tables):
    cosine, sine = tables
    half_dim = values.shape[-1] // 2
    first_half, second_half = (values[..., :half_dim], values[..., half_dim:])
    return jnp.concatenate(
        [first_half * cosine - second_half * sine, second_half * cosine + first_half * sine],
        axis=-1,
    )


def rotate_back(gradient, tables):
    cosine, sine = tables
    half_dim = gradient.shape[-1] // 2
    first_half, second_half = (gradient[..., :half_dim], gradient[..., half_dim:])
    return jnp.concatenate(
        [first_half * cosine + second_half * sine, second_half * cosine - first_half * sine],
        axis=-1,
    )


def shift_down(values, offset):
    filler = jnp.zeros((offset,) + values.shape[1:], values.dtype)
    return jnp.concatenate([filler, values[: values.shape[0] - offset]], axis=0)


def shift_up(values, offset):
    filler = jnp.zeros((offset,) + values.shape[1:], values.dtype)
    return jnp.concatenate([values[offset:], filler], axis=0)


def same_document(segment, offset):
    places = jnp.arange(segment.shape[0], dtype=jnp.int32)
    return (segment == shift_down(segment, offset)) & (places >= offset)


def rms_forward(values, norm_gain):
    inverse = lax.rsqrt(jnp.mean(values * values, axis=-1, keepdims=True) + epsilon)
    return (values * inverse * norm_gain, inverse)


def rms_backward(upstream, values, inverse, norm_gain):
    scaled = upstream * norm_gain
    inner = jnp.mean(scaled * values, axis=-1, keepdims=True)
    grad_values = inverse * scaled - values * inverse**3 * inner
    leading = tuple(range(values.ndim - 1))
    grad_gain = jnp.sum(upstream * values * inverse, axis=leading)
    return (grad_values, grad_gain)


def widen(shard):
    return lax.all_gather(shard, "tensor", axis=1, tiled=True)


def narrow(partial_sum):
    return lax.psum_scatter(partial_sum, "tensor", scatter_dimension=1, tiled=True)


def widen_grad(gradient):
    return lax.all_gather(gradient.astype(jnp.bfloat16), "tensor", axis=1, tiled=True)


def narrow_grad(partial_grad):
    return lax.psum_scatter(
        partial_grad.astype(jnp.bfloat16), "tensor", scatter_dimension=1, tiled=True
    ).astype(jnp.float32)


def fetch_ffn(gate_up, down, layer_index):
    return (
        lax.all_gather(gate_up[layer_index], "dp", axis=0, tiled=True),
        lax.all_gather(down[layer_index], "dp", axis=1, tiled=True),
    )


def sum_ffn_grads(local_grads):
    return (
        lax.psum_scatter(local_grads[0], "dp", scatter_dimension=0, tiled=True),
        lax.psum_scatter(local_grads[1], "dp", scatter_dimension=1, tiled=True),
    )


def block_scores(query_low, key_low, segment, block_start, block_rows, score_scale):
    length, kv_local, head_dim = key_low.shape
    groups = query_low.shape[1] // kv_local
    query_block = query_low[block_start : block_start + block_rows].reshape(
        block_rows, kv_local, groups, head_dim
    )
    raw = (
        jnp.einsum("bkgd,skd->kgbs", query_block, key_low, preferred_element_type=jnp.float32)
        * score_scale
    )
    query_places = block_start + jnp.arange(block_rows, dtype=jnp.int32)
    key_places = jnp.arange(length, dtype=jnp.int32)
    segment_block = segment[block_start : block_start + block_rows]
    allowed = (key_places[None, :] <= query_places[:, None]) & (
        segment[None, :] == segment_block[:, None]
    )
    return (jnp.where(allowed, raw, -1e30), query_block)


def conv_forward(stream, norm_gain, conv_in, conv_kernel, conv_out, segment):
    full_rows = widen(stream)
    normed, inverse = rms_forward(full_rows, norm_gain)
    length = full_rows.shape[0]
    projected = jnp.dot(
        normed.astype(jnp.bfloat16),
        conv_in.reshape(conv_in.shape[0], -1),
        preferred_element_type=jnp.float32,
    ).reshape(length, 3, -1)
    gated = projected[:, 0] * projected[:, 2]
    summed = conv_kernel[0] * gated
    for offset in range(1, conv_kernel.shape[0]):
        summed = summed + conv_kernel[offset] * jnp.where(
            same_document(segment, offset)[:, None], shift_down(gated, offset), 0.0
        )
    mixed_low = (projected[:, 1] * summed).astype(jnp.bfloat16)
    branch = narrow(jnp.dot(mixed_low, conv_out, preferred_element_type=jnp.float32))
    return (stream + branch, (full_rows, inverse, projected, summed, mixed_low))


def conv_backward(upstream, norm_gain, conv_in, conv_kernel, conv_out, segment, stored):
    full_rows, inverse, projected, summed, mixed_low = stored
    length = full_rows.shape[0]
    gathered = widen_grad(upstream)
    grad_mixed = jnp.dot(gathered, conv_out.T, preferred_element_type=jnp.float32)
    grad_conv_out = jnp.dot(mixed_low.T, gathered, preferred_element_type=jnp.float32)
    gate_b, gate_c, values_x = (projected[:, 0], projected[:, 1], projected[:, 2])
    gated = gate_b * values_x
    grad_c = grad_mixed * summed
    grad_summed = grad_mixed * gate_c
    grad_gated = conv_kernel[0] * grad_summed
    kernel_rows = [jnp.sum(grad_summed * gated, axis=0)]
    for offset in range(1, conv_kernel.shape[0]):
        masked = jnp.where(same_document(segment, offset)[:, None], grad_summed, 0.0)
        grad_gated = grad_gated + conv_kernel[offset] * shift_up(masked, offset)
        kernel_rows.append(jnp.sum(masked * shift_down(gated, offset), axis=0))
    grad_projected = (
        jnp.stack([grad_gated * values_x, grad_c, grad_gated * gate_b], axis=1)
        .astype(jnp.bfloat16)
        .reshape(length, -1)
    )
    normed_low = (full_rows * inverse * norm_gain).astype(jnp.bfloat16)
    grad_conv_in = jnp.dot(
        normed_low.T, grad_projected, preferred_element_type=jnp.float32
    ).reshape(conv_in.shape)
    grad_normed = jnp.dot(
        grad_projected, conv_in.reshape(conv_in.shape[0], -1).T, preferred_element_type=jnp.float32
    )
    grad_rows, grad_gain = rms_backward(grad_normed, full_rows, inverse, norm_gain)
    return (
        upstream + narrow_grad(grad_rows),
        grad_gain,
        jnp.stack(kernel_rows),
        grad_conv_in,
        grad_conv_out,
    )


def ffn_forward(stream, norm_gain, weights):
    gate_up_w, down_w = weights
    full_rows = widen(stream)
    normed, inverse = rms_forward(full_rows, norm_gain)
    length = full_rows.shape[0]
    hidden = jnp.dot(
        normed.astype(jnp.bfloat16),
        gate_up_w.reshape(gate_up_w.shape[0], -1),
        preferred_element_type=jnp.float32,
    ).reshape(length, 2, -1)
    active = (jax.nn.silu(hidden[:, 0]) * hidden[:, 1]).astype(jnp.bfloat16)
    branch = narrow(jnp.dot(active, down_w, preferred_element_type=jnp.float32))
    return (stream + branch, (full_rows, inverse, hidden, active))


def ffn_backward(upstream, norm_gain, weights, stored):
    gate_up_w, down_w = weights
    full_rows, inverse, hidden, active = stored
    length = full_rows.shape[0]
    gathered = widen_grad(upstream)
    grad_active = jnp.dot(gathered, down_w.T, preferred_element_type=jnp.float32)
    grad_down = jnp.dot(active.T, gathered, preferred_element_type=jnp.float32)
    gate_part, up_part = (hidden[:, 0], hidden[:, 1])
    sigmoid_gate = jax.nn.sigmoid(gate_part)
    grad_gate = grad_active * up_part * sigmoid_gate * (1.0 + gate_part * (1.0 - sigmoid_gate))
    grad_up = grad_active * jax.nn.silu(gate_part)
    grad_hidden = jnp.stack([grad_gate, grad_up], axis=1).astype(jnp.bfloat16).reshape(length, -1)
    normed_low = (full_rows * inverse * norm_gain).astype(jnp.bfloat16)
    grad_gate_up = jnp.dot(normed_low.T, grad_hidden, preferred_element_type=jnp.float32).reshape(
        gate_up_w.shape
    )
    grad_normed = jnp.dot(
        grad_hidden, gate_up_w.reshape(gate_up_w.shape[0], -1).T, preferred_element_type=jnp.float32
    )
    grad_rows, grad_gain = rms_backward(grad_normed, full_rows, inverse, norm_gain)
    return (upstream + narrow_grad(grad_rows), grad_gain, (grad_gate_up, grad_down))


def attention_forward(stream, norm_gain, head_gains, query_w, kv_w, out_w, segment, tables):
    head_dim = head_gains.shape[1]
    full_rows = widen(stream)
    normed, inverse = rms_forward(full_rows, norm_gain)
    normed_low = normed.astype(jnp.bfloat16)
    length = full_rows.shape[0]
    query_raw = jnp.dot(normed_low, query_w, preferred_element_type=jnp.float32).reshape(
        length, -1, head_dim
    )
    pair_raw = jnp.dot(
        normed_low, kv_w.reshape(kv_w.shape[0], -1), preferred_element_type=jnp.float32
    ).reshape(length, 2, -1, head_dim)
    query_normed, query_inverse = rms_forward(query_raw, head_gains[0])
    key_normed, key_inverse = rms_forward(pair_raw[:, 0], head_gains[1])
    query_low = rotate(query_normed, tables).astype(jnp.bfloat16)
    key_low = rotate(key_normed, tables).astype(jnp.bfloat16)
    value_low = pair_raw[:, 1].astype(jnp.bfloat16)
    score_scale = head_dim ** (-0.5)
    block_rows = min(length, 512)
    outputs = []
    logsums = []
    for block_number in range(length // block_rows):
        scores, query_block = block_scores(
            query_low, key_low, segment, block_number * block_rows, block_rows, score_scale
        )
        top = jnp.max(scores, axis=-1, keepdims=True)
        weights = jnp.exp(scores - top)
        totals = jnp.sum(weights, axis=-1, keepdims=True)
        probs = weights / totals
        logsums.append(top + jnp.log(totals))
        attended = jnp.einsum(
            "kgbs,skd->bkgd",
            probs.astype(jnp.bfloat16),
            value_low,
            preferred_element_type=jnp.float32,
        )
        outputs.append(attended.reshape(block_rows, -1))
    attended_low = jnp.concatenate(outputs, axis=0).astype(jnp.bfloat16)
    branch = narrow(jnp.dot(attended_low, out_w, preferred_element_type=jnp.float32))
    stored = (
        full_rows,
        inverse,
        query_raw,
        pair_raw,
        query_inverse,
        key_inverse,
        query_low,
        key_low,
        value_low,
        logsums,
        attended_low,
    )
    return (stream + branch, stored)


def attention_backward(
    upstream, norm_gain, head_gains, query_w, kv_w, out_w, segment, tables, stored
):
    (
        full_rows,
        inverse,
        query_raw,
        pair_raw,
        query_inverse,
        key_inverse,
        query_low,
        key_low,
        value_low,
        logsums,
        attended_low,
    ) = stored
    head_dim = head_gains.shape[1]
    length, kv_local = (key_low.shape[0], key_low.shape[1])
    groups = query_low.shape[1] // kv_local
    score_scale = head_dim ** (-0.5)
    block_rows = min(length, 512)
    gathered = widen_grad(upstream)
    grad_out_w = jnp.dot(attended_low.T, gathered, preferred_element_type=jnp.float32)
    grad_attended = (
        jnp.dot(gathered, out_w.T, preferred_element_type=jnp.float32)
        .astype(jnp.bfloat16)
        .reshape(length, kv_local, groups, head_dim)
    )
    grad_query_parts = []
    grad_key = jnp.zeros((length, kv_local, head_dim), jnp.float32)
    grad_value = jnp.zeros((length, kv_local, head_dim), jnp.float32)
    for block_number in range(length // block_rows):
        block_start = block_number * block_rows
        scores, query_block = block_scores(
            query_low, key_low, segment, block_start, block_rows, score_scale
        )
        probs = jnp.exp(scores - logsums[block_number])
        grad_block = grad_attended[block_start : block_start + block_rows]
        grad_probs = jnp.einsum(
            "bkgd,skd->kgbs", grad_block, value_low, preferred_element_type=jnp.float32
        )
        inner = jnp.sum(probs * grad_probs, axis=-1, keepdims=True)
        grad_scores = (probs * (grad_probs - inner)).astype(jnp.bfloat16)
        grad_query_parts.append(
            jnp.einsum("kgbs,skd->bkgd", grad_scores, key_low, preferred_element_type=jnp.float32)
            * score_scale
        )
        grad_key = (
            grad_key
            + jnp.einsum(
                "kgbs,bkgd->skd", grad_scores, query_block, preferred_element_type=jnp.float32
            )
            * score_scale
        )
        grad_value = grad_value + jnp.einsum(
            "kgbs,bkgd->skd",
            probs.astype(jnp.bfloat16),
            grad_block,
            preferred_element_type=jnp.float32,
        )
    grad_query = jnp.concatenate(grad_query_parts, axis=0).reshape(length, -1, head_dim)
    grad_query_raw, grad_query_gain = rms_backward(
        rotate_back(grad_query, tables), query_raw, query_inverse, head_gains[0]
    )
    grad_key_raw, grad_key_gain = rms_backward(
        rotate_back(grad_key, tables), pair_raw[:, 0], key_inverse, head_gains[1]
    )
    grad_query_low = grad_query_raw.astype(jnp.bfloat16).reshape(length, -1)
    grad_pair_low = (
        jnp.stack([grad_key_raw, grad_value], axis=1).astype(jnp.bfloat16).reshape(length, -1)
    )
    normed_low = (full_rows * inverse * norm_gain).astype(jnp.bfloat16)
    grad_query_w = jnp.dot(normed_low.T, grad_query_low, preferred_element_type=jnp.float32)
    grad_kv_w = jnp.dot(normed_low.T, grad_pair_low, preferred_element_type=jnp.float32).reshape(
        kv_w.shape
    )
    grad_normed = jnp.dot(grad_query_low, query_w.T, preferred_element_type=jnp.float32) + jnp.dot(
        grad_pair_low, kv_w.reshape(kv_w.shape[0], -1).T, preferred_element_type=jnp.float32
    )
    grad_rows, grad_gain = rms_backward(grad_normed, full_rows, inverse, norm_gain)
    head_grads = jnp.stack([grad_query_gain, grad_key_gain])
    return (
        upstream + narrow_grad(grad_rows),
        grad_gain,
        head_grads,
        (grad_query_w, grad_kv_w, grad_out_w),
    )


def local(
    tokens,
    doc_lengths,
    grad_out,
    norm_gains,
    head_gains,
    conv_in,
    conv_kernel,
    conv_out,
    query_w,
    kv_w,
    out_w,
    gate_up,
    down,
):
    length = tokens.shape[0]
    head_dim = head_gains.shape[1]
    segment, position = doc_layout(doc_lengths[0], length)
    tables = rope_tables(position, head_dim)
    stream_input = tokens.astype(jnp.float32)
    after_conv, conv_stored = conv_forward(
        stream_input, norm_gains[0], conv_in, conv_kernel, conv_out, segment
    )
    ffn_first = fetch_ffn(gate_up, down, 0)
    after_ffn_one, ffn_stored_one = ffn_forward(after_conv, norm_gains[1], ffn_first)
    after_attention, attention_stored = attention_forward(
        after_ffn_one, norm_gains[2], head_gains, query_w, kv_w, out_w, segment, tables
    )
    ffn_second = fetch_ffn(gate_up, down, 1)
    after_ffn_two, ffn_stored_two = ffn_forward(after_attention, norm_gains[3], ffn_second)
    output = after_ffn_two.astype(jnp.bfloat16)
    upstream = grad_out.astype(jnp.float32)
    back_second = fetch_ffn(gate_up, down, 1)
    upstream, gain_three, local_two = ffn_backward(
        upstream, norm_gains[3], back_second, ffn_stored_two
    )
    ffn_grads_two = sum_ffn_grads(local_two)
    upstream, gain_two, head_grads, attention_grads = attention_backward(
        upstream, norm_gains[2], head_gains, query_w, kv_w, out_w, segment, tables, attention_stored
    )
    back_first = fetch_ffn(gate_up, down, 0)
    upstream, gain_one, local_one = ffn_backward(
        upstream, norm_gains[1], back_first, ffn_stored_one
    )
    ffn_grads_one = sum_ffn_grads(local_one)
    upstream, gain_zero, kernel_grad, conv_in_grad, conv_out_grad = conv_backward(
        upstream, norm_gains[0], conv_in, conv_kernel, conv_out, segment, conv_stored
    )
    mixer_sums = (
        lax.psum_scatter(conv_in_grad, "dp", scatter_dimension=0, tiled=True),
        lax.psum_scatter(conv_out_grad, "dp", scatter_dimension=1, tiled=True),
        lax.psum_scatter(attention_grads[0], "dp", scatter_dimension=0, tiled=True),
        lax.psum_scatter(attention_grads[1], "dp", scatter_dimension=0, tiled=True),
        lax.psum_scatter(attention_grads[2], "dp", scatter_dimension=1, tiled=True),
    )
    channels = conv_kernel.shape[1]
    kernel_full = jnp.zeros((conv_kernel.shape[0], norm_gains.shape[1]), jnp.float32)
    kernel_full = lax.dynamic_update_slice_in_dim(
        kernel_full, kernel_grad, lax.axis_index("tensor") * channels, 1
    )
    gain_stack = jnp.stack([gain_zero, gain_one, gain_two, gain_three])
    gain_sums, head_sums, kernel_sums = lax.psum(
        (gain_stack, head_grads, kernel_full), ("dp", "tensor")
    )
    grad_gate_up = jnp.stack([ffn_grads_one[0], ffn_grads_two[0]])
    grad_down = jnp.stack([ffn_grads_one[1], ffn_grads_two[1]])
    return (
        output,
        upstream,
        gain_sums,
        head_sums,
        mixer_sums[0],
        kernel_sums,
        mixer_sums[1],
        mixer_sums[2],
        mixer_sums[3],
        mixer_sums[4],
        grad_gate_up,
        grad_down,
    )


def solution(mesh):
    return jax.shard_map(
        local,
        mesh=mesh,
        in_specs=(
            P("dp", "tensor"),
            P("dp", None),
            P("dp", "tensor"),
            P(),
            P(),
            P(None, None, "tensor"),
            P(None, "tensor"),
            P("tensor", None),
            P(None, "tensor"),
            P(None, None, "tensor"),
            P("tensor", None),
            P(None, "dp", None, "tensor"),
            P(None, "tensor", "dp"),
        ),
        out_specs=(
            P("dp", "tensor"),
            P("dp", "tensor"),
            P(),
            P(),
            P("dp", None, "tensor"),
            P(),
            P("tensor", "dp"),
            P("dp", "tensor"),
            P("dp", None, "tensor"),
            P("tensor", "dp"),
            P(None, "dp", None, "tensor"),
            P(None, "tensor", "dp"),
        ),
        check_vma=False,
    )
```

profile of v0, /device:TPU:1, one launch (start us, length us, event | category | flops | bytes accessed | tf_op | source)
XLA Modules:
  0.0 1682.0 jit_solution(16583637000300992529)
XLA Ops:
  13.1 80.8 %all-gather.17.cloned.1.call-done = f32[1024,1024]{1,0:T(8,128)} async-done(((f32[1024,256]{1,0:T(8,128)}), f32[1024,1024]{1,0:T(8,128)}) %all-gather.17.cloned.1.call-update) | async-done | bytes 4194320 | tf_op jit(solution)/shard_map/all_gather | solution.py:76
  93.9 2.7 multiply_reduce_fusion.8
  103.3 2.7 fusion.127
  109.9 71.6 %reduce-scatter.18.cloned.1.call-done = f32[1024,256]{1,0:T(8,128)} async-done(((f32[1024,1024]{1,0:T(8,128)}), f32[1024,256]{1,0:T(8,128)}) %reduce-scatter.18.cloned.1.call-update) | async-done | bytes 1048592 | tf_op jit(solution)/shard_map/reduce_scatter | solution.py:80
  184.9 6.6 copy.68
  191.5 73.5 %all-gather.19.cloned.1.call-done = f32[1024,1024]{1,0:T(8,128)} async-done(((f32[1024,256]{1,0:T(8,128)}), f32[1024,1024]{1,0:T(8,128)}) %all-gather.19.cloned.1.call-update) | async-done | bytes 4194320 | tf_op jit(solution)/shard_map/all_gather | solution.py:76
  265.0 2.7 multiply_reduce_fusion.7
  268.5 7.7 fusion.16
  276.2 3.7 copy-done.25
  281.3 14.4 all-gather.35.cloned.1.call-done
  295.7 6.0 fusion.44
  301.8 76.5 %reduce-scatter.20.cloned.1.call-done = f32[1024,256]{1,0:T(8,128)} async-done(((f32[1024,1024]{1,0:T(8,128)}), f32[1024,256]{1,0:T(8,128)}) %reduce-scatter.20.cloned.1.call-update) | async-done | bytes 1048592 | tf_op jit(solution)/shard_map/reduce_scatter | solution.py:80
  383.4 78.4 %all-gather.21.cloned.1.call-done = f32[1024,1024]{1,0:T(8,128)} async-done(((f32[1024,256]{1,0:T(8,128)}), f32[1024,1024]{1,0:T(8,128)}) %all-gather.21.cloned.1.call-update) | async-done | bytes 4194320 | tf_op jit(solution)/shard_map/all_gather | solution.py:76
  461.8 2.7 multiply_reduce_fusion.6
  484.3 2.8 fusion.95
  489.1 73.5 %reduce-scatter.22.cloned.1.call-done = f32[1024,256]{1,0:T(8,128)} async-done(((f32[1024,1024]{1,0:T(8,128)}), f32[1024,256]{1,0:T(8,128)}) %reduce-scatter.22.cloned.1.call-update) | async-done | bytes 1048592 | tf_op jit(solution)/shard_map/reduce_scatter | solution.py:80
  566.2 6.7 copy.73
  572.9 73.2 %all-gather.23.cloned.1.call-done = f32[1024,1024]{1,0:T(8,128)} async-done(((f32[1024,256]{1,0:T(8,128)}), f32[1024,1024]{1,0:T(8,128)}) %all-gather.23.cloned.1.call-update) | async-done | bytes 4194320 | tf_op jit(solution)/shard_map/all_gather | solution.py:76
  646.1 2.7 multiply_reduce_fusion.5
  649.6 9.9 fusion.14
  659.5 32.1 %all-gather.25.cloned.1.call-done = bf16[1024,1024]{1,0:T(8,128)(2,1)} async-done(((bf16[1024,256]{1,0:T(8,128)(2,1)}), bf16[1024,1024]{1,0:T(8,128)(2,1)}) %all-gather.25.cloned.1.call-update) | async-done | bytes 2097168 | tf_op jit(solution)/shard_map/all_gather | solution.py:84
  691.6 31.0 %all-gather.39.cloned.1.call-done = bf16[1,1152,1024]{2,1,0:T(8,128)(2,1)} async-done(((bf16[1,1152,128]{2,1,0:T(8,128)(2,1)}), bf16[1,1152,1024]{2,1,0:T(8,128)(2,1)}) %all-gather.39.cloned.1.call-update) | async-done | bytes 2359312 | tf_op jit(solution)/shard_map/all_gather | solution.py:96
  722.6 9.1 multiply_bitcast_fusion.3
  731.8 10.0 fusion.33
  743.9 43.4 %reduce-scatter.26.cloned.1.call-done = bf16[1024,256]{1,0:T(8,128)(2,1)} async-done(((bf16[1024,1024]{1,0:T(8,128)(2,1)}), bf16[1024,256]{1,0:T(8,128)(2,1)}) %reduce-scatter.26.cloned.1.call-update) | async-done | bytes 524304 | tf_op jit(solution)/shard_map/reduce_scatter | solution.py:88
  789.6 44.8 %all-gather.27.cloned.1.call-done = bf16[1024,1024]{1,0:T(8,128)(2,1)} async-done(((bf16[1024,256]{1,0:T(8,128)(2,1)}), bf16[1024,1024]{1,0:T(8,128)(2,1)}) %all-gather.27.cloned.1.call-update) | async-done | bytes 2097168 | tf_op jit(solution)/shard_map/all_gather | solution.py:84
  834.5 2.5 convolution_convert_fusion
  837.0 5.7 fusion.59
  844.7 2.5 fusion.5
  866.9 42.5 %reduce-scatter.28.cloned.1.call-done = bf16[1024,256]{1,0:T(8,128)(2,1)} async-done(((bf16[1024,1024]{1,0:T(8,128)(2,1)}), bf16[1024,256]{1,0:T(8,128)(2,1)}) %reduce-scatter.28.cloned.1.call-update) | async-done | bytes 524304 | tf_op jit(solution)/shard_map/reduce_scatter | solution.py:88
  911.5 45.2 %all-gather.29.cloned.1.call-done = bf16[1024,1024]{1,0:T(8,128)(2,1)} async-done(((bf16[1024,256]{1,0:T(8,128)(2,1)}), bf16[1024,1024]{1,0:T(8,128)(2,1)}) %all-gather.29.cloned.1.call-update) | async-done | bytes 2097168 | tf_op jit(solution)/shard_map/all_gather | solution.py:84
  956.6 9.1 multiply_bitcast_fusion.1
  965.9 9.3 fusion.31
  977.4 42.7 %reduce-scatter.30.cloned.1.call-done = bf16[1024,256]{1,0:T(8,128)(2,1)} async-done(((bf16[1024,1024]{1,0:T(8,128)(2,1)}), bf16[1024,256]{1,0:T(8,128)(2,1)}) %reduce-scatter.30.cloned.1.call-update) | async-done | bytes 524304 | tf_op jit(solution)/shard_map/reduce_scatter | solution.py:88
  1022.3 4.6 multiply_convert_fusion
  1028.3 4.4 fusion.40
  1034.3 2.8 fusion.51
  1037.6 7.1 fusion.132
  1046.3 6.0 fusion.131
  1052.4 14.8 all-gather.31.cloned.1.call-done
  1067.2 2.7 multiply_reduce_fusion.11
  1075.9 2.5 fusion.29
  1080.7 5.0 maximum_convert_fusion
  1085.7 6.7 copy.85
  1092.4 11.5 fusion.10
  1104.0 5.1 maximum_convert_fusion.1
  1109.0 6.7 copy.83
  1115.7 11.3 fusion.12
  1128.0 3.4 fusion.94
  1131.5 2.8 fusion.130
  1134.4 3.6 fusion.129
  1138.3 6.1 fusion.55
  1146.8 37.9 %reduce-scatter.40.cloned.1.call-done = f32[128,2,128]{2,0,1:T(8,128)} async-done(((f32[1024,2,128]{2,0,1:T(8,128)}), f32[128,2,128]{2,0,1:T(8,128)}) %reduce-scatter.40.cloned.1.call-update) | async-done | bytes 131088 | tf_op jit(solution)/shard_map/reduce_scatter | solution.py:418
  1186.4 56.2 %reduce-scatter.50.cloned.1.call-done = f32[1152,128]{1,0:T(8,128)} async-done(((f32[1152,1024]{1,0:T(8,128)}), f32[1152,128]{1,0:T(8,128)}) %reduce-scatter.50.cloned.1.call-update) | async-done | bytes 589840 | tf_op jit(solution)/shard_map/reduce_scatter | solution.py:103
  1242.6 57.1 %reduce-scatter.48.cloned.1.call-done = f32[1152,128]{1,0:T(8,128)} async-done(((f32[1152,1024]{1,0:T(8,128)}), f32[1152,128]{1,0:T(8,128)}) %reduce-scatter.48.cloned.1.call-update) | async-done | bytes 589840 | tf_op jit(solution)/shard_map/reduce_scatter | solution.py:103
  1302.0 42.7 %all-reduce.5 = (f32[4,1024]{1,0:T(4,128)}, f32[2,64]{1,0:T(2,128)}, f32[3,1024]{1,0:T(4,128)}) all-reduce(f32[4,1024]{1,0:T(4,128)S(1)} %pad_maximum_fusion.9, f32[2,64]{1,0:T(2,128)S(1)} %pad_maximum_fusion.10, f32[3,1024]{1,0:T(4,128)S(1)} %maximum_dynamic-update-slice_fusion), channel_id=1, replica_groups=mesh['dp'=8,'tensor'=4] {'dp','tensor'}, use_global_device_ids=true, to_apply=%region_33.34 | all-reduce | flops 7296 | bytes 58368 | tf_op jit(solution)/shard_map/psum | solution.py:427
  1346.4 2.5 convert_add_fusion
  1348.9 76.9 %reduce-scatter.46.cloned.1.call-done = f32[128,2,1152]{2,0,1:T(8,128)} async-done(((f32[1024,2,1152]{2,0,1:T(8,128)}), f32[128,2,1152]{2,0,1:T(8,128)}) %reduce-scatter.46.cloned.1.call-update) | async-done | bytes 1179664 | tf_op jit(solution)/shard_map/reduce_scatter | solution.py:102
  1425.7 79.9 %reduce-scatter.44.cloned.1.call-done = f32[128,2,1152]{2,0,1:T(8,128)} async-done(((f32[1024,2,1152]{2,0,1:T(8,128)}), f32[128,2,1152]{2,0,1:T(8,128)}) %reduce-scatter.44.cloned.1.call-update) | async-done | bytes 1179664 | tf_op jit(solution)/shard_map/reduce_scatter | solution.py:102
  1507.4 3.2 copy.88
  1510.6 34.5 %reduce-scatter.42.cloned.1.call-done = f32[256,128]{1,0:T(8,128)} async-done(((f32[256,1024]{1,0:T(8,128)}), f32[256,128]{1,0:T(8,128)}) %reduce-scatter.42.cloned.1.call-update) | async-done | bytes 131088 | tf_op jit(solution)/shard_map/reduce_scatter | solution.py:419
  1545.1 39.7 %reduce-scatter.38.cloned.1.call-done = f32[128,256]{1,0:T(8,128)} async-done(((f32[1024,256]{1,0:T(8,128)}), f32[128,256]{1,0:T(8,128)}) %reduce-scatter.38.cloned.1.call-update) | async-done | bytes 131088 | tf_op jit(solution)/shard_map/reduce_scatter | solution.py:417
  1584.9 39.6 %reduce-scatter.36.cloned.1.call-done = f32[256,128]{1,0:T(8,128)} async-done(((f32[256,1024]{1,0:T(8,128)}), f32[256,128]{1,0:T(8,128)}) %reduce-scatter.36.cloned.1.call-update) | async-done | bytes 131088 | tf_op jit(solution)/shard_map/reduce_scatter | solution.py:416
  1624.4 50.3 %reduce-scatter.34.cloned.1.call-done = f32[128,3,256]{2,0,1:T(8,128)} async-done(((f32[1024,3,256]{2,0,1:T(8,128)}), f32[128,3,256]{2,0,1:T(8,128)}) %reduce-scatter.34.cloned.1.call-update) | async-done | bytes 393232 | tf_op jit(solution)/shard_map/reduce_scatter | solution.py:415
  (400 shorter events, 108.4 us)
Async XLA Ops:
  8.0 95.3 %copy-start = (bf16[256,1024]{1,0:T(8,128)(2,1)S(1)}, bf16[256,1024]{1,0:T(8,128)(2,1)}, u32[]{:S(2)}) copy-start(bf16[256,1024]{1,0:T(8,128)(2,1)} %param.20) | copy-start | bytes 1572868
  8.1 85.9 %all-gather.17.cloned.1.call-start = ((), (), s32[]{:S(2)}) async-start(), calls=%async_computation.17 | async-start | bytes 5242880 | tf_op jit(solution)/shard_map/all_gather | solution.py:76
  10.3 171.3 %reduce-scatter.18.cloned.1.call-start = ((), (), s32[]{:S(2)}) async-start(), calls=%async_computation.18 | async-start | bytes 5242880 | tf_op jit(solution)/shard_map/reduce_scatter | solution.py:80
  12.4 87.2 %copy-start.101 = (pred[1024]{0:T(1024)(128)(4,1)}, pred[1024]{0:T(1024)(128)(4,1)S(1)}, u32[]{:S(2)}) copy-start(pred[1024]{0:T(1024)(128)(4,1)S(1)} %get-tuple-element.124) | copy-start | bytes 3076
  12.4 87.2 %copy-start.103 = (pred[1024]{0:T(1024)(128)(4,1)}, pred[1024]{0:T(1024)(128)(4,1)S(1)}, u32[]{:S(2)}) copy-start(pred[1024]{0:T(1024)(128)(4,1)S(1)} %get-tuple-element.125) | copy-start | bytes 3076
  12.4 87.1 %copy-start.95 = (f32[1,256]{1,0:T(1,128)}, f32[1,256]{1,0:T(1,128)S(1)}, u32[]{:S(2)}) copy-start(f32[1,256]{1,0:T(1,128)S(1)} %get-tuple-element.121) | copy-start | bytes 3076
  12.5 87.1 %copy-start.97 = (f32[1,256]{1,0:T(1,128)}, f32[1,256]{1,0:T(1,128)S(1)}, u32[]{:S(2)}) copy-start(f32[1,256]{1,0:T(1,128)S(1)} %get-tuple-element.122) | copy-start | bytes 3076
  12.5 87.1 %copy-start.99 = (f32[1,256]{1,0:T(1,128)}, f32[1,256]{1,0:T(1,128)S(1)}, u32[]{:S(2)}) copy-start(f32[1,256]{1,0:T(1,128)S(1)} %get-tuple-element.123) | copy-start | bytes 3076
  13.1 86.3 %copy-start.88 = (f32[1,1024]{1,0:T(1,128)}, f32[1,1024]{1,0:T(1,128)S(1)}, u32[]{:S(2)}) copy-start(f32[1,1024]{1,0:T(1,128)S(1)} %get-tuple-element.103) | copy-start | bytes 12292
  13.1 255.2 %copy-start.90 = (f32[1,1024]{1,0:T(1,128)}, f32[1,1024]{1,0:T(1,128)S(1)}, u32[]{:S(2)}) copy-start(f32[1,1024]{1,0:T(1,128)S(1)} %get-tuple-element.102) | copy-start | bytes 12292
  13.1 452.0 %copy-start.75 = (f32[1,1024]{1,0:T(1,128)}, f32[1,1024]{1,0:T(1,128)S(1)}, u32[]{:S(2)}) copy-start(f32[1,1024]{1,0:T(1,128)S(1)} %get-tuple-element.104) | copy-start | bytes 12292
  106.0 75.5 %copy-start.42 = (bf16[1024,256]{1,0:T(8,128)(2,1)S(1)}, bf16[1024,256]{1,0:T(8,128)(2,1)}, u32[]{:S(2)}) copy-start(bf16[1024,256]{1,0:T(8,128)(2,1)} %param.13) | copy-start | bytes 1572868
  106.0 77.8 %copy-start.61 = (bf16[2,1152,128]{2,1,0:T(8,128)(2,1)S(1)}, bf16[2,1152,128]{2,1,0:T(8,128)(2,1)}, u32[]{:S(2)}) copy-start(bf16[2,1152,128]{2,1,0:T(8,128)(2,1)} %param.25) | copy-start | bytes 1769476
  106.1 78.8 %all-gather.33.cloned.1.call-start = ((), (), s32[]{:S(2)}) async-start(), calls=%async_computation.42 | async-start | bytes 5308416 | tf_op jit(solution)/shard_map/all_gather | solution.py:95
  109.8 155.2 %all-gather.19.cloned.1.call-start = ((), (), s32[]{:S(2)}) async-start(), calls=%async_computation.19 | async-start | bytes 5242880 | tf_op jit(solution)/shard_map/all_gather | solution.py:76
  183.8 111.8 %all-gather.35.cloned.1.call-start = ((), (), s32[]{:S(2)}) async-start(), calls=%async_computation.43 | async-start | bytes 2654208 | tf_op jit(solution)/shard_map/all_gather | solution.py:96
  184.8 193.5 %reduce-scatter.20.cloned.1.call-start = ((), (), s32[]{:S(2)}) async-start(), calls=%async_computation.20 | async-start | bytes 5242880 | tf_op jit(solution)/shard_map/reduce_scatter | solution.py:80
  281.3 14.4 copy-start.36
  301.7 76.6 %copy-start.24 = (f32[1024,256]{1,0:T(8,128)S(1)}, f32[1024,256]{1,0:T(8,128)}, u32[]{:S(2)}) copy-start(f32[1024,256]{1,0:T(8,128)} %convert_add_fusion.4) | copy-start | bytes 3145732
  301.7 79.1 %copy-start.45 = (bf16[1024,2,128]{2,1,0:T(2,128)(2,1)S(1)}, bf16[1024,2,128]{2,1,0:T(2,128)(2,1)}, u32[]{:S(2)}) copy-start(bf16[1024,2,128]{2,1,0:T(2,128)(2,1)} %param.22) | copy-start | bytes 1572868
  301.7 79.4 %copy-start.111 = (f32[2,64]{1,0:T(2,128)S(1)}, f32[2,64]{1,0:T(2,128)}, u32[]{:S(2)}) copy-start(f32[2,64]{1,0:T(2,128)} %param.17) | copy-start | bytes 1540
  301.7 160.1 %all-gather.21.cloned.1.call-start = ((), (), s32[]{:S(2)}) async-start(), calls=%async_computation.21 | async-start | bytes 5242880 | tf_op jit(solution)/shard_map/all_gather | solution.py:76
  380.6 182.0 %reduce-scatter.22.cloned.1.call-start = ((), (), s32[]{:S(2)}) async-start(), calls=%async_computation.22 | async-start | bytes 5242880 | tf_op jit(solution)/shard_map/reduce_scatter | solution.py:80
  381.2 87.9 %copy-start.105 = (f32[64]{0:T(128)}, f32[64]{0:T(128)S(1)}, u32[]{:S(2)}) copy-start(f32[64]{0:T(128)S(1)} %get-tuple-element.126) | copy-start | bytes 772
  381.2 88.1 %copy-start.107 = (f32[64]{0:T(128)}, f32[64]{0:T(128)S(1)}, u32[]{:S(2)}) copy-start(f32[64]{0:T(128)S(1)} %get-tuple-element.127) | copy-start | bytes 772
  381.8 88.2 %copy-start.33 = (f32[1024,32]{0,1:T(8,128)}, f32[1024,32]{0,1:T(8,128)S(1)}, u32[]{:S(2)}) copy-start(f32[1024,32]{0,1:T(8,128)S(1)} %get-tuple-element.108) | copy-start | bytes 393220
  466.9 12.7 copy-start.19
  487.1 75.5 %copy-start.22 = (f32[1024,256]{1,0:T(8,128)S(1)}, f32[1024,256]{1,0:T(8,128)}, u32[]{:S(2)}) copy-start(f32[1024,256]{1,0:T(8,128)} %add.236) | copy-start | bytes 3145732
  487.1 79.1 %all-gather.37.cloned.1.call-start = ((), (), s32[]{:S(2)}) async-start(), calls=%async_computation.44 | async-start | bytes 5308416 | tf_op jit(solution)/shard_map/all_gather | solution.py:95
  489.0 157.1 %all-gather.23.cloned.1.call-start = ((), (), s32[]{:S(2)}) async-start(), calls=%async_computation.23 | async-start | bytes 5242880 | tf_op jit(solution)/shard_map/all_gather | solution.py:76
  564.9 126.6 %all-gather.25.cloned.1.call-start = ((), (), s32[]{:S(2)}) async-start(), calls=%async_computation.25 | async-start | bytes 2621440 | tf_op jit(solution)/shard_map/all_gather | solution.py:84
  565.5 157.1 %all-gather.39.cloned.1.call-start = ((), (), s32[]{:S(2)}) async-start(), calls=%async_computation.45 | async-start | bytes 2654208 | tf_op jit(solution)/shard_map/all_gather | solution.py:96
  566.1 221.2 %reduce-scatter.26.cloned.1.call-start = ((), (), s32[]{:S(2)}) async-start(), calls=%async_computation.26 | async-start | bytes 2621440 | tf_op jit(solution)/shard_map/reduce_scatter | solution.py:88
  572.9 76.0 %copy-start.92 = (f32[1,1024]{1,0:T(1,128)S(1)}, f32[1,1024]{1,0:T(1,128)}, u32[]{:S(2)}) copy-start(f32[1,1024]{1,0:T(1,128)} %get-tuple-element.101) | copy-start | bytes 12292
  648.8 93.0 %copy-start.85 = (f32[1024]{0:T(1024)}, f32[1024]{0:T(1024)S(1)}, u32[]{:S(2)}) copy-start(f32[1024]{0:T(1024)S(1)} %get-tuple-element.116) | copy-start | bytes 12292
  741.8 45.5 %copy-start.18 = (bf16[1024,256]{1,0:T(8,128)(2,1)S(1)}, bf16[1024,256]{1,0:T(8,128)(2,1)}, u32[]{:S(2)}) copy-start(bf16[1024,256]{1,0:T(8,128)(2,1)} %param.15) | copy-start | bytes 1572868
  743.8 45.7 %copy-start.108 = (f32[64]{0:T(128)S(1)}, f32[64]{0:T(128)}, u32[]{:S(2)}) copy-start(f32[64]{0:T(128)} %copy-done.107) | copy-start | bytes 772
  743.8 90.7 %copy-start.63 = (bf16[256,1024]{1,0:T(8,128)(2,1)S(1)}, bf16[256,1024]{1,0:T(8,128)(2,1)}, u32[]{:S(2)}) copy-start(bf16[256,1024]{1,0:T(8,128)(2,1)} %param.23) | copy-start | bytes 1572868
  743.8 90.6 %all-gather.27.cloned.1.call-start = ((), (), s32[]{:S(2)}) async-start(), calls=%async_computation.27 | async-start | bytes 2621440 | tf_op jit(solution)/shard_map/all_gather | solution.py:84
  789.3 120.1 %reduce-scatter.28.cloned.1.call-start = ((), (), s32[]{:S(2)}) async-start(), calls=%async_computation.28 | async-start | bytes 2621440 | tf_op jit(solution)/shard_map/reduce_scatter | solution.py:88
  864.5 44.8 %copy-start.26 = (bf16[1024,256]{1,0:T(8,128)(2,1)S(1)}, bf16[1024,256]{1,0:T(8,128)(2,1)}, u32[]{:S(2)}) copy-start(bf16[1024,256]{1,0:T(8,128)(2,1)} %reduce-scatter.26.cloned.1.call-done) | copy-start | bytes 1572868
  866.6 90.1 %all-gather.29.cloned.1.call-start = ((), (), s32[]{:S(2)}) async-start(), calls=%async_computation.29 | async-start | bytes 2621440 | tf_op jit(solution)/shard_map/all_gather | solution.py:84
  911.4 54.4 %copy-start.83 = (f32[1024]{0:T(1024)S(1)}, f32[1024]{0:T(1024)}, u32[]{:S(2)}) copy-start(f32[1024]{0:T(1024)} %copy-done.82) | copy-start | bytes 12292
  911.4 54.4 %copy-start.91 = (f32[1,1024]{1,0:T(1,128)S(1)}, f32[1,1024]{1,0:T(1,128)}, u32[]{:S(2)}) copy-start(f32[1,1024]{1,0:T(1,128)} %copy-done.90) | copy-start | bytes 12292
  911.4 108.7 %reduce-scatter.30.cloned.1.call-start = ((), (), s32[]{:S(2)}) async-start(), calls=%async_computation.30 | async-start | bytes 2621440 | tf_op jit(solution)/shard_map/reduce_scatter | solution.py:88
  975.2 44.9 %copy-start.29 = (bf16[1024,256]{1,0:T(8,128)(2,1)S(1)}, bf16[1024,256]{1,0:T(8,128)(2,1)}, u32[]{:S(2)}) copy-start(bf16[1024,256]{1,0:T(8,128)(2,1)} %reduce-scatter.28.cloned.1.call-done) | copy-start | bytes 1572868
  977.4 89.9 %all-gather.31.cloned.1.call-start = ((), (), s32[]{:S(2)}) async-start(), calls=%async_computation.31 | async-start | bytes 2621440 | tf_op jit(solution)/shard_map/all_gather | solution.py:84
  1022.2 122.5 %reduce-scatter.24.cloned.1.call-start = ((), (), s32[]{:S(2)}) async-start(), calls=%async_computation.24 | async-start | bytes 5242880 | tf_op jit(solution)/shard_map/reduce_scatter | solution.py:80
  1032.7 152.0 %reduce-scatter.40.cloned.1.call-start = ((), (), s32[]{:S(2)}) async-start(), calls=%async_computation.36 | async-start | bytes 1179648 | tf_op jit(solution)/shard_map/reduce_scatter | solution.py:418
  1037.1 205.4 %reduce-scatter.50.cloned.1.call-start = ((), (), s32[]{:S(2)}) async-start(), calls=%async_computation.41 | async-start | bytes 5308416 | tf_op jit(solution)/shard_map/reduce_scatter | solution.py:103
  1044.7 255.0 %reduce-scatter.48.cloned.1.call-start = ((), (), s32[]{:S(2)}) async-start(), calls=%async_computation.40 | async-start | bytes 5308416 | tf_op jit(solution)/shard_map/reduce_scatter | solution.py:103
  1052.3 14.9 copy-start.6
  1052.3 17.6 %copy-start.102 = (pred[1024]{0:T(1024)(128)(4,1)S(1)}, pred[1024]{0:T(1024)(128)(4,1)}, u32[]{:S(2)}) copy-start(pred[1024]{0:T(1024)(128)(4,1)} %copy-done.101) | copy-start | bytes 3076
  1052.3 17.6 %copy-start.104 = (pred[1024]{0:T(1024)(128)(4,1)S(1)}, pred[1024]{0:T(1024)(128)(4,1)}, u32[]{:S(2)}) copy-start(pred[1024]{0:T(1024)(128)(4,1)} %copy-done.103) | copy-start | bytes 3076
  1052.3 294.0 %reduce-scatter.32.cloned.1.call-start = ((), (), s32[]{:S(2)}) async-start(), calls=%async_computation.32 | async-start | bytes 2621440 | tf_op jit(solution)/shard_map/reduce_scatter | solution.py:88
  1080.5 345.2 %reduce-scatter.46.cloned.1.call-start = ((), (), s32[]{:S(2)}) async-start(), calls=%async_computation.39 | async-start | bytes 10616832 | tf_op jit(solution)/shard_map/reduce_scatter | solution.py:102
  1103.9 401.6 %reduce-scatter.44.cloned.1.call-start = ((), (), s32[]{:S(2)}) async-start(), calls=%async_computation.38 | async-start | bytes 10616832 | tf_op jit(solution)/shard_map/reduce_scatter | solution.py:102
  1127.1 418.0 %reduce-scatter.42.cloned.1.call-start = ((), (), s32[]{:S(2)}) async-start(), calls=%async_computation.37 | async-start | bytes 1179648 | tf_op jit(solution)/shard_map/reduce_scatter | solution.py:419
  1131.4 453.4 %reduce-scatter.38.cloned.1.call-start = ((), (), s32[]{:S(2)}) async-start(), calls=%async_computation.35 | async-start | bytes 1179648 | tf_op jit(solution)/shard_map/reduce_scatter | solution.py:417
  1134.3 490.1 %reduce-scatter.36.cloned.1.call-start = ((), (), s32[]{:S(2)}) async-start(), calls=%async_computation.34 | async-start | bytes 1179648 | tf_op jit(solution)/shard_map/reduce_scatter | solution.py:416
  1138.0 536.7 %reduce-scatter.34.cloned.1.call-start = ((), (), s32[]{:S(2)}) async-start(), calls=%async_computation.33 | async-start | bytes 3538944 | tf_op jit(solution)/shard_map/reduce_scatter | solution.py:415
  1144.4 157.6 %copy-start.109 = (f32[1024]{0:T(1024)S(1)}, f32[1024]{0:T(1024)}, u32[]{:S(2)}) copy-start(f32[1024]{0:T(1024)} %get-tuple-element.54) | copy-start | bytes 12292
  1144.4 202.0 %copy-start.27 = (bf16[1024,256]{1,0:T(8,128)(2,1)S(1)}, bf16[1024,256]{1,0:T(8,128)(2,1)}, u32[]{:S(2)}) copy-start(bf16[1024,256]{1,0:T(8,128)(2,1)} %reduce-scatter.26.cloned.1.call-done) | copy-start | bytes 1572868
  1144.4 202.0 %copy-start.30 = (bf16[1024,256]{1,0:T(8,128)(2,1)S(1)}, bf16[1024,256]{1,0:T(8,128)(2,1)}, u32[]{:S(2)}) copy-start(bf16[1024,256]{1,0:T(8,128)(2,1)} %reduce-scatter.28.cloned.1.call-done) | copy-start | bytes 1572868
  (84 other events, 316.7 us)
Sparse Core Ops, SparseCore 0:
  11.0 82.8 all-gather.16
  106.2 75.2 reduce-scatter.17
  301.8 76.3 reduce-scatter.19
  487.2 75.3 reduce-scatter.21
  744.0 43.2 reduce-scatter.25
  789.4 45.0 all-gather.26
  866.7 42.5 reduce-scatter.27
  911.6 45.0 all-gather.28
  977.5 42.5 reduce-scatter.29
Sparse Core Ops, SparseCore 1:
  109.9 37.7 all-gather.32
  183.9 81.0 all-gather.18
  267.5 28.1 all-gather.34
  380.7 81.1 all-gather.20
  490.5 37.7 all-gather.36
  565.0 81.0 all-gather.22
  647.6 43.9 all-gather.24
  694.1 28.5 all-gather.38
  1022.3 44.9 all-gather.30
  1069.5 75.1 reduce-scatter.23
  1148.0 36.6 reduce-scatter.39
  1188.6 53.9 reduce-scatter.49
  1245.9 53.7 reduce-scatter.47
  1302.1 44.2 reduce-scatter.31
  1349.9 75.8 reduce-scatter.45
  1429.2 76.3 reduce-scatter.43
  1509.4 35.7 reduce-scatter.41
  1548.9 35.9 reduce-scatter.37
  1588.5 35.9 reduce-scatter.35
  1628.4 46.2 reduce-scatter.33
where the time goes:
time: 1690 us; the launch traced here: 1680 us
  waiting for transfers between devices  1310 us (78%)
  matrix products  162 us (10%)
  other arithmetic  77.9 us (5%)
  local copies, waits for them, and re-layouts  65.3 us (4%)
  blocking collectives  42.7 us (3%)
  between operations  17.4 us (1%)
    all_gather x4, waiting for transfers between devices, widen(): return lax.all_gather(shard, 'tensor', axis=1, tiled=True)  306 us
    reduce_scatter x4, waiting for transfers between devices, narrow(): lax.psum_scatter(partial_sum, 'tensor', scatter_dimension=1, tiled=True)  222 us
    reduce_scatter x2, waiting for transfers between devices, sum_ffn_grads(): lax.psum_scatter(local_grads[0], 'dp', scatter_dimension=0, tiled=True)  157 us
    all_gather x4, waiting for transfers between devices, widen_grad(): lax.all_gather(gradient.astype(jnp.bfloat16), 'tensor', axis=1, tiled=True)  137 us
    reduce_scatter x4, waiting for transfers between devices, narrow_grad(): lax.psum_scatter(partial_grad.astype(jnp.bfloat16), 'tensor', scatter_dim...  130 us
    reduce_scatter x2, waiting for transfers between devices, sum_ffn_grads(): lax.psum_scatter(local_grads[1], 'dp', scatter_dimension=1, tiled=True)  113 us
    reduce_scatter x1, waiting for transfers between devices, local(): lax.psum_scatter(conv_in_grad, 'dp', scatter_dimension=0, tiled=True)  50.3 us
    all_gather x2, waiting for transfers between devices, fetch_ffn(): lax.all_gather(down[layer_index], 'dp', axis=1, tiled=True)  45.4 us
  transfers between devices with their start and end apart: 29, of which 27 were waited for; matrix products, arithmetic and copies ran while one was open for 10% of the time, Pallas kernels for 0%

commit v1 on v0

v1 whole, which is shorter than its diff:
```python
import jax
import jax.numpy as jnp
from jax import lax
from jax.sharding import Mesh, PartitionSpec as P

epsilon = 1e-05
rope_base = 1000000.0
TP = ("c", "zl")
DP = ("r", "zh")
BF = jnp.bfloat16
F32 = jnp.float32


def doc_layout(lengths_row, length):
    count = lengths_row.shape[0]
    upto = jnp.arange(count)[:, None] >= jnp.arange(count)[None, :]
    doc_ends = jnp.sum(jnp.where(upto, lengths_row[None, :], 0), axis=1)
    places = jnp.arange(length, dtype=jnp.int32)
    passed = places[:, None] >= doc_ends[None, :]
    segment = jnp.sum(passed.astype(jnp.int32), axis=1)
    doc_start = jnp.max(jnp.where(passed, doc_ends[None, :], 0), axis=1)
    return (segment, places - doc_start)


def rope_tables(position, head_dim):
    half_dim = head_dim // 2
    inverse = rope_base ** (-2.0 * jnp.arange(half_dim, dtype=F32) / head_dim)
    angles = position.astype(F32)[:, None] * inverse[None, :]
    return (jnp.cos(angles)[:, None, :], jnp.sin(angles)[:, None, :])


def rotate(values, tables):
    cosine, sine = tables
    half_dim = values.shape[-1] // 2
    first_half, second_half = (values[..., :half_dim], values[..., half_dim:])
    return jnp.concatenate(
        [first_half * cosine - second_half * sine, second_half * cosine + first_half * sine],
        axis=-1,
    )


def rotate_back(gradient, tables):
    cosine, sine = tables
    half_dim = gradient.shape[-1] // 2
    first_half, second_half = (gradient[..., :half_dim], gradient[..., half_dim:])
    return jnp.concatenate(
        [first_half * cosine + second_half * sine, second_half * cosine - first_half * sine],
        axis=-1,
    )


def shift_down(values, offset):
    filler = jnp.zeros((offset,) + values.shape[1:], values.dtype)
    return jnp.concatenate([filler, values[: values.shape[0] - offset]], axis=0)


def shift_up(values, offset):
    filler = jnp.zeros((offset,) + values.shape[1:], values.dtype)
    return jnp.concatenate([values[offset:], filler], axis=0)


def rms_forward(values, norm_gain):
    inverse = lax.rsqrt(jnp.mean(values * values, axis=-1, keepdims=True) + epsilon)
    return (values * inverse * norm_gain, inverse)


def rms_backward(upstream, values, inverse, norm_gain):
    scaled = upstream * norm_gain
    inner = jnp.mean(scaled * values, axis=-1, keepdims=True)
    grad_values = inverse * scaled - values * inverse**3 * inner
    leading = tuple(range(values.ndim - 1))
    grad_gain = jnp.sum(upstream * values * inverse, axis=leading)
    return (grad_values, grad_gain)


def dot(a, b):
    return jnp.dot(a, b, preferred_element_type=F32)


def swap(x):
    return lax.ppermute(x, ("c", "zh"), [(0, 0), (1, 2), (2, 1), (3, 3)])


def gather_rows(block):
    return lax.all_gather(block, TP, axis=0, tiled=True)


def scatter_rows(partial):
    return lax.psum_scatter(partial.astype(BF), TP, scatter_dimension=0, tiled=True).astype(F32)


def gather_dp(shard, axis):
    return lax.all_gather(shard, DP, axis=axis, tiled=True)


def scatter_dp(partial, axis):
    return lax.psum_scatter(partial.astype(BF), DP, scatter_dimension=axis, tiled=True)


def conv_local(normed, conv_in, conv_kernel, same):
    projected = dot(normed, conv_in)
    width = conv_kernel.shape[1]
    gated = projected[:, :width] * projected[:, 2 * width :]
    summed = conv_kernel[0] * gated
    for offset in range(1, conv_kernel.shape[0]):
        summed = summed + conv_kernel[offset] * jnp.where(
            same[offset][:, None], shift_down(gated, offset), 0.0
        )
    mixed = (projected[:, width : 2 * width] * summed).astype(BF)
    return projected, summed, mixed


def ffn_local(normed, w, v):
    hidden = dot(normed, w)
    half = hidden.shape[1] // 2
    active = (jax.nn.silu(hidden[:, :half]) * hidden[:, half:]).astype(BF)
    return hidden, active, dot(active, v)


def local(
    tokens, doc_lengths, grad_out, norm_gains, head_gains, conv_in, conv_kernel, conv_out,
    query_w, kv_w, out_w, gate_up, down,
):
    length = tokens.shape[0]
    head_dim = head_gains.shape[1]
    quarter = lax.axis_index("c") * 2 + lax.axis_index("zl")
    group = 4
    rows = length // group
    segment, position = doc_layout(swap(doc_lengths)[0], length)
    places = jnp.arange(length, dtype=jnp.int32)
    same = [None] + [position >= j for j in range(1, conv_kernel.shape[0])]
    tables = rope_tables(position, head_dim)
    conv_in = swap(conv_in.reshape(conv_in.shape[0], -1))
    conv_kernel = swap(conv_kernel)
    conv_out = swap(conv_out)
    query_w = swap(query_w)
    kv_w = swap(kv_w.reshape(kv_w.shape[0], -1))
    out_w = swap(out_w)
    ws = [gather_dp(swap(gate_up[l].reshape(gate_up.shape[1], -1)), 0) for l in (0, 1)]
    vs = [gather_dp(swap(down[l]), 1) for l in (0, 1)]

    x_full = lax.all_gather(swap(tokens), TP, axis=1, tiled=True)
    up_full = lax.all_gather(swap(grad_out), TP, axis=1, tiled=True)
    my = lambda a: lax.dynamic_slice_in_dim(a, quarter * rows, rows, 0)
    n0 = rms_forward(x_full.astype(F32), norm_gains[0])[0].astype(BF)
    h0 = my(x_full).astype(F32)
    projected, summed, mixed = conv_local(n0, conv_in, conv_kernel, same)
    h1 = h0 + scatter_rows(dot(mixed, conv_out))
    n1 = gather_rows(rms_forward(h1, norm_gains[1])[0].astype(BF))
    hidden0, active0, part = ffn_local(n1, ws[0], vs[0])
    h2 = h1 + scatter_rows(part)
    n2 = gather_rows(rms_forward(h2, norm_gains[2])[0].astype(BF))

    kv_heads = kv_w.shape[1] // 2 // head_dim
    qr = dot(n2, query_w).reshape(length, -1, head_dim)
    pair = dot(n2, kv_w).reshape(length, 2, kv_heads, head_dim)
    qn, qinv = rms_forward(qr, head_gains[0])
    kn, kinv = rms_forward(pair[:, 0], head_gains[1])
    q = rotate(qn, tables).astype(BF)
    k = rotate(kn, tables).astype(BF)
    v = pair[:, 1].astype(BF)
    groups = q.shape[1] // kv_heads
    scale = head_dim ** (-0.5)
    q4 = q.reshape(length, kv_heads, groups, head_dim)
    allowed = (places[None, :] <= places[:, None]) & (segment[None, :] == segment[:, None])
    scores = jnp.einsum("bkgd,skd->kgbs", q4, k, preferred_element_type=F32) * scale
    scores = jnp.where(allowed, scores, -1e30)
    top = jnp.max(scores, axis=-1, keepdims=True)
    weights = jnp.exp(scores - top)
    probs = weights / jnp.sum(weights, axis=-1, keepdims=True)
    probs_low = probs.astype(BF)
    o = jnp.einsum("kgbs,skd->bkgd", probs_low, v, preferred_element_type=F32)
    o = o.reshape(length, -1).astype(BF)
    h3 = h2 + scatter_rows(dot(o, out_w))
    n3 = gather_rows(rms_forward(h3, norm_gains[3])[0].astype(BF))
    hidden1, active1, part = ffn_local(n3, ws[1], vs[1])
    h4 = h3 + scatter_rows(part)
    output = swap(lax.all_to_all(h4.astype(BF), TP, 1, 0, tiled=True))

    def ffn_back(gathered, dh, h, normed, hidden, active, w, vv, gain):
        grad_active = dot(gathered, vv.T)
        grad_down = dot(active.T, gathered)
        half = hidden.shape[1] // 2
        gate, upp = hidden[:, :half], hidden[:, half:]
        s = jax.nn.sigmoid(gate)
        grad_hidden = jnp.concatenate(
            [grad_active * upp * s * (1.0 + gate * (1.0 - s)), grad_active * (gate * s)], axis=1
        ).astype(BF)
        grad_w = dot(normed.T, grad_hidden)
        dn = scatter_rows(dot(grad_hidden, w.T))
        inverse = rms_forward(h, gain)[1]
        term, grad_gain = rms_backward(dn, h, inverse, gain)
        return dh + term, grad_gain, grad_w, grad_down

    dh4 = my(up_full).astype(F32)
    dh3, gain3, gw1, gv1 = ffn_back(up_full, dh4, h3, n3, hidden1, active1, ws[1], vs[1], norm_gains[3])
    dz = gather_rows(dh3.astype(BF))
    grad_out_w = dot(o.T, dz)
    do = dot(dz, out_w.T).astype(BF).reshape(length, kv_heads, groups, head_dim)
    dp = jnp.einsum("bkgd,skd->kgbs", do, v, preferred_element_type=F32)
    inner = jnp.sum(probs * dp, axis=-1, keepdims=True)
    ds = (probs * (dp - inner)).astype(BF)
    dq = jnp.einsum("kgbs,skd->bkgd", ds, k, preferred_element_type=F32) * scale
    dk = jnp.einsum("kgbs,bkgd->skd", ds, q4, preferred_element_type=F32) * scale
    dv = jnp.einsum("kgbs,bkgd->skd", probs_low, do, preferred_element_type=F32)
    dq = dq.reshape(length, -1, head_dim)
    dqr, gq = rms_backward(rotate_back(dq, tables), qr, qinv, head_gains[0])
    dkr, gk = rms_backward(rotate_back(dk, tables), pair[:, 0], kinv, head_gains[1])
    dqr = dqr.astype(BF).reshape(length, -1)
    dpair = jnp.concatenate([dkr.reshape(length, -1), dv.reshape(length, -1)], axis=1).astype(BF)
    gqw = dot(n2.T, dqr)
    gkvw = dot(n2.T, dpair)
    dn2 = scatter_rows(dot(dqr, query_w.T) + dot(dpair, kv_w.T))
    term, gain2 = rms_backward(dn2, h2, rms_forward(h2, norm_gains[2])[1], norm_gains[2])
    dh2 = dh3 + term
    dh1, gain1, gw0, gv0 = ffn_back(
        gather_rows(dh2.astype(BF)), dh2, h1, n1, hidden0, active0, ws[0], vs[0], norm_gains[1]
    )
    dz = gather_rows(dh1.astype(BF))
    gco = dot(mixed.T, dz)
    dy = dot(dz, conv_out.T)
    width = conv_kernel.shape[1]
    gb, gc, gx = (projected[:, i * width : (i + 1) * width] for i in range(3))
    gated = gb * gx
    grad_c = dy * summed
    gs = dy * gc
    gg = conv_kernel[0] * gs
    kernel_rows = [jnp.sum(gs * gated, axis=0)]
    for offset in range(1, conv_kernel.shape[0]):
        masked = jnp.where(same[offset][:, None], gs, 0.0)
        gg = gg + conv_kernel[offset] * shift_up(masked, offset)
        kernel_rows.append(jnp.sum(masked * shift_down(gated, offset), axis=0))
    dprojected = jnp.concatenate([gg * gx, grad_c, gg * gb], axis=1).astype(BF)
    gci = dot(n0.T, dprojected)
    dn0 = scatter_rows(dot(dprojected, conv_in.T))
    term, gain0 = rms_backward(dn0, h0, rms_forward(h0, norm_gains[0])[1], norm_gains[0])
    dh0 = dh1 + term
    grad_tokens = swap(lax.all_to_all(dh0, TP, 1, 0, tiled=True))

    back = lambda g, axis: swap(scatter_dp(g, axis)).astype(F32)
    kernel_full = jnp.zeros((conv_kernel.shape[0], norm_gains.shape[1]), F32)
    kernel_full = lax.dynamic_update_slice_in_dim(
        kernel_full, jnp.stack(kernel_rows), quarter * width, 1
    )
    gains, heads, kernels = lax.psum(
        (jnp.stack([gain0, gain1, gain2, gain3]), jnp.stack([gq, gk]), kernel_full),
        ("r", "c", "zh", "zl"),
    )
    eighth = gate_up.shape[1]
    return (
        output,
        grad_tokens,
        gains,
        heads,
        back(gci, 0).reshape(-1, 3, width),
        kernels,
        back(gco, 1),
        back(gqw, 0),
        back(gkvw, 0).reshape(-1, 2, kv_heads * head_dim),
        back(grad_out_w, 1),
        jnp.stack([back(gw0, 0), back(gw1, 0)]).reshape(2, eighth, 2, -1),
        jnp.stack([back(gv0, 1), back(gv1, 1)]),
    )


def solution(mesh):
    devices = mesh.devices
    dp, tp = devices.shape
    inner = Mesh(devices.reshape(dp // 2, 2, 2, tp // 2), ("r", "c", "zh", "zl"))
    D = ("r", "c")
    T = ("zh", "zl")
    return jax.shard_map(
        local,
        mesh=inner,
        in_specs=(
            P(D, T), P(D, None), P(D, T), P(), P(), P(None, None, T), P(None, T), P(T, None),
            P(None, T), P(None, None, T), P(T, None), P(None, D, None, T), P(None, T, D),
        ),
        out_specs=(
            P(D, T), P(D, T), P(), P(), P(D, None, T), P(), P(T, D), P(D, T), P(D, None, T),
            P(T, D), P(None, D, None, T), P(None, T, D),
        ),
        check_vma=False,
    )
```

time: 1690 us -> 1840 us (1.089)
  starting transfers between devices: 2.6 us -> 98.1 us
  waiting for transfers between devices: 1310 us -> 1370 us
  matrix products: 162 us -> 188 us
  other arithmetic: 77.9 us -> 57.8 us
    reduce_scatter x17 -> x13, waiting for transfers between devices: 824 us -> 530 us  [the longest x8 270 us: scatter_rows(): lax.psum_scatter(partial.astype(BF), TP, scatter_dimension=0, tiled=True)]
    unnamed x29 -> x33, waiting for transfers between devices: 1.51 us -> 189 us
    ppermute x0 -> x24, waiting for transfers between devices: none -> 146 us  [swap(): return lax.ppermute(x, ('c', 'zh'), [(0, 0), (1, 2), (2, 1), (3, 3)])]
    ppermute x0 -> x24, starting transfers between devices: none -> 86.4 us  [swap(): return lax.ppermute(x, ('c', 'zh'), [(0, 0), (1, 2), (2, 1), (3, 3)])]
    dot_general x39 -> x32, matrix products: 162 us -> 176 us  [the longest x27 144 us: dot(): return jnp.dot(a, b, preferred_element_type=F32)]
    convert_element_type x19 -> x13, other arithmetic: 41.8 us -> 28.9 us  [the longest x1 8.47 us: local(): ds = (probs * (dp - inner)).astype(BF)]
    unnamed x244 -> x201, local copies, waits for them, and re-layouts: 34.5 us -> 42.2 us
  transfers between devices with their start and end apart: 29 -> 55, of which waited for: 27 -> 40; matrix products, arithmetic and copies ran while one was open for 10% -> 9% of each run, Pallas kernels for 0% -> 0%
where the time goes in v1:
time: 1840 us; the launch traced here: 1830 us
  waiting for transfers between devices  1370 us (74%)
  matrix products  188 us (10%)
  starting transfers between devices  98.1 us (5%)
  other arithmetic  57.8 us (3%)
  local copies, waits for them, and re-layouts  56.7 us (3%)
  blocking collectives  37.6 us (2%)
    reduce_scatter x8, waiting for transfers between devices, scatter_rows(): lax.psum_scatter(partial.astype(BF), TP, scatter_dimension=0, tiled=True)  270 us
    reduce_scatter x5, waiting for transfers between devices, scatter_dp(): lax.psum_scatter(partial.astype(BF), DP, scatter_dimension=axis, tiled=True)  260 us
    all_gather x6, waiting for transfers between devices, gather_rows(): return lax.all_gather(block, TP, axis=0, tiled=True)  258 us
    unnamed x33, waiting for transfers between devices  189 us
    all_gather x4, waiting for transfers between devices, gather_dp(): return lax.all_gather(shard, DP, axis=axis, tiled=True)  177 us
    ppermute x24, waiting for transfers between devices, swap(): return lax.ppermute(x, ('c', 'zh'), [(0, 0), (1, 2), (2, 1), (3, 3)])  146 us
    dot_general x27, matrix products, dot(): return jnp.dot(a, b, preferred_element_type=F32)  144 us
    ppermute x24, starting transfers between devices, swap(): return lax.ppermute(x, ('c', 'zh'), [(0, 0), (1, 2), (2, 1), (3, 3)])  86.4 us
  transfers between devices with their start and end apart: 55, of which 40 were waited for; matrix products, arithmetic and copies ran while one was open for 9% of the time, Pallas kernels for 0%

profile of v1, /device:TPU:1, one launch (start us, length us, event | category | flops | bytes accessed | tf_op | source)
XLA Modules:
  0.0 1829.7 jit_solution(12708159388996510701)
XLA Ops:
  8.1 5.6 collective-permute-start
  13.7 12.7 collective-permute-done
  42.6 23.3 %collective-permute-done.3 = s32[1,6]{1,0:T(1,128)S(1)} collective-permute-done((s32[1,6]{1,0:T(1,128)S(1)}, s32[1,6]{1,0:T(1,128)S(1)}, u32[]{:S(2)}, u32[]{:S(2)}) %collective-permute-start.3) | collective-permute-done | bytes 56 | tf_op jit(solution)/shard_map/ppermute | solution.py:81
  66.2 27.4 %all-gather.13.cloned.1.call-done = bf16[1024,1024]{1,0:T(8,128)(2,1)} async-done(((bf16[1024,256]{1,0:T(8,128)(2,1)}), bf16[1024,1024]{1,0:T(8,128)(2,1)}) %all-gather.13.cloned.1.call-update) | async-done | bytes 2097168 | tf_op jit(solution)/shard_map/all_gather | solution.py:142
  111.2 19.4 %collective-permute-done.5 = bf16[128,2304]{1,0:T(8,128)(2,1)S(1)} collective-permute-done((bf16[128,2304]{1,0:T(8,128)(2,1)S(1)}, bf16[128,2304]{1,0:T(8,128)(2,1)S(1)}, u32[]{:S(2)}, u32[]{:S(2)}) %collective-permute-start.5) | collective-permute-done | bytes 589856 | tf_op jit(solution)/shard_map/ppermute | solution.py:81
  131.5 27.7 %reduce-scatter.26.cloned.1.call-done = bf16[256,1024]{1,0:T(8,128)(2,1)} async-done(((bf16[1024,1024]{1,0:T(8,128)(2,1)}), bf16[256,1024]{1,0:T(8,128)(2,1)}) %reduce-scatter.26.cloned.1.call-update) | async-done | bytes 524304 | tf_op jit(solution)/shard_map/reduce_scatter | solution.py:89
  168.4 16.7 collective-permute-done.6
  186.1 41.3 %all-gather.17.cloned.1.call-done = bf16[1024,2304]{1,0:T(8,128)(2,1)} async-done(((bf16[128,2304]{1,0:T(8,128)(2,1)}), bf16[1024,2304]{1,0:T(8,128)(2,1)}) %all-gather.17.cloned.1.call-update) | async-done | bytes 4718608 | tf_op jit(solution)/shard_map/all_gather | solution.py:93
  227.4 44.8 %all-gather.15.cloned.1.call-done = bf16[1024,1024]{1,0:T(8,128)(2,1)} async-done(((bf16[256,1024]{1,0:T(8,128)(2,1)}), bf16[1024,1024]{1,0:T(8,128)(2,1)}) %all-gather.15.cloned.1.call-update) | async-done | bytes 2097168 | tf_op jit(solution)/shard_map/all_gather | solution.py:85
  272.2 8.0 fusion.112
  286.4 56.2 %all-gather.19.cloned.1.call-done = bf16[1152,1024]{1,0:T(8,128)(2,1)} async-done(((bf16[1152,128]{1,0:T(8,128)(2,1)}), bf16[1152,1024]{1,0:T(8,128)(2,1)}) %all-gather.19.cloned.1.call-update) | async-done | bytes 2359312 | tf_op jit(solution)/shard_map/all_gather | solution.py:93
  342.6 6.6 convolution_convert_fusion.5
  349.3 42.0 %reduce-scatter.28.cloned.1.call-done = bf16[256,1024]{1,0:T(8,128)(2,1)} async-done(((bf16[1024,1024]{1,0:T(8,128)(2,1)}), bf16[256,1024]{1,0:T(8,128)(2,1)}) %reduce-scatter.28.cloned.1.call-update) | async-done | bytes 524304 | tf_op jit(solution)/shard_map/reduce_scatter | solution.py:89
  402.1 4.9 collective-permute-start.9
  409.8 4.9 collective-permute-done.7
  414.6 40.5 %all-gather.21.cloned.1.call-done = bf16[1024,1024]{1,0:T(8,128)(2,1)} async-done(((bf16[256,1024]{1,0:T(8,128)(2,1)}), bf16[1024,1024]{1,0:T(8,128)(2,1)}) %all-gather.21.cloned.1.call-update) | async-done | bytes 2097168 | tf_op jit(solution)/shard_map/all_gather | solution.py:85
  463.0 11.7 fusion.111
  474.7 7.3 fusion.24
  488.1 15.3 collective-permute-done.10
  504.3 35.5 %reduce-scatter.30.cloned.1.call-done = bf16[256,1024]{1,0:T(8,128)(2,1)} async-done(((bf16[1024,1024]{1,0:T(8,128)(2,1)}), bf16[256,1024]{1,0:T(8,128)(2,1)}) %reduce-scatter.30.cloned.1.call-update) | async-done | bytes 524304 | tf_op jit(solution)/shard_map/reduce_scatter | solution.py:89
  546.2 15.3 collective-permute-done.13
  564.3 30.5 %collective-permute-done.11 = bf16[1152,128]{1,0:T(8,128)(2,1)S(1)} collective-permute-done((bf16[1152,128]{1,0:T(8,128)(2,1)S(1)}, bf16[1152,128]{1,0:T(8,128)(2,1)S(1)}, u32[]{:S(2)}, u32[]{:S(2)}) %collective-permute-start.11) | collective-permute-done | bytes 294944 | tf_op jit(solution)/shard_map/ppermute | solution.py:81
  595.8 8.5 all-gather.25.cloned.1.call-done
  604.3 44.4 %all-gather.23.cloned.1.call-done = bf16[1024,1024]{1,0:T(8,128)(2,1)} async-done(((bf16[256,1024]{1,0:T(8,128)(2,1)}), bf16[1024,1024]{1,0:T(8,128)(2,1)}) %all-gather.23.cloned.1.call-update) | async-done | bytes 2097168 | tf_op jit(solution)/shard_map/all_gather | solution.py:85
  648.7 10.1 fusion.114
  658.7 35.2 %all-gather.29.cloned.1.call-done = bf16[1024,1024]{1,0:T(8,128)(2,1)} async-done(((bf16[1024,256]{1,0:T(8,128)(2,1)}), bf16[1024,1024]{1,0:T(8,128)(2,1)}) %all-gather.29.cloned.1.call-update) | async-done | bytes 2097168 | tf_op jit(solution)/shard_map/all_gather | solution.py:143
  693.9 70.9 %all-gather.27.cloned.1.call-done = bf16[1152,1024]{1,0:T(8,128)(2,1)} async-done(((bf16[1152,128]{1,0:T(8,128)(2,1)}), bf16[1152,1024]{1,0:T(8,128)(2,1)}) %all-gather.27.cloned.1.call-update) | async-done | bytes 2359312 | tf_op jit(solution)/shard_map/all_gather | solution.py:93
  764.9 10.7 multiply_convert_fusion.3
  777.8 8.7 fusion.22
  786.5 42.0 %reduce-scatter.34.cloned.1.call-done = bf16[256,1024]{1,0:T(8,128)(2,1)} async-done(((bf16[1024,1024]{1,0:T(8,128)(2,1)}), bf16[256,1024]{1,0:T(8,128)(2,1)}) %reduce-scatter.34.cloned.1.call-update) | async-done | bytes 524304 | tf_op jit(solution)/shard_map/reduce_scatter | solution.py:89
  835.5 41.5 %all-gather.31.cloned.1.call-done = bf16[1024,1024]{1,0:T(8,128)(2,1)} async-done(((bf16[256,1024]{1,0:T(8,128)(2,1)}), bf16[1024,1024]{1,0:T(8,128)(2,1)}) %all-gather.31.cloned.1.call-update) | async-done | bytes 2097168 | tf_op jit(solution)/shard_map/all_gather | solution.py:85
  880.3 9.4 fusion.39
  889.9 9.5 fusion.1
  899.4 8.5 fusion.3
  919.8 6.6 convolution_convert_fusion.4
  926.4 36.2 %reduce-scatter.36.cloned.1.call-done = bf16[256,1024]{1,0:T(8,128)(2,1)} async-done(((bf16[1024,1024]{1,0:T(8,128)(2,1)}), bf16[256,1024]{1,0:T(8,128)(2,1)}) %reduce-scatter.36.cloned.1.call-update) | async-done | bytes 524304 | tf_op jit(solution)/shard_map/reduce_scatter | solution.py:89
  964.0 43.8 %reduce-scatter.32.cloned.1.call-done = bf16[256,1024]{1,0:T(8,128)(2,1)} async-done(((bf16[1024,1024]{1,0:T(8,128)(2,1)}), bf16[256,1024]{1,0:T(8,128)(2,1)}) %reduce-scatter.32.cloned.1.call-update) | async-done | bytes 524304 | tf_op jit(solution)/shard_map/reduce_scatter | solution.py:89
  1011.8 43.2 %all-gather.33.cloned.1.call-done = bf16[1024,1024]{1,0:T(8,128)(2,1)} async-done(((bf16[256,1024]{1,0:T(8,128)(2,1)}), bf16[1024,1024]{1,0:T(8,128)(2,1)}) %all-gather.33.cloned.1.call-update) | async-done | bytes 2097168 | tf_op jit(solution)/shard_map/all_gather | solution.py:85
  1055.0 9.2 multiply_convert_fusion.1
  1066.4 8.7 fusion.23
  1075.2 43.0 %reduce-scatter.38.cloned.1.call-done = bf16[256,1024]{1,0:T(8,128)(2,1)} async-done(((bf16[1024,1024]{1,0:T(8,128)(2,1)}), bf16[256,1024]{1,0:T(8,128)(2,1)}) %reduce-scatter.38.cloned.1.call-update) | async-done | bytes 524304 | tf_op jit(solution)/shard_map/reduce_scatter | solution.py:89
  1123.1 43.6 %all-gather.35.cloned.1.call-done = bf16[1024,1024]{1,0:T(8,128)(2,1)} async-done(((bf16[256,1024]{1,0:T(8,128)(2,1)}), bf16[1024,1024]{1,0:T(8,128)(2,1)}) %all-gather.35.cloned.1.call-update) | async-done | bytes 2097168 | tf_op jit(solution)/shard_map/all_gather | solution.py:85
  1178.6 9.5 convolution_convert_fusion
  1195.1 6.5 convolution_convert_fusion.2
  1206.0 6.4 convolution_convert_fusion.3
  1220.1 9.5 convolution_convert_fusion.1
  1234.3 4.6 convolution_convert_fusion.9
  1240.9 4.9 all-to-all-start
  1249.6 10.5 all-to-all-done
  1264.5 48.3 %reduce-scatter.50.cloned.1.call-done = bf16[128,2304]{1,0:T(8,128)(2,1)} async-done(((bf16[1024,2304]{1,0:T(8,128)(2,1)}), bf16[128,2304]{1,0:T(8,128)(2,1)}) %reduce-scatter.50.cloned.1.call-update) | async-done | bytes 589840 | tf_op jit(solution)/shard_map/reduce_scatter | solution.py:97
  1319.3 38.7 %reduce-scatter.54.cloned.1.call-done = bf16[128,256]{1,0:T(8,128)(2,1)} async-done(((bf16[1024,256]{1,0:T(8,128)(2,1)}), bf16[128,256]{1,0:T(8,128)(2,1)}) %reduce-scatter.54.cloned.1.call-update) | async-done | bytes 65552
  1359.0 5.5 collective-permute-start.19
  1364.5 32.6 %reduce-scatter.44.cloned.1.call-done = bf16[128,256]{1,0:T(8,128)(2,1)} async-done(((bf16[1024,256]{1,0:T(8,128)(2,1)}), bf16[128,256]{1,0:T(8,128)(2,1)}) %reduce-scatter.44.cloned.1.call-update) | async-done | bytes 65552 | tf_op jit(solution)/shard_map/reduce_scatter | solution.py:97
  1397.1 6.2 collective-permute-start.17
  1403.3 59.2 %reduce-scatter.58.cloned.1.call-done = bf16[128,1152]{1,0:T(8,128)(2,1)} async-done(((bf16[1024,1152]{1,0:T(8,128)(2,1)}), bf16[128,1152]{1,0:T(8,128)(2,1)}) %reduce-scatter.58.cloned.1.call-update) | async-done | bytes 294928
  1466.2 58.1 %reduce-scatter.56.cloned.1.call-done = bf16[128,1152]{1,0:T(8,128)(2,1)} async-done(((bf16[1024,1152]{1,0:T(8,128)(2,1)}), bf16[128,1152]{1,0:T(8,128)(2,1)}) %reduce-scatter.56.cloned.1.call-update) | async-done | bytes 294928
  1528.1 33.1 %reduce-scatter.46.cloned.1.call-done = bf16[128,256]{1,0:T(8,128)(2,1)} async-done(((bf16[1024,256]{1,0:T(8,128)(2,1)}), bf16[128,256]{1,0:T(8,128)(2,1)}) %reduce-scatter.46.cloned.1.call-update) | async-done | bytes 65552 | tf_op jit(solution)/shard_map/reduce_scatter | solution.py:97
  1561.2 6.3 collective-permute-start.18
  1569.6 4.6 collective-permute-start.14
  1574.3 100.4 %reduce-scatter.48.cloned.1.call-done = bf16[128,2304]{1,0:T(8,128)(2,1)} async-done(((bf16[1024,2304]{1,0:T(8,128)(2,1)}), bf16[128,2304]{1,0:T(8,128)(2,1)}) %reduce-scatter.48.cloned.1.call-update) | async-done | bytes 589840 | tf_op jit(solution)/shard_map/reduce_scatter | solution.py:97
  1681.1 32.9 %reduce-scatter.52.cloned.1.call-done = bf16[128,256]{1,0:T(8,128)(2,1)} async-done(((bf16[1024,256]{1,0:T(8,128)(2,1)}), bf16[128,256]{1,0:T(8,128)(2,1)}) %reduce-scatter.52.cloned.1.call-update) | async-done | bytes 65552
  1714.9 5.4 collective-permute-start.16
  1724.9 45.7 %reduce-scatter.42.cloned.1.call-done = bf16[128,768]{1,0:T(8,128)(2,1)} async-done(((bf16[1024,768]{1,0:T(8,128)(2,1)}), bf16[128,768]{1,0:T(8,128)(2,1)}) %reduce-scatter.42.cloned.1.call-update) | async-done | bytes 196624 | tf_op jit(solution)/shard_map/reduce_scatter | solution.py:97
  1781.4 37.6 %all-reduce.4 = (f32[4,1024]{1,0:T(4,128)}, f32[2,64]{1,0:T(2,128)}, f32[3,1024]{1,0:T(4,128)}) all-reduce(f32[4,1024]{1,0:T(4,128)S(1)} %pad_maximum_fusion.26, f32[2,64]{1,0:T(2,128)S(1)} %pad_maximum_fusion.27, f32[3,1024]{1,0:T(4,128)S(1)} %maximum_dynamic-update-slice_fusion), channel_id=1, replica_groups=mesh['r'=4,'c'=2,'zh'=2,'zl'=2] {'r','c','zh','zl'}, use_global_device_ids=true, to_apply=%region_31.32 | all-reduce | flops 7296 | bytes 58368 | tf_op jit(solution)/shard_map/psum | solution.py:245
  (393 shorter events, 214.0 us)
Async XLA Ops:
  8.0 85.5 %all-gather.13.cloned.1.call-start = ((), (), s32[]{:S(2)}) async-start(), calls=%async_computation.19 | async-start | bytes 2621440 | tf_op jit(solution)/shard_map/all_gather | solution.py:142
  8.1 18.3 collective-permute-start
  27.2 132.0 %reduce-scatter.26.cloned.1.call-start = ((), (), s32[]{:S(2)}) async-start(), calls=%async_computation.20 | async-start | bytes 2621440 | tf_op jit(solution)/shard_map/reduce_scatter | solution.py:89
  29.0 66.7 %collective-permute-start.1 = (bf16[1024,768]{0,1:T(8,128)(2,1)S(1)}, bf16[1024,768]{0,1:T(8,128)(2,1)}, u32[]{:S(2)}, u32[]{:S(2)}) collective-permute-start(bf16[1024,768]{0,1:T(8,128)(2,1)S(1)} %bitcast.265), channel_id=1, source_target_pairs={{0,0},{2,4},{4,2},{6,6},{1,1},{3,5},{5,3},{7,7},{8,8},{10,12},{12,... | collective-permute-start | bytes 4718600 | tf_op jit(solution)/shard_map/ppermute | solution.py:81
  30.9 35.0 %collective-permute-start.3 = (s32[1,6]{1,0:T(1,128)S(1)}, s32[1,6]{1,0:T(1,128)S(1)}, u32[]{:S(2)}, u32[]{:S(2)}) collective-permute-start(s32[1,6]{1,0:T(1,128)S(1)} %copy-done.84), channel_id=1, source_target_pairs={{0,0},{2,4},{4,2},{6,6},{1,1},{3,5},{5,3},{7,7},{8,8},{10,12},{12,... | collective-permute-start | bytes 80 | tf_op jit(solution)/shard_map/ppermute | solution.py:81
  35.5 30.7 %collective-permute-start.2 = (f32[3,256]{1,0:T(4,128)S(1)}, f32[3,256]{1,0:T(4,128)S(1)}, u32[]{:S(2)}, u32[]{:S(2)}) collective-permute-start(f32[3,256]{1,0:T(4,128)S(1)} %copy-done.83), channel_id=1, source_target_pairs={{0,0},{2,4},{4,2},{6,6},{1,1},{3,5},{5,3},{7,7},{8,8},{10,12},{12,... | collective-permute-start | bytes 9224 | tf_op jit(solution)/shard_map/ppermute | solution.py:81
  37.4 64.5 %collective-permute-start.4 = (bf16[256,1024]{1,0:T(8,128)(2,1)}, bf16[256,1024]{1,0:T(8,128)(2,1)S(1)}, u32[]{:S(2)}, u32[]{:S(2)}) collective-permute-start(bf16[256,1024]{1,0:T(8,128)(2,1)} %param.20), channel_id=1, source_target_pairs={{0,0},{2,4},{4,2},{6,6},{1,1},{3,5},{5,3},{7,7},{8,8},{10,12},{12,... | collective-permute-start | bytes 1572872 | tf_op jit(solution)/shard_map/ppermute | solution.py:81
  42.6 118.5 %copy-start.42 = (f32[1,1024]{1,0:T(1,128)}, f32[1,1024]{1,0:T(1,128)S(1)}, u32[]{:S(2)}) copy-start(f32[1,1024]{1,0:T(1,128)S(1)} %get-tuple-element.121) | copy-start | bytes 12292
  42.6 350.9 %copy-start.39 = (f32[1,1024]{1,0:T(1,128)}, f32[1,1024]{1,0:T(1,128)S(1)}, u32[]{:S(2)}) copy-start(f32[1,1024]{1,0:T(1,128)S(1)} %get-tuple-element.120) | copy-start | bytes 12292
  104.7 122.7 %all-gather.17.cloned.1.call-start = ((), (), s32[]{:S(2)}) async-start(), calls=%async_computation.22 | async-start | bytes 5308416 | tf_op jit(solution)/shard_map/all_gather | solution.py:93
  107.9 22.8 %collective-permute-start.5 = (bf16[128,2304]{1,0:T(8,128)(2,1)S(1)}, bf16[128,2304]{1,0:T(8,128)(2,1)S(1)}, u32[]{:S(2)}, u32[]{:S(2)}) collective-permute-start(bf16[128,2304]{1,0:T(8,128)(2,1)S(1)} %bitcast.272), channel_id=1, source_target_pairs={{0,0},{2,4},{4,2},{6,6},{1,1},{3,5},{5,3},{7,7},{8,8},{10,12},{12,... | collective-permute-start | bytes 1769480 | tf_op jit(solution)/shard_map/ppermute | solution.py:81
  131.5 140.8 %all-gather.15.cloned.1.call-start = ((), (), s32[]{:S(2)}) async-start(), calls=%async_computation.21 | async-start | bytes 2621440 | tf_op jit(solution)/shard_map/all_gather | solution.py:85
  161.1 119.2 %copy-start.54 = (f32[256]{0:T(256)}, f32[256]{0:T(256)S(1)}, u32[]{:S(2)}) copy-start(f32[256]{0:T(256)S(1)} %get-tuple-element.136) | copy-start | bytes 3076
  163.1 179.5 %all-gather.19.cloned.1.call-start = ((), (), s32[]{:S(2)}) async-start(), calls=%async_computation.23 | async-start | bytes 2654208 | tf_op jit(solution)/shard_map/all_gather | solution.py:93
  165.0 20.1 %collective-permute-start.6 = (bf16[1152,128]{1,0:T(8,128)(2,1)S(1)}, bf16[1152,128]{1,0:T(8,128)(2,1)S(1)}, u32[]{:S(2)}, u32[]{:S(2)}) collective-permute-start(bf16[1152,128]{1,0:T(8,128)(2,1)S(1)} %get-tuple-element.116), channel_id=1, source_target_pairs={{0,0},{2,4},{4,2},{6,6},{1,1},{3,5},{5,3},{7,7},{8,8},{10,12},{12,... | collective-permute-start | bytes 884744 | tf_op jit(solution)/shard_map/ppermute | solution.py:81
  185.9 205.5 %reduce-scatter.28.cloned.1.call-start = ((), (), s32[]{:S(2)}) async-start(), calls=%async_computation.24 | async-start | bytes 2621440 | tf_op jit(solution)/shard_map/reduce_scatter | solution.py:89
  349.3 105.9 %all-gather.21.cloned.1.call-start = ((), (), s32[]{:S(2)}) async-start(), calls=%async_computation.25 | async-start | bytes 2621440 | tf_op jit(solution)/shard_map/all_gather | solution.py:85
  394.4 145.4 %reduce-scatter.30.cloned.1.call-start = ((), (), s32[]{:S(2)}) async-start(), calls=%async_computation.26 | async-start | bytes 2621440 | tf_op jit(solution)/shard_map/reduce_scatter | solution.py:89
  395.6 19.0 %collective-permute-start.7 = (bf16[1024,256]{1,0:T(8,128)(2,1)S(1)}, bf16[1024,256]{1,0:T(8,128)(2,1)S(1)}, u32[]{:S(2)}, u32[]{:S(2)}) collective-permute-start(bf16[1024,256]{1,0:T(8,128)(2,1)S(1)} %bitcast.275), channel_id=1, source_target_pairs={{0,0},{2,4},{4,2},{6,6},{1,1},{3,5},{5,3},{7,7},{8,8},{10,12},{12,... | collective-permute-start | bytes 1572872 | tf_op jit(solution)/shard_map/ppermute | solution.py:81
  400.2 58.3 %collective-permute-start.8 = (bf16[1024,256]{1,0:T(8,128)(2,1)}, bf16[1024,256]{1,0:T(8,128)(2,1)}, u32[]{:S(2)}, u32[]{:S(2)}) collective-permute-start(bf16[1024,256]{1,0:T(8,128)(2,1)} %param.21), channel_id=1, source_target_pairs={{0,0},{2,4},{4,2},{6,6},{1,1},{3,5},{5,3},{7,7},{8,8},{10,12},{12,... | collective-permute-start | bytes 1572872 | tf_op jit(solution)/shard_map/ppermute | solution.py:81
  402.1 80.0 %collective-permute-start.9 = (bf16[256,1024]{1,0:T(8,128)(2,1)}, bf16[256,1024]{1,0:T(8,128)(2,1)}, u32[]{:S(2)}, u32[]{:S(2)}) collective-permute-start(bf16[256,1024]{1,0:T(8,128)(2,1)} %param.23), channel_id=1, source_target_pairs={{0,0},{2,4},{4,2},{6,6},{1,1},{3,5},{5,3},{7,7},{8,8},{10,12},{12,... | collective-permute-start | bytes 1572872 | tf_op jit(solution)/shard_map/ppermute | solution.py:81
  486.0 118.2 %all-gather.25.cloned.1.call-start = ((), (), s32[]{:S(2)}) async-start(), calls=%async_computation.28 | async-start | bytes 5308416 | tf_op jit(solution)/shard_map/all_gather | solution.py:93
  486.2 17.3 collective-permute-start.10
  504.3 144.4 %all-gather.23.cloned.1.call-start = ((), (), s32[]{:S(2)}) async-start(), calls=%async_computation.27 | async-start | bytes 2621440 | tf_op jit(solution)/shard_map/all_gather | solution.py:85
  541.1 289.5 %copy-start.47 = (f32[256]{0:T(256)}, f32[256]{0:T(256)S(1)}, u32[]{:S(2)}) copy-start(f32[256]{0:T(256)S(1)} %get-tuple-element.140) | copy-start | bytes 3076
  541.1 289.5 %copy-start.56 = (f32[256]{0:T(256)}, f32[256]{0:T(256)S(1)}, u32[]{:S(2)}) copy-start(f32[256]{0:T(256)S(1)} %get-tuple-element.139) | copy-start | bytes 3076
  543.2 150.8 %all-gather.29.cloned.1.call-start = ((), (), s32[]{:S(2)}) async-start(), calls=%async_computation.31 | async-start | bytes 2621440 | tf_op jit(solution)/shard_map/all_gather | solution.py:143
  543.2 18.3 collective-permute-start.13
  562.3 202.6 %all-gather.27.cloned.1.call-start = ((), (), s32[]{:S(2)}) async-start(), calls=%async_computation.29 | async-start | bytes 2654208 | tf_op jit(solution)/shard_map/all_gather | solution.py:93
  562.4 32.5 %collective-permute-start.11 = (bf16[1152,128]{1,0:T(8,128)(2,1)S(1)}, bf16[1152,128]{1,0:T(8,128)(2,1)S(1)}, u32[]{:S(2)}, u32[]{:S(2)}) collective-permute-start(bf16[1152,128]{1,0:T(8,128)(2,1)S(1)} %copy-done.32), channel_id=1, source_target_pairs={{0,0},{2,4},{4,2},{6,6},{1,1},{3,5},{5,3},{7,7},{8,8},{10,12},{12,... | collective-permute-start | bytes 884744 | tf_op jit(solution)/shard_map/ppermute | solution.py:81
  595.6 233.0 %reduce-scatter.34.cloned.1.call-start = ((), (), s32[]{:S(2)}) async-start(), calls=%async_computation.32 | async-start | bytes 2621440 | tf_op jit(solution)/shard_map/reduce_scatter | solution.py:89
  786.5 90.5 %all-gather.31.cloned.1.call-start = ((), (), s32[]{:S(2)}) async-start(), calls=%async_computation.33 | async-start | bytes 2621440 | tf_op jit(solution)/shard_map/all_gather | solution.py:85
  833.0 129.7 %reduce-scatter.36.cloned.1.call-start = ((), (), s32[]{:S(2)}) async-start(), calls=%async_computation.34 | async-start | bytes 2621440 | tf_op jit(solution)/shard_map/reduce_scatter | solution.py:89
  919.7 88.2 %reduce-scatter.32.cloned.1.call-start = ((), (), s32[]{:S(2)}) async-start(), calls=%async_computation.30 | async-start | bytes 2621440 | tf_op jit(solution)/shard_map/reduce_scatter | solution.py:89
  926.3 81.5 %copy-start.57 = (f32[256]{0:T(256)S(1)}, f32[256]{0:T(256)}, u32[]{:S(2)}) copy-start(f32[256]{0:T(256)} %copy-done.56) | copy-start | bytes 3076
  926.3 81.5 %copy-start.59 = (f32[256]{0:T(256)S(1)}, f32[256]{0:T(256)}, u32[]{:S(2)}) copy-start(f32[256]{0:T(256)} %copy-done.58) | copy-start | bytes 3076
  926.3 81.5 %copy-start.76 = (f32[256]{0:T(256)S(1)}, f32[256]{0:T(256)}, u32[]{:S(2)}) copy-start(f32[256]{0:T(256)} %get-tuple-element.137) | copy-start | bytes 3076
  926.4 128.6 %all-gather.33.cloned.1.call-start = ((), (), s32[]{:S(2)}) async-start(), calls=%async_computation.35 | async-start | bytes 2621440 | tf_op jit(solution)/shard_map/all_gather | solution.py:85
  1011.3 106.9 %reduce-scatter.38.cloned.1.call-start = ((), (), s32[]{:S(2)}) async-start(), calls=%async_computation.36 | async-start | bytes 2621440 | tf_op jit(solution)/shard_map/reduce_scatter | solution.py:89
  1075.1 91.6 %copy-start.1 = (f32[1024,256]{1,0:T(8,128)S(1)}, f32[1024,256]{1,0:T(8,128)}, u32[]{:S(2)}) copy-start(f32[1024,256]{1,0:T(8,128)} %copy-done) | copy-start | bytes 3145732
  1075.1 91.5 %all-gather.35.cloned.1.call-start = ((), (), s32[]{:S(2)}) async-start(), calls=%async_computation.37 | async-start | bytes 2621440 | tf_op jit(solution)/shard_map/all_gather | solution.py:85
  1123.0 122.8 %reduce-scatter.40.cloned.1.call-start = ((), (), s32[]{:S(2)}) async-start(), calls=%async_computation.38 | async-start | bytes 2621440 | tf_op jit(solution)/shard_map/reduce_scatter | solution.py:89
  1178.5 134.3 %reduce-scatter.50.cloned.1.call-start = ((), (), s32[]{:S(2)}) async-start(), calls=%async_computation.43 | async-start | bytes 5308416 | tf_op jit(solution)/shard_map/reduce_scatter | solution.py:97
  1188.1 170.0 %reduce-scatter.54.cloned.1.call-start = ((), (), s32[]{:S(2)}) async-start(), calls=%async_computation.45 | async-start | bytes 589824
  1191.8 205.2 %reduce-scatter.44.cloned.1.call-start = ((), (), s32[]{:S(2)}) async-start(), calls=%async_computation.40 | async-start | bytes 589824 | tf_op jit(solution)/shard_map/reduce_scatter | solution.py:97
  1195.0 267.4 %reduce-scatter.58.cloned.1.call-start = ((), (), s32[]{:S(2)}) async-start(), calls=%async_computation.47 | async-start | bytes 2654208
  1206.0 318.3 %reduce-scatter.56.cloned.1.call-start = ((), (), s32[]{:S(2)}) async-start(), calls=%async_computation.46 | async-start | bytes 2654208
  1216.8 344.4 %reduce-scatter.46.cloned.1.call-start = ((), (), s32[]{:S(2)}) async-start(), calls=%async_computation.41 | async-start | bytes 589824 | tf_op jit(solution)/shard_map/reduce_scatter | solution.py:97
  1220.0 454.6 %reduce-scatter.48.cloned.1.call-start = ((), (), s32[]{:S(2)}) async-start(), calls=%async_computation.42 | async-start | bytes 5308416 | tf_op jit(solution)/shard_map/reduce_scatter | solution.py:97
  1229.7 484.3 %reduce-scatter.52.cloned.1.call-start = ((), (), s32[]{:S(2)}) async-start(), calls=%async_computation.44 | async-start | bytes 589824
  1234.0 536.5 %reduce-scatter.42.cloned.1.call-start = ((), (), s32[]{:S(2)}) async-start(), calls=%async_computation.39 | async-start | bytes 1769472 | tf_op jit(solution)/shard_map/reduce_scatter | solution.py:97
  1240.9 19.3 %all-to-all-start = ((bf16[256,4,256]{2,0,1:T(8,128)(2,1)}), bf16[256,4,256]{2,0,1:T(8,128)(2,1)}, u32[]{:S(2)}, u32[]{:S(2)}) async-start(bf16[256,4,256]{2,0,1:T(8,128)(2,1)} %bitcast.264), calls=%async_computation.4 | async-start | bytes 1048576 | tf_op jit(solution)/shard_map/all_to_all | solution.py:178
  1260.2 309.5 %all-to-all-start.1 = ((f32[256,4,256]{2,0,1:T(8,128)}), f32[256,4,256]{2,0,1:T(8,128)S(1)}, u32[]{:S(2)}, u32[]{:S(2)}) async-start(f32[256,4,256]{2,0,1:T(8,128)} %bitcast.238), calls=%async_computation.9 | async-start | bytes 2097152 | tf_op jit(solution)/shard_map/all_to_all | solution.py:238
  1312.9 261.4 %collective-permute-start.21 = (bf16[128,2304]{1,0:T(8,128)(2,1)}, bf16[128,2304]{1,0:T(8,128)(2,1)S(1)}, u32[]{:S(2)}, u32[]{:S(2)}) collective-permute-start(bf16[128,2304]{1,0:T(8,128)(2,1)} %reduce-scatter.50.cloned.1.call-done), channel_id=1, source_target_pairs={{0,0},{2,4},{4,2},{6,6},{1,1},{3,5},{5,3},{7,7},{8,8},{10,12},{12,... | collective-permute-start | bytes 1769480 | tf_op jit(solution)/shard_map/ppermute | solution.py:81
  1314.8 364.1 %collective-permute-start.12 = (bf16[1024,256]{1,0:T(8,128)(2,1)}, bf16[1024,256]{1,0:T(8,128)(2,1)}, u32[]{:S(2)}, u32[]{:S(2)}) collective-permute-start(bf16[1024,256]{1,0:T(8,128)(2,1)} %bitcast.27), channel_id=1, source_target_pairs={{0,0},{2,4},{4,2},{6,6},{1,1},{3,5},{5,3},{7,7},{8,8},{10,12},{12,... | collective-permute-start | bytes 1572872 | tf_op jit(solution)/shard_map/ppermute | solution.py:81
  1359.0 167.2 %collective-permute-start.19 = (bf16[256,128]{1,0:T(8,128)(2,1)S(1)}, bf16[256,128]{1,0:T(8,128)(2,1)S(1)}, u32[]{:S(2)}, u32[]{:S(2)}) collective-permute-start(bf16[256,128]{1,0:T(8,128)(2,1)S(1)} %copy.70), channel_id=1, source_target_pairs={{0,0},{2,4},{4,2},{6,6},{1,1},{3,5},{5,3},{7,7},{8,8},{10,12},{12,... | collective-permute-start | bytes 196616 | tf_op jit(solution)/shard_map/ppermute | solution.py:81
  1397.1 164.1 %collective-permute-start.17 = (bf16[128,256]{1,0:T(8,128)(2,1)}, bf16[128,256]{1,0:T(8,128)(2,1)S(1)}, u32[]{:S(2)}, u32[]{:S(2)}) collective-permute-start(bf16[128,256]{1,0:T(8,128)(2,1)} %reduce-scatter.44.cloned.1.call-done), channel_id=1, source_target_pairs={{0,0},{2,4},{4,2},{6,6},{1,1},{3,5},{5,3},{7,7},{8,8},{10,12},{12,... | collective-permute-start | bytes 196616 | tf_op jit(solution)/shard_map/ppermute | solution.py:81
  1464.3 214.6 %collective-permute-start.23 = (bf16[1152,128]{1,0:T(8,128)(2,1)}, bf16[1152,128]{1,0:T(8,128)(2,1)}, u32[]{:S(2)}, u32[]{:S(2)}) collective-permute-start(bf16[1152,128]{1,0:T(8,128)(2,1)} %copy.74), channel_id=1, source_target_pairs={{0,0},{2,4},{4,2},{6,6},{1,1},{3,5},{5,3},{7,7},{8,8},{10,12},{12,... | collective-permute-start | bytes 884744 | tf_op jit(solution)/shard_map/ppermute | solution.py:81
  1526.1 152.8 %collective-permute-start.22 = (bf16[1152,128]{1,0:T(8,128)(2,1)}, bf16[1152,128]{1,0:T(8,128)(2,1)}, u32[]{:S(2)}, u32[]{:S(2)}) collective-permute-start(bf16[1152,128]{1,0:T(8,128)(2,1)} %copy.72), channel_id=1, source_target_pairs={{0,0},{2,4},{4,2},{6,6},{1,1},{3,5},{5,3},{7,7},{8,8},{10,12},{12,... | collective-permute-start | bytes 884744 | tf_op jit(solution)/shard_map/ppermute | solution.py:81
  1561.2 8.4 collective-permute-start.18
  1569.6 249.4 %collective-permute-start.14 = (f32[1024,256]{1,0:T(8,128)S(1)}, f32[1024,256]{1,0:T(8,128)S(1)}, u32[]{:S(2)}, u32[]{:S(2)}) collective-permute-start(f32[1024,256]{1,0:T(8,128)S(1)} %bitcast.271), channel_id=1, source_target_pairs={{0,0},{2,4},{4,2},{6,6},{1,1},{3,5},{5,3},{7,7},{8,8},{10,12},{12,... | collective-permute-start | bytes 3145736 | tf_op jit(solution)/shard_map/ppermute | solution.py:81
  1674.7 48.3 %collective-permute-start.20 = (bf16[128,2304]{1,0:T(8,128)(2,1)}, bf16[128,2304]{1,0:T(8,128)(2,1)}, u32[]{:S(2)}, u32[]{:S(2)}) collective-permute-start(bf16[128,2304]{1,0:T(8,128)(2,1)} %reduce-scatter.48.cloned.1.call-done), channel_id=1, source_target_pairs={{0,0},{2,4},{4,2},{6,6},{1,1},{3,5},{5,3},{7,7},{8,8},{10,12},{12,... | collective-permute-start | bytes 1769480 | tf_op jit(solution)/shard_map/ppermute | solution.py:81
  1714.9 7.4 collective-permute-start.16
  1770.5 9.8 collective-permute-start.15
  (84 other events, 1573.6 us)
Sparse Core Ops, SparseCore 0:
  27.3 66.1 all-gather.12
  104.9 54.2 reduce-scatter.25
  349.4 41.9 reduce-scatter.27
  394.5 60.5 all-gather.20
  486.1 53.6 reduce-scatter.29
  786.6 41.9 reduce-scatter.33
  833.1 43.8 all-gather.30
  919.8 42.8 reduce-scatter.35
  965.1 42.7 reduce-scatter.31
  1075.2 42.9 reduce-scatter.37
  1178.6 42.9 reduce-scatter.39
  1225.5 87.3 reduce-scatter.49
  1315.1 42.8 reduce-scatter.53
  1360.2 36.7 reduce-scatter.43
  1400.8 61.6 reduce-scatter.57
  1467.3 56.9 reduce-scatter.55
  1526.4 34.7 reduce-scatter.45
  1565.6 108.9 reduce-scatter.47
  1677.0 36.9 reduce-scatter.51
  1717.5 52.9 reduce-scatter.41
Sparse Core Ops, SparseCore 1:
  131.6 95.8 all-gather.16
  229.5 42.7 all-gather.14
  274.5 68.0 all-gather.18
  504.3 99.8 all-gather.24
  605.9 42.7 all-gather.22
  650.3 43.6 all-gather.28
  696.8 68.0 all-gather.26
  1011.4 43.5 all-gather.32
  1123.1 43.5 all-gather.34

commit v2 on v1

--- a/solution.py
+++ b/solution.py
@@ -1,6 +1,9 @@
+import functools
 import jax
 import jax.numpy as jnp
 from jax import lax
+from jax.experimental import pallas as pl
+from jax.experimental.pallas import tpu as pltpu
 from jax.sharding import Mesh, PartitionSpec as P
 
 epsilon = 1e-05
@@ -9,6 +12,273 @@
 DP = ("r", "zh")
 BF = jnp.bfloat16
 F32 = jnp.float32
+MESH = pl.DeviceIdType.MESH
+DMA = pltpu.SemaphoreType.DMA
+HBM = pl.BlockSpec(memory_space=pl.ANY)
+INV = pl.BlockSpec(memory_space=pltpu.VMEM)
+PARTS = 2
+LANES = 128
+
+
+class Group:
+    def __init__(self):
+        c, z = lax.axis_index("c"), lax.axis_index("zl")
+        self.partner, self.twin = {"c": 1 - c}, {"zl": 1 - z}
+        self.mine, self.beside = 2 * c + z, 2 * (1 - c) + z
+        self.across, self.far = 2 * c + (1 - z), 2 * (1 - c) + (1 - z)
+        self.barrier = pltpu.get_barrier_semaphore()
+
+    def greet(self):
+        for other in (self.partner, self.twin):
+            pl.semaphore_signal(self.barrier, inc=1, device_id=other, device_id_type=MESH)
+
+    def meet(self):
+        pl.semaphore_wait(self.barrier, 2)
+
+
+def at_rows(block, size, start, count):
+    return pl.ds(pl.multiple_of(block * size + start, 16), count)
+
+
+def send(src, dst, sems, index, where):
+    return pltpu.make_async_remote_copy(
+        src_ref=src, dst_ref=dst, send_sem=sems.at[0, index], recv_sem=sems.at[1, index],
+        device_id=where, device_id_type=MESH,
+    )
+
+
+class Gather:
+    def __init__(self, group, full, size, near, over, onward):
+        self.g, self.full, self.size, self.parts = group, full, size, over.shape[1]
+        self.near, self.over, self.onward = near, over, onward
+        self.step = size // self.parts
+
+    def view(self, block, part):
+        return self.full.at[at_rows(block, self.size, part * self.step, self.step)]
+
+    def link(self, part, block):
+        v = self.view(block, part)
+        return send(v, v, self.over, part, self.g.twin)
+
+    def close(self, part, block):
+        v = self.view(block, part)
+        return send(v, v, self.near, part, self.g.partner)
+
+    def pass_on(self, part, block):
+        v = self.view(block, part)
+        return send(v, v, self.onward, part, self.g.partner)
+
+    def start(self):
+        for p in range(self.parts):
+            self.link(p, self.g.mine).start()
+            self.close(p, self.g.mine).start()
+
+    def wait_beside(self):
+        for p in range(self.parts):
+            self.close(p, self.g.beside).wait_recv()
+
+    def wait_part(self, p):
+        self.link(p, self.g.across).wait_recv()
+        self.pass_on(p, self.g.across).start()
+
+    def wait_far(self, p):
+        self.pass_on(p, self.g.far).wait_recv()
+
+    def finish(self):
+        for p in range(self.parts):
+            self.link(p, self.g.mine).wait_send()
+            self.close(p, self.g.mine).wait_send()
+            self.pass_on(p, self.g.across).wait_send()
+
+
+class Scatter:
+    def __init__(self, group, out_near, in_near, out_over, in_over, near, over, size):
+        self.g, self.size, self.parts = group, size, over.shape[1]
+        self.out_near, self.in_near, self.out_over, self.in_over = out_near, in_near, out_over, in_over
+        self.near, self.over = near, over
+        self.step = size // self.parts
+
+    def rows(self, part):
+        return pl.ds(part * self.step, self.step)
+
+    def close(self, which, part):
+        r = self.rows(part)
+        return send(self.out_near.at[which, r], self.in_near.at[which, r], self.near, which * self.parts + part, self.g.partner)
+
+    def link(self, part):
+        r = self.rows(part)
+        return send(self.out_over.at[r], self.in_over.at[r], self.over, part, self.g.twin)
+
+    def wait_all_sends(self):
+        for p in range(self.parts):
+            self.close(0, p).wait_send()
+            self.close(1, p).wait_send()
+            self.link(p).wait_send()
+
+
+def scatter_scratch(size, width, parts):
+    return [
+        pltpu.VMEM((2, size, width), BF), pltpu.VMEM((2, size, width), BF), pltpu.VMEM((size, width), BF),
+        pltpu.VMEM((size, width), BF), DMA((2, 2 * parts)), DMA((2, parts)),
+    ]
+
+
+def gather_scratch(parts):
+    return [DMA((2, parts)), DMA((2, parts)), DMA((2, parts))]
+
+
+def normalise(h, gain):
+    return h * lax.rsqrt(jnp.mean(h * h, axis=-1, keepdims=True) + epsilon) * gain
+
+
+def mm(a, b):
+    return jnp.dot(a, b, preferred_element_type=F32)
+
+
+def mm_nt(a, b):
+    return lax.dot_general(a, b, (((1,), (1,)), ((), ())), preferred_element_type=F32)
+
+
+def lanes(start, width):
+    return pl.ds(pl.multiple_of(start, LANES), width)
+
+
+def ffn_forward_kernel(
+    h_ref, gain_ref, w_hbm, v_hbm, out_ref, n_hbm, u_hbm,
+    w, v, nf, u, act, tpart, mine, n_near, n_over, n_on, o_near, i_near, o_over, i_over, s_near, s_over,
+    wsem, osem,
+):
+    g = Group()
+    g.greet()
+    size, width = h_ref.shape
+    hidden = v.shape[0]
+    load_w = pltpu.make_async_copy(w_hbm, w, wsem.at[0])
+    load_v = pltpu.make_async_copy(v_hbm, v, wsem.at[1])
+    load_w.start()
+    load_v.start()
+    gather = Gather(g, nf, size, n_near, n_over, n_on)
+    scatter = Scatter(g, o_near, i_near, o_over, i_over, s_near, s_over, size)
+    parts, step = gather.parts, gather.step
+    for p in range(parts):
+        nf[at_rows(g.mine, size, p * step, step), :] = normalise(
+            h_ref[pl.ds(p * step, step), :], gain_ref[...]
+        ).astype(BF)
+    g.meet()
+    gather.start()
+    load_w.wait()
+    load_v.wait()
+
+    def rows_of(places):
+        return jnp.concatenate([nf[r, :] for r, _ in places], axis=0) if len(places) > 1 else nf[places[0][0], :]
+
+    def up(places):
+        def body(t, carry):
+            x = rows_of(places)
+            wt = jnp.concatenate([w[:, lanes(t * LANES, LANES)], w[:, lanes(hidden + t * LANES, LANES)]], axis=1)
+            both = mm(x, wt)
+            gate, upper = both[:, :LANES], both[:, LANES:]
+            a = gate * jax.nn.sigmoid(gate) * upper
+            act[:, lanes(t * LANES, LANES)] = a.astype(BF)
+            at = 0
+            for r, count in places:
+                u[r, lanes(t * LANES, LANES)] = gate[at : at + count].astype(BF)
+                u[r, lanes(hidden + t * LANES, LANES)] = upper[at : at + count].astype(BF)
+                at += count
+            return carry
+
+        lax.fori_loop(0, hidden // LANES, body, 0)
+
+    def down(store):
+        def body(t, carry):
+            cols = lanes(t * 256, 256)
+            store(cols, mm(act[...], v[:, cols]))
+            return carry
+
+        lax.fori_loop(0, width // 256, body, 0)
+
+    def keep(index, r, count):
+        return pltpu.make_async_copy(u.at[r], u_hbm.at[r], osem.at[index])
+
+    whole = lambda block: at_rows(block, size, 0, size)
+    up([(whole(g.mine), size)])
+    keep(0, whole(g.mine), size).start()
+
+    def put_mine(cols, value):
+        mine[:, cols] = value
+
+    down(put_mine)
+    gather.wait_beside()
+    up([(whole(g.beside), size)])
+    keep(1, whole(g.beside), size).start()
+
+    def put_beside(cols, value):
+        o_near[1, :, cols] = value.astype(BF)
+
+    down(put_beside)
+    for p in range(parts):
+        scatter.close(1, p).start()
+    for p in range(parts):
+        gather.wait_part(p)
+        gather.wait_far(p)
+        r_across, r_far = at_rows(g.across, size, p * step, step), at_rows(g.far, size, p * step, step)
+        up([(r_across, step), (r_far, step)])
+        keep(2 + 2 * p, r_across, step).start()
+        keep(3 + 2 * p, r_far, step).start()
+        here = scatter.rows(p)
+
+        def put(cols, value):
+            tpart[:, cols] = value[:step]
+            o_near[0, here, cols] = value[step:].astype(BF)
+
+        down(put)
+        scatter.close(0, p).start()
+        scatter.close(0, p).wait_recv()
+        o_over[here, :] = (tpart[...] + i_near[0, here, :].astype(F32)).astype(BF)
+        scatter.link(p).start()
+    n_out = pltpu.make_async_copy(nf, n_hbm, osem.at[2 + 2 * parts])
+    n_out.start()
+    for p in range(parts):
+        here = scatter.rows(p)
+        scatter.close(1, p).wait_recv()
+        scatter.link(p).wait_recv()
+        out_ref[here, :] = (
+            h_ref[here, :] + mine[here, :] + i_near[1, here, :].astype(F32) + i_over[here, :].astype(F32)
+        )
+    gather.finish()
+    scatter.wait_all_sends()
+    keep(0, whole(g.mine), size).wait()
+    keep(1, whole(g.beside), size).wait()
+    for p in range(parts):
+        keep(2 + 2 * p, at_rows(g.across, size, p * step, step), step).wait()
+        keep(3 + 2 * p, at_rows(g.far, size, p * step, step), step).wait()
+    n_out.wait()
+
+
+def ffn_forward(h, gain, w, v, ident, parts=PARTS):
+    size, width = h.shape
+    hidden = v.shape[0]
+    total = 4 * size
+    return pl.pallas_call(
+        ffn_forward_kernel,
+        out_shape=(
+            jax.ShapeDtypeStruct((size, width), F32),
+            jax.ShapeDtypeStruct((total, width), BF),
+            jax.ShapeDtypeStruct((total, 2 * hidden), BF),
+        ),
+        in_specs=[INV, INV, HBM, HBM],
+        out_specs=(INV, HBM, HBM),
+        scratch_shapes=[
+            pltpu.VMEM((width, 2 * hidden), BF), pltpu.VMEM((hidden, width), BF), pltpu.VMEM((total, width), BF),
+            pltpu.VMEM((total, 2 * hidden), BF), pltpu.VMEM((size, hidden), BF),
+            pltpu.VMEM((size // parts, width), F32), pltpu.VMEM((size, width), F32),
+            *gather_scratch(parts), *scatter_scratch(size, width, parts), DMA((2,)), DMA((3 + 2 * parts,)),
+        ],
+        compiler_params=pltpu.CompilerParams(
+            collective_id=ident, has_side_effects=True, vmem_limit_bytes=56 * 2**20
+        ),
+        cost_estimate=pl.CostEstimate(flops=2 * 3 * total * width * hidden, bytes_accessed=2 * 12 * 2**20, transcendentals=0),
+        name="ffn_forward",
+    )(h, gain, w, v)
 
 
 def doc_layout(lengths_row, length):
@@ -110,11 +380,10 @@
     return projected, summed, mixed
 
 
-def ffn_local(normed, w, v):
-    hidden = dot(normed, w)
+def reactivate(hidden):
+    hidden = hidden.astype(F32)
     half = hidden.shape[1] // 2
-    active = (jax.nn.silu(hidden[:, :half]) * hidden[:, half:]).astype(BF)
-    return hidden, active, dot(active, v)
+    return hidden, (jax.nn.silu(hidden[:, :half]) * hidden[:, half:]).astype(BF)
 
 
 def local(
@@ -146,9 +415,8 @@
     h0 = my(x_full).astype(F32)
     projected, summed, mixed = conv_local(n0, conv_in, conv_kernel, same)
     h1 = h0 + scatter_rows(dot(mixed, conv_out))
-    n1 = gather_rows(rms_forward(h1, norm_gains[1])[0].astype(BF))
-    hidden0, active0, part = ffn_local(n1, ws[0], vs[0])
-    h2 = h1 + scatter_rows(part)
+    h2, n1, hidden0 = ffn_forward(h1, norm_gains[1:2], ws[0], vs[0], 1)
+    hidden0, active0 = reactivate(hidden0)
     n2 = gather_rows(rms_forward(h2, norm_gains[2])[0].astype(BF))
 
     kv_heads = kv_w.shape[1] // 2 // head_dim
@@ -172,9 +440,8 @@
     o = jnp.einsum("kgbs,skd->bkgd", probs_low, v, preferred_element_type=F32)
     o = o.reshape(length, -1).astype(BF)
     h3 = h2 + scatter_rows(dot(o, out_w))
-    n3 = gather_rows(rms_forward(h3, norm_gains[3])[0].astype(BF))
-    hidden1, active1, part = ffn_local(n3, ws[1], vs[1])
-    h4 = h3 + scatter_rows(part)
+    h4, n3, hidden1 = ffn_forward(h3, norm_gains[3:4], ws[1], vs[1], 2)
+    hidden1, active1 = reactivate(hidden1)
     output = swap(lax.all_to_all(h4.astype(BF), TP, 1, 0, tiled=True))
 
     def ffn_back(gathered, dh, h, normed, hidden, active, w, vv, gain):

time: 1840 us -> 1660 us (0.902)
  waiting for transfers between devices: 1370 us -> 1150 us
  Pallas kernels: 0 us -> 78.4 us
  matrix products: 188 us -> 150 us
    reduce_scatter x8 -> x6, waiting for transfers between devices: 270 us -> 154 us  [scatter_rows(): lax.psum_scatter(partial.astype(BF), TP, scatter_dimension=0, tiled=True)]
    all_gather x6 -> x4, waiting for transfers between devices: 258 us -> 159 us  [gather_rows(): return lax.all_gather(block, TP, axis=0, tiled=True)]
    pallas_call x0 -> x2, Pallas kernels: none -> 78.4 us  [ffn_forward(): pl.pallas_call(ffn_forward_kernel, out_shape=(jax.ShapeDtypeStruct((size,...]
    all_gather x4, waiting for transfers between devices: 177 us -> 214 us  [gather_dp(): return lax.all_gather(shard, DP, axis=axis, tiled=True)]
    dot_general x27 -> x23, matrix products: 144 us -> 108 us  [dot(): return jnp.dot(a, b, preferred_element_type=F32)]
    all_gather x1, waiting for transfers between devices: 35.2 us -> 9 us  [local(): up_full = lax.all_gather(swap(grad_out), TP, axis=1, tiled=True)]
    ppermute x24, waiting for transfers between devices: 146 us -> 122 us  [swap(): return lax.ppermute(x, ('c', 'zh'), [(0, 0), (1, 2), (2, 1), (3, 3)])]
    unnamed x201 -> x205, local copies, waits for them, and re-layouts: 42.2 us -> 37.9 us
  transfers between devices with their start and end apart: 55 -> 51, of which waited for: 40 -> 36; matrix products, arithmetic and copies ran while one was open for 9% -> 9% of each run, Pallas kernels for 0% -> 3%
where the time goes in v2:
time: 1660 us; the launch traced here: 1650 us
  waiting for transfers between devices  1150 us (69%)
  matrix products  150 us (9%)
  starting transfers between devices  97.4 us (6%)
  Pallas kernels  78.4 us (5%)
  other arithmetic  69.1 us (4%)
  local copies, waits for them, and re-layouts  52.9 us (3%)
  blocking collectives  37.7 us (2%)
  between operations  17.5 us (1%)
    reduce_scatter x5, waiting for transfers between devices, scatter_dp(): lax.psum_scatter(partial.astype(BF), DP, scatter_dimension=axis, tiled=True)  267 us
    all_gather x4, waiting for transfers between devices, gather_dp(): return lax.all_gather(shard, DP, axis=axis, tiled=True)  214 us
    unnamed x29, waiting for transfers between devices  186 us
    all_gather x4, waiting for transfers between devices, gather_rows(): return lax.all_gather(block, TP, axis=0, tiled=True)  159 us
    reduce_scatter x6, waiting for transfers between devices, scatter_rows(): lax.psum_scatter(partial.astype(BF), TP, scatter_dimension=0, tiled=True)  154 us
    ppermute x24, waiting for transfers between devices, swap(): return lax.ppermute(x, ('c', 'zh'), [(0, 0), (1, 2), (2, 1), (3, 3)])  122 us
    dot_general x23, matrix products, dot(): return jnp.dot(a, b, preferred_element_type=F32)  108 us
    ppermute x24, starting transfers between devices, swap(): return lax.ppermute(x, ('c', 'zh'), [(0, 0), (1, 2), (2, 1), (3, 3)])  85.8 us
  transfers between devices with their start and end apart: 51, of which 36 were waited for; matrix products, arithmetic and copies ran while one was open for 9% of the time, Pallas kernels for 3%

profile of v2, /device:TPU:1, one launch (start us, length us, event | category | flops | bytes accessed | tf_op | source)
XLA Modules:
  0.0 1649.2 jit_solution(15114696232624281135)
XLA Ops:
  8.1 5.6 collective-permute-start
  13.7 12.7 collective-permute-done
  30.9 4.5 collective-permute-start.3
  43.4 22.5 %collective-permute-done.3 = s32[1,6]{1,0:T(1,128)S(1)} collective-permute-done((s32[1,6]{1,0:T(1,128)}, s32[1,6]{1,0:T(1,128)S(1)}, u32[]{:S(2)}, u32[]{:S(2)}) %collective-permute-start.3) | collective-permute-done | bytes 56 | tf_op jit(solution)/shard_map/ppermute | solution.py:351
  66.2 27.4 %all-gather.11.cloned.1.call-done = bf16[1024,1024]{1,0:T(8,128)(2,1)} async-done(((bf16[1024,256]{1,0:T(8,128)(2,1)}), bf16[1024,1024]{1,0:T(8,128)(2,1)}) %all-gather.11.cloned.1.call-update) | async-done | bytes 2097168 | tf_op jit(solution)/shard_map/all_gather | solution.py:411
  109.7 8.8 collective-permute-done.6
  122.2 19.4 %collective-permute-done.5 = bf16[128,2304]{1,0:T(8,128)(2,1)S(1)} collective-permute-done((bf16[128,2304]{1,0:T(8,128)(2,1)S(1)}, bf16[128,2304]{1,0:T(8,128)(2,1)S(1)}, u32[]{:S(2)}, u32[]{:S(2)}) %collective-permute-start.5) | collective-permute-done | bytes 589856 | tf_op jit(solution)/shard_map/ppermute | solution.py:351
  142.5 21.7 %reduce-scatter.24.cloned.1.call-done = bf16[256,1024]{1,0:T(8,128)(2,1)} async-done(((bf16[1024,1024]{1,0:T(8,128)(2,1)}), bf16[256,1024]{1,0:T(8,128)(2,1)}) %reduce-scatter.24.cloned.1.call-update) | async-done | bytes 524304 | tf_op jit(solution)/shard_map/reduce_scatter | solution.py:359
  167.1 21.0 %all-gather.15.cloned.1.call-done.v_hbm = bf16[1152,1024]{1,0:T(8,128)(2,1)} async-done(((bf16[1152,128]{1,0:T(8,128)(2,1)}), bf16[1152,1024]{1,0:T(8,128)(2,1)}) %all-gather.15.cloned.1.call-update) | async-done | bytes 2359312 | tf_op jit(solution)/shard_map/all_gather | solution.py:363
  188.1 87.9 %all-gather.13.cloned.1.call-done.w_hbm = bf16[1024,2304]{1,0:T(8,128)(2,1)} async-done(((bf16[128,2304]{1,0:T(8,128)(2,1)}), bf16[1024,2304]{1,0:T(8,128)(2,1)}) %all-gather.13.cloned.1.call-update) | async-done | bytes 4718608 | tf_op jit(solution)/shard_map/all_gather | solution.py:363
  276.0 33.9 %ffn_forward.2 = (f32[256,1024]{1,0:T(8,128)}, bf16[1024,1024]{1,0:T(8,128)(2,1)}, bf16[1024,2304]{1,0:T(8,128)(2,1)}) custom-call(f32[256,1024]{1,0:T(8,128)} %get-tuple-element.98.h_ref, f32[1,1024]{1,0:T(1,128)} %get-tuple-element.133.gain_ref, bf16[1024,2304]{1,0:T(8,128)(2,1)} %all-gather.13.cloned.1.call-done.w_hbm, ...), custom_call_target="tpu_custom_call" | custom-call | flops 7247757312 | bytes 25165824 | tf_op jit(solution)/shard_map/ffn_forward/pallas_call | solution.py:261
  314.3 5.5 collective-permute-start.7
  321.8 4.8 collective-permute-start.9
  328.7 5.3 collective-permute-done.7
  334.0 41.1 %all-gather.17.cloned.1.call-done = bf16[1024,1024]{1,0:T(8,128)(2,1)} async-done(((bf16[256,1024]{1,0:T(8,128)(2,1)}), bf16[1024,1024]{1,0:T(8,128)(2,1)}) %all-gather.17.cloned.1.call-update) | async-done | bytes 2097168 | tf_op jit(solution)/shard_map/all_gather | solution.py:355
  382.1 10.7 fusion.115
  392.9 7.3 fusion.24
  406.2 9.4 collective-permute-done.11
  418.4 19.4 %collective-permute-done.10 = bf16[128,2304]{1,0:T(8,128)(2,1)S(1)} collective-permute-done((bf16[128,2304]{1,0:T(8,128)(2,1)S(1)}, bf16[128,2304]{1,0:T(8,128)(2,1)S(1)}, u32[]{:S(2)}, u32[]{:S(2)}) %collective-permute-start.10) | collective-permute-done | bytes 589856 | tf_op jit(solution)/shard_map/ppermute | solution.py:351
  438.7 5.3 collective-permute-start.13
  444.0 18.2 %collective-permute-done.13 = bf16[1024,256]{1,0:T(8,128)(2,1)S(1)} collective-permute-done((bf16[1024,256]{1,0:T(8,128)(2,1)}, bf16[1024,256]{1,0:T(8,128)(2,1)S(1)}, u32[]{:S(2)}, u32[]{:S(2)}) %collective-permute-start.13) | collective-permute-done | bytes 524320 | tf_op jit(solution)/shard_map/ppermute | solution.py:351
  463.5 5.6 reduce-scatter.26.cloned.1.call-done
  471.8 17.3 %all-gather.21.cloned.1.call-done.v_hbm = bf16[1152,1024]{1,0:T(8,128)(2,1)} async-done(((bf16[1152,128]{1,0:T(8,128)(2,1)}), bf16[1152,1024]{1,0:T(8,128)(2,1)}) %all-gather.21.cloned.1.call-update) | async-done | bytes 2359312 | tf_op jit(solution)/shard_map/all_gather | solution.py:363
  489.1 87.6 %all-gather.19.cloned.1.call-done.w_hbm = bf16[1024,2304]{1,0:T(8,128)(2,1)} async-done(((bf16[128,2304]{1,0:T(8,128)(2,1)}), bf16[1024,2304]{1,0:T(8,128)(2,1)}) %all-gather.19.cloned.1.call-update) | async-done | bytes 4718608 | tf_op jit(solution)/shard_map/all_gather | solution.py:363
  576.7 44.4 %ffn_forward.3 = (f32[256,1024]{1,0:T(8,128)}, bf16[1024,1024]{1,0:T(8,128)(2,1)}, bf16[1024,2304]{1,0:T(8,128)(2,1)}) custom-call(f32[256,1024]{1,0:T(8,128)} %get-tuple-element.102.h_ref, f32[1,1024]{1,0:T(1,128)} %get-tuple-element.132.gain_ref, bf16[1024,2304]{1,0:T(8,128)(2,1)} %all-gather.19.cloned.1.call-done.w_hbm, ...), custom_call_target="tpu_custom_call" | custom-call | flops 7247757312 | bytes 25165824 | tf_op jit(solution)/shard_map/ffn_forward/pallas_call | solution.py:261
  621.1 6.8 convert_element_type.181
  627.9 9.0 all-gather.23.cloned.1.call-done
  636.9 9.1 multiply_convert_fusion.5
  648.2 8.7 fusion.22
  658.2 40.7 %reduce-scatter.28.cloned.1.call-done = bf16[256,1024]{1,0:T(8,128)(2,1)} async-done(((bf16[1024,1024]{1,0:T(8,128)(2,1)}), bf16[256,1024]{1,0:T(8,128)(2,1)}) %reduce-scatter.28.cloned.1.call-update) | async-done | bytes 524304 | tf_op jit(solution)/shard_map/reduce_scatter | solution.py:359
  711.1 36.7 %all-gather.25.cloned.1.call-done = bf16[1024,1024]{1,0:T(8,128)(2,1)} async-done(((bf16[256,1024]{1,0:T(8,128)(2,1)}), bf16[1024,1024]{1,0:T(8,128)(2,1)}) %all-gather.25.cloned.1.call-update) | async-done | bytes 2097168 | tf_op jit(solution)/shard_map/all_gather | solution.py:355
  751.2 9.4 fusion.39
  760.8 9.5 fusion.1
  770.3 8.3 fusion.3
  789.6 42.9 %reduce-scatter.30.cloned.1.call-done = bf16[256,1024]{1,0:T(8,128)(2,1)} async-done(((bf16[1024,1024]{1,0:T(8,128)(2,1)}), bf16[256,1024]{1,0:T(8,128)(2,1)}) %reduce-scatter.30.cloned.1.call-update) | async-done | bytes 524304 | tf_op jit(solution)/shard_map/reduce_scatter | solution.py:359
  837.0 6.9 convert_element_type.191
  843.9 37.0 %all-gather.27.cloned.1.call-done = bf16[1024,1024]{1,0:T(8,128)(2,1)} async-done(((bf16[256,1024]{1,0:T(8,128)(2,1)}), bf16[1024,1024]{1,0:T(8,128)(2,1)}) %all-gather.27.cloned.1.call-update) | async-done | bytes 2097168 | tf_op jit(solution)/shard_map/all_gather | solution.py:355
  880.9 8.4 multiply_convert_fusion.3
  891.4 8.7 fusion.23
  900.2 42.6 %reduce-scatter.32.cloned.1.call-done = bf16[256,1024]{1,0:T(8,128)(2,1)} async-done(((bf16[1024,1024]{1,0:T(8,128)(2,1)}), bf16[256,1024]{1,0:T(8,128)(2,1)}) %reduce-scatter.32.cloned.1.call-update) | async-done | bytes 524304 | tf_op jit(solution)/shard_map/reduce_scatter | solution.py:359
  947.1 44.0 %all-gather.29.cloned.1.call-done = bf16[1024,1024]{1,0:T(8,128)(2,1)} async-done(((bf16[256,1024]{1,0:T(8,128)(2,1)}), bf16[1024,1024]{1,0:T(8,128)(2,1)}) %all-gather.29.cloned.1.call-update) | async-done | bytes 2097168 | tf_op jit(solution)/shard_map/all_gather | solution.py:355
  997.3 4.6 convolution_convert_fusion.6
  1002.0 9.4 convolution_convert_fusion
  1015.2 7.2 convolution_convert_fusion.2
  1024.9 8.6 convolution_convert_fusion.3
  1041.5 9.5 convolution_convert_fusion.1
  1054.6 5.6 convolution_convert_fusion.7
  1062.7 4.8 all-to-all-start
  1071.3 9.2 all-to-all-done
  1080.5 4.8 all-to-all-start.1
  1088.7 54.1 %reduce-scatter.44.cloned.1.call-done = bf16[128,2304]{1,0:T(8,128)(2,1)} async-done(((bf16[1024,2304]{1,0:T(8,128)(2,1)}), bf16[128,2304]{1,0:T(8,128)(2,1)}) %reduce-scatter.44.cloned.1.call-update) | async-done | bytes 589840 | tf_op jit(solution)/shard_map/reduce_scatter | solution.py:367
  1144.8 37.3 %reduce-scatter.48.cloned.1.call-done = bf16[128,256]{1,0:T(8,128)(2,1)} async-done(((bf16[1024,256]{1,0:T(8,128)(2,1)}), bf16[128,256]{1,0:T(8,128)(2,1)}) %reduce-scatter.48.cloned.1.call-update) | async-done | bytes 65552
  1183.0 5.6 collective-permute-start.19
  1188.6 58.4 %reduce-scatter.52.cloned.1.call-done = bf16[128,1152]{1,0:T(8,128)(2,1)} async-done(((bf16[1024,1152]{1,0:T(8,128)(2,1)}), bf16[128,1152]{1,0:T(8,128)(2,1)}) %reduce-scatter.52.cloned.1.call-update) | async-done | bytes 294928
  1250.8 57.3 %reduce-scatter.50.cloned.1.call-done = bf16[128,1152]{1,0:T(8,128)(2,1)} async-done(((bf16[1024,1152]{1,0:T(8,128)(2,1)}), bf16[128,1152]{1,0:T(8,128)(2,1)}) %reduce-scatter.50.cloned.1.call-update) | async-done | bytes 294928
  1311.9 33.7 %reduce-scatter.38.cloned.1.call-done = bf16[128,256]{1,0:T(8,128)(2,1)} async-done(((bf16[1024,256]{1,0:T(8,128)(2,1)}), bf16[128,256]{1,0:T(8,128)(2,1)}) %reduce-scatter.38.cloned.1.call-update) | async-done | bytes 65552 | tf_op jit(solution)/shard_map/reduce_scatter | solution.py:367
  1345.6 6.5 collective-permute-start.17
  1352.1 31.0 %reduce-scatter.40.cloned.1.call-done = bf16[128,256]{1,0:T(8,128)(2,1)} async-done(((bf16[1024,256]{1,0:T(8,128)(2,1)}), bf16[128,256]{1,0:T(8,128)(2,1)}) %reduce-scatter.40.cloned.1.call-update) | async-done | bytes 65552 | tf_op jit(solution)/shard_map/reduce_scatter | solution.py:367
  1383.1 6.8 collective-permute-start.18
  1392.1 102.0 %reduce-scatter.42.cloned.1.call-done = bf16[128,2304]{1,0:T(8,128)(2,1)} async-done(((bf16[1024,2304]{1,0:T(8,128)(2,1)}), bf16[128,2304]{1,0:T(8,128)(2,1)}) %reduce-scatter.42.cloned.1.call-update) | async-done | bytes 589840 | tf_op jit(solution)/shard_map/reduce_scatter | solution.py:367
  1500.5 32.7 %reduce-scatter.46.cloned.1.call-done = bf16[128,256]{1,0:T(8,128)(2,1)} async-done(((bf16[1024,256]{1,0:T(8,128)(2,1)}), bf16[128,256]{1,0:T(8,128)(2,1)}) %reduce-scatter.46.cloned.1.call-update) | async-done | bytes 65552
  1534.2 5.6 collective-permute-start.16
  1544.2 45.7 %reduce-scatter.36.cloned.1.call-done = bf16[128,768]{1,0:T(8,128)(2,1)} async-done(((bf16[1024,768]{1,0:T(8,128)(2,1)}), bf16[128,768]{1,0:T(8,128)(2,1)}) %reduce-scatter.36.cloned.1.call-update) | async-done | bytes 196624 | tf_op jit(solution)/shard_map/reduce_scatter | solution.py:367
  1601.1 37.7 %all-reduce.4 = (f32[4,1024]{1,0:T(4,128)}, f32[2,64]{1,0:T(2,128)}, f32[3,1024]{1,0:T(4,128)}) all-reduce(f32[4,1024]{1,0:T(4,128)S(1)} %pad_maximum_fusion.26, f32[2,64]{1,0:T(2,128)S(1)} %pad_maximum_fusion.27, f32[3,1024]{1,0:T(4,128)S(1)} %maximum_dynamic-update-slice_fusion), channel_id=1, replica_groups=mesh['r'=4,'c'=2,'zh'=2,'zl'=2] {'r','c','zh','zl'}, use_global_device_ids=true, to_apply=%region_29.30 | all-reduce | flops 7296 | bytes 58368 | tf_op jit(solution)/shard_map/psum | solution.py:512
  (383 shorter events, 177.6 us)
Async XLA Ops:
  8.0 85.5 %all-gather.11.cloned.1.call-start = ((), (), s32[]{:S(2)}) async-start(), calls=%async_computation.17 | async-start | bytes 2621440 | tf_op jit(solution)/shard_map/all_gather | solution.py:411
  8.1 18.3 %collective-permute-start = (bf16[1024,256]{1,0:T(8,128)(2,1)}, bf16[1024,256]{1,0:T(8,128)(2,1)S(1)}, u32[]{:S(2)}, u32[]{:S(2)}) collective-permute-start(bf16[1024,256]{1,0:T(8,128)(2,1)} %param.13), channel_id=1, source_target_pairs={{0,0},{2,4},{4,2},{6,6},{1,1},{3,5},{5,3},{7,7},{8,8},{10,12},{12,... | collective-permute-start | bytes 1572872 | tf_op jit(solution)/shard_map/ppermute | solution.py:351
  27.2 137.0 %reduce-scatter.24.cloned.1.call-start = ((), (), s32[]{:S(2)}) async-start(), calls=%async_computation.18 | async-start | bytes 2621440 | tf_op jit(solution)/shard_map/reduce_scatter | solution.py:359
  28.9 66.7 %collective-permute-start.1 = (bf16[1024,768]{0,1:T(8,128)(2,1)S(1)}, bf16[1024,768]{0,1:T(8,128)(2,1)}, u32[]{:S(2)}, u32[]{:S(2)}) collective-permute-start(bf16[1024,768]{0,1:T(8,128)(2,1)S(1)} %bitcast.255), channel_id=1, source_target_pairs={{0,0},{2,4},{4,2},{6,6},{1,1},{3,5},{5,3},{7,7},{8,8},{10,12},{12,... | collective-permute-start | bytes 4718600 | tf_op jit(solution)/shard_map/ppermute | solution.py:351
  30.9 35.0 %collective-permute-start.3 = (s32[1,6]{1,0:T(1,128)}, s32[1,6]{1,0:T(1,128)S(1)}, u32[]{:S(2)}, u32[]{:S(2)}) collective-permute-start(s32[1,6]{1,0:T(1,128)} %param.14), channel_id=1, source_target_pairs={{0,0},{2,4},{4,2},{6,6},{1,1},{3,5},{5,3},{7,7},{8,8},{10,12},{12,... | collective-permute-start | bytes 80 | tf_op jit(solution)/shard_map/ppermute | solution.py:351
  35.4 30.7 %collective-permute-start.2 = (f32[3,256]{1,0:T(4,128)}, f32[3,256]{1,0:T(4,128)S(1)}, u32[]{:S(2)}, u32[]{:S(2)}) collective-permute-start(f32[3,256]{1,0:T(4,128)} %param.19), channel_id=1, source_target_pairs={{0,0},{2,4},{4,2},{6,6},{1,1},{3,5},{5,3},{7,7},{8,8},{10,12},{12,... | collective-permute-start | bytes 9224 | tf_op jit(solution)/shard_map/ppermute | solution.py:351
  37.3 65.4 %collective-permute-start.4 = (bf16[256,1024]{1,0:T(8,128)(2,1)}, bf16[256,1024]{1,0:T(8,128)(2,1)S(1)}, u32[]{:S(2)}, u32[]{:S(2)}) collective-permute-start(bf16[256,1024]{1,0:T(8,128)(2,1)} %param.20), channel_id=1, source_target_pairs={{0,0},{2,4},{4,2},{6,6},{1,1},{3,5},{5,3},{7,7},{8,8},{10,12},{12,... | collective-permute-start | bytes 1572872 | tf_op jit(solution)/shard_map/ppermute | solution.py:351
  43.4 56.1 %copy-start.50 = (f32[1,1024]{1,0:T(1,128)}, f32[1,1024]{1,0:T(1,128)S(1)}, u32[]{:S(2)}) copy-start(f32[1,1024]{1,0:T(1,128)S(1)} %get-tuple-element.134) | copy-start | bytes 12292
  43.4 268.6 %copy-start.48 = (f32[1,1024]{1,0:T(1,128)}, f32[1,1024]{1,0:T(1,128)S(1)}, u32[]{:S(2)}) copy-start(f32[1,1024]{1,0:T(1,128)S(1)} %get-tuple-element.135) | copy-start | bytes 12292
  105.6 82.6 %all-gather.15.cloned.1.call-start = ((), (), s32[]{:S(2)}) async-start(), calls=%async_computation.20 | async-start | bytes 2654208 | tf_op jit(solution)/shard_map/all_gather | solution.py:363
  106.4 12.2 collective-permute-start.6
  119.3 156.7 %all-gather.13.cloned.1.call-start = ((), (), s32[]{:S(2)}) async-start(), calls=%async_computation.19 | async-start | bytes 5308416 | tf_op jit(solution)/shard_map/all_gather | solution.py:363
  120.3 21.3 %collective-permute-start.5 = (bf16[128,2304]{1,0:T(8,128)(2,1)S(1)}, bf16[128,2304]{1,0:T(8,128)(2,1)S(1)}, u32[]{:S(2)}, u32[]{:S(2)}) collective-permute-start(bf16[128,2304]{1,0:T(8,128)(2,1)S(1)} %bitcast.262), channel_id=1, source_target_pairs={{0,0},{2,4},{4,2},{6,6},{1,1},{3,5},{5,3},{7,7},{8,8},{10,12},{12,... | collective-permute-start | bytes 1769480 | tf_op jit(solution)/shard_map/ppermute | solution.py:351
  142.5 232.6 %all-gather.17.cloned.1.call-start = ((), (), s32[]{:S(2)}) async-start(), calls=%async_computation.21 | async-start | bytes 2621440 | tf_op jit(solution)/shard_map/all_gather | solution.py:355
  314.1 154.9 %reduce-scatter.26.cloned.1.call-start = ((), (), s32[]{:S(2)}) async-start(), calls=%async_computation.22 | async-start | bytes 2621440 | tf_op jit(solution)/shard_map/reduce_scatter | solution.py:359
  314.3 19.7 %collective-permute-start.7 = (bf16[1024,256]{1,0:T(8,128)(2,1)S(1)}, bf16[1024,256]{1,0:T(8,128)(2,1)S(1)}, u32[]{:S(2)}, u32[]{:S(2)}) collective-permute-start(bf16[1024,256]{1,0:T(8,128)(2,1)S(1)} %bitcast.265), channel_id=1, source_target_pairs={{0,0},{2,4},{4,2},{6,6},{1,1},{3,5},{5,3},{7,7},{8,8},{10,12},{12,... | collective-permute-start | bytes 1572872 | tf_op jit(solution)/shard_map/ppermute | solution.py:351
  319.8 58.5 %collective-permute-start.8 = (bf16[1024,256]{1,0:T(8,128)(2,1)}, bf16[1024,256]{1,0:T(8,128)(2,1)}, u32[]{:S(2)}, u32[]{:S(2)}) collective-permute-start(bf16[1024,256]{1,0:T(8,128)(2,1)} %param.21), channel_id=1, source_target_pairs={{0,0},{2,4},{4,2},{6,6},{1,1},{3,5},{5,3},{7,7},{8,8},{10,12},{12,... | collective-permute-start | bytes 1572872 | tf_op jit(solution)/shard_map/ppermute | solution.py:351
  321.8 78.5 %collective-permute-start.9 = (bf16[256,1024]{1,0:T(8,128)(2,1)}, bf16[256,1024]{1,0:T(8,128)(2,1)}, u32[]{:S(2)}, u32[]{:S(2)}) collective-permute-start(bf16[256,1024]{1,0:T(8,128)(2,1)} %param.23), channel_id=1, source_target_pairs={{0,0},{2,4},{4,2},{6,6},{1,1},{3,5},{5,3},{7,7},{8,8},{10,12},{12,... | collective-permute-start | bytes 1572872 | tf_op jit(solution)/shard_map/ppermute | solution.py:351
  326.6 54.2 %copy-start.75 = (f32[64]{0:T(128)}, f32[64]{0:T(128)S(1)}, u32[]{:S(2)}) copy-start(f32[64]{0:T(128)S(1)} %get-tuple-element.153) | copy-start | bytes 772
  326.6 54.4 %copy-start.73 = (f32[64]{0:T(128)}, f32[64]{0:T(128)S(1)}, u32[]{:S(2)}) copy-start(f32[64]{0:T(128)S(1)} %get-tuple-element.154) | copy-start | bytes 772
  400.3 68.8 %copy-start.2 = (f32[256,1024]{1,0:T(8,128)S(1)}, f32[256,1024]{1,0:T(8,128)}, u32[]{:S(2)}) copy-start(f32[256,1024]{1,0:T(8,128)} %get-tuple-element.18) | copy-start | bytes 3145732
  404.2 84.9 %all-gather.21.cloned.1.call-start = ((), (), s32[]{:S(2)}) async-start(), calls=%async_computation.24 | async-start | bytes 2654208 | tf_op jit(solution)/shard_map/all_gather | solution.py:363
  404.3 11.3 collective-permute-start.11
  416.4 160.3 %all-gather.19.cloned.1.call-start = ((), (), s32[]{:S(2)}) async-start(), calls=%async_computation.23 | async-start | bytes 5308416 | tf_op jit(solution)/shard_map/all_gather | solution.py:363
  416.5 21.3 %collective-permute-start.10 = (bf16[128,2304]{1,0:T(8,128)(2,1)S(1)}, bf16[128,2304]{1,0:T(8,128)(2,1)S(1)}, u32[]{:S(2)}, u32[]{:S(2)}) collective-permute-start(bf16[128,2304]{1,0:T(8,128)(2,1)S(1)} %bitcast.263), channel_id=1, source_target_pairs={{0,0},{2,4},{4,2},{6,6},{1,1},{3,5},{5,3},{7,7},{8,8},{10,12},{12,... | collective-permute-start | bytes 1769480 | tf_op jit(solution)/shard_map/ppermute | solution.py:351
  438.7 198.3 %all-gather.23.cloned.1.call-start = ((), (), s32[]{:S(2)}) async-start(), calls=%async_computation.25 | async-start | bytes 2621440 | tf_op jit(solution)/shard_map/all_gather | solution.py:412
  438.7 23.5 %collective-permute-start.13 = (bf16[1024,256]{1,0:T(8,128)(2,1)}, bf16[1024,256]{1,0:T(8,128)(2,1)S(1)}, u32[]{:S(2)}, u32[]{:S(2)}) collective-permute-start(bf16[1024,256]{1,0:T(8,128)(2,1)} %param.15), channel_id=1, source_target_pairs={{0,0},{2,4},{4,2},{6,6},{1,1},{3,5},{5,3},{7,7},{8,8},{10,12},{12,... | collective-permute-start | bytes 1572872 | tf_op jit(solution)/shard_map/ppermute | solution.py:351
  463.0 235.9 %reduce-scatter.28.cloned.1.call-start = ((), (), s32[]{:S(2)}) async-start(), calls=%async_computation.26 | async-start | bytes 2621440 | tf_op jit(solution)/shard_map/reduce_scatter | solution.py:359
  648.2 50.7 %copy-start.5 = (f32[256,1024]{1,0:T(8,128)S(1)}, f32[256,1024]{1,0:T(8,128)}, u32[]{:S(2)}) copy-start(f32[256,1024]{1,0:T(8,128)} %get-tuple-element.102.h_ref) | copy-start | bytes 3145732
  656.9 90.9 %all-gather.25.cloned.1.call-start = ((), (), s32[]{:S(2)}) async-start(), calls=%async_computation.27 | async-start | bytes 2621440 | tf_op jit(solution)/shard_map/all_gather | solution.py:355
  703.9 128.6 %reduce-scatter.30.cloned.1.call-start = ((), (), s32[]{:S(2)}) async-start(), calls=%async_computation.28 | async-start | bytes 2621440 | tf_op jit(solution)/shard_map/reduce_scatter | solution.py:359
  786.3 47.6 %copy-start.13 = (bf16[256,1024]{1,0:T(8,128)(2,1)S(1)}, bf16[256,1024]{1,0:T(8,128)(2,1)}, u32[]{:S(2)}) copy-start(bf16[256,1024]{1,0:T(8,128)(2,1)} %reduce-scatter.28.cloned.1.call-done) | copy-start | bytes 1572868
  789.5 91.3 %all-gather.27.cloned.1.call-start = ((), (), s32[]{:S(2)}) async-start(), calls=%async_computation.29 | async-start | bytes 2621440 | tf_op jit(solution)/shard_map/all_gather | solution.py:355
  836.9 106.0 %reduce-scatter.32.cloned.1.call-start = ((), (), s32[]{:S(2)}) async-start(), calls=%async_computation.30 | async-start | bytes 2621440 | tf_op jit(solution)/shard_map/reduce_scatter | solution.py:359
  891.4 51.4 %copy-start.6 = (f32[256,1024]{1,0:T(8,128)S(1)}, f32[256,1024]{1,0:T(8,128)}, u32[]{:S(2)}) copy-start(f32[256,1024]{1,0:T(8,128)} %get-tuple-element.98.h_ref) | copy-start | bytes 3145732
  891.4 51.4 %copy-start.52 = (f32[1,1024]{1,0:T(1,128)S(1)}, f32[1,1024]{1,0:T(1,128)}, u32[]{:S(2)}) copy-start(f32[1,1024]{1,0:T(1,128)} %get-tuple-element.133.gain_ref) | copy-start | bytes 12292
  900.1 91.0 %copy-start.1 = (f32[1024,256]{1,0:T(8,128)S(1)}, f32[1024,256]{1,0:T(8,128)}, u32[]{:S(2)}) copy-start(f32[1024,256]{1,0:T(8,128)} %copy-done) | copy-start | bytes 3145732
  900.1 91.0 %copy-start.16 = (f32[1024,256]{1,0:T(8,128)S(1)}, f32[1024,256]{1,0:T(8,128)}, u32[]{:S(2)}) copy-start(f32[1024,256]{1,0:T(8,128)} %get-tuple-element.104) | copy-start | bytes 3145732
  900.1 91.0 %all-gather.29.cloned.1.call-start = ((), (), s32[]{:S(2)}) async-start(), calls=%async_computation.31 | async-start | bytes 2621440 | tf_op jit(solution)/shard_map/all_gather | solution.py:355
  947.1 120.4 %reduce-scatter.34.cloned.1.call-start = ((), (), s32[]{:S(2)}) async-start(), calls=%async_computation.32 | async-start | bytes 2621440 | tf_op jit(solution)/shard_map/reduce_scatter | solution.py:359
  1001.9 140.9 %reduce-scatter.44.cloned.1.call-start = ((), (), s32[]{:S(2)}) async-start(), calls=%async_computation.37 | async-start | bytes 5308416 | tf_op jit(solution)/shard_map/reduce_scatter | solution.py:367
  1011.4 170.6 %reduce-scatter.48.cloned.1.call-start = ((), (), s32[]{:S(2)}) async-start(), calls=%async_computation.39 | async-start | bytes 589824
  1015.0 232.0 %reduce-scatter.52.cloned.1.call-start = ((), (), s32[]{:S(2)}) async-start(), calls=%async_computation.41 | async-start | bytes 2654208
  1024.9 283.2 %reduce-scatter.50.cloned.1.call-start = ((), (), s32[]{:S(2)}) async-start(), calls=%async_computation.40 | async-start | bytes 2654208
  1038.1 307.5 %reduce-scatter.38.cloned.1.call-start = ((), (), s32[]{:S(2)}) async-start(), calls=%async_computation.34 | async-start | bytes 589824 | tf_op jit(solution)/shard_map/reduce_scatter | solution.py:367
  1039.8 343.4 %reduce-scatter.40.cloned.1.call-start = ((), (), s32[]{:S(2)}) async-start(), calls=%async_computation.35 | async-start | bytes 589824 | tf_op jit(solution)/shard_map/reduce_scatter | solution.py:367
  1041.4 452.7 %reduce-scatter.42.cloned.1.call-start = ((), (), s32[]{:S(2)}) async-start(), calls=%async_computation.36 | async-start | bytes 5308416 | tf_op jit(solution)/shard_map/reduce_scatter | solution.py:367
  1051.0 482.2 %reduce-scatter.46.cloned.1.call-start = ((), (), s32[]{:S(2)}) async-start(), calls=%async_computation.38 | async-start | bytes 589824
  1054.4 535.6 %reduce-scatter.36.cloned.1.call-start = ((), (), s32[]{:S(2)}) async-start(), calls=%async_computation.33 | async-start | bytes 1769472 | tf_op jit(solution)/shard_map/reduce_scatter | solution.py:367
  1062.7 17.8 %all-to-all-start = ((bf16[256,4,256]{2,0,1:T(8,128)(2,1)}), bf16[256,4,256]{2,0,1:T(8,128)(2,1)}, u32[]{:S(2)}, u32[]{:S(2)}) async-start(bf16[256,4,256]{2,0,1:T(8,128)(2,1)} %bitcast.254), calls=%async_computation.2 | async-start | bytes 1048576 | tf_op jit(solution)/shard_map/all_to_all | solution.py:445
  1080.5 309.5 %all-to-all-start.1 = ((f32[256,4,256]{2,0,1:T(8,128)}), f32[256,4,256]{2,0,1:T(8,128)S(1)}, u32[]{:S(2)}, u32[]{:S(2)}) async-start(f32[256,4,256]{2,0,1:T(8,128)} %bitcast.228), calls=%async_computation.7 | async-start | bytes 2097152 | tf_op jit(solution)/shard_map/all_to_all | solution.py:505
  1085.3 226.6 %collective-permute-start.12 = (bf16[1024,256]{1,0:T(8,128)(2,1)}, bf16[1024,256]{1,0:T(8,128)(2,1)S(1)}, u32[]{:S(2)}, u32[]{:S(2)}) collective-permute-start(bf16[1024,256]{1,0:T(8,128)(2,1)} %bitcast.25), channel_id=1, source_target_pairs={{0,0},{2,4},{4,2},{6,6},{1,1},{3,5},{5,3},{7,7},{8,8},{10,12},{12,... | collective-permute-start | bytes 1572872 | tf_op jit(solution)/shard_map/ppermute | solution.py:351
  1142.9 355.4 %collective-permute-start.21 = (bf16[128,2304]{1,0:T(8,128)(2,1)}, bf16[128,2304]{1,0:T(8,128)(2,1)S(1)}, u32[]{:S(2)}, u32[]{:S(2)}) collective-permute-start(bf16[128,2304]{1,0:T(8,128)(2,1)} %reduce-scatter.44.cloned.1.call-done), channel_id=1, source_target_pairs={{0,0},{2,4},{4,2},{6,6},{1,1},{3,5},{5,3},{7,7},{8,8},{10,12},{12,... | collective-permute-start | bytes 1769480 | tf_op jit(solution)/shard_map/ppermute | solution.py:351
  1183.0 200.1 %collective-permute-start.19 = (bf16[256,128]{1,0:T(8,128)(2,1)S(1)}, bf16[256,128]{1,0:T(8,128)(2,1)S(1)}, u32[]{:S(2)}, u32[]{:S(2)}) collective-permute-start(bf16[256,128]{1,0:T(8,128)(2,1)S(1)} %copy.70), channel_id=1, source_target_pairs={{0,0},{2,4},{4,2},{6,6},{1,1},{3,5},{5,3},{7,7},{8,8},{10,12},{12,... | collective-permute-start | bytes 196616 | tf_op jit(solution)/shard_map/ppermute | solution.py:351
  1248.8 249.5 %collective-permute-start.23 = (bf16[1152,128]{1,0:T(8,128)(2,1)}, bf16[1152,128]{1,0:T(8,128)(2,1)}, u32[]{:S(2)}, u32[]{:S(2)}) collective-permute-start(bf16[1152,128]{1,0:T(8,128)(2,1)} %copy.74), channel_id=1, source_target_pairs={{0,0},{2,4},{4,2},{6,6},{1,1},{3,5},{5,3},{7,7},{8,8},{10,12},{12,... | collective-permute-start | bytes 884744 | tf_op jit(solution)/shard_map/ppermute | solution.py:351
  1309.9 188.4 %collective-permute-start.22 = (bf16[1152,128]{1,0:T(8,128)(2,1)}, bf16[1152,128]{1,0:T(8,128)(2,1)}, u32[]{:S(2)}, u32[]{:S(2)}) collective-permute-start(bf16[1152,128]{1,0:T(8,128)(2,1)} %copy.72), channel_id=1, source_target_pairs={{0,0},{2,4},{4,2},{6,6},{1,1},{3,5},{5,3},{7,7},{8,8},{10,12},{12,... | collective-permute-start | bytes 884744 | tf_op jit(solution)/shard_map/ppermute | solution.py:351
  1311.9 186.3 %copy-start.34 = (bf16[1024,256]{1,0:T(8,128)(2,1)}, bf16[1024,256]{1,0:T(8,128)(2,1)S(1)}, u32[]{:S(2)}) copy-start(bf16[1024,256]{1,0:T(8,128)(2,1)S(1)} %collective-permute-done.12) | copy-start | bytes 1572868
  1345.6 44.4 %collective-permute-start.17 = (bf16[128,256]{1,0:T(8,128)(2,1)}, bf16[128,256]{1,0:T(8,128)(2,1)S(1)}, u32[]{:S(2)}, u32[]{:S(2)}) collective-permute-start(bf16[128,256]{1,0:T(8,128)(2,1)} %reduce-scatter.38.cloned.1.call-done), channel_id=1, source_target_pairs={{0,0},{2,4},{4,2},{6,6},{1,1},{3,5},{5,3},{7,7},{8,8},{10,12},{12,... | collective-permute-start | bytes 196616 | tf_op jit(solution)/shard_map/ppermute | solution.py:351
  1383.1 9.0 collective-permute-start.18
  1390.0 248.8 %collective-permute-start.14 = (f32[1024,256]{1,0:T(8,128)S(1)}, f32[1024,256]{1,0:T(8,128)S(1)}, u32[]{:S(2)}, u32[]{:S(2)}) collective-permute-start(f32[1024,256]{1,0:T(8,128)S(1)} %bitcast.261), channel_id=1, source_target_pairs={{0,0},{2,4},{4,2},{6,6},{1,1},{3,5},{5,3},{7,7},{8,8},{10,12},{12,... | collective-permute-start | bytes 3145736 | tf_op jit(solution)/shard_map/ppermute | solution.py:351
  1494.1 48.2 %collective-permute-start.20 = (bf16[128,2304]{1,0:T(8,128)(2,1)}, bf16[128,2304]{1,0:T(8,128)(2,1)}, u32[]{:S(2)}, u32[]{:S(2)}) collective-permute-start(bf16[128,2304]{1,0:T(8,128)(2,1)} %reduce-scatter.42.cloned.1.call-done), channel_id=1, source_target_pairs={{0,0},{2,4},{4,2},{6,6},{1,1},{3,5},{5,3},{7,7},{8,8},{10,12},{12,... | collective-permute-start | bytes 1769480 | tf_op jit(solution)/shard_map/ppermute | solution.py:351
  1498.4 102.7 %copy-start.57 = (f32[1024]{0:T(1024)S(1)}, f32[1024]{0:T(1024)}, u32[]{:S(2)}) copy-start(f32[1024]{0:T(1024)} %get-tuple-element.80) | copy-start | bytes 12292
  1534.2 7.6 collective-permute-start.16
  1590.0 10.1 collective-permute-start.15
  (82 other events, 980.6 us)
Sparse Core Ops, SparseCore 0:
  27.3 66.1 all-gather.10
  105.7 58.4 reduce-scatter.23
  314.3 60.7 all-gather.16
  404.4 64.6 reduce-scatter.25
  657.0 41.8 reduce-scatter.27
  704.0 43.7 all-gather.24
  789.7 42.7 reduce-scatter.29
  837.0 43.8 all-gather.26
  947.2 43.9 all-gather.28
Sparse Core Ops, SparseCore 1:
  119.4 68.7 all-gather.14
  190.4 85.5 all-gather.12
  416.5 72.6 all-gather.20
  491.3 85.3 all-gather.18
  578.8 58.0 all-gather.22
  900.2 42.6 reduce-scatter.31
  1002.0 42.6 reduce-scatter.33
  1048.6 94.2 reduce-scatter.43
  1145.0 37.0 reduce-scatter.47
  1187.0 59.9 reduce-scatter.51
  1250.7 57.3 reduce-scatter.49
  1310.5 35.0 reduce-scatter.37
  1347.7 35.4 reduce-scatter.39
  1387.7 106.4 reduce-scatter.41
  1496.5 36.6 reduce-scatter.45
  1536.9 53.0 reduce-scatter.35

commit v3 on v2

--- a/solution.py
+++ b/solution.py
@@ -7,9 +7,6 @@
 from jax.sharding import Mesh, PartitionSpec as P
 
 epsilon = 1e-05
-rope_base = 1000000.0
-TP = ("c", "zl")
-DP = ("r", "zh")
 BF = jnp.bfloat16
 F32 = jnp.float32
 MESH = pl.DeviceIdType.MESH
@@ -280,110 +277,773 @@
         name="ffn_forward",
     )(h, gain, w, v)
 
-
-def doc_layout(lengths_row, length):
+def mm_tn(a, b):
+    return lax.dot_general(a, b, (((0,), (0,)), ((), ())), preferred_element_type=F32)
+
+
+def rms_back(dn, h, gain):
+    inverse = lax.rsqrt(jnp.mean(h * h, axis=-1, keepdims=True) + epsilon)
+    scaled = dn * gain
+    inner = jnp.mean(scaled * h, axis=-1, keepdims=True)
+    grad_gain = jnp.sum(dn * h * inverse, axis=0, keepdims=True)
+    return inverse * scaled - h * (inverse * inverse * inverse * inner), grad_gain
+
+
+def close_scatter(scatter, mine, dh_ref, h_ref, gain_ref, out_ref, gg_ref):
+    gg_ref[...] = jnp.zeros_like(gg_ref)
+    for p in range(scatter.parts):
+        here = scatter.rows(p)
+        scatter.close(1, p).wait_recv()
+        scatter.link(p).wait_recv()
+        dn = mine[here, :] + scatter.in_near[1, here, :].astype(F32) + scatter.in_over[here, :].astype(F32)
+        term, grad_gain = rms_back(dn, h_ref[here, :], gain_ref[...])
+        out_ref[here, :] = dh_ref[here, :] + term
+        gg_ref[...] += grad_gain
+
+
+def ffn_backward_kernel(
+    known, dh_ref, h_ref, gain_ref, df_hbm, w_hbm, v_hbm, n_hbm, u_hbm, out_ref, gg_ref, gw_hbm, gv_hbm,
+    w, v, nf, u, act, df, tpart, mine, gtile, n_near, n_over, n_on, o_near, i_near, o_over, i_over, s_near, s_over,
+    wsem, osem,
+):
+    g = Group()
+    g.greet()
+    size, width = dh_ref.shape
+    hidden = v.shape[0]
+    loads = [
+        pltpu.make_async_copy(src, dst, wsem.at[i])
+        for i, (src, dst) in enumerate([(v_hbm, v), (u_hbm, u), (w_hbm, w), (n_hbm, nf)])
+    ]
+    if known:
+        loads.append(pltpu.make_async_copy(df_hbm, df, wsem.at[4]))
+    for load in loads:
+        load.start()
+    gather = Gather(g, df, size, n_near, n_over, n_on)
+    scatter = Scatter(g, o_near, i_near, o_over, i_over, s_near, s_over, size)
+    parts, step = gather.parts, gather.step
+    if not known:
+        df[at_rows(g.mine, size, 0, size), :] = dh_ref[...].astype(BF)
+    g.meet()
+    if not known:
+        gather.start()
+    for load in loads:
+        load.wait()
+
+    third = hidden // 3
+
+    def cat(ref, places, cols):
+        found = [ref[r, cols] for r, _ in places]
+        return found[0] if len(found) == 1 else jnp.concatenate(found, axis=0)
+
+    def first(places):
+        def body(t, carry):
+            cols, more = lanes(t * third, third), lanes(hidden + t * third, third)
+            da = mm_nt(cat(df, places, slice(None)), v[cols, :])
+            gate, upper = cat(u, places, cols).astype(F32), cat(u, places, more).astype(F32)
+            s = jax.nn.sigmoid(gate)
+            lit = gate * s
+            dgate = (da * upper * s * (1.0 + gate * (1.0 - s))).astype(BF)
+            dupper = (da * lit).astype(BF)
+            a = (lit * upper).astype(BF)
+            at = 0
+            for r, count in places:
+                u[r, cols] = dgate[at : at + count]
+                u[r, more] = dupper[at : at + count]
+                act[r, cols] = a[at : at + count]
+                at += count
+            return carry
+
+        lax.fori_loop(0, 3, body, 0)
+
+    def second(places, store):
+        def body(t, carry):
+            cols = lanes(t * 256, 256)
+            store(cols, mm_nt(cat(u, places, slice(None)), w[cols, :]))
+            return carry
+
+        lax.fori_loop(0, width // 256, body, 0)
+
+    whole = lambda block: [(at_rows(block, size, 0, size), size)]
+
+    def put_mine(cols, value):
+        mine[:, cols] = value
+
+    def put_beside(cols, value):
+        o_near[1, :, cols] = value.astype(BF)
+
+    def own():
+        first(whole(g.mine))
+        second(whole(g.mine), put_mine)
+
+    def beside():
+        first(whole(g.beside))
+        second(whole(g.beside), put_beside)
+        for p in range(parts):
+            scatter.close(1, p).start()
+
+    if not known:
+        own()
+        gather.wait_beside()
+        beside()
+    for p in range(parts):
+        if not known:
+            gather.wait_part(p)
+            gather.wait_far(p)
+        pair = [(at_rows(b, size, p * step, step), step) for b in (g.across, g.far)]
+        first(pair)
+        here = scatter.rows(p)
+
+        def put(cols, value):
+            tpart[:, cols] = value[:step]
+            o_near[0, here, cols] = value[step:].astype(BF)
+
+        second(pair, put)
+        scatter.close(0, p).start()
+        scatter.close(0, p).wait_recv()
+        o_over[here, :] = (tpart[...] + i_near[0, here, :].astype(F32)).astype(BF)
+        scatter.link(p).start()
+    if known:
+        beside()
+        own()
+    flush = []
+    count = 0
+
+    def emit(value, dst):
+        nonlocal count
+        slot = count % 2
+        if count >= 2:
+            flush[count - 2].wait()
+        gtile[slot, :, : value.shape[1]] = value.astype(BF)
+        copy = pltpu.make_async_copy(gtile.at[slot, :, : value.shape[1]], dst, osem.at[slot])
+        copy.start()
+        flush.append(copy)
+        count += 1
+
+    tall = gtile.shape[1]
+    for t in range(hidden // tall):
+        emit(mm_tn(act[:, t * tall : (t + 1) * tall], df[...]), gv_hbm.at[pl.ds(t * tall, tall), :])
+    for t in range(width // tall):
+        for k in range(2):
+            cols = slice(k * hidden, (k + 1) * hidden)
+            emit(mm_tn(nf[:, t * tall : (t + 1) * tall], u[:, cols]), gw_hbm.at[pl.ds(t * tall, tall), cols])
+    close_scatter(scatter, mine, dh_ref, h_ref, gain_ref, out_ref, gg_ref)
+    if not known:
+        gather.finish()
+    scatter.wait_all_sends()
+    for copy in flush[-2:]:
+        copy.wait()
+
+
+def ffn_backward(dh, h, gain, df, w, v, n, u, ident, parts=PARTS):
+    size, width = h.shape
+    hidden = v.shape[0]
+    total = 4 * size
+    known = df is not None
+    if not known:
+        df = n
+    return pl.pallas_call(
+        functools.partial(ffn_backward_kernel, known),
+        out_shape=(
+            jax.ShapeDtypeStruct((size, width), F32),
+            jax.ShapeDtypeStruct((1, width), F32),
+            jax.ShapeDtypeStruct((width, 2 * hidden), BF),
+            jax.ShapeDtypeStruct((hidden, width), BF),
+        ),
+        in_specs=[INV, INV, INV, HBM, HBM, HBM, HBM, HBM],
+        out_specs=(INV, INV, HBM, HBM),
+        scratch_shapes=[
+            pltpu.VMEM((width, 2 * hidden), BF), pltpu.VMEM((hidden, width), BF), pltpu.VMEM((total, width), BF),
+            pltpu.VMEM((total, 2 * hidden), BF), pltpu.VMEM((total, hidden), BF), pltpu.VMEM((total, width), BF),
+            pltpu.VMEM((size // parts, width), F32), pltpu.VMEM((size, width), F32),
+            pltpu.VMEM((2, 128, hidden), BF),
+            *gather_scratch(parts), *scatter_scratch(size, width, parts), DMA((5,)), DMA((2,)),
+        ],
+        compiler_params=pltpu.CompilerParams(
+            collective_id=ident, has_side_effects=True, vmem_limit_bytes=56 * 2**20
+        ),
+        cost_estimate=pl.CostEstimate(flops=4 * 3 * total * width * hidden, bytes_accessed=2 * 20 * 2**20, transcendentals=0),
+        name="ffn_backward",
+    )(dh, h, gain, df, w, v, n, u)
+
+MOST_DOC = 512
+
+
+class Columns(Gather):
+    def __init__(self, group, full, near, over, onward):
+        super().__init__(group, full, full.shape[0], near, over, onward)
+        self.cols = full.shape[1] // 4
+
+    def view(self, block, part):
+        return self.full.at[pl.ds(part * self.step, self.step), lanes(block * self.cols, self.cols)]
+
+
+def cat_rows(ref, places, cols=slice(None)):
+    found = [ref[r, cols] for r, _ in places]
+    return found[0] if len(found) == 1 else jnp.concatenate(found, axis=0)
+
+
+def product(src, weight, turned, tile=256):
+    def run(places, store):
+        width = weight.shape[0] if turned else weight.shape[1]
+
+        def body(t, carry):
+            cols = lanes(t * tile, tile)
+            x = cat_rows(src, places)
+            store(cols, mm_nt(x, weight[cols, :]) if turned else mm(x, weight[:, cols]))
+            return carry
+
+        lax.fori_loop(0, width // tile, body, 0)
+
+    return run
+
+
+def scatter_all(g, scatter, run, mine, tpart):
+    size, step = scatter.size, scatter.step
+    for p in range(scatter.parts):
+        here = scatter.rows(p)
+
+        def put(cols, value):
+            tpart[:, cols] = value[:step]
+            scatter.out_near[0, here, cols] = value[step:].astype(BF)
+
+        run([(at_rows(b, size, p * step, step), step) for b in (g.across, g.far)], put)
+        scatter.close(0, p).start()
+        scatter.close(0, p).wait_recv()
+        scatter.out_over[here, :] = (tpart[...] + scatter.in_near[0, here, :].astype(F32)).astype(BF)
+        scatter.link(p).start()
+
+    def put_beside(cols, value):
+        scatter.out_near[1, :, cols] = value.astype(BF)
+
+    run([(at_rows(g.beside, size, 0, size), size)], put_beside)
+    for p in range(scatter.parts):
+        scatter.close(1, p).start()
+
+    def put_mine(cols, value):
+        mine[:, cols] = value
+
+    run([(at_rows(g.mine, size, 0, size), size)], put_mine)
+
+
+def gather_everything(gather):
+    gather.wait_beside()
+    for p in range(gather.parts):
+        gather.wait_part(p)
+    for p in range(gather.parts):
+        gather.wait_far(p)
+
+
+def doc_starts(lengths, places):
+    end = jnp.int32(0)
+    start = jnp.zeros_like(places)
+    for d in range(lengths.shape[1]):
+        end = end + lengths[0, d]
+        start = jnp.where(places >= end, end, start)
+    return start
+
+
+def start_all(pairs, sems):
+    copies = [pltpu.make_async_copy(src, dst, sems.at[i]) for i, (src, dst) in enumerate(pairs)]
+    for copy in copies:
+        copy.start()
+    return copies
+
+
+def wait_all(copies):
+    for copy in copies:
+        copy.wait()
+
+
+def params(ident):
+    return pltpu.CompilerParams(collective_id=ident, has_side_effects=True, vmem_limit_bytes=56 * 2**20)
+
+
+def shaped(shape, dtype):
+    return jax.ShapeDtypeStruct(shape, dtype)
+
+
+SCALARS = pl.BlockSpec(memory_space=pltpu.SMEM)
+
+
+def conv_taps(gated, within, taps):
+    total = gated.shape[0]
+    summed = taps[0] * gated
+    for j in range(1, len(taps)):
+        summed = summed + taps[j] * jnp.where(within >= j, pltpu.roll(gated, j, 0), 0.0)
+    return summed
+
+
+def conv_forward_kernel(
+    lengths, x_ref, gain_ref, taps_ref, win_hbm, wout_hbm, out_ref, block_ref, n_hbm, p_hbm,
+    win, wout, full, nf, proj, low, mixed, tpart, mine, n_near, n_over, n_on, o_near, i_near, o_over, i_over,
+    s_near, s_over, wsem, osem,
+):
+    g = Group()
+    g.greet()
+    size, width = out_ref.shape
+    total, chans = x_ref.shape[0], wout.shape[0]
+    loads = start_all([(win_hbm, win), (wout_hbm, wout)], wsem)
+    gather = Columns(g, full, n_near, n_over, n_on)
+    scatter = Scatter(g, o_near, i_near, o_over, i_over, s_near, s_over, size)
+    full[:, lanes(g.mine * chans, chans)] = x_ref[...]
+    g.meet()
+    gather.start()
+    gather_everything(gather)
+    wait_all(loads)
+
+    def project(t, carry):
+        rows = at_rows(t, size, 0, size)
+        n = normalise(full[rows, :].astype(F32), gain_ref[...]).astype(BF)
+        nf[rows, :] = n
+        p = mm(n, win[...])
+        proj[rows, :] = p
+        low[rows, :] = p.astype(BF)
+        return carry
+
+    lax.fori_loop(0, total // size, project, 0)
+    saves = start_all([(nf, n_hbm), (low, p_hbm)], osem)
+    places = lax.broadcasted_iota(jnp.int32, (total, LANES), 0)
+    within = places - doc_starts(lengths, places)
+    for k in range(chans // LANES):
+        b, c, x = (proj[:, pl.ds(i * chans + k * LANES, LANES)] for i in range(3))
+        taps = [taps_ref[pl.ds(j, 1), pl.ds(k * LANES, LANES)] for j in range(taps_ref.shape[0])]
+        mixed[:, pl.ds(k * LANES, LANES)] = (c * conv_taps(b * x, within, taps)).astype(BF)
+    scatter_all(g, scatter, product(mixed, wout, False), mine, tpart)
+    own = full[at_rows(g.mine, size, 0, size), :]
+    block_ref[...] = own
+    for p in range(scatter.parts):
+        here = scatter.rows(p)
+        scatter.close(1, p).wait_recv()
+        scatter.link(p).wait_recv()
+        out_ref[here, :] = (
+            block_ref[here, :].astype(F32) + mine[here, :] + i_near[1, here, :].astype(F32) + i_over[here, :].astype(F32)
+        )
+    gather.finish()
+    scatter.wait_all_sends()
+    wait_all(saves)
+
+
+def conv_forward(lengths, x, gain, taps, win, wout, ident, parts=PARTS):
+    total, chans = x.shape
+    width = wout.shape[1]
+    size = total // 4
+    return pl.pallas_call(
+        conv_forward_kernel,
+        out_shape=(
+            shaped((size, width), F32), shaped((size, width), BF), shaped((total, width), BF), shaped((total, 3 * chans), BF),
+        ),
+        in_specs=[SCALARS, INV, INV, INV, HBM, HBM],
+        out_specs=(INV, INV, HBM, HBM),
+        scratch_shapes=[
+            pltpu.VMEM((width, 3 * chans), BF), pltpu.VMEM((chans, width), BF), pltpu.VMEM((total, width), BF),
+            pltpu.VMEM((total, width), BF), pltpu.VMEM((total, 3 * chans), F32), pltpu.VMEM((total, 3 * chans), BF),
+            pltpu.VMEM((total, chans), BF), pltpu.VMEM((size // parts, width), F32), pltpu.VMEM((size, width), F32),
+            *gather_scratch(parts), *scatter_scratch(size, width, parts), DMA((2,)), DMA((2,)),
+        ],
+        compiler_params=params(ident),
+        cost_estimate=pl.CostEstimate(flops=2 * 4 * total * width * chans, bytes_accessed=2 * 8 * 2**20, transcendentals=0),
+        name="conv_forward",
+    )(lengths, x, gain, taps, win, wout)
+
+
+def conv_backward_kernel(
+    lengths, dh_ref, h_ref, gain_ref, taps_ref, win_hbm, wout_hbm, n_hbm, p_hbm, out_ref, gg_ref, gt_ref, gin_hbm, gout_hbm,
+    win, wout, nf, low, dz, dy, mixed, dproj, gin, gout, tpart, mine, n_near, n_over, n_on, o_near, i_near, o_over, i_over,
+    s_near, s_over, wsem, osem,
+):
+    g = Group()
+    g.greet()
+    size, width = dh_ref.shape
+    total, chans = 4 * size, wout.shape[0]
+    loads = start_all([(wout_hbm, wout), (p_hbm, low), (win_hbm, win), (n_hbm, nf)], wsem)
+    gather = Gather(g, dz, size, n_near, n_over, n_on)
+    scatter = Scatter(g, o_near, i_near, o_over, i_over, s_near, s_over, size)
+    dz[at_rows(g.mine, size, 0, size), :] = dh_ref[...].astype(BF)
+    g.meet()
+    gather.start()
+    wait_all(loads)
+    places = lax.broadcasted_iota(jnp.int32, (total, LANES), 0)
+    within = places - doc_starts(lengths, places)
+    gather_everything(gather)
+
+    def project(t, carry):
+        rows = at_rows(t, size, 0, size)
+        dy[rows, :] = mm_nt(dz[rows, :], wout[...])
+        return carry
+
+    lax.fori_loop(0, total // size, project, 0)
+    for k in range(chans // LANES):
+        b, c, x = (low[:, pl.ds(i * chans + k * LANES, LANES)].astype(F32) for i in range(3))
+        here = pl.ds(k * LANES, LANES)
+        taps = [taps_ref[pl.ds(j, 1), here] for j in range(taps_ref.shape[0])]
+        gated = b * x
+        summed = conv_taps(gated, within, taps)
+        d = dy[:, here]
+        mixed[:, here] = (c * summed).astype(BF)
+        ds = d * c
+        dg = taps[0] * ds
+        gt_ref[pl.ds(0, 1), here] = jnp.sum(ds * gated, axis=0, keepdims=True)
+        for j in range(1, len(taps)):
+            masked = jnp.where(within >= j, ds, 0.0)
+            dg = dg + taps[j] * pltpu.roll(masked, total - j, 0)
+            gt_ref[pl.ds(j, 1), here] = jnp.sum(masked * pltpu.roll(gated, j, 0), axis=0, keepdims=True)
+        dproj[:, pl.ds(k * LANES, LANES)] = (dg * x).astype(BF)
+        dproj[:, pl.ds(chans + k * LANES, LANES)] = (d * summed).astype(BF)
+        dproj[:, pl.ds(2 * chans + k * LANES, LANES)] = (dg * b).astype(BF)
+    scatter_all(g, scatter, product(dproj, win, True), mine, tpart)
+    gout[...] = mm_tn(mixed[...], dz[...]).astype(BF)
+    save = pltpu.make_async_copy(gout, gout_hbm, osem.at[0])
+    save.start()
+    for t in range(width // 256):
+        gin[pl.ds(t * 256, 256), :] = mm_tn(nf[:, pl.ds(t * 256, 256)], dproj[...]).astype(BF)
+    more = pltpu.make_async_copy(gin, gin_hbm, osem.at[1])
+    more.start()
+    close_scatter(scatter, mine, dh_ref, h_ref, gain_ref, out_ref, gg_ref)
+    gather.finish()
+    scatter.wait_all_sends()
+    save.wait()
+    more.wait()
+
+
+def conv_backward(lengths, dh, h, gain, taps, win, wout, n, p, ident, parts=PARTS):
+    size, width = dh.shape
+    total, chans = 4 * size, wout.shape[0]
+    return pl.pallas_call(
+        conv_backward_kernel,
+        out_shape=(
+            shaped((size, width), F32), shaped((1, width), F32), shaped(taps.shape, F32), shaped((width, 3 * chans), BF),
+            shaped((chans, width), BF),
+        ),
+        in_specs=[SCALARS, INV, INV, INV, INV, HBM, HBM, HBM, HBM],
+        out_specs=(INV, INV, INV, HBM, HBM),
+        scratch_shapes=[
+            pltpu.VMEM((width, 3 * chans), BF), pltpu.VMEM((chans, width), BF), pltpu.VMEM((total, width), BF),
+            pltpu.VMEM((total, 3 * chans), BF), pltpu.VMEM((total, width), BF), pltpu.VMEM((total, chans), F32),
+            pltpu.VMEM((total, chans), BF), pltpu.VMEM((total, 3 * chans), BF), pltpu.VMEM((width, 3 * chans), BF),
+            pltpu.VMEM((chans, width), BF), pltpu.VMEM((size // parts, width), F32), pltpu.VMEM((size, width), F32),
+            *gather_scratch(parts), *scatter_scratch(size, width, parts), DMA((4,)), DMA((2,)),
+        ],
+        compiler_params=params(ident),
+        cost_estimate=pl.CostEstimate(flops=2 * 8 * total * width * chans, bytes_accessed=2 * 12 * 2**20, transcendentals=0),
+        name="conv_backward",
+    )(lengths, dh, h, gain, taps, win, wout, n, p)
+
+
+def head_sums(values, head):
+    width = values.shape[1]
+    a = lax.broadcasted_iota(jnp.int32, (width, width), 0) // head
+    b = lax.broadcasted_iota(jnp.int32, (width, width), 1) // head
+    same = jnp.where(a == b, 1.0, 0.0).astype(BF)
+    high = values.astype(BF)
+    low = (values - high.astype(F32)).astype(BF)
+    return mm(high, same) + mm(low, same)
+
+
+def turn(values, head):
+    width = values.shape[1]
+    lane = lax.broadcasted_iota(jnp.int32, values.shape, 1)
+    return jnp.where(
+        lane % head < head // 2, pltpu.roll(values, width - head // 2, 1), pltpu.roll(values, head // 2, 1)
+    )
+
+
+def wide(table, width):
+    return jnp.concatenate([table] * (width // table.shape[1]), axis=1)
+
+
+def norm_turn(raw, gain, cosine, sine, head):
+    inverse = lax.rsqrt(head_sums(raw * raw, head) * (1.0 / head) + epsilon)
+    v = raw * inverse * gain
+    return v * wide(cosine, raw.shape[1]) + turn(v, head) * wide(sine, raw.shape[1])
+
+
+def norm_turn_back(d, raw, gain, cosine, sine, head):
+    d = d * wide(cosine, raw.shape[1]) - turn(d, head) * wide(sine, raw.shape[1])
+    inverse = lax.rsqrt(head_sums(raw * raw, head) * (1.0 / head) + epsilon)
+    scaled = d * gain
+    inner = head_sums(scaled * raw, head) * (1.0 / head)
+    grad_gain = jnp.sum(d * raw * inverse, axis=0, keepdims=True)
+    return inverse * scaled - raw * (inverse * inverse * inverse * inner), grad_gain
+
+
+def score_tile(q, k, starts, first_key, first_query, scale):
+    raw = mm_nt(k, q) * scale
+    key = first_key + lax.broadcasted_iota(jnp.int32, raw.shape, 0)
+    query = first_query + lax.broadcasted_iota(jnp.int32, (1, starts.shape[1]), 1)
+    copies = raw.shape[1] // starts.shape[1]
+    allowed = (key <= wide(query, raw.shape[1])) & (key >= wide(starts, raw.shape[1]))
+    return jnp.where(allowed, raw, -1e30)
+
+
+def softmax_tile(scores):
+    top = jnp.max(scores, axis=0, keepdims=True)
+    weights = jnp.exp(scores - top)
+    return weights / jnp.sum(weights, axis=0, keepdims=True)
+
+
+def stack_heads(values, head):
+    return jnp.concatenate([values[:, i * head : (i + 1) * head] for i in range(values.shape[1] // head)], axis=0)
+
+
+def attention_tiles(total, tile):
+    back = -(-MOST_DOC // tile)
+    return [(i * tile, max(0, i - back) * tile, (i + 1) * tile) for i in range(total // tile)]
+
+
+def attention_forward_kernel(
+    head, lengths, h_ref, gain_ref, qgain_ref, kgain_ref, cos_ref, sin_ref, wq_hbm, wkv_hbm, wo_hbm,
+    out_ref, n_hbm, raw_hbm, ready_hbm, o_hbm,
+    w, wo, nf, raw, low, ready, vt, o, tpart, mine, n_near, n_over, n_on, o_near, i_near, o_over, i_over,
+    s_near, s_over, wsem, osem,
+):
+    g = Group()
+    g.greet()
+    size, width = h_ref.shape
+    total, qw = 4 * size, wo.shape[0]
+    kw = (w.shape[1] - qw) // 2
+    loads = start_all([(wq_hbm, w.at[:, pl.ds(0, qw)]), (wkv_hbm, w.at[:, pl.ds(qw, 2 * kw)]), (wo_hbm, wo)], wsem)
+    gather = Gather(g, nf, size, n_near, n_over, n_on)
+    scatter = Scatter(g, o_near, i_near, o_over, i_over, s_near, s_over, size)
+    parts, step = gather.parts, gather.step
+    nf[at_rows(g.mine, size, 0, size), :] = normalise(h_ref[...], gain_ref[...]).astype(BF)
+    g.meet()
+    gather.start()
+    wait_all(loads)
+
+    def project(block):
+        rows = at_rows(block, size, 0, size)
+        raw = mm(nf[rows, :], w[...])
+        low[rows, :] = raw.astype(BF)
+        cosine, sine = cos_ref[rows, :], sin_ref[rows, :]
+        ready[rows, pl.ds(0, qw)] = norm_turn(raw[:, :qw], qgain_ref[...], cosine, sine, head).astype(BF)
+        ready[rows, pl.ds(qw, kw)] = norm_turn(raw[:, qw : qw + kw], kgain_ref[...], cosine, sine, head).astype(BF)
+        ready[rows, pl.ds(qw + kw, kw)] = raw[:, qw + kw :].astype(BF)
+
+    project(g.mine)
+    gather.wait_beside()
+    project(g.beside)
+    for p in range(parts):
+        gather.wait_part(p)
+    for p in range(parts):
+        gather.wait_far(p)
+
+    def rest(i, carry):
+        project(jnp.where(i == 0, g.across, g.far))
+        return carry
+
+    lax.fori_loop(0, 2, rest, 0)
+    saves = start_all([(nf, n_hbm), (low, raw_hbm), (ready, ready_hbm)], osem)
+    vt[...] = jnp.transpose(ready[:, pl.ds(qw + kw, kw)].astype(F32)).astype(BF)
+    groups = qw // kw
+    tile = 256
+    scale = head ** (-0.5)
+    starts = doc_starts(lengths, lax.broadcasted_iota(jnp.int32, (1, total), 1))
+    for first, low_key, high_key in attention_tiles(total, tile):
+        keys = pl.ds(low_key, high_key - low_key)
+        for kv in range(kw // head):
+            q = stack_heads(ready[pl.ds(first, tile), pl.ds(kv * groups * head, groups * head)], head)
+            k = ready[keys, pl.ds(qw, kw)][:, kv * head : (kv + 1) * head]
+            p = softmax_tile(score_tile(q, k, starts[:, first : first + tile], low_key, first, scale)).astype(BF)
+            ot = mm(vt[pl.ds(kv * head, head), keys], p)
+            joined = jnp.concatenate([ot[:, i * tile : (i + 1) * tile] for i in range(groups)], axis=0)
+            o[pl.ds(first, tile), pl.ds(kv * groups * head, groups * head)] = jnp.transpose(joined).astype(BF)
+    save_o = pltpu.make_async_copy(o, o_hbm, osem.at[3])
+    save_o.start()
+    scatter_all(g, scatter, product(o, wo, False), mine, tpart)
+    for p in range(parts):
+        here = scatter.rows(p)
+        scatter.close(1, p).wait_recv()
+        scatter.link(p).wait_recv()
+        out_ref[here, :] = (
+            h_ref[here, :] + mine[here, :] + i_near[1, here, :].astype(F32) + i_over[here, :].astype(F32)
+        )
+    gather.finish()
+    scatter.wait_all_sends()
+    wait_all(saves)
+    save_o.wait()
+
+
+def attention_forward(head, lengths, h, gain, qgain, kgain, cosine, sine, wq, wkv, wo, ident, parts=PARTS):
+    size, width = h.shape
+    total, qw = 4 * size, wo.shape[0]
+    kw = wkv.shape[1] // 2
+    every = qw + 2 * kw
+    return pl.pallas_call(
+        functools.partial(attention_forward_kernel, head),
+        out_shape=(
+            shaped((size, width), F32), shaped((total, width), BF), shaped((total, every), BF), shaped((total, every), BF),
+            shaped((total, qw), BF),
+        ),
+        in_specs=[SCALARS, INV, INV, INV, INV, INV, INV, HBM, HBM, HBM],
+        out_specs=(INV, HBM, HBM, HBM, HBM),
+        scratch_shapes=[
+            pltpu.VMEM((width, every), BF), pltpu.VMEM((qw, width), BF), pltpu.VMEM((total, width), BF),
+            pltpu.VMEM((8, 128), F32), pltpu.VMEM((total, every), BF), pltpu.VMEM((total, every), BF),
+            pltpu.VMEM((kw, total), BF), pltpu.VMEM((total, qw), BF),
+            pltpu.VMEM((size // parts, width), F32), pltpu.VMEM((size, width), F32),
+            *gather_scratch(parts), *scatter_scratch(size, width, parts), DMA((3,)), DMA((4,)),
+        ],
+        compiler_params=params(ident),
+        cost_estimate=pl.CostEstimate(flops=2 * total * width * (every + qw), bytes_accessed=2 * 12 * 2**20, transcendentals=0),
+        name="attention_forward",
+    )(lengths, h, gain, qgain, kgain, cosine, sine, wq, wkv, wo)
+
+
+def attention_backward_kernel(
+    head, lengths, dh_ref, h_ref, gain_ref, qgain_ref, kgain_ref, cos_ref, sin_ref, wq_hbm, wkv_hbm, wo_hbm,
+    n_hbm, raw_hbm, ready_hbm, o_hbm, out_ref, gg_ref, gq_ref, gk_ref, gw_hbm, gwo_hbm,
+    w, wo, nf, low, ready, kt, o, dz, do, dq, dkv, dlow, gw, gwo, tpart, mine,
+    n_near, n_over, n_on, o_near, i_near, o_over, i_over, s_near, s_over, wsem, osem,
+):
+    g = Group()
+    g.greet()
+    size, width = h_ref.shape
+    total, qw = 4 * size, wo.shape[0]
+    kw = (w.shape[1] - qw) // 2
+    loads = start_all(
+        [
+            (ready_hbm, ready), (wo_hbm, wo), (o_hbm, o), (raw_hbm, low), (wq_hbm, w.at[:, pl.ds(0, qw)]),
+            (wkv_hbm, w.at[:, pl.ds(qw, 2 * kw)]), (n_hbm, nf),
+        ],
+        wsem,
+    )
+    gather = Gather(g, dz, size, n_near, n_over, n_on)
+    scatter = Scatter(g, o_near, i_near, o_over, i_over, s_near, s_over, size)
+    dz[at_rows(g.mine, size, 0, size), :] = dh_ref[...].astype(BF)
+    g.meet()
+    gather.start()
+    wait_all(loads)
+    kt[...] = jnp.transpose(ready[:, pl.ds(qw, kw)].astype(F32)).astype(BF)
+    dkv[...] = jnp.zeros_like(dkv)
+    gather_everything(gather)
+
+    def project(t, carry):
+        rows = at_rows(t, size, 0, size)
+        do[rows, :] = mm_nt(dz[rows, :], wo[...]).astype(BF)
+        return carry
+
+    lax.fori_loop(0, total // size, project, 0)
+    groups = qw // kw
+    tile = 256
+    scale = head ** (-0.5)
+    starts = doc_starts(lengths, lax.broadcasted_iota(jnp.int32, (1, total), 1))
+    for first, low_key, high_key in attention_tiles(total, tile):
+        keys = pl.ds(low_key, high_key - low_key)
+        for kv in range(kw // head):
+            cols = pl.ds(kv * groups * head, groups * head)
+            lane = slice(kv * head, (kv + 1) * head)
+            q = stack_heads(ready[pl.ds(first, tile), cols], head)
+            k, v = ready[keys, pl.ds(qw, kw)][:, lane], ready[keys, pl.ds(qw + kw, kw)][:, lane]
+            p = softmax_tile(score_tile(q, k, starts[:, first : first + tile], low_key, first, scale))
+            d = stack_heads(do[pl.ds(first, tile), cols], head)
+            dp = mm_nt(v, d)
+            inner = jnp.sum(p * dp, axis=0, keepdims=True)
+            ds = (p * (dp - inner)).astype(BF)
+            both = jnp.concatenate([mm(ds, q) * scale, mm(p.astype(BF), d)], axis=1)
+            dkv[kv, keys, :] += both
+            dqt = mm(kt[pl.ds(kv * head, head), keys], ds) * scale
+            joined = jnp.concatenate([dqt[:, i * tile : (i + 1) * tile] for i in range(groups)], axis=0)
+            dq[pl.ds(first, tile), cols] = jnp.transpose(joined)
+    gq_ref[...] = jnp.zeros_like(gq_ref)
+    gk_ref[...] = jnp.zeros_like(gk_ref)
+
+    def finish(t, carry):
+        rows = at_rows(t, size, 0, size)
+        cosine, sine = cos_ref[rows, :], sin_ref[rows, :]
+        d, gq = norm_turn_back(dq[rows, :], low[rows, pl.ds(0, qw)].astype(F32), qgain_ref[...], cosine, sine, head)
+        gq_ref[...] += gq
+        dlow[rows, pl.ds(0, qw)] = d.astype(BF)
+        pairs = [dkv[kv, rows, :] for kv in range(kw // head)]
+        dk = jnp.concatenate([x[:, :head] for x in pairs], axis=1)
+        dv = jnp.concatenate([x[:, head:] for x in pairs], axis=1)
+        d, gk = norm_turn_back(dk, low[rows, pl.ds(qw, kw)].astype(F32), kgain_ref[...], cosine, sine, head)
+        gk_ref[...] += gk
+        dlow[rows, pl.ds(qw, kw)] = d.astype(BF)
+        dlow[rows, pl.ds(qw + kw, kw)] = dv.astype(BF)
+        return carry
+
+    lax.fori_loop(0, total // size, finish, 0)
+    scatter_all(g, scatter, product(dlow, w, True), mine, tpart)
+    gwo[...] = mm_tn(o[...], dz[...]).astype(BF)
+    save = pltpu.make_async_copy(gwo, gwo_hbm, osem.at[0])
+    save.start()
+    for t in range(width // 256):
+        gw[pl.ds(t * 256, 256), :] = mm_tn(nf[:, pl.ds(t * 256, 256)], dlow[...]).astype(BF)
+    more = pltpu.make_async_copy(gw, gw_hbm, osem.at[1])
+    more.start()
+    close_scatter(scatter, mine, dh_ref, h_ref, gain_ref, out_ref, gg_ref)
+    gather.finish()
+    scatter.wait_all_sends()
+    save.wait()
+    more.wait()
+
+
+def attention_backward(
+    head, lengths, dh, h, gain, qgain, kgain, cosine, sine, wq, wkv, wo, n, raw, ready, o, ident, parts=PARTS
+):
+    size, width = h.shape
+    total, qw = 4 * size, wo.shape[0]
+    kw = wkv.shape[1] // 2
+    every = qw + 2 * kw
+    return pl.pallas_call(
+        functools.partial(attention_backward_kernel, head),
+        out_shape=(
+            shaped((size, width), F32), shaped((1, width), F32), shaped((1, qw), F32), shaped((1, kw), F32),
+            shaped((width, every), BF), shaped((qw, width), BF),
+        ),
+        in_specs=[SCALARS] + [INV] * 7 + [HBM] * 7,
+        out_specs=(INV, INV, INV, INV, HBM, HBM),
+        scratch_shapes=[
+            pltpu.VMEM((width, every), BF), pltpu.VMEM((qw, width), BF), pltpu.VMEM((total, width), BF),
+            pltpu.VMEM((total, every), BF), pltpu.VMEM((total, every), BF), pltpu.VMEM((kw, total), BF),
+            pltpu.VMEM((total, qw), BF), pltpu.VMEM((total, width), BF), pltpu.VMEM((total, qw), BF),
+            pltpu.VMEM((total, qw), F32), pltpu.VMEM((kw // head, total, 2 * head), F32), pltpu.VMEM((total, every), BF),
+            pltpu.VMEM((width, every), BF), pltpu.VMEM((qw, width), BF),
+            pltpu.VMEM((size // parts, width), F32), pltpu.VMEM((size, width), F32),
+            *gather_scratch(parts), *scatter_scratch(size, width, parts), DMA((7,)), DMA((2,)),
+        ],
+        compiler_params=params(ident),
+        cost_estimate=pl.CostEstimate(flops=4 * total * width * (every + qw), bytes_accessed=2 * 20 * 2**20, transcendentals=0),
+        name="attention_backward",
+    )(lengths, dh, h, gain, qgain, kgain, cosine, sine, wq, wkv, wo, n, raw, ready, o)
+
+
+rope_base = 1000000.0
+TP = ("c", "zl")
+DP = ("r", "s", "zh")
+
+
+def doc_positions(lengths_row, length):
     count = lengths_row.shape[0]
     upto = jnp.arange(count)[:, None] >= jnp.arange(count)[None, :]
     doc_ends = jnp.sum(jnp.where(upto, lengths_row[None, :], 0), axis=1)
     places = jnp.arange(length, dtype=jnp.int32)
     passed = places[:, None] >= doc_ends[None, :]
-    segment = jnp.sum(passed.astype(jnp.int32), axis=1)
-    doc_start = jnp.max(jnp.where(passed, doc_ends[None, :], 0), axis=1)
-    return (segment, places - doc_start)
+    return places - jnp.max(jnp.where(passed, doc_ends[None, :], 0), axis=1)
 
 
 def rope_tables(position, head_dim):
     half_dim = head_dim // 2
     inverse = rope_base ** (-2.0 * jnp.arange(half_dim, dtype=F32) / head_dim)
     angles = position.astype(F32)[:, None] * inverse[None, :]
-    return (jnp.cos(angles)[:, None, :], jnp.sin(angles)[:, None, :])
-
-
-def rotate(values, tables):
-    cosine, sine = tables
-    half_dim = values.shape[-1] // 2
-    first_half, second_half = (values[..., :half_dim], values[..., half_dim:])
-    return jnp.concatenate(
-        [first_half * cosine - second_half * sine, second_half * cosine + first_half * sine],
-        axis=-1,
+    cosine, sine = jnp.cos(angles), jnp.sin(angles)
+    copies = LANES // head_dim
+    return (
+        jnp.concatenate([cosine, cosine] * copies, axis=1),
+        jnp.concatenate([-sine, sine] * copies, axis=1),
     )
-
-
-def rotate_back(gradient, tables):
-    cosine, sine = tables
-    half_dim = gradient.shape[-1] // 2
-    first_half, second_half = (gradient[..., :half_dim], gradient[..., half_dim:])
-    return jnp.concatenate(
-        [first_half * cosine + second_half * sine, second_half * cosine - first_half * sine],
-        axis=-1,
-    )
-
-
-def shift_down(values, offset):
-    filler = jnp.zeros((offset,) + values.shape[1:], values.dtype)
-    return jnp.concatenate([filler, values[: values.shape[0] - offset]], axis=0)
-
-
-def shift_up(values, offset):
-    filler = jnp.zeros((offset,) + values.shape[1:], values.dtype)
-    return jnp.concatenate([values[offset:], filler], axis=0)
-
-
-def rms_forward(values, norm_gain):
-    inverse = lax.rsqrt(jnp.mean(values * values, axis=-1, keepdims=True) + epsilon)
-    return (values * inverse * norm_gain, inverse)
-
-
-def rms_backward(upstream, values, inverse, norm_gain):
-    scaled = upstream * norm_gain
-    inner = jnp.mean(scaled * values, axis=-1, keepdims=True)
-    grad_values = inverse * scaled - values * inverse**3 * inner
-    leading = tuple(range(values.ndim - 1))
-    grad_gain = jnp.sum(upstream * values * inverse, axis=leading)
-    return (grad_values, grad_gain)
-
-
-def dot(a, b):
-    return jnp.dot(a, b, preferred_element_type=F32)
 
 
 def swap(x):
     return lax.ppermute(x, ("c", "zh"), [(0, 0), (1, 2), (2, 1), (3, 3)])
 
 
-def gather_rows(block):
-    return lax.all_gather(block, TP, axis=0, tiled=True)
-
-
-def scatter_rows(partial):
-    return lax.psum_scatter(partial.astype(BF), TP, scatter_dimension=0, tiled=True).astype(F32)
-
-
 def gather_dp(shard, axis):
     return lax.all_gather(shard, DP, axis=axis, tiled=True)
 
 
 def scatter_dp(partial, axis):
     return lax.psum_scatter(partial.astype(BF), DP, scatter_dimension=axis, tiled=True)
-
-
-def conv_local(normed, conv_in, conv_kernel, same):
-    projected = dot(normed, conv_in)
-    width = conv_kernel.shape[1]
-    gated = projected[:, :width] * projected[:, 2 * width :]
-    summed = conv_kernel[0] * gated
-    for offset in range(1, conv_kernel.shape[0]):
-        summed = summed + conv_kernel[offset] * jnp.where(
-            same[offset][:, None], shift_down(gated, offset), 0.0
-        )
-    mixed = (projected[:, width : 2 * width] * summed).astype(BF)
-    return projected, summed, mixed
-
-
-def reactivate(hidden):
-    hidden = hidden.astype(F32)
-    half = hidden.shape[1] // 2
-    return hidden, (jax.nn.silu(hidden[:, :half]) * hidden[:, half:]).astype(BF)
 
 
 def local(
@@ -393,12 +1053,9 @@
     length = tokens.shape[0]
     head_dim = head_gains.shape[1]
     quarter = lax.axis_index("c") * 2 + lax.axis_index("zl")
-    group = 4
-    rows = length // group
-    segment, position = doc_layout(swap(doc_lengths)[0], length)
-    places = jnp.arange(length, dtype=jnp.int32)
-    same = [None] + [position >= j for j in range(1, conv_kernel.shape[0])]
-    tables = rope_tables(position, head_dim)
+    rows = length // 4
+    lengths = swap(doc_lengths)
+    cosine, sine = rope_tables(doc_positions(lengths[0], length), head_dim)
     conv_in = swap(conv_in.reshape(conv_in.shape[0], -1))
     conv_kernel = swap(conv_kernel)
     conv_out = swap(conv_out)
@@ -407,124 +1064,51 @@
     out_w = swap(out_w)
     ws = [gather_dp(swap(gate_up[l].reshape(gate_up.shape[1], -1)), 0) for l in (0, 1)]
     vs = [gather_dp(swap(down[l]), 1) for l in (0, 1)]
-
-    x_full = lax.all_gather(swap(tokens), TP, axis=1, tiled=True)
+    kv_width = kv_w.shape[1] // 2
+    qgain = jnp.tile(head_gains[0:1], (1, query_w.shape[1] // head_dim))
+    kgain = jnp.tile(head_gains[1:2], (1, kv_width // head_dim))
+    gain = [norm_gains[i : i + 1] for i in range(4)]
+
     up_full = lax.all_gather(swap(grad_out), TP, axis=1, tiled=True)
-    my = lambda a: lax.dynamic_slice_in_dim(a, quarter * rows, rows, 0)
-    n0 = rms_forward(x_full.astype(F32), norm_gains[0])[0].astype(BF)
-    h0 = my(x_full).astype(F32)
-    projected, summed, mixed = conv_local(n0, conv_in, conv_kernel, same)
-    h1 = h0 + scatter_rows(dot(mixed, conv_out))
-    h2, n1, hidden0 = ffn_forward(h1, norm_gains[1:2], ws[0], vs[0], 1)
-    hidden0, active0 = reactivate(hidden0)
-    n2 = gather_rows(rms_forward(h2, norm_gains[2])[0].astype(BF))
-
-    kv_heads = kv_w.shape[1] // 2 // head_dim
-    qr = dot(n2, query_w).reshape(length, -1, head_dim)
-    pair = dot(n2, kv_w).reshape(length, 2, kv_heads, head_dim)
-    qn, qinv = rms_forward(qr, head_gains[0])
-    kn, kinv = rms_forward(pair[:, 0], head_gains[1])
-    q = rotate(qn, tables).astype(BF)
-    k = rotate(kn, tables).astype(BF)
-    v = pair[:, 1].astype(BF)
-    groups = q.shape[1] // kv_heads
-    scale = head_dim ** (-0.5)
-    q4 = q.reshape(length, kv_heads, groups, head_dim)
-    allowed = (places[None, :] <= places[:, None]) & (segment[None, :] == segment[:, None])
-    scores = jnp.einsum("bkgd,skd->kgbs", q4, k, preferred_element_type=F32) * scale
-    scores = jnp.where(allowed, scores, -1e30)
-    top = jnp.max(scores, axis=-1, keepdims=True)
-    weights = jnp.exp(scores - top)
-    probs = weights / jnp.sum(weights, axis=-1, keepdims=True)
-    probs_low = probs.astype(BF)
-    o = jnp.einsum("kgbs,skd->bkgd", probs_low, v, preferred_element_type=F32)
-    o = o.reshape(length, -1).astype(BF)
-    h3 = h2 + scatter_rows(dot(o, out_w))
-    h4, n3, hidden1 = ffn_forward(h3, norm_gains[3:4], ws[1], vs[1], 2)
-    hidden1, active1 = reactivate(hidden1)
+    h1, x_block, n0, projected = conv_forward(lengths, swap(tokens), gain[0], conv_kernel, conv_in, conv_out, 0)
+    h2, n1, hidden0 = ffn_forward(h1, gain[1], ws[0], vs[0], 1)
+    h3, n2, raw, ready, attended = attention_forward(
+        head_dim, lengths, h2, gain[2], qgain, kgain, cosine, sine, query_w, kv_w, out_w, 2
+    )
+    h4, n3, hidden1 = ffn_forward(h3, gain[3], ws[1], vs[1], 3)
     output = swap(lax.all_to_all(h4.astype(BF), TP, 1, 0, tiled=True))
 
-    def ffn_back(gathered, dh, h, normed, hidden, active, w, vv, gain):
-        grad_active = dot(gathered, vv.T)
-        grad_down = dot(active.T, gathered)
-        half = hidden.shape[1] // 2
-        gate, upp = hidden[:, :half], hidden[:, half:]
-        s = jax.nn.sigmoid(gate)
-        grad_hidden = jnp.concatenate(
-            [grad_active * upp * s * (1.0 + gate * (1.0 - s)), grad_active * (gate * s)], axis=1
-        ).astype(BF)
-        grad_w = dot(normed.T, grad_hidden)
-        dn = scatter_rows(dot(grad_hidden, w.T))
-        inverse = rms_forward(h, gain)[1]
-        term, grad_gain = rms_backward(dn, h, inverse, gain)
-        return dh + term, grad_gain, grad_w, grad_down
-
-    dh4 = my(up_full).astype(F32)
-    dh3, gain3, gw1, gv1 = ffn_back(up_full, dh4, h3, n3, hidden1, active1, ws[1], vs[1], norm_gains[3])
-    dz = gather_rows(dh3.astype(BF))
-    grad_out_w = dot(o.T, dz)
-    do = dot(dz, out_w.T).astype(BF).reshape(length, kv_heads, groups, head_dim)
-    dp = jnp.einsum("bkgd,skd->kgbs", do, v, preferred_element_type=F32)
-    inner = jnp.sum(probs * dp, axis=-1, keepdims=True)
-    ds = (probs * (dp - inner)).astype(BF)
-    dq = jnp.einsum("kgbs,skd->bkgd", ds, k, preferred_element_type=F32) * scale
-    dk = jnp.einsum("kgbs,bkgd->skd", ds, q4, preferred_element_type=F32) * scale
-    dv = jnp.einsum("kgbs,bkgd->skd", probs_low, do, preferred_element_type=F32)
-    dq = dq.reshape(length, -1, head_dim)
-    dqr, gq = rms_backward(rotate_back(dq, tables), qr, qinv, head_gains[0])
-    dkr, gk = rms_backward(rotate_back(dk, tables), pair[:, 0], kinv, head_gains[1])
-    dqr = dqr.astype(BF).reshape(length, -1)
-    dpair = jnp.concatenate([dkr.reshape(length, -1), dv.reshape(length, -1)], axis=1).astype(BF)
-    gqw = dot(n2.T, dqr)
-    gkvw = dot(n2.T, dpair)
-    dn2 = scatter_rows(dot(dqr, query_w.T) + dot(dpair, kv_w.T))
-    term, gain2 = rms_backward(dn2, h2, rms_forward(h2, norm_gains[2])[1], norm_gains[2])
-    dh2 = dh3 + term
-    dh1, gain1, gw0, gv0 = ffn_back(
-        gather_rows(dh2.astype(BF)), dh2, h1, n1, hidden0, active0, ws[0], vs[0], norm_gains[1]
+    dh4 = lax.dynamic_slice_in_dim(up_full, quarter * rows, rows, 0).astype(F32)
+    dh3, gain3, gw1, gv1 = ffn_backward(dh4, h3, gain[3], up_full, ws[1], vs[1], n3, hidden1, 4)
+    dh2, gain2, gq, gk, gqkv, gow = attention_backward(
+        head_dim, lengths, dh3, h2, gain[2], qgain, kgain, cosine, sine, query_w, kv_w, out_w, n2, raw, ready, attended, 5
     )
-    dz = gather_rows(dh1.astype(BF))
-    gco = dot(mixed.T, dz)
-    dy = dot(dz, conv_out.T)
-    width = conv_kernel.shape[1]
-    gb, gc, gx = (projected[:, i * width : (i + 1) * width] for i in range(3))
-    gated = gb * gx
-    grad_c = dy * summed
-    gs = dy * gc
-    gg = conv_kernel[0] * gs
-    kernel_rows = [jnp.sum(gs * gated, axis=0)]
-    for offset in range(1, conv_kernel.shape[0]):
-        masked = jnp.where(same[offset][:, None], gs, 0.0)
-        gg = gg + conv_kernel[offset] * shift_up(masked, offset)
-        kernel_rows.append(jnp.sum(masked * shift_down(gated, offset), axis=0))
-    dprojected = jnp.concatenate([gg * gx, grad_c, gg * gb], axis=1).astype(BF)
-    gci = dot(n0.T, dprojected)
-    dn0 = scatter_rows(dot(dprojected, conv_in.T))
-    term, gain0 = rms_backward(dn0, h0, rms_forward(h0, norm_gains[0])[1], norm_gains[0])
-    dh0 = dh1 + term
+    dh1, gain1, gw0, gv0 = ffn_backward(dh2, h1, gain[1], None, ws[0], vs[0], n1, hidden0, 6)
+    dh0, gain0, gtaps, gci, gco = conv_backward(
+        lengths, dh1, x_block.astype(F32), gain[0], conv_kernel, conv_in, conv_out, n0, projected, 7
+    )
     grad_tokens = swap(lax.all_to_all(dh0, TP, 1, 0, tiled=True))
 
     back = lambda g, axis: swap(scatter_dp(g, axis)).astype(F32)
     kernel_full = jnp.zeros((conv_kernel.shape[0], norm_gains.shape[1]), F32)
-    kernel_full = lax.dynamic_update_slice_in_dim(
-        kernel_full, jnp.stack(kernel_rows), quarter * width, 1
-    )
+    kernel_full = lax.dynamic_update_slice_in_dim(kernel_full, gtaps, quarter * conv_kernel.shape[1], 1)
+    head_grads = jnp.stack([jnp.sum(x.reshape(-1, head_dim), axis=0) for x in (gq, gk)])
     gains, heads, kernels = lax.psum(
-        (jnp.stack([gain0, gain1, gain2, gain3]), jnp.stack([gq, gk]), kernel_full),
-        ("r", "c", "zh", "zl"),
+        (jnp.concatenate([gain0, gain1, gain2, gain3]), head_grads, kernel_full), ("r", "s", "c", "zh", "zl")
     )
     eighth = gate_up.shape[1]
+    gqkv = back(gqkv, 0)
     return (
         output,
         grad_tokens,
         gains,
         heads,
-        back(gci, 0).reshape(-1, 3, width),
+        back(gci, 0).reshape(-1, 3, conv_kernel.shape[1]),
         kernels,
         back(gco, 1),
-        back(gqw, 0),
-        back(gkvw, 0).reshape(-1, 2, kv_heads * head_dim),
-        back(grad_out_w, 1),
+        gqkv[:, : query_w.shape[1]],
+        gqkv[:, query_w.shape[1] :].reshape(-1, 2, kv_width),
+        back(gow, 1),
         jnp.stack([back(gw0, 0), back(gw1, 0)]).reshape(2, eighth, 2, -1),
         jnp.stack([back(gv0, 1), back(gv1, 1)]),
     )
@@ -533,8 +1117,8 @@
 def solution(mesh):
     devices = mesh.devices
     dp, tp = devices.shape
-    inner = Mesh(devices.reshape(dp // 2, 2, 2, tp // 2), ("r", "c", "zh", "zl"))
-    D = ("r", "c")
+    inner = Mesh(devices.reshape(dp // 4, 2, 2, 2, tp // 2), ("r", "s", "c", "zh", "zl"))
+    D = ("r", "s", "c")
     T = ("zh", "zl")
     return jax.shard_map(
         local,

time: 1660 us -> 1170 us (0.70)
  waiting for transfers between devices: 1150 us -> 609 us
  Pallas kernels: 78.4 us -> 354 us
  matrix products: 150 us -> 0 us
  other arithmetic: 69.1 us -> 16.8 us
    pallas_call x0 -> x6, Pallas kernels: none -> 281 us  [the longest x2 90.1 us: ffn_backward(): pl.pallas_call(functools.partial(ffn_backward_kernel, known), out_shape=(...]
    all_gather x5 -> x0, waiting for transfers between devices: 186 us -> none  [the longest x4 159 us: gather_rows(): return lax.all_gather(block, TP, axis=0, tiled=True)]
    reduce_scatter x6 -> x0, waiting for transfers between devices: 154 us -> none  [scatter_rows(): lax.psum_scatter(partial.astype(BF), TP, scatter_dimension=0, tiled=True)]
    dot_general x28 -> x0, matrix products: 139 us -> none  [the longest x23 108 us: dot(): return jnp.dot(a, b, preferred_element_type=F32)]
    all_gather x4, waiting for transfers between devices: 214 us -> 85.6 us  [gather_dp(): return lax.all_gather(shard, DP, axis=axis, tiled=True)]
    reduce_scatter x5 -> x4, waiting for transfers between devices: 267 us -> 187 us  [scatter_dp(): lax.psum_scatter(partial.astype(BF), DP, scatter_dimension=axis, tiled=True)]
    ppermute x24 -> x23, waiting for transfers between devices: 122 us -> 157 us  [swap(): return lax.ppermute(x, ('c', 'zh'), [(0, 0), (1, 2), (2, 1), (3, 3)])]
    unnamed x29 -> x17, waiting for transfers between devices: 186 us -> 152 us
  transfers between devices with their start and end apart: 51 -> 38, of which waited for: 36 -> 19; matrix products, arithmetic and copies ran while one was open for 9% -> 4% of each run, Pallas kernels for 3% -> 20%
where the time goes in v3:
time: 1170 us; the launch traced here: 1160 us
  waiting for transfers between devices  609 us (52%)
  Pallas kernels  354 us (30%)
  starting transfers between devices  81.5 us (7%)
  blocking collectives  46.6 us (4%)
  local copies, waits for them, and re-layouts  37.6 us (3%)
  other arithmetic  16.8 us (1%)
  between operations  14.9 us (1%)
    reduce_scatter x4, waiting for transfers between devices, scatter_dp(): lax.psum_scatter(partial.astype(BF), DP, scatter_dimension=axis, tiled=True)  187 us
    ppermute x23, waiting for transfers between devices, swap(): return lax.ppermute(x, ('c', 'zh'), [(0, 0), (1, 2), (2, 1), (3, 3)])  157 us
    unnamed x17, waiting for transfers between devices  152 us
    pallas_call x2, Pallas kernels, ffn_backward(): pl.pallas_call(functools.partial(ffn_backward_kernel, known), out_shape=(...  90.1 us
    all_gather x4, waiting for transfers between devices, gather_dp(): return lax.all_gather(shard, DP, axis=axis, tiled=True)  85.6 us
    pallas_call x2, Pallas kernels, ffn_forward(): pl.pallas_call(ffn_forward_kernel, out_shape=(jax.ShapeDtypeStruct((size,...  73.6 us
    ppermute x23, starting transfers between devices, swap(): return lax.ppermute(x, ('c', 'zh'), [(0, 0), (1, 2), (2, 1), (3, 3)])  71.6 us
    pallas_call x1, Pallas kernels, attention_forward(): pl.pallas_call(functools.partial(attention_forward_kernel, head), out_sha...  54.3 us
  transfers between devices with their start and end apart: 38, of which 19 were waited for; matrix products, arithmetic and copies ran while one was open for 4% of the time, Pallas kernels for 20%

profile of v3, /device:TPU:1, one launch (start us, length us, event | category | flops | bytes accessed | tf_op | source)
XLA Modules:
  0.0 1160.5 jit_solution(18188638220792246995)
XLA Ops:
  7.2 5.7 collective-permute-start.13
  13.0 12.7 %collective-permute-done.13 = bf16[1024,256]{1,0:T(8,128)(2,1)S(1)} collective-permute-done((bf16[1024,256]{1,0:T(8,128)(2,1)}, bf16[1024,256]{1,0:T(8,128)(2,1)S(1)}, u32[]{:S(2)}, u32[]{:S(2)}) %collective-permute-start.13) | collective-permute-done | bytes 524320 | tf_op jit(solution)/shard_map/ppermute | solution.py:1038
  27.6 1.9 collective-permute-start.6
  29.5 10.3 collective-permute-done.6
  41.5 2.1 collective-permute-start.5
  43.6 15.8 %collective-permute-done.5 = bf16[128,2304]{1,0:T(8,128)(2,1)S(1)} collective-permute-done((bf16[128,2304]{1,0:T(8,128)(2,1)S(1)}, bf16[128,2304]{1,0:T(8,128)(2,1)S(1)}, u32[]{:S(2)}, u32[]{:S(2)}) %collective-permute-start.5) | collective-permute-done | bytes 589856 | tf_op jit(solution)/shard_map/ppermute | solution.py:1038
  60.3 5.3 collective-permute-start.11
  65.6 8.2 collective-permute-done.11
  74.7 5.3 collective-permute-start.10
  80.0 13.9 %collective-permute-done.10 = bf16[128,2304]{1,0:T(8,128)(2,1)S(1)} collective-permute-done((bf16[128,2304]{1,0:T(8,128)(2,1)S(1)}, bf16[128,2304]{1,0:T(8,128)(2,1)S(1)}, u32[]{:S(2)}, u32[]{:S(2)}) %collective-permute-start.10) | collective-permute-done | bytes 589856 | tf_op jit(solution)/shard_map/ppermute | solution.py:1038
  96.4 1.9 collective-permute-start.3
  98.4 4.5 collective-permute-start
  102.9 1.9 collective-permute-start.1
  104.8 4.5 collective-permute-start.2
  109.4 1.9 collective-permute-start.4
  114.3 68.9 %collective-permute-done.lengths = s32[1,6]{1,0:T(1,128)S(1)} collective-permute-done((s32[1,6]{1,0:T(1,128)S(1)}, s32[1,6]{1,0:T(1,128)S(1)}, u32[]{:S(2)}, u32[]{:S(2)}) %collective-permute-start) | collective-permute-done | bytes 56 | tf_op jit(solution)/shard_map/ppermute | solution.py:1038
  183.3 1.9 collective-permute-start.7
  185.4 1.9 fusion
  187.3 1.9 pad_maximum_fusion
  189.2 7.3 collective-permute-done.2.taps_ref
  196.5 1.9 collective-permute-start.8
  198.4 4.5 collective-permute-start.9
  203.0 14.5 %collective-permute-done.4.wout_hbm = bf16[256,1024]{1,0:T(8,128)(2,1)} collective-permute-done((bf16[256,1024]{1,0:T(8,128)(2,1)}, bf16[256,1024]{1,0:T(8,128)(2,1)}, u32[]{:S(2)}, u32[]{:S(2)}) %collective-permute-start.4) | collective-permute-done | bytes 524320 | tf_op jit(solution)/shard_map/ppermute | solution.py:1038
  217.5 52.2 %conv_forward.1 = (f32[256,1024]{1,0:T(8,128)}, bf16[256,1024]{1,0:T(8,128)(2,1)}, bf16[1024,1024]{1,0:T(8,128)(2,1)}, bf16[1024,768]{1,0:T(8,128)(2,1)}) custom-call(s32[1,6]{1,0:T(1,128)} %copy-done.25, bf16[1024,256]{1,0:T(8,128)(2,1)} %collective-permute-done.1.x_ref, f32[1,1024]{1,0:T(1,128)} %get-tuple-element.151.gain_ref, f32[3,256]{1,0:T(4,128)} %copy-done.23, ...), custom_call_target="tpu_custom_call" | custom-call | flops 2147483648 | bytes 16777216 | tf_op jit(solution)/shard_map/conv_forward/pallas_call | solution.py:630
  269.7 2.1 dynamic-slice_convert_fusion.dh_ref
  271.8 22.3 %all-gather.6.cloned.1.call-done.w_hbm = bf16[1024,2304]{1,0:T(8,128)(2,1)} async-done(((bf16[128,2304]{1,0:T(8,128)(2,1)}), bf16[1024,2304]{1,0:T(8,128)(2,1)}) %all-gather.6.cloned.1.call-update) | async-done | bytes 4718608 | tf_op jit(solution)/shard_map/all_gather | solution.py:1042
  294.1 39.5 %ffn_forward.2 = (f32[256,1024]{1,0:T(8,128)}, bf16[1024,1024]{1,0:T(8,128)(2,1)}, bf16[1024,2304]{1,0:T(8,128)(2,1)}) custom-call(f32[256,1024]{1,0:T(8,128)} %get-tuple-element.46.h_ref, f32[1,1024]{1,0:T(1,128)} %get-tuple-element.150.gain_ref, bf16[1024,2304]{1,0:T(8,128)(2,1)} %all-gather.6.cloned.1.call-done.w_hbm, ...), custom_call_target="tpu_custom_call" | custom-call | flops 7247757312 | bytes 25165824 | tf_op jit(solution)/shard_map/ffn_forward/pallas_call | solution.py:258
  334.5 54.3 %attention_forward.1 = (f32[256,1024]{1,0:T(8,128)}, bf16[1024,1024]{1,0:T(8,128)(2,1)}, bf16[1024,512]{1,0:T(8,128)(2,1)}, bf16[1024,512]{1,0:T(8,128)(2,1)}, bf16[1024,256]{1,0:T(8,128)(2,1)}) custom-call(s32[1,6]{1,0:T(1,128)} %copy-done.25, f32[256,1024]{1,0:T(8,128)} %get-tuple-element.47.h_ref, f32[1,1024]{1,0:T(1,128)} %get-tuple-element.152.gain_ref, ...), custom_call_target="tpu_custom_call" | custom-call | flops 1610612736 | bytes 25165824 | tf_op jit(solution)/shard_map/attention_forward/pallas_call | solution.py:871
  388.8 63.3 %all-gather.10.cloned.1.call-done.w_hbm = bf16[1024,2304]{1,0:T(8,128)(2,1)} async-done(((bf16[128,2304]{1,0:T(8,128)(2,1)}), bf16[1024,2304]{1,0:T(8,128)(2,1)}) %all-gather.10.cloned.1.call-update) | async-done | bytes 4718608 | tf_op jit(solution)/shard_map/all_gather | solution.py:1042
  452.1 34.0 %ffn_forward.3 = (f32[256,1024]{1,0:T(8,128)}, bf16[1024,1024]{1,0:T(8,128)(2,1)}, bf16[1024,2304]{1,0:T(8,128)(2,1)}) custom-call(f32[256,1024]{1,0:T(8,128)} %get-tuple-element.48.h_ref, f32[1,1024]{1,0:T(1,128)} %get-tuple-element.149.gain_ref, bf16[1024,2304]{1,0:T(8,128)(2,1)} %all-gather.10.cloned.1.call-done.w_hbm, ...), custom_call_target="tpu_custom_call" | custom-call | flops 7247757312 | bytes 25165824 | tf_op jit(solution)/shard_map/ffn_forward/pallas_call | solution.py:258
  486.1 40.7 %ffn_backward.2 = (f32[256,1024]{1,0:T(8,128)}, f32[1,1024]{1,0:T(1,128)}, bf16[1024,2304]{1,0:T(8,128)(2,1)}, bf16[1152,1024]{1,0:T(8,128)(2,1)}) custom-call(f32[256,1024]{1,0:T(8,128)} %dynamic-slice_convert_fusion.dh_ref, f32[256,1024]{1,0:T(8,128)} %get-tuple-element.48.h_ref, f32[1,1024]{1,0:T(1,128)} %get-tuple-element.149.gain_ref, ...), custom_call_target="tpu_custom_call" | custom-call | flops 14495514624 | bytes 41943040 | tf_op jit(solution)/shard_map/ffn_backward/pallas_call | solution.py:444
  526.8 47.4 %attention_backward.1 = (f32[256,1024]{1,0:T(8,128)}, f32[1,1024]{1,0:T(1,128)}, f32[1,256]{1,0:T(1,128)}, f32[1,128]{1,0:T(1,128)}, bf16[1024,512]{1,0:T(8,128)(2,1)}, /*index=5*/bf16[256,1024]{1,0:T(8,128)(2,1)}) custom-call(s32[1,6]{1,0:T(1,128)} %copy-done.25, f32[256,1024]{1,0:T(8,128)} %get-tuple-element.52.dh_ref, ...), custom_call_target="tpu_custom_call" | custom-call | flops 3221225472 | bytes 41943040 | tf_op jit(solution)/shard_map/attention_backward/pallas_call | solution.py:988
  575.4 49.4 %ffn_backward.3 = (f32[256,1024]{1,0:T(8,128)}, f32[1,1024]{1,0:T(1,128)}, bf16[1024,2304]{1,0:T(8,128)(2,1)}, bf16[1152,1024]{1,0:T(8,128)(2,1)}) custom-call(f32[256,1024]{1,0:T(8,128)} %get-tuple-element.57.dh_ref, f32[256,1024]{1,0:T(8,128)} %get-tuple-element.46.h_ref, f32[1,1024]{1,0:T(1,128)} %get-tuple-element.150.gain_ref, ...), custom_call_target="tpu_custom_call" | custom-call | flops 14495514624 | bytes 41943040 | tf_op jit(solution)/shard_map/ffn_backward/pallas_call | solution.py:444
  624.8 36.9 %conv_backward.1 = (f32[256,1024]{1,0:T(8,128)}, f32[1,1024]{1,0:T(1,128)}, f32[3,256]{1,0:T(4,128)}, bf16[1024,768]{1,0:T(8,128)(2,1)}, bf16[256,1024]{1,0:T(8,128)(2,1)}) custom-call(s32[1,6]{1,0:T(1,128)} %copy-done.25, f32[256,1024]{1,0:T(8,128)} %get-tuple-element.60.dh_ref, f32[256,1024]{1,0:T(8,128)} %convert_element_type.33.h_ref, ...), custom_call_target="tpu_custom_call" | custom-call | flops 4294967296 | bytes 25165824 | tf_op jit(solution)/shard_map/conv_backward/pallas_call | solution.py:711
  661.8 2.2 copy.54
  665.2 2.4 copy.60
  669.3 2.6 copy.58
  675.0 5.3 all-to-all-start.1
  681.3 18.7 %all-to-all-done.1 = f32[256,4,256]{2,0,1:T(8,128)S(1)} async-done(((f32[256,4,256]{2,0,1:T(8,128)}), f32[256,4,256]{2,0,1:T(8,128)S(1)}, u32[]{:S(2)}, u32[]{:S(2)}) %all-to-all-start.1) | async-done | bytes 1048608 | tf_op jit(solution)/shard_map/all_to_all | solution.py:1090
  699.9 4.1 all-to-all-start
  704.0 1.9 collective-permute-start.14
  705.9 8.2 all-to-all-done
  714.2 2.0 collective-permute-start.12
  716.2 4.4 collective-permute-start.17
  724.8 2.0 collective-permute-start.16
  726.8 32.3 %reduce-scatter.27.cloned.1.call-done = bf16[128,256]{1,0:T(8,128)(2,1)} async-done(((bf16[1024,256]{1,0:T(8,128)(2,1)}), bf16[128,256]{1,0:T(8,128)(2,1)}) %reduce-scatter.27.cloned.1.call-update) | async-done | bytes 65552
  760.1 4.8 collective-permute-start.18
  766.8 58.2 %reduce-scatter.31.cloned.1.call-done = bf16[128,1152]{1,0:T(8,128)(2,1)} async-done(((bf16[1024,1152]{1,0:T(8,128)(2,1)}), bf16[128,1152]{1,0:T(8,128)(2,1)}) %reduce-scatter.31.cloned.1.call-update) | async-done | bytes 294928
  825.0 1.8 copy.61
  826.9 59.4 %reduce-scatter.29.cloned.1.call-done = bf16[128,1152]{1,0:T(8,128)(2,1)} async-done(((bf16[1024,1152]{1,0:T(8,128)(2,1)}), bf16[128,1152]{1,0:T(8,128)(2,1)}) %reduce-scatter.29.cloned.1.call-update) | async-done | bytes 294928
  886.3 1.8 copy.59
  888.1 1.9 collective-permute-start.22
  890.1 4.5 collective-permute-start.21
  894.6 88.9 %reduce-scatter.23.cloned.1.call-done = bf16[128,2304]{1,0:T(8,128)(2,1)} async-done(((bf16[1024,2304]{1,0:T(8,128)(2,1)}), bf16[128,2304]{1,0:T(8,128)(2,1)}) %reduce-scatter.23.cloned.1.call-update) | async-done | bytes 589840 | tf_op jit(solution)/shard_map/reduce_scatter | solution.py:1046
  983.5 1.9 collective-permute-start.20
  985.5 93.5 %reduce-scatter.21.cloned.1.call-done = bf16[128,2304]{1,0:T(8,128)(2,1)} async-done(((bf16[1024,2304]{1,0:T(8,128)(2,1)}), bf16[128,2304]{1,0:T(8,128)(2,1)}) %reduce-scatter.21.cloned.1.call-update) | async-done | bytes 589840 | tf_op jit(solution)/shard_map/reduce_scatter | solution.py:1046
  1078.9 1.9 collective-permute-start.19
  1081.5 46.6 %all-reduce = (f32[4,1024]{1,0:T(4,128)}, f32[2,64]{1,0:T(2,128)}, f32[3,1024]{1,0:T(4,128)}) all-reduce(f32[4,1024]{1,0:T(4,128)S(1)} %pad_maximum_fusion.2, f32[2,64]{1,0:T(2,128)S(1)} %pad_maximum_fusion.3, f32[3,1024]{1,0:T(4,128)} %constant_dynamic-update-slice_fusion), channel_id=1, replica_groups=mesh['r'=2,'s'=2,'c'=2,'zh'=2,'zl'=2] {'r','s','c','zh','zl'}, use_global_device_ids=true, to_apply=%region_2.3 | all-reduce | flops 7296 | bytes 58368 | tf_op jit(solution)/shard_map/psum | solution.py:1096
  1129.4 4.3 reduce-scatter.17.cloned.1.call-done
  1133.7 2.6 collective-permute-start.15
  1137.7 5.8 collective-permute-done.15
  1144.6 2.1 maximum_convert_fusion.1
  1146.9 2.1 stack.37
  1149.0 2.9 maximum_convert_fusion
  (143 shorter events, 33.1 us)
Async XLA Ops:
  7.2 33.4 %copy-start.3 = (bf16[2,128,2,1152]{3,2,1,0:T(2,128)(2,1)S(1)}, bf16[2,128,2,1152]{3,2,1,0:T(2,128)(2,1)}, u32[]{:S(2)}) copy-start(bf16[2,128,2,1152]{3,2,1,0:T(2,128)(2,1)} %param.24) | copy-start | bytes 3538948
  7.2 262.5 %all-gather.14.cloned.1.call-start = ((), (), s32[]{:S(2)}) async-start(), calls=%async_computation.14 | async-start | bytes 2621440 | tf_op jit(solution)/shard_map/all_gather | solution.py:1072
  7.2 18.4 %collective-permute-start.13 = (bf16[1024,256]{1,0:T(8,128)(2,1)}, bf16[1024,256]{1,0:T(8,128)(2,1)S(1)}, u32[]{:S(2)}, u32[]{:S(2)}) collective-permute-start(bf16[1024,256]{1,0:T(8,128)(2,1)} %param.15), channel_id=1, source_target_pairs={{0,0},{2,4},{4,2},{6,6},{1,1},{3,5},{5,3},{7,7},{8,8},{10,12},{12,... | collective-permute-start | bytes 1572872 | tf_op jit(solution)/shard_map/ppermute | solution.py:1038
  25.7 0.8 copy-start.9
  26.5 245.4 %all-gather.8.cloned.1.call-start = ((), (), s32[]{:S(2)}) async-start(), calls=%async_computation.11 | async-start | bytes 2654208 | tf_op jit(solution)/shard_map/all_gather | solution.py:1042
  27.6 12.2 %collective-permute-start.6 = (bf16[1152,128]{1,0:T(8,128)(2,1)S(1)}, bf16[1152,128]{1,0:T(8,128)(2,1)S(1)}, u32[]{:S(2)}, u32[]{:S(2)}) collective-permute-start(bf16[1152,128]{1,0:T(8,128)(2,1)S(1)} %get-tuple-element.146), channel_id=1, source_target_pairs={{0,0},{2,4},{4,2},{6,6},{1,1},{3,5},{5,3},{7,7},{8,8},{10,12},{12,... | collective-permute-start | bytes 884744 | tf_op jit(solution)/shard_map/ppermute | solution.py:1038
  40.6 253.6 %all-gather.6.cloned.1.call-start = ((), (), s32[]{:S(2)}) async-start(), calls=%async_computation.10 | async-start | bytes 5308416 | tf_op jit(solution)/shard_map/all_gather | solution.py:1042
  41.4 53.3 %copy-start.2 = (bf16[1024,3,256]{2,0,1:T(8,128)(2,1)S(1)}, bf16[1024,3,256]{2,0,1:T(8,128)(2,1)}, u32[]{:S(2)}) copy-start(bf16[1024,3,256]{2,0,1:T(8,128)(2,1)} %param.18) | copy-start | bytes 4718596
  41.5 17.9 %collective-permute-start.5 = (bf16[128,2304]{1,0:T(8,128)(2,1)S(1)}, bf16[128,2304]{1,0:T(8,128)(2,1)S(1)}, u32[]{:S(2)}, u32[]{:S(2)}) collective-permute-start(bf16[128,2304]{1,0:T(8,128)(2,1)S(1)} %bitcast.58), channel_id=1, source_target_pairs={{0,0},{2,4},{4,2},{6,6},{1,1},{3,5},{5,3},{7,7},{8,8},{10,12},{12,... | collective-permute-start | bytes 1769480 | tf_op jit(solution)/shard_map/ppermute | solution.py:1038
  59.4 0.8 copy-start.6
  60.3 328.6 %all-gather.12.cloned.1.call-start = ((), (), s32[]{:S(2)}) async-start(), calls=%async_computation.13 | async-start | bytes 2654208 | tf_op jit(solution)/shard_map/all_gather | solution.py:1042
  60.3 13.5 %collective-permute-start.11 = (bf16[1152,128]{1,0:T(8,128)(2,1)S(1)}, bf16[1152,128]{1,0:T(8,128)(2,1)S(1)}, u32[]{:S(2)}, u32[]{:S(2)}) collective-permute-start(bf16[1152,128]{1,0:T(8,128)(2,1)S(1)} %get-tuple-element.145), channel_id=1, source_target_pairs={{0,0},{2,4},{4,2},{6,6},{1,1},{3,5},{5,3},{7,7},{8,8},{10,12},{12,... | collective-permute-start | bytes 884744 | tf_op jit(solution)/shard_map/ppermute | solution.py:1038
  73.8 0.7 copy-start.12
  74.5 377.6 %all-gather.10.cloned.1.call-start = ((), (), s32[]{:S(2)}) async-start(), calls=%async_computation.12 | async-start | bytes 5308416 | tf_op jit(solution)/shard_map/all_gather | solution.py:1042
  74.7 19.2 %collective-permute-start.10 = (bf16[128,2304]{1,0:T(8,128)(2,1)S(1)}, bf16[128,2304]{1,0:T(8,128)(2,1)S(1)}, u32[]{:S(2)}, u32[]{:S(2)}) collective-permute-start(bf16[128,2304]{1,0:T(8,128)(2,1)S(1)} %bitcast.59), channel_id=1, source_target_pairs={{0,0},{2,4},{4,2},{6,6},{1,1},{3,5},{5,3},{7,7},{8,8},{10,12},{12,... | collective-permute-start | bytes 1769480 | tf_op jit(solution)/shard_map/ppermute | solution.py:1038
  93.9 0.8 copy-start.7
  94.7 621.5 %reduce-scatter.19.cloned.1.call-start = ((), (), s32[]{:S(2)}) async-start(), calls=%async_computation.16 | async-start | bytes 1179648 | tf_op jit(solution)/shard_map/reduce_scatter | solution.py:1046
  95.7 2.7 copy-start.24
  95.7 9.2 copy-start.22
  95.7 15.7 %copy-start.18 = (f32[2,64]{1,0:T(2,128)S(1)}, f32[2,64]{1,0:T(2,128)}, u32[]{:S(2)}) copy-start(f32[2,64]{1,0:T(2,128)} %param.17) | copy-start | bytes 1540
  95.7 18.0 %copy-start.13 = (f32[4,1024]{1,0:T(4,128)S(1)}, f32[4,1024]{1,0:T(4,128)}, u32[]{:S(2)}) copy-start(f32[4,1024]{1,0:T(4,128)} %param.16) | copy-start | bytes 49156
  96.4 121.1 %collective-permute-start.3 = (bf16[1024,768]{1,0:T(8,128)(2,1)S(1)}, bf16[1024,768]{1,0:T(8,128)(2,1)}, u32[]{:S(2)}, u32[]{:S(2)}) collective-permute-start(bf16[1024,768]{1,0:T(8,128)(2,1)S(1)} %copy.48), channel_id=1, source_target_pairs={{0,0},{2,4},{4,2},{6,6},{1,1},{3,5},{5,3},{7,7},{8,8},{10,12},{12,... | collective-permute-start | bytes 4718600 | tf_op jit(solution)/shard_map/ppermute | solution.py:1038
  98.4 84.9 %collective-permute-start = (s32[1,6]{1,0:T(1,128)S(1)}, s32[1,6]{1,0:T(1,128)S(1)}, u32[]{:S(2)}, u32[]{:S(2)}) collective-permute-start(s32[1,6]{1,0:T(1,128)S(1)} %copy-done.24), channel_id=1, source_target_pairs={{0,0},{2,4},{4,2},{6,6},{1,1},{3,5},{5,3},{7,7},{8,8},{10,12},{12,... | collective-permute-start | bytes 80 | tf_op jit(solution)/shard_map/ppermute | solution.py:1038
  102.9 95.5 %collective-permute-start.1 = (bf16[1024,256]{1,0:T(8,128)(2,1)}, bf16[1024,256]{1,0:T(8,128)(2,1)}, u32[]{:S(2)}, u32[]{:S(2)}) collective-permute-start(bf16[1024,256]{1,0:T(8,128)(2,1)} %param.13), channel_id=1, source_target_pairs={{0,0},{2,4},{4,2},{6,6},{1,1},{3,5},{5,3},{7,7},{8,8},{10,12},{12,... | collective-permute-start | bytes 1572872 | tf_op jit(solution)/shard_map/ppermute | solution.py:1038
  104.8 91.6 %collective-permute-start.2 = (f32[3,256]{1,0:T(4,128)S(1)}, f32[3,256]{1,0:T(4,128)S(1)}, u32[]{:S(2)}, u32[]{:S(2)}) collective-permute-start(f32[3,256]{1,0:T(4,128)S(1)} %copy-done.22), channel_id=1, source_target_pairs={{0,0},{2,4},{4,2},{6,6},{1,1},{3,5},{5,3},{7,7},{8,8},{10,12},{12,... | collective-permute-start | bytes 9224 | tf_op jit(solution)/shard_map/ppermute | solution.py:1038
  109.4 108.1 %collective-permute-start.4 = (bf16[256,1024]{1,0:T(8,128)(2,1)}, bf16[256,1024]{1,0:T(8,128)(2,1)}, u32[]{:S(2)}, u32[]{:S(2)}) collective-permute-start(bf16[256,1024]{1,0:T(8,128)(2,1)} %param.20), channel_id=1, source_target_pairs={{0,0},{2,4},{4,2},{6,6},{1,1},{3,5},{5,3},{7,7},{8,8},{10,12},{12,... | collective-permute-start | bytes 1572872 | tf_op jit(solution)/shard_map/ppermute | solution.py:1038
  183.3 5.9 copy-start.25
  183.3 150.4 %collective-permute-start.7 = (bf16[1024,256]{1,0:T(8,128)(2,1)}, bf16[1024,256]{1,0:T(8,128)(2,1)S(1)}, u32[]{:S(2)}, u32[]{:S(2)}) collective-permute-start(bf16[1024,256]{1,0:T(8,128)(2,1)} %param.21), channel_id=1, source_target_pairs={{0,0},{2,4},{4,2},{6,6},{1,1},{3,5},{5,3},{7,7},{8,8},{10,12},{12,... | collective-permute-start | bytes 1572872 | tf_op jit(solution)/shard_map/ppermute | solution.py:1038
  185.4 13.0 %copy-start.20 = (bf16[256,1024]{1,0:T(8,128)(2,1)S(1)}, bf16[256,1024]{1,0:T(8,128)(2,1)}, u32[]{:S(2)}) copy-start(bf16[256,1024]{1,0:T(8,128)(2,1)} %param.23) | copy-start | bytes 1572868
  196.5 21.0 %copy-start.23 = (f32[3,256]{1,0:T(4,128)}, f32[3,256]{1,0:T(4,128)S(1)}, u32[]{:S(2)}) copy-start(f32[3,256]{1,0:T(4,128)S(1)} %collective-permute-done.2.taps_ref) | copy-start | bytes 9220
  196.5 137.2 %collective-permute-start.8 = (bf16[1024,256]{1,0:T(8,128)(2,1)S(1)}, bf16[1024,256]{1,0:T(8,128)(2,1)}, u32[]{:S(2)}, u32[]{:S(2)}) collective-permute-start(bf16[1024,256]{1,0:T(8,128)(2,1)S(1)} %bitcast.61), channel_id=1, source_target_pairs={{0,0},{2,4},{4,2},{6,6},{1,1},{3,5},{5,3},{7,7},{8,8},{10,12},{12,... | collective-permute-start | bytes 1572872 | tf_op jit(solution)/shard_map/ppermute | solution.py:1038
  198.4 135.3 %collective-permute-start.9 = (bf16[256,1024]{1,0:T(8,128)(2,1)S(1)}, bf16[256,1024]{1,0:T(8,128)(2,1)}, u32[]{:S(2)}, u32[]{:S(2)}) collective-permute-start(bf16[256,1024]{1,0:T(8,128)(2,1)S(1)} %copy-done.20), channel_id=1, source_target_pairs={{0,0},{2,4},{4,2},{6,6},{1,1},{3,5},{5,3},{7,7},{8,8},{10,12},{12,... | collective-permute-start | bytes 1572872 | tf_op jit(solution)/shard_map/ppermute | solution.py:1038
  333.7 0.8 copy-start.21
  526.8 47.5 %copy-start.8 = (bf16[256,1024]{1,0:T(8,128)(2,1)S(1)}, bf16[256,1024]{1,0:T(8,128)(2,1)}, u32[]{:S(2)}) copy-start(bf16[256,1024]{1,0:T(8,128)(2,1)} %get-tuple-element.61) | copy-start | bytes 1572868
  574.3 149.5 %reduce-scatter.25.cloned.1.call-start = ((), (), s32[]{:S(2)}) async-start(), calls=%async_computation.19 | async-start | bytes 589824
  624.8 39.2 %copy-start.10 = (bf16[256,1024]{1,0:T(8,128)(2,1)S(1)}, bf16[256,1024]{1,0:T(8,128)(2,1)}, u32[]{:S(2)}) copy-start(bf16[256,1024]{1,0:T(8,128)(2,1)} %get-tuple-element.75) | copy-start | bytes 1572868
  661.8 3.4 copy-start
  664.0 95.1 %reduce-scatter.27.cloned.1.call-start = ((), (), s32[]{:S(2)}) async-start(), calls=%async_computation.20 | async-start | bytes 589824
  665.1 159.9 %reduce-scatter.31.cloned.1.call-start = ((), (), s32[]{:S(2)}) async-start(), calls=%async_computation.22 | async-start | bytes 2654208
  667.6 1.7 copy-start.1
  667.6 218.6 %reduce-scatter.29.cloned.1.call-start = ((), (), s32[]{:S(2)}) async-start(), calls=%async_computation.21 | async-start | bytes 2654208
  671.9 311.6 %reduce-scatter.23.cloned.1.call-start = ((), (), s32[]{:S(2)}) async-start(), calls=%async_computation.18 | async-start | bytes 5308416 | tf_op jit(solution)/shard_map/reduce_scatter | solution.py:1046
  672.6 406.3 %reduce-scatter.21.cloned.1.call-start = ((), (), s32[]{:S(2)}) async-start(), calls=%async_computation.17 | async-start | bytes 5308416 | tf_op jit(solution)/shard_map/reduce_scatter | solution.py:1046
  672.7 1.3 copy-start.5
  673.2 460.5 %reduce-scatter.17.cloned.1.call-start = ((), (), s32[]{:S(2)}) async-start(), calls=%async_computation.15 | async-start | bytes 1769472 | tf_op jit(solution)/shard_map/reduce_scatter | solution.py:1046
  674.0 6.4 copy-start.4
  675.0 24.9 %all-to-all-start.1 = ((f32[256,4,256]{2,0,1:T(8,128)}), f32[256,4,256]{2,0,1:T(8,128)S(1)}, u32[]{:S(2)}, u32[]{:S(2)}) async-start(f32[256,4,256]{2,0,1:T(8,128)} %bitcast.44), calls=%async_computation.1 | async-start | bytes 2097152 | tf_op jit(solution)/shard_map/all_to_all | solution.py:1090
  680.3 40.3 %copy-start.14 = (f32[1,1024]{1,0:T(1,128)S(1)}, f32[1,1024]{1,0:T(1,128)}, u32[]{:S(2)}) copy-start(f32[1,1024]{1,0:T(1,128)} %get-tuple-element.68) | copy-start | bytes 12292
  680.3 40.4 %copy-start.15 = (f32[1,1024]{1,0:T(1,128)S(1)}, f32[1,1024]{1,0:T(1,128)}, u32[]{:S(2)}) copy-start(f32[1,1024]{1,0:T(1,128)} %get-tuple-element.67) | copy-start | bytes 12292
  680.3 40.4 %copy-start.16 = (f32[1,1024]{1,0:T(1,128)S(1)}, f32[1,1024]{1,0:T(1,128)}, u32[]{:S(2)}) copy-start(f32[1,1024]{1,0:T(1,128)} %get-tuple-element.66) | copy-start | bytes 12292
  680.3 40.4 %copy-start.17 = (f32[1,1024]{1,0:T(1,128)S(1)}, f32[1,1024]{1,0:T(1,128)}, u32[]{:S(2)}) copy-start(f32[1,1024]{1,0:T(1,128)} %get-tuple-element.65) | copy-start | bytes 12292
  680.3 40.9 %copy-start.26 = (f32[1,128]{1,0:T(1,128)S(1)}, f32[1,128]{1,0:T(1,128)}, u32[]{:S(2)}) copy-start(f32[1,128]{1,0:T(1,128)} %get-tuple-element.70) | copy-start | bytes 1540
  680.3 41.7 %copy-start.19 = (f32[1,256]{1,0:T(1,128)S(1)}, f32[1,256]{1,0:T(1,128)}, u32[]{:S(2)}) copy-start(f32[1,256]{1,0:T(1,128)} %get-tuple-element.69) | copy-start | bytes 3076
  699.9 14.2 %all-to-all-start = ((bf16[256,4,256]{2,0,1:T(8,128)(2,1)}), bf16[256,4,256]{2,0,1:T(8,128)(2,1)S(1)}, u32[]{:S(2)}, u32[]{:S(2)}) async-start(bf16[256,4,256]{2,0,1:T(8,128)(2,1)} %bitcast.46), calls=%async_computation | async-start | bytes 1048576 | tf_op jit(solution)/shard_map/all_to_all | solution.py:1079
  704.0 425.4 %collective-permute-start.14 = (f32[1024,256]{1,0:T(8,128)S(1)}, f32[1024,256]{1,0:T(8,128)S(1)}, u32[]{:S(2)}, u32[]{:S(2)}) collective-permute-start(f32[1024,256]{1,0:T(8,128)S(1)} %bitcast.56), channel_id=1, source_target_pairs={{0,0},{2,4},{4,2},{6,6},{1,1},{3,5},{5,3},{7,7},{8,8},{10,12},{12,... | collective-permute-start | bytes 3145736 | tf_op jit(solution)/shard_map/ppermute | solution.py:1038
  714.2 180.5 %collective-permute-start.12 = (bf16[1024,256]{1,0:T(8,128)(2,1)S(1)}, bf16[1024,256]{1,0:T(8,128)(2,1)S(1)}, u32[]{:S(2)}, u32[]{:S(2)}) collective-permute-start(bf16[1024,256]{1,0:T(8,128)(2,1)S(1)} %bitcast.62), channel_id=1, source_target_pairs={{0,0},{2,4},{4,2},{6,6},{1,1},{3,5},{5,3},{7,7},{8,8},{10,12},{12,... | collective-permute-start | bytes 1572872 | tf_op jit(solution)/shard_map/ppermute | solution.py:1038
  716.2 269.2 %collective-permute-start.17 = (bf16[128,512]{1,0:T(8,128)(2,1)}, bf16[128,512]{1,0:T(8,128)(2,1)S(1)}, u32[]{:S(2)}, u32[]{:S(2)}) collective-permute-start(bf16[128,512]{1,0:T(8,128)(2,1)} %reduce-scatter.19.cloned.1.call-done), channel_id=1, source_target_pairs={{0,0},{2,4},{4,2},{6,6},{1,1},{3,5},{5,3},{7,7},{8,8},{10,12},{12,... | collective-permute-start | bytes 393224 | tf_op jit(solution)/shard_map/ppermute | solution.py:1038
  724.8 163.4 %collective-permute-start.16 = (bf16[256,128]{1,0:T(8,128)(2,1)S(1)}, bf16[256,128]{1,0:T(8,128)(2,1)S(1)}, u32[]{:S(2)}, u32[]{:S(2)}) collective-permute-start(bf16[256,128]{1,0:T(8,128)(2,1)S(1)} %copy.55), channel_id=1, source_target_pairs={{0,0},{2,4},{4,2},{6,6},{1,1},{3,5},{5,3},{7,7},{8,8},{10,12},{12,... | collective-permute-start | bytes 196616 | tf_op jit(solution)/shard_map/ppermute | solution.py:1038
  760.1 130.0 %collective-permute-start.18 = (bf16[256,128]{1,0:T(8,128)(2,1)S(1)}, bf16[256,128]{1,0:T(8,128)(2,1)S(1)}, u32[]{:S(2)}, u32[]{:S(2)}) collective-permute-start(bf16[256,128]{1,0:T(8,128)(2,1)S(1)} %copy.57), channel_id=1, source_target_pairs={{0,0},{2,4},{4,2},{6,6},{1,1},{3,5},{5,3},{7,7},{8,8},{10,12},{12,... | collective-permute-start | bytes 196616 | tf_op jit(solution)/shard_map/ppermute | solution.py:1038
  888.1 256.4 %collective-permute-start.22 = (bf16[1152,128]{1,0:T(8,128)(2,1)}, bf16[1152,128]{1,0:T(8,128)(2,1)}, u32[]{:S(2)}, u32[]{:S(2)}) collective-permute-start(bf16[1152,128]{1,0:T(8,128)(2,1)} %copy.61), channel_id=1, source_target_pairs={{0,0},{2,4},{4,2},{6,6},{1,1},{3,5},{5,3},{7,7},{8,8},{10,12},{12,... | collective-permute-start | bytes 884744 | tf_op jit(solution)/shard_map/ppermute | solution.py:1038
  890.1 254.5 %collective-permute-start.21 = (bf16[1152,128]{1,0:T(8,128)(2,1)}, bf16[1152,128]{1,0:T(8,128)(2,1)}, u32[]{:S(2)}, u32[]{:S(2)}) collective-permute-start(bf16[1152,128]{1,0:T(8,128)(2,1)} %copy.59), channel_id=1, source_target_pairs={{0,0},{2,4},{4,2},{6,6},{1,1},{3,5},{5,3},{7,7},{8,8},{10,12},{12,... | collective-permute-start | bytes 884744 | tf_op jit(solution)/shard_map/ppermute | solution.py:1038
  983.5 163.2 %collective-permute-start.20 = (bf16[128,2304]{1,0:T(8,128)(2,1)}, bf16[128,2304]{1,0:T(8,128)(2,1)S(1)}, u32[]{:S(2)}, u32[]{:S(2)}) collective-permute-start(bf16[128,2304]{1,0:T(8,128)(2,1)} %reduce-scatter.23.cloned.1.call-done), channel_id=1, source_target_pairs={{0,0},{2,4},{4,2},{6,6},{1,1},{3,5},{5,3},{7,7},{8,8},{10,12},{12,... | collective-permute-start | bytes 1769480 | tf_op jit(solution)/shard_map/ppermute | solution.py:1038
  1078.9 67.9 %collective-permute-start.19 = (bf16[128,2304]{1,0:T(8,128)(2,1)}, bf16[128,2304]{1,0:T(8,128)(2,1)}, u32[]{:S(2)}, u32[]{:S(2)}) collective-permute-start(bf16[128,2304]{1,0:T(8,128)(2,1)} %reduce-scatter.21.cloned.1.call-done), channel_id=1, source_target_pairs={{0,0},{2,4},{4,2},{6,6},{1,1},{3,5},{5,3},{7,7},{8,8},{10,12},{12,... | collective-permute-start | bytes 1769480 | tf_op jit(solution)/shard_map/ppermute | solution.py:1038
  1133.7 9.8 collective-permute-start.15
  (1 other events, 0.7 us)
Sparse Core Ops, SparseCore 0:
  26.6 62.6 all-gather.13
  92.0 100.3 all-gather.7
  195.2 98.9 all-gather.5
  296.2 67.4 all-gather.11
  366.3 85.7 all-gather.9
  574.4 50.8 reduce-scatter.18
  664.1 36.0 reduce-scatter.24
  702.5 56.5 reduce-scatter.26
  763.6 61.3 reduce-scatter.30
  829.3 56.9 reduce-scatter.28
  890.3 93.1 reduce-scatter.22
  987.4 91.4 reduce-scatter.20
  1082.6 51.0 reduce-scatter.16

commit v4 on v3

--- a/solution.py
+++ b/solution.py
@@ -18,19 +18,20 @@
 
 
 class Group:
-    def __init__(self):
+    def __init__(self, others=()):
         c, z = lax.axis_index("c"), lax.axis_index("zl")
         self.partner, self.twin = {"c": 1 - c}, {"zl": 1 - z}
         self.mine, self.beside = 2 * c + z, 2 * (1 - c) + z
         self.across, self.far = 2 * c + (1 - z), 2 * (1 - c) + (1 - z)
+        self.known = [self.partner, self.twin, *others]
         self.barrier = pltpu.get_barrier_semaphore()
 
     def greet(self):
-        for other in (self.partner, self.twin):
+        for other in self.known:
             pl.semaphore_signal(self.barrier, inc=1, device_id=other, device_id_type=MESH)
 
     def meet(self):
-        pl.semaphore_wait(self.barrier, 2)
+        pl.semaphore_wait(self.barrier, len(self.known))
 
 
 def at_rows(block, size, start, count):
@@ -140,19 +141,344 @@
     return pl.ds(pl.multiple_of(start, LANES), width)
 
 
+def start_all(pairs, sems):
+    copies = [pltpu.make_async_copy(src, dst, sems.at[i]) for i, (src, dst) in enumerate(pairs)]
+    for copy in copies:
+        copy.start()
+    return copies
+
+
+def wait_all(copies):
+    for copy in copies:
+        copy.wait()
+
+
+def params(ident):
+    return pltpu.CompilerParams(collective_id=ident, has_side_effects=True, vmem_limit_bytes=56 * 2**20)
+
+
+def shaped(shape, dtype):
+    return jax.ShapeDtypeStruct(shape, dtype)
+
+
+SCALARS = pl.BlockSpec(memory_space=pltpu.SMEM)
+
+
+class Place:
+    def __init__(self):
+        self.y, self.x, self.c, self.zh = (lax.axis_index(a) for a in ("r", "s", "c", "zh"))
+        self.across_x, self.across_y = {"s": 1 - self.x}, {"r": 1 - self.y}
+        self.partner = {"c": 1 - self.c}
+        self.plain = self.c == self.zh
+
+    def over(self, core):
+        return {"c": core, "zh": 1 - self.zh}
+
+    def others(self):
+        return [self.across_x, self.across_y, self.over(self.c), self.over(1 - self.c)]
+
+    def piece(self, flip_y, flip_x, a):
+        y = 1 - self.y if flip_y else self.y
+        x = 1 - self.x if flip_x else self.x
+        return 4 * y + 2 * x + a
+
+
+class Fetch:
+    steps = 4
+
+    def __init__(self, shard, sources=None):
+        rows, cols = shard.shape
+        self.ins = [shard]
+        self.outs = [jax.ShapeDtypeStruct((8, rows, cols), shard.dtype)]
+        self.out_specs = [HBM]
+        self.scratch = [DMA((9,)), DMA((8,)), DMA((1,))]
+
+    def bind(self, ins, outs, scratch):
+        (self.own,), (self.out,) = ins, outs
+        self.sent, self.come, self.sem = scratch
+        self.p = Place()
+
+    def copy(self, src, piece, sent, come, where):
+        return pltpu.make_async_remote_copy(
+            src_ref=src, dst_ref=self.out.at[piece], send_sem=self.sent.at[sent], recv_sem=self.come.at[come],
+            device_id=where, device_id_type=MESH,
+        )
+
+    def to_plane(self):
+        p = self.p
+        return self.copy(self.own, p.piece(0, 0, p.c), 0, p.c, p.over(p.zh))
+
+    def to_partner(self):
+        p = self.p
+        return self.copy(self.own, p.piece(0, 0, p.c), 1, p.c, p.partner)
+
+    def arrived(self, a):
+        return self.copy(self.own, self.p.piece(0, 0, a), 0, a, self.p.partner).wait_recv()
+
+    def keep(self):
+        return pltpu.make_async_copy(self.own, self.out.at[self.p.piece(0, 0, self.p.c)], self.sem.at[0])
+
+    def to_x(self, a, src):
+        return self.copy(src, self.p.piece(0, 0, a), 2 + a, 2 + a, self.p.across_x)
+
+    def to_y(self, a, src):
+        return self.copy(src, self.p.piece(0, 0, a), 4 + a, 4 + a, self.p.across_y)
+
+    def spread(self, a, src):
+        self.to_x(a, src).start()
+        self.to_y(a, src).start()
+
+    def slot(self, a):
+        return self.out.at[self.p.piece(0, 0, a)]
+
+    def on_y(self):
+        piece = self.p.piece(0, 1, 0)
+        return self.copy(self.out.at[piece], piece, 6, 6, self.p.across_y)
+
+    def on_x(self):
+        piece = self.p.piece(1, 0, 1)
+        return self.copy(self.out.at[piece], piece, 7, 7, self.p.across_x)
+
+    def step(self, k):
+        p = self.p
+        if k == 0:
+            self.to_plane().start()
+
+            @pl.when(p.plain)
+            def _():
+                self.keep().start()
+                self.spread(p.c, self.own)
+
+            @pl.when(jnp.logical_not(p.plain))
+            def _():
+                self.to_partner().start()
+
+        elif k == 1:
+
+            @pl.when(p.plain)
+            def _():
+                self.arrived(1 - p.c)
+                self.spread(1 - p.c, self.slot(1 - p.c))
+
+            @pl.when(jnp.logical_not(p.plain))
+            def _():
+                for a in (0, 1):
+                    self.arrived(a)
+                    self.spread(a, self.slot(a))
+
+        elif k == 2:
+            self.to_x(0, self.slot(0)).wait_recv()
+            self.on_y().start()
+            self.to_y(1, self.slot(1)).wait_recv()
+            self.on_x().start()
+        else:
+            self.to_x(1, self.slot(1)).wait_recv()
+            self.to_y(0, self.slot(0)).wait_recv()
+            self.on_y().wait()
+            self.on_x().wait()
+            self.to_plane().wait_send()
+            for a in (0, 1):
+                self.to_x(a, self.slot(a)).wait_send()
+                self.to_y(a, self.slot(a)).wait_send()
+
+            @pl.when(p.plain)
+            def _():
+                self.keep().wait()
+
+            @pl.when(jnp.logical_not(p.plain))
+            def _():
+                self.to_partner().wait_send()
+
+
+class Reduce:
+    steps = 4
+
+    def __init__(self, grad, first, rows):
+        self.first, self.rows = first, rows
+        cols = grad.shape[2]
+        self.ins = [grad]
+        self.outs = [jax.ShapeDtypeStruct((rows, cols), F32)]
+        self.out_specs = [INV]
+        self.scratch = [
+            pltpu.VMEM((4, rows, cols), BF), pltpu.VMEM((4, rows, cols), BF), pltpu.VMEM((2, rows, cols), BF),
+            pltpu.VMEM((2, rows, cols), BF), DMA((9,)), DMA((8,)), DMA((4,)),
+        ]
+
+    def bind(self, ins, outs, scratch):
+        (self.grad,), (self.out,) = ins, outs
+        self.held, self.in1, self.in2, self.in3, self.sent, self.come, self.sem = scratch
+        self.p = Place()
+
+    def piece(self, flip_y, flip_x, a):
+        return self.grad.at[self.p.piece(flip_y, flip_x, a), pl.ds(self.first, self.rows)]
+
+    def copy(self, src, dst, sent, come, where):
+        return pltpu.make_async_remote_copy(
+            src_ref=src, dst_ref=dst, send_sem=self.sent.at[sent], recv_sem=self.come.at[come],
+            device_id=where, device_id_type=MESH,
+        )
+
+    def loads(self):
+        kept = [(0, 0, 0), (0, 1, 0), (0, 0, 1), (1, 0, 1)]
+        return [pltpu.make_async_copy(self.piece(*k), self.held.at[i], self.sem.at[i]) for i, k in enumerate(kept)]
+
+    def first_hops(self):
+        p = self.p
+        return [
+            self.copy(self.piece(1, 0, 0), self.in1.at[0], 0, 0, p.across_y),
+            self.copy(self.piece(1, 1, 0), self.in1.at[1], 1, 1, p.across_y),
+            self.copy(self.piece(0, 1, 1), self.in1.at[2], 2, 2, p.across_x),
+            self.copy(self.piece(1, 1, 1), self.in1.at[3], 3, 3, p.across_x),
+        ]
+
+    def second_hops(self):
+        return [
+            self.copy(self.held.at[1], self.in2.at[0], 4, 4, self.p.across_x),
+            self.copy(self.held.at[3], self.in2.at[1], 5, 5, self.p.across_y),
+        ]
+
+    def to_owner(self, a):
+        return self.copy(self.held.at[2 * a], self.in3.at[0], 6 + a, 6, self.p.over(a))
+
+    def to_partner(self):
+        return self.copy(self.held.at[2 * (1 - self.p.c)], self.in3.at[1], 8, 7, self.p.partner)
+
+    def add(self, i, other):
+        self.held[i] = (self.held[i].astype(F32) + other.astype(F32)).astype(BF)
+
+    def step(self, k):
+        p = self.p
+        if k == 0:
+            for hop in [self.first_hops()[i] for i in (1, 3, 0, 2)]:
+                hop.start()
+            for load in self.loads():
+                load.start()
+        elif k == 1:
+            for load in self.loads():
+                load.wait()
+            hops, after = self.first_hops(), self.second_hops()
+            for i in (1, 3):
+                hops[i].wait_recv()
+                self.add(i, self.in1[i])
+                after[i // 2].start()
+            for i in (0, 2):
+                hops[i].wait_recv()
+                self.add(i, self.in1[i])
+        elif k == 2:
+            for i, hop in enumerate(self.second_hops()):
+                hop.wait_recv()
+                self.add(2 * i, self.in2[i])
+
+            @pl.when(p.plain)
+            def _():
+                self.to_partner().start()
+
+            @pl.when(jnp.logical_not(p.plain))
+            def _():
+                self.to_owner(0).start()
+                self.to_owner(1).start()
+
+        else:
+            self.to_owner(0).wait_recv()
+
+            @pl.when(p.plain)
+            def _():
+                self.out[...] = self.held[2 * p.c].astype(F32) + self.in3[0].astype(F32)
+                self.to_partner().wait_send()
+
+            @pl.when(jnp.logical_not(p.plain))
+            def _():
+                self.to_partner().wait_recv()
+                self.out[...] = self.in3[1].astype(F32) + self.in3[0].astype(F32)
+                self.to_owner(0).wait_send()
+                self.to_owner(1).wait_send()
+
+            for hop in self.first_hops() + self.second_hops():
+                hop.wait_send()
+
+
+class Background:
+    def __init__(self, tasks):
+        self.tasks = tasks
+        self.others = Place().others() if tasks else []
+
+    def step(self, k):
+        for task in self.tasks:
+            task.step(k)
+
+
+def hosted(kernel, ident, name, ins, in_specs, outs, out_specs, scratch, tasks, flops, traffic):
+    groups = ([], [], [])
+    for group, own in zip(groups, (ins, outs, scratch)):
+        group.append(len(own))
+    ins, in_specs, outs, out_specs, scratch = list(ins), list(in_specs), list(outs), list(out_specs), list(scratch)
+    for task in tasks:
+        for group, more in zip(groups, (task.ins, task.outs, task.scratch)):
+            group.append(len(more))
+        ins += task.ins
+        in_specs += [HBM] * len(task.ins)
+        outs += task.outs
+        out_specs += task.out_specs
+        scratch += task.scratch
+
+    def split(refs, counts):
+        at, found = 0, []
+        for count in counts:
+            found.append(refs[at : at + count])
+            at += count
+        return found
+
+    def body(*refs):
+        parts = [split(part, group) for part, group in zip(split(refs, [sum(g) for g in groups]), groups)]
+        for task, *mine in zip(tasks, *(part[1:] for part in parts)):
+            task.bind(*mine)
+        kernel(*parts[0][0], *parts[1][0], *parts[2][0], Background(tasks))
+
+    results = pl.pallas_call(
+        body,
+        out_shape=tuple(outs),
+        in_specs=in_specs,
+        out_specs=tuple(out_specs),
+        scratch_shapes=scratch,
+        compiler_params=params(ident),
+        cost_estimate=pl.CostEstimate(flops=flops, bytes_accessed=traffic, transcendentals=0),
+        name=name,
+    )(*ins)
+    results = split(list(results), groups[1])
+    return results[0], [r[0] for r in results[1:]]
+
+
+def put_rows(scratch, first, value):
+    tall = scratch.shape[1]
+    done = 0
+    while done < value.shape[0]:
+        piece, at = divmod(first + done, tall)
+        count = min(tall - at, value.shape[0] - done)
+        scratch[piece, pl.ds(at, count), :] = value[done : done + count]
+        done += count
+
+
+def put_columns(scratch, first, value):
+    wide_piece = scratch.shape[2]
+    for piece in range(scratch.shape[0]):
+        scratch[piece, pl.ds(first, value.shape[0]), :] = value[:, piece * wide_piece : (piece + 1) * wide_piece]
+
+
+def column_loads(pieces, whole):
+    each = pieces.shape[2]
+    return [(pieces.at[i], whole.at[:, pl.ds(i * each, each)]) for i in range(pieces.shape[0])]
+
+
 def ffn_forward_kernel(
     h_ref, gain_ref, w_hbm, v_hbm, out_ref, n_hbm, u_hbm,
     w, v, nf, u, act, tpart, mine, n_near, n_over, n_on, o_near, i_near, o_over, i_over, s_near, s_over,
-    wsem, osem,
+    wsem, osem, bg,
 ):
-    g = Group()
+    g = Group(bg.others)
     g.greet()
     size, width = h_ref.shape
     hidden = v.shape[0]
-    load_w = pltpu.make_async_copy(w_hbm, w, wsem.at[0])
-    load_v = pltpu.make_async_copy(v_hbm, v, wsem.at[1])
-    load_w.start()
-    load_v.start()
+    loads = start_all([(w_hbm, w)] + column_loads(v_hbm, v), wsem)
     gather = Gather(g, nf, size, n_near, n_over, n_on)
     scatter = Scatter(g, o_near, i_near, o_over, i_over, s_near, s_over, size)
     parts, step = gather.parts, gather.step
@@ -162,8 +488,8 @@
         ).astype(BF)
     g.meet()
     gather.start()
-    load_w.wait()
-    load_v.wait()
+    bg.step(0)
+    wait_all(loads)
 
     def rows_of(places):
         return jnp.concatenate([nf[r, :] for r, _ in places], axis=0) if len(places) > 1 else nf[places[0][0], :]
@@ -214,6 +540,7 @@
     down(put_beside)
     for p in range(parts):
         scatter.close(1, p).start()
+    bg.step(1)
     for p in range(parts):
         gather.wait_part(p)
         gather.wait_far(p)
@@ -234,6 +561,7 @@
         scatter.link(p).start()
     n_out = pltpu.make_async_copy(nf, n_hbm, osem.at[2 + 2 * parts])
     n_out.start()
+    bg.step(2)
     for p in range(parts):
         here = scatter.rows(p)
         scatter.close(1, p).wait_recv()
@@ -249,33 +577,25 @@
         keep(2 + 2 * p, at_rows(g.across, size, p * step, step), step).wait()
         keep(3 + 2 * p, at_rows(g.far, size, p * step, step), step).wait()
     n_out.wait()
-
-
-def ffn_forward(h, gain, w, v, ident, parts=PARTS):
+    bg.step(3)
+
+
+def ffn_forward(h, gain, w, v, ident, tasks=(), parts=PARTS):
     size, width = h.shape
-    hidden = v.shape[0]
+    hidden = v.shape[1]
     total = 4 * size
-    return pl.pallas_call(
-        ffn_forward_kernel,
-        out_shape=(
-            jax.ShapeDtypeStruct((size, width), F32),
-            jax.ShapeDtypeStruct((total, width), BF),
-            jax.ShapeDtypeStruct((total, 2 * hidden), BF),
-        ),
-        in_specs=[INV, INV, HBM, HBM],
-        out_specs=(INV, HBM, HBM),
-        scratch_shapes=[
+    return hosted(
+        ffn_forward_kernel, ident, "ffn_forward", [h, gain, w, v], [INV, INV, HBM, HBM],
+        [shaped((size, width), F32), shaped((total, width), BF), shaped((total, 2 * hidden), BF)], [INV, HBM, HBM],
+        [
             pltpu.VMEM((width, 2 * hidden), BF), pltpu.VMEM((hidden, width), BF), pltpu.VMEM((total, width), BF),
             pltpu.VMEM((total, 2 * hidden), BF), pltpu.VMEM((size, hidden), BF),
             pltpu.VMEM((size // parts, width), F32), pltpu.VMEM((size, width), F32),
-            *gather_scratch(parts), *scatter_scratch(size, width, parts), DMA((2,)), DMA((3 + 2 * parts,)),
+            *gather_scratch(parts), *scatter_scratch(size, width, parts), DMA((1 + v.shape[0],)), DMA((3 + 2 * parts,)),
         ],
-        compiler_params=pltpu.CompilerParams(
-            collective_id=ident, has_side_effects=True, vmem_limit_bytes=56 * 2**20
-        ),
-        cost_estimate=pl.CostEstimate(flops=2 * 3 * total * width * hidden, bytes_accessed=2 * 12 * 2**20, transcendentals=0),
-        name="ffn_forward",
-    )(h, gain, w, v)
+        tasks, 6 * total * width * hidden, 2**24,
+    )
+
 
 def mm_tn(a, b):
     return lax.dot_general(a, b, (((0,), (0,)), ((), ())), preferred_element_type=F32)
@@ -303,21 +623,15 @@
 
 def ffn_backward_kernel(
     known, dh_ref, h_ref, gain_ref, df_hbm, w_hbm, v_hbm, n_hbm, u_hbm, out_ref, gg_ref, gw_hbm, gv_hbm,
-    w, v, nf, u, act, df, tpart, mine, gtile, n_near, n_over, n_on, o_near, i_near, o_over, i_over, s_near, s_over,
-    wsem, osem,
+    w, v, nf, u, act, df, tpart, mine, gtile, gv, n_near, n_over, n_on, o_near, i_near, o_over, i_over, s_near, s_over,
+    wsem, osem, bg,
 ):
-    g = Group()
+    g = Group(bg.others)
     g.greet()
     size, width = dh_ref.shape
     hidden = v.shape[0]
-    loads = [
-        pltpu.make_async_copy(src, dst, wsem.at[i])
-        for i, (src, dst) in enumerate([(v_hbm, v), (u_hbm, u), (w_hbm, w), (n_hbm, nf)])
-    ]
-    if known:
-        loads.append(pltpu.make_async_copy(df_hbm, df, wsem.at[4]))
-    for load in loads:
-        load.start()
+    loads = column_loads(v_hbm, v) + [(u_hbm, u), (w_hbm, w), (n_hbm, nf)]
+    loads = start_all(loads + [(df_hbm, df)] if known else loads, wsem)
     gather = Gather(g, df, size, n_near, n_over, n_on)
     scatter = Scatter(g, o_near, i_near, o_over, i_over, s_near, s_over, size)
     parts, step = gather.parts, gather.step
@@ -326,8 +640,8 @@
     g.meet()
     if not known:
         gather.start()
-    for load in loads:
-        load.wait()
+    bg.step(0)
+    wait_all(loads)
 
     third = hidden // 3
 
@@ -420,50 +734,53 @@
         count += 1
 
     tall = gtile.shape[1]
-    for t in range(hidden // tall):
-        emit(mm_tn(act[:, t * tall : (t + 1) * tall], df[...]), gv_hbm.at[pl.ds(t * tall, tall), :])
+    for t in range(3):
+        put_columns(gv, t * third, mm_tn(act[:, t * third : (t + 1) * third], df[...]).astype(BF))
+    save = pltpu.make_async_copy(gv, gv_hbm, osem.at[2])
+    save.start()
+    bg.step(1)
+    each = gw_hbm.shape[1]
     for t in range(width // tall):
+        piece, at = divmod(t * tall, each)
         for k in range(2):
             cols = slice(k * hidden, (k + 1) * hidden)
-            emit(mm_tn(nf[:, t * tall : (t + 1) * tall], u[:, cols]), gw_hbm.at[pl.ds(t * tall, tall), cols])
+            emit(mm_tn(nf[:, t * tall : (t + 1) * tall], u[:, cols]), gw_hbm.at[piece, pl.ds(at, tall), cols])
+    bg.step(2)
     close_scatter(scatter, mine, dh_ref, h_ref, gain_ref, out_ref, gg_ref)
     if not known:
         gather.finish()
     scatter.wait_all_sends()
     for copy in flush[-2:]:
         copy.wait()
-
-
-def ffn_backward(dh, h, gain, df, w, v, n, u, ident, parts=PARTS):
+    save.wait()
+    bg.step(3)
+
+
+def ffn_backward(dh, h, gain, df, w, v, n, u, ident, tasks=(), parts=PARTS):
     size, width = h.shape
-    hidden = v.shape[0]
+    pieces, hidden = v.shape[:2]
     total = 4 * size
     known = df is not None
     if not known:
         df = n
-    return pl.pallas_call(
-        functools.partial(ffn_backward_kernel, known),
-        out_shape=(
-            jax.ShapeDtypeStruct((size, width), F32),
-            jax.ShapeDtypeStruct((1, width), F32),
-            jax.ShapeDtypeStruct((width, 2 * hidden), BF),
-            jax.ShapeDtypeStruct((hidden, width), BF),
-        ),
-        in_specs=[INV, INV, INV, HBM, HBM, HBM, HBM, HBM],
-        out_specs=(INV, INV, HBM, HBM),
-        scratch_shapes=[
+    return hosted(
+        functools.partial(ffn_backward_kernel, known), ident, "ffn_backward", [dh, h, gain, df, w, v, n, u],
+        [INV, INV, INV] + [HBM] * 5,
+        [
+            shaped((size, width), F32), shaped((1, width), F32), shaped((pieces, width // pieces, 2 * hidden), BF),
+            shaped((pieces, hidden, width // pieces), BF),
+        ],
+        [INV, INV, HBM, HBM],
+        [
             pltpu.VMEM((width, 2 * hidden), BF), pltpu.VMEM((hidden, width), BF), pltpu.VMEM((total, width), BF),
             pltpu.VMEM((total, 2 * hidden), BF), pltpu.VMEM((total, hidden), BF), pltpu.VMEM((total, width), BF),
             pltpu.VMEM((size // parts, width), F32), pltpu.VMEM((size, width), F32),
-            pltpu.VMEM((2, 128, hidden), BF),
-            *gather_scratch(parts), *scatter_scratch(size, width, parts), DMA((5,)), DMA((2,)),
+            pltpu.VMEM((2, 128, hidden), BF), pltpu.VMEM((pieces, hidden, width // pieces), BF),
+            *gather_scratch(parts), *scatter_scratch(size, width, parts), DMA((4 + pieces,)), DMA((3,)),
         ],
-        compiler_params=pltpu.CompilerParams(
-            collective_id=ident, has_side_effects=True, vmem_limit_bytes=56 * 2**20
-        ),
-        cost_estimate=pl.CostEstimate(flops=4 * 3 * total * width * hidden, bytes_accessed=2 * 20 * 2**20, transcendentals=0),
-        name="ffn_backward",
-    )(dh, h, gain, df, w, v, n, u)
+        tasks, 12 * total * width * hidden, 2**25,
+    )
+
 
 MOST_DOC = 512
 
@@ -542,29 +859,6 @@
     return start
 
 
-def start_all(pairs, sems):
-    copies = [pltpu.make_async_copy(src, dst, sems.at[i]) for i, (src, dst) in enumerate(pairs)]
-    for copy in copies:
-        copy.start()
-    return copies
-
-
-def wait_all(copies):
-    for copy in copies:
-        copy.wait()
-
-
-def params(ident):
-    return pltpu.CompilerParams(collective_id=ident, has_side_effects=True, vmem_limit_bytes=56 * 2**20)
-
-
-def shaped(shape, dtype):
-    return jax.ShapeDtypeStruct(shape, dtype)
-
-
-SCALARS = pl.BlockSpec(memory_space=pltpu.SMEM)
-
-
 def conv_taps(gated, within, taps):
     total = gated.shape[0]
     summed = taps[0] * gated
@@ -576,9 +870,9 @@
 def conv_forward_kernel(
     lengths, x_ref, gain_ref, taps_ref, win_hbm, wout_hbm, out_ref, block_ref, n_hbm, p_hbm,
     win, wout, full, nf, proj, low, mixed, tpart, mine, n_near, n_over, n_on, o_near, i_near, o_over, i_over,
-    s_near, s_over, wsem, osem,
+    s_near, s_over, wsem, osem, bg,
 ):
-    g = Group()
+    g = Group(bg.others)
     g.greet()
     size, width = out_ref.shape
     total, chans = x_ref.shape[0], wout.shape[0]
@@ -588,6 +882,7 @@
     full[:, lanes(g.mine * chans, chans)] = x_ref[...]
     g.meet()
     gather.start()
+    bg.step(0)
     gather_everything(gather)
     wait_all(loads)
 
@@ -609,6 +904,7 @@
         taps = [taps_ref[pl.ds(j, 1), pl.ds(k * LANES, LANES)] for j in range(taps_ref.shape[0])]
         mixed[:, pl.ds(k * LANES, LANES)] = (c * conv_taps(b * x, within, taps)).astype(BF)
     scatter_all(g, scatter, product(mixed, wout, False), mine, tpart)
+    bg.step(1)
     own = full[at_rows(g.mine, size, 0, size), :]
     block_ref[...] = own
     for p in range(scatter.parts):
@@ -618,40 +914,40 @@
         out_ref[here, :] = (
             block_ref[here, :].astype(F32) + mine[here, :] + i_near[1, here, :].astype(F32) + i_over[here, :].astype(F32)
         )
+    bg.step(2)
     gather.finish()
     scatter.wait_all_sends()
     wait_all(saves)
-
-
-def conv_forward(lengths, x, gain, taps, win, wout, ident, parts=PARTS):
+    bg.step(3)
+
+
+def conv_forward(lengths, x, gain, taps, win, wout, ident, tasks=(), parts=PARTS):
     total, chans = x.shape
     width = wout.shape[1]
     size = total // 4
-    return pl.pallas_call(
-        conv_forward_kernel,
-        out_shape=(
+    return hosted(
+        conv_forward_kernel, ident, "conv_forward", [lengths, x, gain, taps, win, wout],
+        [SCALARS, INV, INV, INV, HBM, HBM],
+        [
             shaped((size, width), F32), shaped((size, width), BF), shaped((total, width), BF), shaped((total, 3 * chans), BF),
-        ),
-        in_specs=[SCALARS, INV, INV, INV, HBM, HBM],
-        out_specs=(INV, INV, HBM, HBM),
-        scratch_shapes=[
+        ],
+        [INV, INV, HBM, HBM],
+        [
             pltpu.VMEM((width, 3 * chans), BF), pltpu.VMEM((chans, width), BF), pltpu.VMEM((total, width), BF),
             pltpu.VMEM((total, width), BF), pltpu.VMEM((total, 3 * chans), F32), pltpu.VMEM((total, 3 * chans), BF),
             pltpu.VMEM((total, chans), BF), pltpu.VMEM((size // parts, width), F32), pltpu.VMEM((size, width), F32),
             *gather_scratch(parts), *scatter_scratch(size, width, parts), DMA((2,)), DMA((2,)),
         ],
-        compiler_params=params(ident),
-        cost_estimate=pl.CostEstimate(flops=2 * 4 * total * width * chans, bytes_accessed=2 * 8 * 2**20, transcendentals=0),
-        name="conv_forward",
-    )(lengths, x, gain, taps, win, wout)
+        tasks, 8 * total * width * chans, 2**24,
+    )
 
 
 def conv_backward_kernel(
     lengths, dh_ref, h_ref, gain_ref, taps_ref, win_hbm, wout_hbm, n_hbm, p_hbm, out_ref, gg_ref, gt_ref, gin_hbm, gout_hbm,
     win, wout, nf, low, dz, dy, mixed, dproj, gin, gout, tpart, mine, n_near, n_over, n_on, o_near, i_near, o_over, i_over,
-    s_near, s_over, wsem, osem,
+    s_near, s_over, wsem, osem, bg,
 ):
-    g = Group()
+    g = Group(bg.others)
     g.greet()
     size, width = dh_ref.shape
     total, chans = 4 * size, wout.shape[0]
@@ -661,6 +957,7 @@
     dz[at_rows(g.mine, size, 0, size), :] = dh_ref[...].astype(BF)
     g.meet()
     gather.start()
+    bg.step(0)
     wait_all(loads)
     places = lax.broadcasted_iota(jnp.int32, (total, LANES), 0)
     within = places - doc_starts(lengths, places)
@@ -691,42 +988,44 @@
         dproj[:, pl.ds(chans + k * LANES, LANES)] = (d * summed).astype(BF)
         dproj[:, pl.ds(2 * chans + k * LANES, LANES)] = (dg * b).astype(BF)
     scatter_all(g, scatter, product(dproj, win, True), mine, tpart)
-    gout[...] = mm_tn(mixed[...], dz[...]).astype(BF)
+    put_columns(gout, 0, mm_tn(mixed[...], dz[...]).astype(BF))
     save = pltpu.make_async_copy(gout, gout_hbm, osem.at[0])
     save.start()
     for t in range(width // 256):
-        gin[pl.ds(t * 256, 256), :] = mm_tn(nf[:, pl.ds(t * 256, 256)], dproj[...]).astype(BF)
+        put_rows(gin, t * 256, mm_tn(nf[:, pl.ds(t * 256, 256)], dproj[...]).astype(BF))
     more = pltpu.make_async_copy(gin, gin_hbm, osem.at[1])
     more.start()
+    bg.step(1)
     close_scatter(scatter, mine, dh_ref, h_ref, gain_ref, out_ref, gg_ref)
     gather.finish()
     scatter.wait_all_sends()
     save.wait()
     more.wait()
-
-
-def conv_backward(lengths, dh, h, gain, taps, win, wout, n, p, ident, parts=PARTS):
+    bg.step(2)
+    bg.step(3)
+
+
+def conv_backward(lengths, dh, h, gain, taps, win, wout, n, p, pieces, ident, tasks=(), parts=PARTS):
     size, width = dh.shape
     total, chans = 4 * size, wout.shape[0]
-    return pl.pallas_call(
-        conv_backward_kernel,
-        out_shape=(
-            shaped((size, width), F32), shaped((1, width), F32), shaped(taps.shape, F32), shaped((width, 3 * chans), BF),
-            shaped((chans, width), BF),
-        ),
-        in_specs=[SCALARS, INV, INV, INV, INV, HBM, HBM, HBM, HBM],
-        out_specs=(INV, INV, INV, HBM, HBM),
-        scratch_shapes=[
+    each = width // pieces
+    return hosted(
+        conv_backward_kernel, ident, "conv_backward", [lengths, dh, h, gain, taps, win, wout, n, p],
+        [SCALARS, INV, INV, INV, INV, HBM, HBM, HBM, HBM],
+        [
+            shaped((size, width), F32), shaped((1, width), F32), shaped(taps.shape, F32),
+            shaped((pieces, each, 3 * chans), BF), shaped((pieces, chans, each), BF),
+        ],
+        [INV, INV, INV, HBM, HBM],
+        [
             pltpu.VMEM((width, 3 * chans), BF), pltpu.VMEM((chans, width), BF), pltpu.VMEM((total, width), BF),
             pltpu.VMEM((total, 3 * chans), BF), pltpu.VMEM((total, width), BF), pltpu.VMEM((total, chans), F32),
-            pltpu.VMEM((total, chans), BF), pltpu.VMEM((total, 3 * chans), BF), pltpu.VMEM((width, 3 * chans), BF),
-            pltpu.VMEM((chans, width), BF), pltpu.VMEM((size // parts, width), F32), pltpu.VMEM((size, width), F32),
+            pltpu.VMEM((total, chans), BF), pltpu.VMEM((total, 3 * chans), BF), pltpu.VMEM((pieces, each, 3 * chans), BF),
+            pltpu.VMEM((pieces, chans, each), BF), pltpu.VMEM((size // parts, width), F32), pltpu.VMEM((size, width), F32),
             *gather_scratch(parts), *scatter_scratch(size, width, parts), DMA((4,)), DMA((2,)),
         ],
-        compiler_params=params(ident),
-        cost_estimate=pl.CostEstimate(flops=2 * 8 * total * width * chans, bytes_accessed=2 * 12 * 2**20, transcendentals=0),
-        name="conv_backward",
-    )(lengths, dh, h, gain, taps, win, wout, n, p)
+        tasks, 16 * total * width * chans, 2**24,
+    )
 
 
 def head_sums(values, head):
@@ -793,10 +1092,10 @@
 def attention_forward_kernel(
     head, lengths, h_ref, gain_ref, qgain_ref, kgain_ref, cos_ref, sin_ref, wq_hbm, wkv_hbm, wo_hbm,
     out_ref, n_hbm, raw_hbm, ready_hbm, o_hbm,
-    w, wo, nf, raw, low, ready, vt, o, tpart, mine, n_near, n_over, n_on, o_near, i_near, o_over, i_over,
-    s_near, s_over, wsem, osem,
+    w, wo, nf, low, ready, vt, o, tpart, mine, n_near, n_over, n_on, o_near, i_near, o_over, i_over,
+    s_near, s_over, wsem, osem, bg,
 ):
-    g = Group()
+    g = Group(bg.others)
     g.greet()
     size, width = h_ref.shape
     total, qw = 4 * size, wo.shape[0]
@@ -808,6 +1107,7 @@
     nf[at_rows(g.mine, size, 0, size), :] = normalise(h_ref[...], gain_ref[...]).astype(BF)
     g.meet()
     gather.start()
+    bg.step(0)
     wait_all(loads)
 
     def project(block):
@@ -832,6 +1132,7 @@
         return carry
 
     lax.fori_loop(0, 2, rest, 0)
+    bg.step(1)
     saves = start_all([(nf, n_hbm), (low, raw_hbm), (ready, ready_hbm)], osem)
     vt[...] = jnp.transpose(ready[:, pl.ds(qw + kw, kw)].astype(F32)).astype(BF)
     groups = qw // kw
@@ -847,6 +1148,7 @@
             ot = mm(vt[pl.ds(kv * head, head), keys], p)
             joined = jnp.concatenate([ot[:, i * tile : (i + 1) * tile] for i in range(groups)], axis=0)
             o[pl.ds(first, tile), pl.ds(kv * groups * head, groups * head)] = jnp.transpose(joined).astype(BF)
+    bg.step(2)
     save_o = pltpu.make_async_copy(o, o_hbm, osem.at[3])
     save_o.start()
     scatter_all(g, scatter, product(o, wo, False), mine, tpart)
@@ -861,41 +1163,40 @@
     scatter.wait_all_sends()
     wait_all(saves)
     save_o.wait()
-
-
-def attention_forward(head, lengths, h, gain, qgain, kgain, cosine, sine, wq, wkv, wo, ident, parts=PARTS):
+    bg.step(3)
+
+
+def attention_forward(head, lengths, h, gain, qgain, kgain, cosine, sine, wq, wkv, wo, ident, tasks=(), parts=PARTS):
     size, width = h.shape
     total, qw = 4 * size, wo.shape[0]
     kw = wkv.shape[1] // 2
     every = qw + 2 * kw
-    return pl.pallas_call(
-        functools.partial(attention_forward_kernel, head),
-        out_shape=(
+    return hosted(
+        functools.partial(attention_forward_kernel, head), ident, "attention_forward",
+        [lengths, h, gain, qgain, kgain, cosine, sine, wq, wkv, wo], [SCALARS] + [INV] * 6 + [HBM] * 3,
+        [
             shaped((size, width), F32), shaped((total, width), BF), shaped((total, every), BF), shaped((total, every), BF),
             shaped((total, qw), BF),
-        ),
-        in_specs=[SCALARS, INV, INV, INV, INV, INV, INV, HBM, HBM, HBM],
-        out_specs=(INV, HBM, HBM, HBM, HBM),
-        scratch_shapes=[
+        ],
+        [INV] + [HBM] * 4,
+        [
             pltpu.VMEM((width, every), BF), pltpu.VMEM((qw, width), BF), pltpu.VMEM((total, width), BF),
-            pltpu.VMEM((8, 128), F32), pltpu.VMEM((total, every), BF), pltpu.VMEM((total, every), BF),
+            pltpu.VMEM((total, every), BF), pltpu.VMEM((total, every), BF),
             pltpu.VMEM((kw, total), BF), pltpu.VMEM((total, qw), BF),
             pltpu.VMEM((size // parts, width), F32), pltpu.VMEM((size, width), F32),
             *gather_scratch(parts), *scatter_scratch(size, width, parts), DMA((3,)), DMA((4,)),
         ],
-        compiler_params=params(ident),
-        cost_estimate=pl.CostEstimate(flops=2 * total * width * (every + qw), bytes_accessed=2 * 12 * 2**20, transcendentals=0),
-        name="attention_forward",
-    )(lengths, h, gain, qgain, kgain, cosine, sine, wq, wkv, wo)
+        tasks, 2 * total * width * (every + qw), 2**24,
+    )
 
 
 def attention_backward_kernel(
     head, lengths, dh_ref, h_ref, gain_ref, qgain_ref, kgain_ref, cos_ref, sin_ref, wq_hbm, wkv_hbm, wo_hbm,
     n_hbm, raw_hbm, ready_hbm, o_hbm, out_ref, gg_ref, gq_ref, gk_ref, gw_hbm, gwo_hbm,
     w, wo, nf, low, ready, kt, o, dz, do, dq, dkv, dlow, gw, gwo, tpart, mine,
-    n_near, n_over, n_on, o_near, i_near, o_over, i_over, s_near, s_over, wsem, osem,
+    n_near, n_over, n_on, o_near, i_near, o_over, i_over, s_near, s_over, wsem, osem, bg,
 ):
-    g = Group()
+    g = Group(bg.others)
     g.greet()
     size, width = h_ref.shape
     total, qw = 4 * size, wo.shape[0]
@@ -912,6 +1213,7 @@
     dz[at_rows(g.mine, size, 0, size), :] = dh_ref[...].astype(BF)
     g.meet()
     gather.start()
+    bg.step(0)
     wait_all(loads)
     kt[...] = jnp.transpose(ready[:, pl.ds(qw, kw)].astype(F32)).astype(BF)
     dkv[...] = jnp.zeros_like(dkv)
@@ -944,6 +1246,7 @@
             dqt = mm(kt[pl.ds(kv * head, head), keys], ds) * scale
             joined = jnp.concatenate([dqt[:, i * tile : (i + 1) * tile] for i in range(groups)], axis=0)
             dq[pl.ds(first, tile), cols] = jnp.transpose(joined)
+    bg.step(1)
     gq_ref[...] = jnp.zeros_like(gq_ref)
     gk_ref[...] = jnp.zeros_like(gk_ref)
 
@@ -964,48 +1267,65 @@
 
     lax.fori_loop(0, total // size, finish, 0)
     scatter_all(g, scatter, product(dlow, w, True), mine, tpart)
-    gwo[...] = mm_tn(o[...], dz[...]).astype(BF)
+    put_columns(gwo, 0, mm_tn(o[...], dz[...]).astype(BF))
     save = pltpu.make_async_copy(gwo, gwo_hbm, osem.at[0])
     save.start()
     for t in range(width // 256):
-        gw[pl.ds(t * 256, 256), :] = mm_tn(nf[:, pl.ds(t * 256, 256)], dlow[...]).astype(BF)
+        put_rows(gw, t * 256, mm_tn(nf[:, pl.ds(t * 256, 256)], dlow[...]).astype(BF))
     more = pltpu.make_async_copy(gw, gw_hbm, osem.at[1])
     more.start()
+    bg.step(2)
     close_scatter(scatter, mine, dh_ref, h_ref, gain_ref, out_ref, gg_ref)
     gather.finish()
     scatter.wait_all_sends()
     save.wait()
     more.wait()
+    bg.step(3)
 
 
 def attention_backward(
-    head, lengths, dh, h, gain, qgain, kgain, cosine, sine, wq, wkv, wo, n, raw, ready, o, ident, parts=PARTS
+    head, lengths, dh, h, gain, qgain, kgain, cosine, sine, wq, wkv, wo, n, raw, ready, o, pieces, ident, tasks=(),
+    parts=PARTS,
 ):
     size, width = h.shape
     total, qw = 4 * size, wo.shape[0]
     kw = wkv.shape[1] // 2
     every = qw + 2 * kw
-    return pl.pallas_call(
-        functools.partial(attention_backward_kernel, head),
-        out_shape=(
+    each = width // pieces
+    return hosted(
+        functools.partial(attention_backward_kernel, head), ident, "attention_backward",
+        [lengths, dh, h, gain, qgain, kgain, cosine, sine, wq, wkv, wo, n, raw, ready, o], [SCALARS] + [INV] * 7 + [HBM] * 7,
+        [
             shaped((size, width), F32), shaped((1, width), F32), shaped((1, qw), F32), shaped((1, kw), F32),
-            shaped((width, every), BF), shaped((qw, width), BF),
-        ),
-        in_specs=[SCALARS] + [INV] * 7 + [HBM] * 7,
-        out_specs=(INV, INV, INV, INV, HBM, HBM),
-        scratch_shapes=[
+            shaped((pieces, each, every), BF), shaped((pieces, qw, each), BF),
+        ],
+        [INV, INV, INV, INV, HBM, HBM],
+        [
             pltpu.VMEM((width, every), BF), pltpu.VMEM((qw, width), BF), pltpu.VMEM((total, width), BF),
             pltpu.VMEM((total, every), BF), pltpu.VMEM((total, every), BF), pltpu.VMEM((kw, total), BF),
             pltpu.VMEM((total, qw), BF), pltpu.VMEM((total, width), BF), pltpu.VMEM((total, qw), BF),
             pltpu.VMEM((total, qw), F32), pltpu.VMEM((kw // head, total, 2 * head), F32), pltpu.VMEM((total, every), BF),
-            pltpu.VMEM((width, every), BF), pltpu.VMEM((qw, width), BF),
+            pltpu.VMEM((pieces, each, every), BF), pltpu.VMEM((pieces, qw, each), BF),
             pltpu.VMEM((size // parts, width), F32), pltpu.VMEM((size, width), F32),
             *gather_scratch(parts), *scatter_scratch(size, width, parts), DMA((7,)), DMA((2,)),
         ],
-        compiler_params=params(ident),
-        cost_estimate=pl.CostEstimate(flops=4 * total * width * (every + qw), bytes_accessed=2 * 20 * 2**20, transcendentals=0),
-        name="attention_backward",
-    )(lengths, dh, h, gain, qgain, kgain, cosine, sine, wq, wkv, wo, n, raw, ready, o)
+        tasks, 4 * total * width * (every + qw), 2**25,
+    )
+
+
+def tail_kernel(token_ref, done_ref, bg):
+    g = Group(bg.others)
+    g.greet()
+    g.meet()
+    done_ref[...] = token_ref[...]
+    for k in range(4):
+        bg.step(k)
+
+
+def tail(token, ident, tasks):
+    return hosted(
+        tail_kernel, ident, "tail", [token], [INV], [shaped(token.shape, token.dtype)], [INV], [], tasks, 0, 2**22
+    )
 
 
 rope_base = 1000000.0
@@ -1039,15 +1359,15 @@
 
 
 def gather_dp(shard, axis):
-    return lax.all_gather(shard, DP, axis=axis, tiled=True)
+    return lax.all_gather(swap(shard), DP, axis=axis, tiled=True)
 
 
 def scatter_dp(partial, axis):
-    return lax.psum_scatter(partial.astype(BF), DP, scatter_dimension=axis, tiled=True)
+    return swap(lax.psum_scatter(partial, DP, scatter_dimension=axis, tiled=True)).astype(F32)
 
 
 def local(
-    tokens, doc_lengths, grad_out, norm_gains, head_gains, conv_in, conv_kernel, conv_out,
+    planes, tokens, doc_lengths, grad_out, norm_gains, head_gains, conv_in, conv_kernel, conv_out,
     query_w, kv_w, out_w, gate_up, down,
 ):
     length = tokens.shape[0]
@@ -1062,55 +1382,88 @@
     query_w = swap(query_w)
     kv_w = swap(kv_w.reshape(kv_w.shape[0], -1))
     out_w = swap(out_w)
-    ws = [gather_dp(swap(gate_up[l].reshape(gate_up.shape[1], -1)), 0) for l in (0, 1)]
-    vs = [gather_dp(swap(down[l]), 1) for l in (0, 1)]
+    own_w = [gate_up[l].reshape(gate_up.shape[1], -1) for l in (0, 1)]
+    own_v = [down[l] for l in (0, 1)]
+    pieces = 8 if planes else 1
     kv_width = kv_w.shape[1] // 2
     qgain = jnp.tile(head_gains[0:1], (1, query_w.shape[1] // head_dim))
     kgain = jnp.tile(head_gains[1:2], (1, kv_width // head_dim))
     gain = [norm_gains[i : i + 1] for i in range(4)]
+    ws, vs = [None, None], [None, None]
+
+    def take_w(l, pieces_of):
+        ws[l] = pieces_of.reshape(-1, pieces_of.shape[-1])
+
+    if not planes:
+        for l in (0, 1):
+            take_w(l, gather_dp(own_w[l], 0))
+            vs[l] = gather_dp(own_v[l], 1)[None]
 
     up_full = lax.all_gather(swap(grad_out), TP, axis=1, tiled=True)
-    h1, x_block, n0, projected = conv_forward(lengths, swap(tokens), gain[0], conv_kernel, conv_in, conv_out, 0)
-    h2, n1, hidden0 = ffn_forward(h1, gain[1], ws[0], vs[0], 1)
-    h3, n2, raw, ready, attended = attention_forward(
-        head_dim, lengths, h2, gain[2], qgain, kgain, cosine, sine, query_w, kv_w, out_w, 2
-    )
-    h4, n3, hidden1 = ffn_forward(h3, gain[3], ws[1], vs[1], 3)
+    (h1, x_block, n0, projected), got = conv_forward(
+        lengths, swap(tokens), gain[0], conv_kernel, conv_in, conv_out, 0, list(([Fetch(own_w[0]), Fetch(own_v[0])] if planes else ()))
+    )
+    if planes:
+        take_w(0, got[0])
+        vs[0] = got[1]
+    (h2, n1, hidden0), got = ffn_forward(h1, gain[1], ws[0], vs[0], 1, list(([Fetch(own_v[1])] if planes else ())))
+    if planes:
+        vs[1] = got[0]
+    (h3, n2, raw, ready, attended), got = attention_forward(
+        head_dim, lengths, h2, gain[2], qgain, kgain, cosine, sine, query_w, kv_w, out_w, 2, list(([Fetch(own_w[1])] if planes else ()))
+    )
+    if planes:
+        take_w(1, got[0])
+    (h4, n3, hidden1), _ = ffn_forward(h3, gain[3], ws[1], vs[1], 3)
     output = swap(lax.all_to_all(h4.astype(BF), TP, 1, 0, tiled=True))
 
+    def halves(grad):
+        half = grad.shape[1] // 2
+        return [Reduce(grad, 0, half), Reduce(grad, half, half)]
+
+    def whole(grad):
+        return [Reduce(grad, 0, grad.shape[1])]
+
     dh4 = lax.dynamic_slice_in_dim(up_full, quarter * rows, rows, 0).astype(F32)
-    dh3, gain3, gw1, gv1 = ffn_backward(dh4, h3, gain[3], up_full, ws[1], vs[1], n3, hidden1, 4)
-    dh2, gain2, gq, gk, gqkv, gow = attention_backward(
-        head_dim, lengths, dh3, h2, gain[2], qgain, kgain, cosine, sine, query_w, kv_w, out_w, n2, raw, ready, attended, 5
-    )
-    dh1, gain1, gw0, gv0 = ffn_backward(dh2, h1, gain[1], None, ws[0], vs[0], n1, hidden0, 6)
-    dh0, gain0, gtaps, gci, gco = conv_backward(
-        lengths, dh1, x_block.astype(F32), gain[0], conv_kernel, conv_in, conv_out, n0, projected, 7
+    (dh3, gain3, gw1, gv1), _ = ffn_backward(dh4, h3, gain[3], up_full, ws[1], vs[1], n3, hidden1, 4)
+    (dh2, gain2, gq, gk, gqkv, gow), sums_w1 = attention_backward(
+        head_dim, lengths, dh3, h2, gain[2], qgain, kgain, cosine, sine, query_w, kv_w, out_w, n2, raw, ready, attended,
+        pieces, 5, list((halves(gw1) if planes else ())),
+    )
+    (dh1, gain1, gw0, gv0), sums_v1 = ffn_backward(
+        dh2, h1, gain[1], None, ws[0], vs[0], n1, hidden0, 6, list((whole(gv1) + whole(gqkv) + whole(gow) if planes else ()))
+    )
+    (dh0, gain0, gtaps, gci, gco), sums_w0 = conv_backward(
+        lengths, dh1, x_block.astype(F32), gain[0], conv_kernel, conv_in, conv_out, n0, projected, pieces, 7,
+        list((halves(gw0) if planes else ())),
     )
     grad_tokens = swap(lax.all_to_all(dh0, TP, 1, 0, tiled=True))
-
-    back = lambda g, axis: swap(scatter_dp(g, axis)).astype(F32)
+    if planes:
+        _, (gv0, gci, gco) = tail(gain0, 8, whole(gv0) + whole(gci) + whole(gco))
+        gv1, gqkv, gow = sums_v1
+        gw0, gw1 = (jnp.concatenate(sums, axis=0) for sums in (sums_w0, sums_w1))
+    else:
+        gw0, gw1, gci, gqkv = (scatter_dp(g[0], 0) for g in (gw0, gw1, gci, gqkv))
+        gv0, gv1, gco, gow = (scatter_dp(g[0], 1) for g in (gv0, gv1, gco, gow))
     kernel_full = jnp.zeros((conv_kernel.shape[0], norm_gains.shape[1]), F32)
     kernel_full = lax.dynamic_update_slice_in_dim(kernel_full, gtaps, quarter * conv_kernel.shape[1], 1)
     head_grads = jnp.stack([jnp.sum(x.reshape(-1, head_dim), axis=0) for x in (gq, gk)])
     gains, heads, kernels = lax.psum(
         (jnp.concatenate([gain0, gain1, gain2, gain3]), head_grads, kernel_full), ("r", "s", "c", "zh", "zl")
     )
-    eighth = gate_up.shape[1]
-    gqkv = back(gqkv, 0)
     return (
         output,
         grad_tokens,
         gains,
         heads,
-        back(gci, 0).reshape(-1, 3, conv_kernel.shape[1]),
+        gci.reshape(-1, 3, conv_kernel.shape[1]),
         kernels,
-        back(gco, 1),
+        gco,
         gqkv[:, : query_w.shape[1]],
         gqkv[:, query_w.shape[1] :].reshape(-1, 2, kv_width),
-        back(gow, 1),
-        jnp.stack([back(gw0, 0), back(gw1, 0)]).reshape(2, eighth, 2, -1),
-        jnp.stack([back(gv0, 1), back(gv1, 1)]),
+        gow,
+        jnp.stack([gw0, gw1]).reshape(2, gate_up.shape[1], 2, -1),
+        jnp.stack([gv0, gv1]),
     )
 
 
@@ -1121,7 +1474,7 @@
     D = ("r", "s", "c")
     T = ("zh", "zl")
     return jax.shard_map(
-        local,
+        functools.partial(local, dp == 8),
         mesh=inner,
         in_specs=(
             P(D, T), P(D, None), P(D, T), P(), P(), P(None, None, T), P(None, T), P(T, None),

time: 1170 us -> 787 us (0.67)
  waiting for transfers between devices: 609 us -> 57.7 us
  Pallas kernels: 354 us -> 577 us
  starting transfers between devices: 81.5 us -> 48 us
    pallas_call x8 -> x9, Pallas kernels: 354 us -> 577 us  [hosted(): pl.pallas_call(body, out_shape=tuple(outs), in_specs=in_specs, out_specs=...]
    reduce_scatter x4 -> x0, waiting for transfers between devices: 187 us -> none  [scatter_dp(): lax.psum_scatter(partial.astype(BF), DP, scatter_dimension=axis, tiled=True)]
    unnamed x17 -> x1, waiting for transfers between devices: 152 us -> 0.02 us
    ppermute x23 -> x11, waiting for transfers between devices: 157 us -> 56.4 us  [swap(): return lax.ppermute(x, ('c', 'zh'), [(0, 0), (1, 2), (2, 1), (3, 3)])]
    all_gather x4 -> x0, waiting for transfers between devices: 85.6 us -> none  [gather_dp(): return lax.all_gather(shard, DP, axis=axis, tiled=True)]
    ppermute x23 -> x11, starting transfers between devices: 71.6 us -> 38.3 us  [swap(): return lax.ppermute(x, ('c', 'zh'), [(0, 0), (1, 2), (2, 1), (3, 3)])]
    all_to_all x1, waiting for transfers between devices: 18.7 us -> 1.27 us  [local(): grad_tokens = swap(lax.all_to_all(dh0, TP, 1, 0, tiled=True))]
    unnamed x69 -> x67, local copies, waits for them, and re-layouts: 24.9 us -> 14 us
  transfers between devices with their start and end apart: 38 -> 14, of which waited for: 19 -> 4; matrix products, arithmetic and copies ran while one was open for 4% -> 5% of each run, Pallas kernels for 20% -> 74%
where the time goes in v4:
time: 787 us; the launch traced here: 778 us
  Pallas kernels  577 us (73%)
  waiting for transfers between devices  57.7 us (7%)
  starting transfers between devices  48 us (6%)
  blocking collectives  36.6 us (5%)
  local copies, waits for them, and re-layouts  26.8 us (3%)
  other arithmetic  17.3 us (2%)
  between operations  14.8 us (2%)
    pallas_call x9, Pallas kernels, hosted(): pl.pallas_call(body, out_shape=tuple(outs), in_specs=in_specs, out_specs=...  577 us
    ppermute x11, waiting for transfers between devices, swap(): return lax.ppermute(x, ('c', 'zh'), [(0, 0), (1, 2), (2, 1), (3, 3)])  56.4 us
    ppermute x11, starting transfers between devices, swap(): return lax.ppermute(x, ('c', 'zh'), [(0, 0), (1, 2), (2, 1), (3, 3)])  38.3 us
    psum x1, blocking collectives, local(): lax.psum((jnp.concatenate([gain0, gain1, gain2, gain3]), head_grads, kern...  36.6 us
  transfers between devices with their start and end apart: 14, of which 4 were waited for; matrix products, arithmetic and copies ran while one was open for 5% of the time, Pallas kernels for 74%

profile of v4, /device:TPU:1, one launch (start us, length us, event | category | flops | bytes accessed | tf_op | source)
XLA Modules:
  0.0 778.3 jit_solution(15222845184895111427)
XLA Ops:
  7.2 5.6 collective-permute-start
  12.8 1.9 collective-permute-start.1
  14.8 4.5 collective-permute-start.2
  19.3 1.7 copy.47
  21.1 1.6 copy.48
  22.6 2.0 collective-permute-start.3
  24.7 4.5 collective-permute-start.9
  29.2 0.8 fusion.1
  30.1 0.9 copy.56
  31.0 0.6 tile.24.refs_3_.refs_4_
  31.6 0.6 tile.27.refs_4_.refs_5_
  32.2 1.9 copy.63
  34.1 0.9 copy.58
  35.0 0.6 fusion.3
  35.6 39.6 %collective-permute-done.9 = bf16[1024,256]{1,0:T(8,128)(2,1)} collective-permute-done((bf16[1024,256]{1,0:T(8,128)(2,1)}, bf16[1024,256]{1,0:T(8,128)(2,1)}, u32[]{:S(2)}, u32[]{:S(2)}) %collective-permute-start.9) | collective-permute-done | bytes 524320 | tf_op jit(solution)/shard_map/ppermute | solution.py:1358
  75.2 1.9 collective-permute-start.4
  77.2 0.8 slice_bitcast_fusion
  78.0 4.5 collective-permute-start.5
  82.8 1.9 fusion
  84.7 1.9 pad_maximum_fusion.4
  86.6 1.9 collective-permute-start.6
  88.5 5.0 collective-permute-start.7
  93.5 3.8 collective-permute-done.4.refs_5_.refs_6_
  97.4 0.8 copy-done.7
  98.7 113.5 %conv_forward.1 = (f32[256,1024]{1,0:T(8,128)}, bf16[256,1024]{1,0:T(8,128)(2,1)}, bf16[1024,1024]{1,0:T(8,128)(2,1)}, bf16[1024,768]{1,0:T(8,128)(2,1)}, bf16[8...) custom-call(s32[1,6]{1,0:T(1,128)} %copy-done.24, bf16[1024,256]{1,0:T(8,128)(2,1)} %collective-permute-done.1.refs_1_, ...), custom_call_target="tpu_custom_call" | custom-call | flops 2147483648 | bytes 16777216 | tf_op jit(solution)/shard_map/conv_forward/pallas_call | solution.py:437
  212.2 43.2 %ffn_forward.2 = (f32[256,1024]{1,0:T(8,128)}, bf16[1024,1024]{1,0:T(8,128)(2,1)}, bf16[1024,2304]{1,0:T(8,128)(2,1)}, bf16[8,1152,128]{2,1,0:T(8,128)(2,1)}) custom-call(f32[256,1024]{1,0:T(8,128)} %get-tuple-element.60.refs_0_.refs_1_, f32[1,1024]{1,0:T(1,128)} %get-tuple-element.178.refs_1_.refs_2_, bf16[1024,2304]{1,0:T(8,128)(2,1)} %bitcast.57, ...), custom_call_target="tpu_custom_call" | custom-call | flops 7247757312 | bytes 16777216 | tf_op jit(solution)/shard_map/ffn_forward/pallas_call | solution.py:437
  255.5 0.7 copy-done.8
  256.6 71.8 %attention_forward.1 = (f32[256,1024]{1,0:T(8,128)}, bf16[1024,1024]{1,0:T(8,128)(2,1)}, bf16[1024,512]{1,0:T(8,128)(2,1)}, bf16[1024,512]{1,0:T(8,128)(2,1)}, b...) custom-call(s32[1,6]{1,0:T(1,128)} %copy-done.24, f32[256,1024]{1,0:T(8,128)} %get-tuple-element.63.refs_1_.refs_2_, ...), custom_call_target="tpu_custom_call" | custom-call | flops 1610612736 | bytes 16777216 | tf_op jit(solution)/shard_map/attention_forward/pallas_call | solution.py:437
  328.4 37.5 %ffn_forward.3 = (f32[256,1024]{1,0:T(8,128)}, bf16[1024,1024]{1,0:T(8,128)(2,1)}, bf16[1024,2304]{1,0:T(8,128)(2,1)}) custom-call(f32[256,1024]{1,0:T(8,128)} %get-tuple-element.64.refs_0_.refs_1_, f32[1,1024]{1,0:T(1,128)} %get-tuple-element.177.refs_1_.refs_2_, bf16[1024,2304]{1,0:T(8,128)(2,1)} %bitcast.59, ...), custom_call_target="tpu_custom_call" | custom-call | flops 7247757312 | bytes 16777216 | tf_op jit(solution)/shard_map/ffn_forward/pallas_call | solution.py:437
  366.0 1.4 convert_element_type.17
  367.3 0.9 copy.64
  368.2 5.3 all-to-all-start
  373.4 1.1 convert_element_type.19.refs_2_
  374.5 2.1 dynamic-slice_convert_fusion.refs_0_
  376.7 39.0 %ffn_backward.2 = (f32[256,1024]{1,0:T(8,128)}, f32[1,1024]{1,0:T(1,128)}, bf16[8,128,2304]{2,1,0:T(8,128)(2,1)}, bf16[8,1152,128]{2,1,0:T(8,128)(2,1)}) custom-call(f32[256,1024]{1,0:T(8,128)} %dynamic-slice_convert_fusion.refs_0_, f32[256,1024]{1,0:T(8,128)} %get-tuple-element.64.refs_0_.refs_1_, f32[1,1024]{1,0:T(1,128)} %get-tuple-element.177.refs_1_.refs_2_, ...), custom_call_target="tpu_custom_call" | custom-call | flops 14495514624 | bytes 33554432 | tf_op jit(solution)/shard_map/ffn_backward/pallas_call | solution.py:437
  415.7 72.4 %attention_backward.1 = (f32[256,1024]{1,0:T(8,128)}, f32[1,1024]{1,0:T(1,128)}, f32[1,256]{1,0:T(1,128)}, f32[1,128]{1,0:T(1,128)}, bf16[8,128,512]{2,1,0:T(8,1...) custom-call(s32[1,6]{1,0:T(1,128)} %copy-done.24, ...), custom_call_target="tpu_custom_call" | custom-call | flops 3221225472 | bytes 33554432 | tf_op jit(solution)/shard_map/attention_backward/pallas_call | solution.py:437
  488.1 64.2 %ffn_backward.3 = (f32[256,1024]{1,0:T(8,128)}, f32[1,1024]{1,0:T(1,128)}, bf16[8,128,2304]{2,1,0:T(8,128)(2,1)}, bf16[8,1152,128]{2,1,0:T(8,128)(2,1)}, f32[115...) custom-call(f32[256,1024]{1,0:T(8,128)} %get-tuple-element.76.refs_0_, ...), custom_call_target="tpu_custom_call" | custom-call | flops 14495514624 | bytes 33554432 | tf_op jit(solution)/shard_map/ffn_backward/pallas_call | solution.py:437
  552.3 67.0 %conv_backward.1 = (f32[256,1024]{1,0:T(8,128)}, f32[1,1024]{1,0:T(1,128)}, f32[3,256]{1,0:T(4,128)}, bf16[8,128,768]{2,1,0:T(8,128)(2,1)}, bf16[8,256,128]{2,1,...) custom-call(s32[1,6]{1,0:T(1,128)} %copy-done.24, f32[256,1024]{1,0:T(8,128)} %get-tuple-element.82.refs_1_, ...), custom_call_target="tpu_custom_call" | custom-call | flops 4294967296 | bytes 16777216 | tf_op jit(solution)/shard_map/conv_backward/pallas_call | solution.py:437
  619.2 2.3 copy.62
  621.5 4.4 all-to-all-start.1
  625.9 2.3 collective-permute-start.8
  628.2 13.0 %collective-permute-done.8 = bf16[1024,256]{1,0:T(8,128)(2,1)S(1)} collective-permute-done((bf16[1024,256]{1,0:T(8,128)(2,1)S(1)}, bf16[1024,256]{1,0:T(8,128)(2,1)S(1)}, u32[]{:S(2)}, u32[]{:S(2)}) %collective-permute-start.8) | collective-permute-done | bytes 524320 | tf_op jit(solution)/shard_map/ppermute | solution.py:1358
  641.2 0.8 copy-done.13
  642.2 1.3 all-to-all-done.1
  643.5 4.0 collective-permute-start.10
  647.5 0.7 fusion.2
  648.7 0.7 reduce.6
  649.5 0.7 reduce.7
  650.2 0.5 reduce_sum.29
  651.3 68.6 %tail.1 = (f32[1,1024]{1,0:T(1,128)}, f32[1152,128]{1,0:T(8,128)}, f32[128,768]{1,0:T(8,128)}, f32[256,128]{1,0:T(8,128)}) custom-call(f32[1,1024]{1,0:T(1,128)} %get-tuple-element.88.refs_0_, bf16[8,1152,128]{2,1,0:T(8,128)(2,1)} %get-tuple-element.94.refs_1_, bf16[8,128,768]{2,1,0:T(8,128)(2,1)} %get-tuple-element.95.refs_2_, ...), custom_call_target="tpu_custom_call" | custom-call | bytes 4194304 | tf_op jit(solution)/shard_map/tail/pallas_call | solution.py:437
  719.8 1.2 copy.52
  721.0 0.9 copy.53
  721.9 0.7 reshape.91
  722.6 0.7 stack.31
  723.4 0.7 stack.30
  724.0 0.7 pad_maximum_fusion.7
  724.8 0.7 pad_maximum_fusion.6
  725.5 36.6 %all-reduce = (f32[4,1024]{1,0:T(4,128)}, f32[2,64]{1,0:T(2,128)}, f32[3,1024]{1,0:T(4,128)}) all-reduce(f32[4,1024]{1,0:T(4,128)S(1)} %pad_maximum_fusion.6, f32[2,64]{1,0:T(2,128)S(1)} %pad_maximum_fusion.7, f32[3,1024]{1,0:T(4,128)S(1)} %constant_dynamic-update-slice_fusion), channel_id=1, replica_groups=mesh['r'=2,'s'=2,'c'=2,'zh'=2,'zl'=2] {'r','s','c','zh','zl'}, use_global_device_ids=true, to_apply=%region_2.3 | all-reduce | flops 7296 | bytes 58368 | tf_op jit(solution)/shard_map/psum | solution.py:1451
  762.1 2.3 pad_maximum_fusion.3
  764.4 2.5 pad_maximum_fusion
  766.9 0.8 copy.70
  767.7 2.3 copy.71
  770.0 0.7 copy.72
  770.7 0.7 copy.73
  (82 shorter events, 2.7 us)
Async XLA Ops:
  7.2 367.4 %all-gather.2.cloned.1.call-start = ((), (), s32[]{:S(2)}) async-start(), calls=%async_computation.2 | async-start | bytes 2621440 | tf_op jit(solution)/shard_map/all_gather | solution.py:1402
  7.2 70.8 %collective-permute-start = (s32[1,6]{1,0:T(1,128)}, s32[1,6]{1,0:T(1,128)S(1)}, u32[]{:S(2)}, u32[]{:S(2)}) collective-permute-start(s32[1,6]{1,0:T(1,128)} %param.14), channel_id=1, source_target_pairs={{0,0},{2,4},{4,2},{6,6},{1,1},{3,5},{5,3},{7,7},{8,8},{10,12},{12,... | collective-permute-start | bytes 80 | tf_op jit(solution)/shard_map/ppermute | solution.py:1358
  12.8 75.7 %collective-permute-start.1 = (bf16[1024,256]{1,0:T(8,128)(2,1)}, bf16[1024,256]{1,0:T(8,128)(2,1)}, u32[]{:S(2)}, u32[]{:S(2)}) collective-permute-start(bf16[1024,256]{1,0:T(8,128)(2,1)} %param.13), channel_id=1, source_target_pairs={{0,0},{2,4},{4,2},{6,6},{1,1},{3,5},{5,3},{7,7},{8,8},{10,12},{12,... | collective-permute-start | bytes 1572872 | tf_op jit(solution)/shard_map/ppermute | solution.py:1358
  14.8 71.8 %collective-permute-start.2 = (f32[3,256]{1,0:T(4,128)}, f32[3,256]{1,0:T(4,128)S(1)}, u32[]{:S(2)}, u32[]{:S(2)}) collective-permute-start(f32[3,256]{1,0:T(4,128)} %param.19), channel_id=1, source_target_pairs={{0,0},{2,4},{4,2},{6,6},{1,1},{3,5},{5,3},{7,7},{8,8},{10,12},{12,... | collective-permute-start | bytes 9224 | tf_op jit(solution)/shard_map/ppermute | solution.py:1358
  21.0 8.2 %copy-start.1 = (bf16[2,128,2,1152]{3,2,1,0:T(2,128)(2,1)S(1)}, bf16[2,128,2,1152]{3,2,1,0:T(2,128)(2,1)}, u32[]{:S(2)}) copy-start(bf16[2,128,2,1152]{3,2,1,0:T(2,128)(2,1)} %param.24) | copy-start | bytes 3538948
  22.6 8.3 %copy-start.25 = (f32[2,64]{1,0:T(2,128)S(1)}, f32[2,64]{1,0:T(2,128)}, u32[]{:S(2)}) copy-start(f32[2,64]{1,0:T(2,128)} %param.17) | copy-start | bytes 1540
  22.6 74.8 %collective-permute-start.3 = (bf16[1024,768]{1,0:T(8,128)(2,1)}, bf16[1024,768]{1,0:T(8,128)(2,1)S(1)}, u32[]{:S(2)}, u32[]{:S(2)}) collective-permute-start(bf16[1024,768]{1,0:T(8,128)(2,1)} %copy.48), channel_id=1, source_target_pairs={{0,0},{2,4},{4,2},{6,6},{1,1},{3,5},{5,3},{7,7},{8,8},{10,12},{12,... | collective-permute-start | bytes 4718600 | tf_op jit(solution)/shard_map/ppermute | solution.py:1358
  24.7 50.5 %collective-permute-start.9 = (bf16[1024,256]{1,0:T(8,128)(2,1)}, bf16[1024,256]{1,0:T(8,128)(2,1)}, u32[]{:S(2)}, u32[]{:S(2)}) collective-permute-start(bf16[1024,256]{1,0:T(8,128)(2,1)} %param.15), channel_id=1, source_target_pairs={{0,0},{2,4},{4,2},{6,6},{1,1},{3,5},{5,3},{7,7},{8,8},{10,12},{12,... | collective-permute-start | bytes 1572872 | tf_op jit(solution)/shard_map/ppermute | solution.py:1358
  30.1 5.0 copy-start.19
  30.9 46.2 %copy-start.2 = (bf16[2,1152,128]{2,1,0:T(8,128)(2,1)S(1)}, bf16[2,1152,128]{2,1,0:T(8,128)(2,1)}, u32[]{:S(2)}) copy-start(bf16[2,1152,128]{2,1,0:T(8,128)(2,1)} %param.25) | copy-start | bytes 1769476
  75.2 22.2 %collective-permute-start.4 = (bf16[256,1024]{1,0:T(8,128)(2,1)}, bf16[256,1024]{1,0:T(8,128)(2,1)S(1)}, u32[]{:S(2)}, u32[]{:S(2)}) collective-permute-start(bf16[256,1024]{1,0:T(8,128)(2,1)} %param.20), channel_id=1, source_target_pairs={{0,0},{2,4},{4,2},{6,6},{1,1},{3,5},{5,3},{7,7},{8,8},{10,12},{12,... | collective-permute-start | bytes 1572872 | tf_op jit(solution)/shard_map/ppermute | solution.py:1358
  78.0 8.5 %copy-start.24 = (s32[1,6]{1,0:T(1,128)}, s32[1,6]{1,0:T(1,128)S(1)}, u32[]{:S(2)}) copy-start(s32[1,6]{1,0:T(1,128)S(1)} %collective-permute-done.refs_0_) | copy-start | bytes 76
  78.0 177.5 %collective-permute-start.5 = (bf16[1024,256]{1,0:T(8,128)(2,1)}, bf16[1024,256]{1,0:T(8,128)(2,1)S(1)}, u32[]{:S(2)}, u32[]{:S(2)}) collective-permute-start(bf16[1024,256]{1,0:T(8,128)(2,1)} %param.21), channel_id=1, source_target_pairs={{0,0},{2,4},{4,2},{6,6},{1,1},{3,5},{5,3},{7,7},{8,8},{10,12},{12,... | collective-permute-start | bytes 1572872 | tf_op jit(solution)/shard_map/ppermute | solution.py:1358
  84.7 1.9 copy-start.12
  84.7 3.8 copy-start.27
  86.6 10.8 %copy-start.20 = (f32[3,256]{1,0:T(4,128)}, f32[3,256]{1,0:T(4,128)S(1)}, u32[]{:S(2)}) copy-start(f32[3,256]{1,0:T(4,128)S(1)} %collective-permute-done.2.refs_3_.refs_4_) | copy-start | bytes 9220
  86.6 168.9 %collective-permute-start.6 = (bf16[1024,256]{1,0:T(8,128)(2,1)S(1)}, bf16[1024,256]{1,0:T(8,128)(2,1)S(1)}, u32[]{:S(2)}, u32[]{:S(2)}) collective-permute-start(bf16[1024,256]{1,0:T(8,128)(2,1)S(1)} %bitcast.52), channel_id=1, source_target_pairs={{0,0},{2,4},{4,2},{6,6},{1,1},{3,5},{5,3},{7,7},{8,8},{10,12},{12,... | collective-permute-start | bytes 1572872 | tf_op jit(solution)/shard_map/ppermute | solution.py:1358
  88.5 167.0 %collective-permute-start.7 = (bf16[256,1024]{1,0:T(8,128)(2,1)S(1)}, bf16[256,1024]{1,0:T(8,128)(2,1)S(1)}, u32[]{:S(2)}, u32[]{:S(2)}) collective-permute-start(bf16[256,1024]{1,0:T(8,128)(2,1)S(1)} %copy-done.27), channel_id=1, source_target_pairs={{0,0},{2,4},{4,2},{6,6},{1,1},{3,5},{5,3},{7,7},{8,8},{10,12},{12,... | collective-permute-start | bytes 1572872 | tf_op jit(solution)/shard_map/ppermute | solution.py:1358
  97.4 0.8 copy-start.7
  97.4 1.3 copy-start
  255.5 0.8 copy-start.8
  255.5 1.0 copy-start.9
  255.5 1.1 copy-start.10
  365.9 7.5 copy-start.11
  368.2 253.4 %all-to-all-start = ((bf16[256,4,256]{2,0,1:T(8,128)(2,1)}), bf16[256,4,256]{2,0,1:T(8,128)(2,1)S(1)}, u32[]{:S(2)}, u32[]{:S(2)}) async-start(bf16[256,4,256]{2,0,1:T(8,128)(2,1)} %bitcast.40), calls=%async_computation | async-start | bytes 1048576 | tf_op jit(solution)/shard_map/all_to_all | solution.py:1418
  621.5 20.5 %copy-start.3 = (f32[64,2304]{1,0:T(8,128)S(1)}, f32[64,2304]{1,0:T(8,128)}, u32[]{:S(2)}) copy-start(f32[64,2304]{1,0:T(8,128)} %get-tuple-element.104) | copy-start | bytes 1769476
  621.5 20.5 %copy-start.4 = (f32[64,2304]{1,0:T(8,128)S(1)}, f32[64,2304]{1,0:T(8,128)}, u32[]{:S(2)}) copy-start(f32[64,2304]{1,0:T(8,128)} %get-tuple-element.105) | copy-start | bytes 1769476
  621.5 22.0 %all-to-all-start.1 = ((f32[256,4,256]{2,0,1:T(8,128)}), f32[256,4,256]{2,0,1:T(8,128)}, u32[]{:S(2)}, u32[]{:S(2)}) async-start(f32[256,4,256]{2,0,1:T(8,128)} %bitcast.38), calls=%async_computation.1 | async-start | bytes 2097152 | tf_op jit(solution)/shard_map/all_to_all | solution.py:1440
  625.9 16.2 %copy-start.5 = (f32[64,2304]{1,0:T(8,128)S(1)}, f32[64,2304]{1,0:T(8,128)}, u32[]{:S(2)}) copy-start(f32[64,2304]{1,0:T(8,128)} %get-tuple-element.102) | copy-start | bytes 1769476
  625.9 16.2 %copy-start.6 = (f32[64,2304]{1,0:T(8,128)S(1)}, f32[64,2304]{1,0:T(8,128)}, u32[]{:S(2)}) copy-start(f32[64,2304]{1,0:T(8,128)} %get-tuple-element.103) | copy-start | bytes 1769476
  625.9 15.3 %collective-permute-start.8 = (bf16[1024,256]{1,0:T(8,128)(2,1)S(1)}, bf16[1024,256]{1,0:T(8,128)(2,1)S(1)}, u32[]{:S(2)}, u32[]{:S(2)}) collective-permute-start(bf16[1024,256]{1,0:T(8,128)(2,1)S(1)} %bitcast.53), channel_id=1, source_target_pairs={{0,0},{2,4},{4,2},{6,6},{1,1},{3,5},{5,3},{7,7},{8,8},{10,12},{12,... | collective-permute-start | bytes 1572872 | tf_op jit(solution)/shard_map/ppermute | solution.py:1358
  641.2 0.8 copy-start.13
  642.1 5.4 copy-start.15
  642.1 6.6 copy-start.28
  642.1 7.4 copy-start.26
  643.5 123.4 %collective-permute-start.10 = (f32[1024,256]{1,0:T(8,128)}, f32[1024,256]{1,0:T(8,128)}, u32[]{:S(2)}, u32[]{:S(2)}) collective-permute-start(f32[1024,256]{1,0:T(8,128)} %bitcast.11), channel_id=1, source_target_pairs={{0,0},{2,4},{4,2},{6,6},{1,1},{3,5},{5,3},{7,7},{8,8},{10,12},{12,... | collective-permute-start | bytes 3145736 | tf_op jit(solution)/shard_map/ppermute | solution.py:1358
  723.3 1.4 copy-start.21
  723.3 1.4 copy-start.18
  723.3 1.4 copy-start.22
  723.3 1.4 copy-start.23
  764.4 2.5 copy-start.14
  766.9 3.1 copy-start.17
  766.9 3.7 copy-start.16
Sparse Core Ops, SparseCore 0:
  77.3 107.5 all-gather.1

commit v5 on v4

--- a/solution.py
+++ b/solution.py
@@ -18,13 +18,14 @@
 
 
 class Group:
-    def __init__(self, others=()):
+    def __init__(self, others=(), calls=True):
         c, z = lax.axis_index("c"), lax.axis_index("zl")
         self.partner, self.twin = {"c": 1 - c}, {"zl": 1 - z}
         self.mine, self.beside = 2 * c + z, 2 * (1 - c) + z
         self.across, self.far = 2 * c + (1 - z), 2 * (1 - c) + (1 - z)
         self.known = [self.partner, self.twin, *others]
-        self.barrier = pltpu.get_barrier_semaphore()
+        self.c, self.z = c, z
+        self.barrier = pltpu.get_barrier_semaphore() if calls else None
 
     def greet(self):
         for other in self.known:
@@ -161,9 +162,6 @@
     return jax.ShapeDtypeStruct(shape, dtype)
 
 
-SCALARS = pl.BlockSpec(memory_space=pltpu.SMEM)
-
-
 class Place:
     def __init__(self):
         self.y, self.x, self.c, self.zh = (lax.axis_index(a) for a in ("r", "s", "c", "zh"))
@@ -174,8 +172,20 @@
     def over(self, core):
         return {"c": core, "zh": 1 - self.zh}
 
-    def others(self):
-        return [self.across_x, self.across_y, self.over(self.c), self.over(1 - self.c)]
+    def swapped(self):
+        return self.over(self.zh)
+
+    PLANES = ("x", "y")
+    ENDS = ("end", "swap")
+    COLUMN = ("end", "swap", "z core", "z end", "z swap")
+
+    def called(self, name):
+        z = 1 - lax.axis_index("zl")
+        other, far = 1 - self.c, 1 - self.zh
+        return {
+            "x": self.across_x, "y": self.across_y, "end": self.over(self.c), "swap": self.over(other),
+            "z core": {"c": other, "zl": z}, "z end": {"zh": far, "zl": z}, "z swap": {"c": other, "zh": far, "zl": z},
+        }[name]
 
     def piece(self, flip_y, flip_x, a):
         y = 1 - self.y if flip_y else self.y
@@ -184,10 +194,9 @@
 
 
 class Fetch:
-    steps = 4
-
-    def __init__(self, shard, sources=None):
+    def __init__(self, shard, at):
         rows, cols = shard.shape
+        self.at = at
         self.ins = [shard]
         self.outs = [jax.ShapeDtypeStruct((8, rows, cols), shard.dtype)]
         self.out_specs = [HBM]
@@ -239,10 +248,12 @@
         piece = self.p.piece(1, 0, 1)
         return self.copy(self.out.at[piece], piece, 7, 7, self.p.across_x)
 
+    def greets(self):
+        return Place.PLANES + Place.ENDS
+
     def step(self, k):
         p = self.p
         if k == 0:
-            self.to_plane().start()
 
             @pl.when(p.plain)
             def _():
@@ -254,11 +265,14 @@
                 self.to_partner().start()
 
         elif k == 1:
+            self.to_plane().start()
 
             @pl.when(p.plain)
             def _():
                 self.arrived(1 - p.c)
                 self.spread(1 - p.c, self.slot(1 - p.c))
+
+        elif k == 2:
 
             @pl.when(jnp.logical_not(p.plain))
             def _():
@@ -266,7 +280,7 @@
                     self.arrived(a)
                     self.spread(a, self.slot(a))
 
-        elif k == 2:
+        elif k == 3:
             self.to_x(0, self.slot(0)).wait_recv()
             self.on_y().start()
             self.to_y(1, self.slot(1)).wait_recv()
@@ -290,24 +304,299 @@
                 self.to_partner().wait_send()
 
 
+class Take(Fetch):
+    def __init__(self, whole, at, inside=None):
+        rows, cols = whole.shape
+        self.at, self.each = at, rows // 8
+        self.ins = [whole]
+        self.outs = [] if inside else [jax.ShapeDtypeStruct((rows, cols), whole.dtype)]
+        self.out_specs = [] if inside else [HBM]
+        self.scratch = [DMA((9,)), DMA((8,)), DMA((1,))]
+
+    def bind(self, ins, outs, scratch):
+        (self.own,) = ins
+        self.whole = outs[0] if outs else None
+        self.sent, self.come, self.sem = scratch
+        self.p = Place()
+
+    def rows(self, piece):
+        return pl.ds(pl.multiple_of(piece * self.each, 16), self.each)
+
+    def copy(self, src, piece, sent, come, where):
+        return pltpu.make_async_remote_copy(
+            src_ref=self.own.at[self.rows(piece)] if src is None else src, dst_ref=self.whole.at[self.rows(piece)],
+            send_sem=self.sent.at[sent], recv_sem=self.come.at[come], device_id=where, device_id_type=MESH,
+        )
+
+    def to_plane(self):
+        p = self.p
+        return self.copy(None, p.piece(0, 0, p.c), 0, p.c, p.over(p.zh))
+
+    def arrived(self, a):
+        return self.copy(None, self.p.piece(0, 0, a), 0, a, self.p.partner).wait_recv()
+
+    def keep(self):
+        return pltpu.make_async_copy(self.own, self.whole, self.sem.at[0])
+
+    def slot(self, a):
+        return self.whole.at[self.rows(self.p.piece(0, 0, a))]
+
+    def on_y(self):
+        piece = self.p.piece(0, 1, 0)
+        return self.copy(self.whole.at[self.rows(piece)], piece, 6, 6, self.p.across_y)
+
+    def on_x(self):
+        piece = self.p.piece(1, 0, 1)
+        return self.copy(self.whole.at[self.rows(piece)], piece, 7, 7, self.p.across_x)
+
+    def step(self, k):
+        p = self.p
+        if k == 0:
+
+            @pl.when(p.plain)
+            def _():
+                self.keep().start()
+
+        elif k == 1:
+            self.to_plane().start()
+        elif k == 2:
+
+            @pl.when(jnp.logical_not(p.plain))
+            def _():
+                for a in (0, 1):
+                    self.arrived(a)
+                    self.spread(a, self.slot(a))
+
+        elif k == 3:
+
+            @pl.when(jnp.logical_not(p.plain))
+            def _():
+                self.to_x(0, self.slot(0)).wait_recv()
+                self.on_y().start()
+                self.to_y(1, self.slot(1)).wait_recv()
+                self.on_x().start()
+
+        else:
+            self.to_plane().wait_send()
+
+            @pl.when(p.plain)
+            def _():
+                self.keep().wait()
+
+            @pl.when(jnp.logical_not(p.plain))
+            def _():
+                self.to_x(1, self.slot(1)).wait_recv()
+                self.to_y(0, self.slot(0)).wait_recv()
+                self.on_y().wait()
+                self.on_x().wait()
+                for a in (0, 1):
+                    self.to_x(a, self.slot(a)).wait_send()
+                    self.to_y(a, self.slot(a)).wait_send()
+
+
+class Exchange:
+    def __init__(self, src, dst, there, sems, sem, index=0):
+        self.p = Place()
+        self.src, self.dst, self.there, self.sems, self.sem, self.index = src, dst, there, sems, sem, index
+
+    def stay(self):
+        return pltpu.make_async_copy(self.src, self.dst, self.sem.at[self.index])
+
+    def leave(self):
+        return send(self.src, self.there, self.sems, self.index, self.p.swapped())
+
+    def come(self):
+        return send(self.src, self.dst, self.sems, self.index, self.p.swapped())
+
+    def both(self, stay, leave):
+        pl.when(self.p.plain)(stay)
+        pl.when(jnp.logical_not(self.p.plain))(leave)
+
+    def start(self):
+        self.both(lambda: self.stay().start(), lambda: self.leave().start())
+
+    def arrive(self):
+        self.both(lambda: self.stay().wait(), lambda: self.come().wait_recv())
+
+    def finish(self):
+        pl.when(jnp.logical_not(self.p.plain))(lambda: self.leave().wait_send())
+
+
+class Spread:
+    def __init__(self, block, at, parts=2):
+        rows, cols = block.shape
+        self.at, self.parts = at, parts
+        self.ins = [block]
+        self.outs = [jax.ShapeDtypeStruct((rows, 4 * cols), block.dtype)]
+        self.out_specs = [HBM]
+        self.scratch = [*gather_scratch(parts), DMA((2, 1)), DMA((1,))]
+
+    def bind(self, ins, outs, scratch):
+        (self.block,), (self.full,) = ins, outs
+        near, over, onward, sems, sem = scratch
+        self.p, self.g = Place(), Group(calls=False)
+        self.gather = Columns(self.g, self.full, near, over, onward)
+        cols = self.block.shape[1]
+        mine, there = (self.full.at[:, lanes(b * cols, cols)] for b in (self.g.mine, self.g.beside))
+        self.exchange = Exchange(self.block, mine, there, sems, sem)
+
+    def greets(self):
+        return Place.ENDS
+
+    def step(self, k):
+        if k == 0:
+            self.exchange.start()
+        elif k == 1:
+            self.exchange.arrive()
+            self.gather.start()
+        elif k == 2:
+            for p in range(self.parts):
+                self.gather.wait_part(p)
+        elif k == 4:
+            self.gather.wait_beside()
+            for p in range(self.parts):
+                self.gather.wait_far(p)
+            self.gather.finish()
+            self.exchange.finish()
+
+
+class Deliver:
+    def __init__(self, block, at):
+        rows, width = block.shape
+        self.at = at
+        self.ins = [block]
+        self.outs = [jax.ShapeDtypeStruct((4 * rows, width // 4), BF)]
+        self.out_specs = [HBM]
+        self.scratch = [pltpu.VMEM((rows, width), BF), DMA((4,)), DMA((4,)), DMA((2,))]
+        if block.dtype != BF:
+            self.scratch.append(pltpu.VMEM((rows, width), block.dtype))
+
+    def bind(self, ins, outs, scratch):
+        (self.block,), (self.out,) = ins, outs
+        self.low, self.sent, self.come, self.sem = scratch[:4]
+        self.wide = scratch[4] if len(scratch) > 4 else self.low
+        self.p, self.g = Place(), Group(calls=False)
+
+    def greets(self):
+        return Place.COLUMN
+
+    def load(self):
+        return pltpu.make_async_copy(self.block, self.wide, self.sem.at[0])
+
+    def parts(self):
+        rows, width = self.low.shape
+        cols = width // 4
+        dst = self.out.at[at_rows(self.g.mine, rows, 0, rows)]
+        for f in range(4):
+            half, z = divmod(f, 2)
+            here = (self.p.c == self.p.zh) & (self.p.zh == half) & (self.g.z == z)
+            src = self.low.at[:, pl.ds(f * cols, cols)]
+            where = {"c": self.p.zh, "zh": jnp.int32(half), "zl": jnp.int32(z)}
+            yield here, pltpu.make_async_copy(src, dst, self.sem.at[1]), pltpu.make_async_remote_copy(
+                src_ref=src, dst_ref=dst, send_sem=self.sent.at[f], recv_sem=self.come.at[self.g.mine],
+                device_id=where, device_id_type=MESH,
+            )
+
+    def step(self, k):
+        if k == 0:
+            self.load().start()
+        elif k == 1:
+            self.load().wait()
+            if self.wide is not self.low:
+                self.low[...] = self.wide[...].astype(BF)
+            for here, stay, leave in self.parts():
+                pl.when(here)(lambda stay=stay: stay.start())
+                pl.when(jnp.logical_not(here))(lambda leave=leave: leave.start())
+        elif k == 4:
+            rows, width = self.low.shape
+            for here, stay, leave in self.parts():
+                pl.when(here)(lambda stay=stay: stay.wait())
+                pl.when(jnp.logical_not(here))(lambda leave=leave: leave.wait_send())
+            for b in range(4):
+                core, z = divmod(b, 2)
+                here = (self.p.c == self.p.zh) & (self.p.c == core) & (self.g.z == z)
+                come = pltpu.make_async_remote_copy(
+                    src_ref=self.low.at[:, pl.ds(0, width // 4)], dst_ref=self.out.at[pl.ds(b * rows, rows)],
+                    send_sem=self.sent.at[0], recv_sem=self.come.at[b], device_id=self.p.partner, device_id_type=MESH,
+                )
+                pl.when(jnp.logical_not(here))(lambda come=come: come.wait_recv())
+
+
+class Total:
+    def __init__(self, pieces, at, count, axes):
+        self.at, self.count, self.axes = at, count, axes
+        self.ins = pieces
+        self.in_specs = [INV] * len(pieces)
+        width = pieces[0].shape[1]
+        self.outs = [jax.ShapeDtypeStruct((8, width), F32)]
+        self.out_specs = [INV]
+        self.scratch = [
+            pltpu.VMEM((len(self.axes), 8, width), F32), pltpu.VMEM((len(self.axes), 8, width), F32),
+            DMA((2, len(self.axes))),
+        ]
+
+    def bind(self, ins, outs, scratch):
+        self.pieces, (self.out,) = ins, outs
+        self.sum, self.other, self.sems = scratch
+        self.p, self.g = Place(), Group(calls=False)
+
+    def greets(self):
+        return ("x",) + Place.ENDS + (("y",) if "r" in self.axes else ())
+
+    def hop(self, i):
+        axis = self.axes[i]
+        return send(self.sum.at[i], self.other.at[i], self.sems, i, {axis: 1 - lax.axis_index(axis)})
+
+    def step(self, k):
+        if k == 0:
+            gains, taps, heads = self.pieces[:4], self.pieces[4], self.pieces[5:]
+            self.sum[0] = jnp.zeros(self.sum.shape[1:], F32)
+            for i, gain in enumerate(gains):
+                self.sum[0, pl.ds(i, 1), :] = gain[...]
+            cols = taps.shape[1]
+            self.sum[0, pl.ds(4, self.count), lanes(self.g.mine * cols, cols)] = taps[pl.ds(0, self.count), :]
+            done = 0
+            for head in heads:
+                self.sum[0, pl.ds(7, 1), pl.ds(done, head.shape[1])] = head[...]
+                done += head.shape[1]
+            self.hop(0).start()
+        elif k < 5:
+            last = len(self.axes) if k == 4 else k
+            for i in range(k - 1, last):
+                self.hop(i).wait()
+                value = self.sum[i] + self.other[i]
+                if i + 1 < len(self.axes):
+                    self.sum[i + 1] = value
+                    self.hop(i + 1).start()
+                else:
+                    self.out[...] = value
+
+
 class Reduce:
-    steps = 4
-
-    def __init__(self, grad, first, rows):
-        self.first, self.rows = first, rows
+    def __init__(self, grad, first, rows, at, last=True):
+        self.first, self.rows, self.at, self.last = first, rows, at, last
         cols = grad.shape[2]
         self.ins = [grad]
-        self.outs = [jax.ShapeDtypeStruct((rows, cols), F32)]
+        self.outs = [shaped((rows, cols), F32) if last else shaped((2, rows, cols), BF)]
         self.out_specs = [INV]
         self.scratch = [
             pltpu.VMEM((4, rows, cols), BF), pltpu.VMEM((4, rows, cols), BF), pltpu.VMEM((2, rows, cols), BF),
-            pltpu.VMEM((2, rows, cols), BF), DMA((9,)), DMA((8,)), DMA((4,)),
+            DMA((9,)), DMA((8,)), DMA((4,)),
         ]
+        if last:
+            self.scratch.append(pltpu.VMEM((2, rows, cols), BF))
 
     def bind(self, ins, outs, scratch):
         (self.grad,), (self.out,) = ins, outs
-        self.held, self.in1, self.in2, self.in3, self.sent, self.come, self.sem = scratch
+        self.held, self.in1, self.in2, self.sent, self.come, self.sem = scratch[:6]
+        self.in3 = scratch[6] if self.last else None
         self.p = Place()
+
+    def greets(self):
+        return Place.PLANES + (Place.ENDS if self.last else ())
+
+    def fin(self, a):
+        return self.held.at[2 * a]
 
     def piece(self, flip_y, flip_x, a):
         return self.grad.at[self.p.piece(flip_y, flip_x, a), pl.ds(self.first, self.rows)]
@@ -338,10 +627,10 @@
         ]
 
     def to_owner(self, a):
-        return self.copy(self.held.at[2 * a], self.in3.at[0], 6 + a, 6, self.p.over(a))
+        return self.copy(self.fin(a), self.in3.at[0], 6 + a, 6, self.p.over(a))
 
     def to_partner(self):
-        return self.copy(self.held.at[2 * (1 - self.p.c)], self.in3.at[1], 8, 7, self.p.partner)
+        return self.copy(self.fin(1 - self.p.c), self.in3.at[1], 8, 7, self.p.partner)
 
     def add(self, i, other):
         self.held[i] = (self.held[i].astype(F32) + other.astype(F32)).astype(BF)
@@ -367,47 +656,105 @@
         elif k == 2:
             for i, hop in enumerate(self.second_hops()):
                 hop.wait_recv()
-                self.add(2 * i, self.in2[i])
-
-            @pl.when(p.plain)
-            def _():
-                self.to_partner().start()
-
-            @pl.when(jnp.logical_not(p.plain))
-            def _():
-                self.to_owner(0).start()
-                self.to_owner(1).start()
-
-        else:
-            self.to_owner(0).wait_recv()
-
-            @pl.when(p.plain)
-            def _():
-                self.out[...] = self.held[2 * p.c].astype(F32) + self.in3[0].astype(F32)
-                self.to_partner().wait_send()
-
-            @pl.when(jnp.logical_not(p.plain))
-            def _():
-                self.to_partner().wait_recv()
-                self.out[...] = self.in3[1].astype(F32) + self.in3[0].astype(F32)
-                self.to_owner(0).wait_send()
-                self.to_owner(1).wait_send()
-
+                if self.last:
+                    self.add(2 * i, self.in2[i])
+                else:
+                    self.out[i] = (self.held[2 * i].astype(F32) + self.in2[i].astype(F32)).astype(BF)
+            if self.last:
+                self.settle()
+        elif k == 4:
+            if self.last:
+                self.close()
             for hop in self.first_hops() + self.second_hops():
                 hop.wait_send()
 
+    def settle(self):
+        @pl.when(self.p.plain)
+        def _():
+            self.to_partner().start()
+
+        @pl.when(jnp.logical_not(self.p.plain))
+        def _():
+            self.to_owner(0).start()
+            self.to_owner(1).start()
+
+    def close(self):
+        p = self.p
+        self.to_owner(0).wait_recv()
+
+        @pl.when(p.plain)
+        def _():
+            self.out[...] = self.own(p.c).astype(F32) + self.in3[0].astype(F32)
+            self.to_partner().wait_send()
+
+        @pl.when(jnp.logical_not(p.plain))
+        def _():
+            self.to_partner().wait_recv()
+            self.out[...] = self.in3[1].astype(F32) + self.in3[0].astype(F32)
+            self.to_owner(0).wait_send()
+            self.to_owner(1).wait_send()
+
+    def own(self, a):
+        return self.held[2 * a]
+
+
+class Settle(Reduce):
+    def __init__(self, sums, at):
+        _, rows, cols = sums.shape
+        self.at = at
+        self.ins = [sums]
+        self.outs = [shaped((rows, cols), F32)]
+        self.out_specs = [INV]
+        self.scratch = [pltpu.VMEM((rows, cols), BF), pltpu.VMEM((2, rows, cols), BF), DMA((9,)), DMA((8,)), DMA((1,))]
+
+    def bind(self, ins, outs, scratch):
+        (self.sums,), (self.out,) = ins, outs
+        self.kept, self.in3, self.sent, self.come, self.sem = scratch
+        self.p = Place()
+
+    def greets(self):
+        return Place.ENDS
+
+    def fin(self, a):
+        return self.sums.at[a]
+
+    def own(self, a):
+        return self.kept[...]
+
+    def load(self):
+        return pltpu.make_async_copy(self.sums.at[self.p.c], self.kept, self.sem.at[0])
+
+    def step(self, k):
+        if k == 0:
+            self.load().start()
+            self.settle()
+        elif k == 4:
+            self.load().wait()
+            self.close()
+
 
 class Background:
-    def __init__(self, tasks):
-        self.tasks = tasks
-        self.others = Place().others() if tasks else []
+    def __init__(self, tasks, greets):
+        self.tasks, self.done, names = tasks, [], list(greets)
+        for task in tasks:
+            names += [name for name in task.greets() if name not in names]
+        place = Place()
+        self.others = [place.called(name) for name in names]
 
     def step(self, k):
-        for task in self.tasks:
-            task.step(k)
-
-
-def hosted(kernel, ident, name, ins, in_specs, outs, out_specs, scratch, tasks, flops, traffic):
+        for i in range(4):
+            for task in self.tasks:
+                if i < len(task.at) and task.at[i] == k:
+                    task.step(i)
+
+    def finish(self, tasks=None):
+        for task in self.tasks if tasks is None else tasks:
+            if task not in self.done:
+                task.step(4)
+                self.done.append(task)
+
+
+def hosted(kernel, ident, name, ins, in_specs, outs, out_specs, scratch, tasks, flops, traffic, greets=()):
     groups = ([], [], [])
     for group, own in zip(groups, (ins, outs, scratch)):
         group.append(len(own))
@@ -416,7 +763,7 @@
         for group, more in zip(groups, (task.ins, task.outs, task.scratch)):
             group.append(len(more))
         ins += task.ins
-        in_specs += [HBM] * len(task.ins)
+        in_specs += getattr(task, "in_specs", [HBM] * len(task.ins))
         outs += task.outs
         out_specs += task.out_specs
         scratch += task.scratch
@@ -432,7 +779,7 @@
         parts = [split(part, group) for part, group in zip(split(refs, [sum(g) for g in groups]), groups)]
         for task, *mine in zip(tasks, *(part[1:] for part in parts)):
             task.bind(*mine)
-        kernel(*parts[0][0], *parts[1][0], *parts[2][0], Background(tasks))
+        kernel(*parts[0][0], *parts[1][0], *parts[2][0], Background(tasks, greets))
 
     results = pl.pallas_call(
         body,
@@ -445,7 +792,7 @@
         name=name,
     )(*ins)
     results = split(list(results), groups[1])
-    return results[0], [r[0] for r in results[1:]]
+    return results[0], [r[0] for r in results[1:] if r]
 
 
 def put_rows(scratch, first, value):
@@ -577,7 +924,7 @@
         keep(2 + 2 * p, at_rows(g.across, size, p * step, step), step).wait()
         keep(3 + 2 * p, at_rows(g.far, size, p * step, step), step).wait()
     n_out.wait()
-    bg.step(3)
+    bg.finish()
 
 
 def ffn_forward(h, gain, w, v, ident, tasks=(), parts=PARTS):
@@ -699,6 +1046,7 @@
         own()
         gather.wait_beside()
         beside()
+    bg.step(1)
     for p in range(parts):
         if not known:
             gather.wait_part(p)
@@ -716,6 +1064,7 @@
         scatter.close(0, p).wait_recv()
         o_over[here, :] = (tpart[...] + i_near[0, here, :].astype(F32)).astype(BF)
         scatter.link(p).start()
+    bg.step(2)
     if known:
         beside()
         own()
@@ -738,14 +1087,14 @@
         put_columns(gv, t * third, mm_tn(act[:, t * third : (t + 1) * third], df[...]).astype(BF))
     save = pltpu.make_async_copy(gv, gv_hbm, osem.at[2])
     save.start()
-    bg.step(1)
+    bg.step(3)
     each = gw_hbm.shape[1]
     for t in range(width // tall):
         piece, at = divmod(t * tall, each)
         for k in range(2):
             cols = slice(k * hidden, (k + 1) * hidden)
             emit(mm_tn(nf[:, t * tall : (t + 1) * tall], u[:, cols]), gw_hbm.at[piece, pl.ds(at, tall), cols])
-    bg.step(2)
+    bg.step(4)
     close_scatter(scatter, mine, dh_ref, h_ref, gain_ref, out_ref, gg_ref)
     if not known:
         gather.finish()
@@ -753,7 +1102,7 @@
     for copy in flush[-2:]:
         copy.wait()
     save.wait()
-    bg.step(3)
+    bg.finish()
 
 
 def ffn_backward(dh, h, gain, df, w, v, n, u, ident, tasks=(), parts=PARTS):
@@ -850,12 +1199,13 @@
         gather.wait_far(p)
 
 
-def doc_starts(lengths, places):
-    end = jnp.int32(0)
+def doc_starts(docs, lengths, places):
+    row = lengths[pl.ds(0, 1), :]
+    end = jnp.zeros((1, 1), F32)
     start = jnp.zeros_like(places)
-    for d in range(lengths.shape[1]):
-        end = end + lengths[0, d]
-        start = jnp.where(places >= end, end, start)
+    for d in range(docs):
+        end = end + row[:, d : d + 1]
+        start = jnp.where(places >= end.astype(jnp.int32), end.astype(jnp.int32), start)
     return start
 
 
@@ -868,22 +1218,51 @@
 
 
 def conv_forward_kernel(
-    lengths, x_ref, gain_ref, taps_ref, win_hbm, wout_hbm, out_ref, block_ref, n_hbm, p_hbm,
+    docs, count, inside, lens_ref, x_hbm, gain_ref, taps_ref, win_hbm, wout_hbm,
+    out_ref, block_ref, n_hbm, p_hbm, lengths, taps_out, win_out, wout_out,
     win, wout, full, nf, proj, low, mixed, tpart, mine, n_near, n_over, n_on, o_near, i_near, o_over, i_over,
-    s_near, s_over, wsem, osem, bg,
+    s_near, s_over, wsem, osem, xsem, xlocal, bg,
 ):
     g = Group(bg.others)
     g.greet()
     size, width = out_ref.shape
-    total, chans = x_ref.shape[0], wout.shape[0]
-    loads = start_all([(win_hbm, win), (wout_hbm, wout)], wsem)
+    total, chans = x_hbm.shape[0], wout.shape[0]
+    loads = []
+    if inside:
+        bg.tasks[0].whole, bg.tasks[1].whole = win, wout
+    else:
+        loads = start_all([(win_hbm, win), (wout_hbm, wout)], wsem)
     gather = Columns(g, full, n_near, n_over, n_on)
     scatter = Scatter(g, o_near, i_near, o_over, i_over, s_near, s_over, size)
-    full[:, lanes(g.mine * chans, chans)] = x_ref[...]
+    parts = gather.parts
+    blocks = [
+        Exchange(
+            x_hbm.at[pl.ds(p * gather.step, gather.step)],
+            *(full.at[pl.ds(p * gather.step, gather.step), lanes(b * chans, chans)] for b in (g.mine, g.beside)),
+            xsem, xlocal, p,
+        )
+        for p in range(parts)
+    ]
+    small = [Exchange(lens_ref, lengths, lengths, xsem, xlocal, parts), Exchange(taps_ref, taps_out, taps_out, xsem, xlocal, parts + 1)]
     g.meet()
-    gather.start()
+    for block in blocks + small:
+        block.start()
     bg.step(0)
-    gather_everything(gather)
+    for p in range(parts):
+        blocks[p].arrive()
+        gather.link(p, g.mine).start()
+        gather.close(p, g.mine).start()
+    gather.wait_beside()
+    bg.step(1)
+    for p in range(parts):
+        gather.wait_part(p)
+    for p in range(parts):
+        gather.wait_far(p)
+    for block in small:
+        block.arrive()
+    bg.step(2)
+    if inside:
+        bg.finish(bg.tasks[:2])
     wait_all(loads)
 
     def project(t, carry):
@@ -896,17 +1275,16 @@
         return carry
 
     lax.fori_loop(0, total // size, project, 0)
-    saves = start_all([(nf, n_hbm), (low, p_hbm)], osem)
+    saves = start_all([(nf, n_hbm), (low, p_hbm), (win, win_out), (wout, wout_out)], osem)
     places = lax.broadcasted_iota(jnp.int32, (total, LANES), 0)
-    within = places - doc_starts(lengths, places)
+    within = places - doc_starts(docs, lengths, places)
     for k in range(chans // LANES):
         b, c, x = (proj[:, pl.ds(i * chans + k * LANES, LANES)] for i in range(3))
-        taps = [taps_ref[pl.ds(j, 1), pl.ds(k * LANES, LANES)] for j in range(taps_ref.shape[0])]
+        taps = [taps_out[pl.ds(j, 1), pl.ds(k * LANES, LANES)] for j in range(count)]
         mixed[:, pl.ds(k * LANES, LANES)] = (c * conv_taps(b * x, within, taps)).astype(BF)
     scatter_all(g, scatter, product(mixed, wout, False), mine, tpart)
-    bg.step(1)
-    own = full[at_rows(g.mine, size, 0, size), :]
-    block_ref[...] = own
+    bg.step(3)
+    block_ref[...] = full[at_rows(g.mine, size, 0, size), :]
     for p in range(scatter.parts):
         here = scatter.rows(p)
         scatter.close(1, p).wait_recv()
@@ -914,36 +1292,39 @@
         out_ref[here, :] = (
             block_ref[here, :].astype(F32) + mine[here, :] + i_near[1, here, :].astype(F32) + i_over[here, :].astype(F32)
         )
-    bg.step(2)
+    for block in blocks + small:
+        block.finish()
     gather.finish()
     scatter.wait_all_sends()
     wait_all(saves)
-    bg.step(3)
-
-
-def conv_forward(lengths, x, gain, taps, win, wout, ident, tasks=(), parts=PARTS):
+    bg.finish()
+
+
+def conv_forward(docs, count, lens, x, gain, taps, win, wout, inside, ident, tasks=(), parts=PARTS, cuts=4):
     total, chans = x.shape
     width = wout.shape[1]
     size = total // 4
     return hosted(
-        conv_forward_kernel, ident, "conv_forward", [lengths, x, gain, taps, win, wout],
-        [SCALARS, INV, INV, INV, HBM, HBM],
+        functools.partial(conv_forward_kernel, docs, count, inside), ident, "conv_forward",
+        [lens, x, gain, taps, win, wout], [INV, HBM, INV, INV, HBM, HBM],
         [
             shaped((size, width), F32), shaped((size, width), BF), shaped((total, width), BF), shaped((total, 3 * chans), BF),
+            shaped(lens.shape, F32), shaped(taps.shape, F32), shaped(win.shape, BF), shaped(wout.shape, BF),
         ],
-        [INV, INV, HBM, HBM],
+        [INV, INV, HBM, HBM, INV, INV, HBM, HBM],
         [
             pltpu.VMEM((width, 3 * chans), BF), pltpu.VMEM((chans, width), BF), pltpu.VMEM((total, width), BF),
             pltpu.VMEM((total, width), BF), pltpu.VMEM((total, 3 * chans), F32), pltpu.VMEM((total, 3 * chans), BF),
             pltpu.VMEM((total, chans), BF), pltpu.VMEM((size // parts, width), F32), pltpu.VMEM((size, width), F32),
-            *gather_scratch(parts), *scatter_scratch(size, width, parts), DMA((2,)), DMA((2,)),
+            *gather_scratch(cuts), *scatter_scratch(size, width, parts), DMA((2,)), DMA((4,)),
+            DMA((2, cuts + 2)), DMA((cuts + 2,)),
         ],
-        tasks, 8 * total * width * chans, 2**24,
+        tasks, 8 * total * width * chans, 2**24, ("swap",),
     )
 
 
 def conv_backward_kernel(
-    lengths, dh_ref, h_ref, gain_ref, taps_ref, win_hbm, wout_hbm, n_hbm, p_hbm, out_ref, gg_ref, gt_ref, gin_hbm, gout_hbm,
+    docs, count, lengths, dh_ref, h_ref, gain_ref, taps_ref, win_hbm, wout_hbm, n_hbm, p_hbm, out_ref, gg_ref, gt_ref, gin_hbm, gout_hbm,
     win, wout, nf, low, dz, dy, mixed, dproj, gin, gout, tpart, mine, n_near, n_over, n_on, o_near, i_near, o_over, i_over,
     s_near, s_over, wsem, osem, bg,
 ):
@@ -960,8 +1341,9 @@
     bg.step(0)
     wait_all(loads)
     places = lax.broadcasted_iota(jnp.int32, (total, LANES), 0)
-    within = places - doc_starts(lengths, places)
+    within = places - doc_starts(docs, lengths, places)
     gather_everything(gather)
+    bg.step(1)
 
     def project(t, carry):
         rows = at_rows(t, size, 0, size)
@@ -972,7 +1354,7 @@
     for k in range(chans // LANES):
         b, c, x = (low[:, pl.ds(i * chans + k * LANES, LANES)].astype(F32) for i in range(3))
         here = pl.ds(k * LANES, LANES)
-        taps = [taps_ref[pl.ds(j, 1), here] for j in range(taps_ref.shape[0])]
+        taps = [taps_ref[pl.ds(j, 1), here] for j in range(count)]
         gated = b * x
         summed = conv_taps(gated, within, taps)
         d = dy[:, here]
@@ -987,7 +1369,9 @@
         dproj[:, pl.ds(k * LANES, LANES)] = (dg * x).astype(BF)
         dproj[:, pl.ds(chans + k * LANES, LANES)] = (d * summed).astype(BF)
         dproj[:, pl.ds(2 * chans + k * LANES, LANES)] = (dg * b).astype(BF)
+    bg.step(2)
     scatter_all(g, scatter, product(dproj, win, True), mine, tpart)
+    bg.step(3)
     put_columns(gout, 0, mm_tn(mixed[...], dz[...]).astype(BF))
     save = pltpu.make_async_copy(gout, gout_hbm, osem.at[0])
     save.start()
@@ -995,23 +1379,24 @@
         put_rows(gin, t * 256, mm_tn(nf[:, pl.ds(t * 256, 256)], dproj[...]).astype(BF))
     more = pltpu.make_async_copy(gin, gin_hbm, osem.at[1])
     more.start()
-    bg.step(1)
+    bg.step(4)
     close_scatter(scatter, mine, dh_ref, h_ref, gain_ref, out_ref, gg_ref)
     gather.finish()
     scatter.wait_all_sends()
     save.wait()
     more.wait()
-    bg.step(2)
-    bg.step(3)
-
-
-def conv_backward(lengths, dh, h, gain, taps, win, wout, n, p, pieces, ident, tasks=(), parts=PARTS):
+    bg.step(5)
+    bg.finish()
+
+
+def conv_backward(docs, count, lengths, dh, h, gain, taps, win, wout, n, p, pieces, ident, tasks=(), parts=PARTS):
     size, width = dh.shape
     total, chans = 4 * size, wout.shape[0]
     each = width // pieces
     return hosted(
-        conv_backward_kernel, ident, "conv_backward", [lengths, dh, h, gain, taps, win, wout, n, p],
-        [SCALARS, INV, INV, INV, INV, HBM, HBM, HBM, HBM],
+        functools.partial(conv_backward_kernel, docs, count), ident, "conv_backward",
+        [lengths, dh, h, gain, taps, win, wout, n, p],
+        [INV, INV, INV, INV, INV, HBM, HBM, HBM, HBM],
         [
             shaped((size, width), F32), shaped((1, width), F32), shaped(taps.shape, F32),
             shaped((pieces, each, 3 * chans), BF), shaped((pieces, chans, each), BF),
@@ -1090,7 +1475,7 @@
 
 
 def attention_forward_kernel(
-    head, lengths, h_ref, gain_ref, qgain_ref, kgain_ref, cos_ref, sin_ref, wq_hbm, wkv_hbm, wo_hbm,
+    head, docs, lengths, h_ref, gain_ref, qgain_ref, kgain_ref, cos_ref, sin_ref, wq_hbm, wkv_hbm, wo_hbm,
     out_ref, n_hbm, raw_hbm, ready_hbm, o_hbm,
     w, wo, nf, low, ready, vt, o, tpart, mine, n_near, n_over, n_on, o_near, i_near, o_over, i_over,
     s_near, s_over, wsem, osem, bg,
@@ -1138,7 +1523,7 @@
     groups = qw // kw
     tile = 256
     scale = head ** (-0.5)
-    starts = doc_starts(lengths, lax.broadcasted_iota(jnp.int32, (1, total), 1))
+    starts = doc_starts(docs, lengths, lax.broadcasted_iota(jnp.int32, (1, total), 1))
     for first, low_key, high_key in attention_tiles(total, tile):
         keys = pl.ds(low_key, high_key - low_key)
         for kv in range(kw // head):
@@ -1148,10 +1533,13 @@
             ot = mm(vt[pl.ds(kv * head, head), keys], p)
             joined = jnp.concatenate([ot[:, i * tile : (i + 1) * tile] for i in range(groups)], axis=0)
             o[pl.ds(first, tile), pl.ds(kv * groups * head, groups * head)] = jnp.transpose(joined).astype(BF)
-    bg.step(2)
+        if first == tile:
+            bg.step(2)
+    bg.step(3)
     save_o = pltpu.make_async_copy(o, o_hbm, osem.at[3])
     save_o.start()
     scatter_all(g, scatter, product(o, wo, False), mine, tpart)
+    bg.step(4)
     for p in range(parts):
         here = scatter.rows(p)
         scatter.close(1, p).wait_recv()
@@ -1163,17 +1551,17 @@
     scatter.wait_all_sends()
     wait_all(saves)
     save_o.wait()
-    bg.step(3)
-
-
-def attention_forward(head, lengths, h, gain, qgain, kgain, cosine, sine, wq, wkv, wo, ident, tasks=(), parts=PARTS):
+    bg.finish()
+
+
+def attention_forward(head, docs, lengths, h, gain, qgain, kgain, cosine, sine, wq, wkv, wo, ident, tasks=(), parts=PARTS):
     size, width = h.shape
     total, qw = 4 * size, wo.shape[0]
     kw = wkv.shape[1] // 2
     every = qw + 2 * kw
     return hosted(
-        functools.partial(attention_forward_kernel, head), ident, "attention_forward",
-        [lengths, h, gain, qgain, kgain, cosine, sine, wq, wkv, wo], [SCALARS] + [INV] * 6 + [HBM] * 3,
+        functools.partial(attention_forward_kernel, head, docs), ident, "attention_forward",
+        [lengths, h, gain, qgain, kgain, cosine, sine, wq, wkv, wo], [INV] * 7 + [HBM] * 3,
         [
             shaped((size, width), F32), shaped((total, width), BF), shaped((total, every), BF), shaped((total, every), BF),
             shaped((total, qw), BF),
@@ -1191,7 +1579,7 @@
 
 
 def attention_backward_kernel(
-    head, lengths, dh_ref, h_ref, gain_ref, qgain_ref, kgain_ref, cos_ref, sin_ref, wq_hbm, wkv_hbm, wo_hbm,
+    head, docs, lengths, dh_ref, h_ref, gain_ref, qgain_ref, kgain_ref, cos_ref, sin_ref, wq_hbm, wkv_hbm, wo_hbm,
     n_hbm, raw_hbm, ready_hbm, o_hbm, out_ref, gg_ref, gq_ref, gk_ref, gw_hbm, gwo_hbm,
     w, wo, nf, low, ready, kt, o, dz, do, dq, dkv, dlow, gw, gwo, tpart, mine,
     n_near, n_over, n_on, o_near, i_near, o_over, i_over, s_near, s_over, wsem, osem, bg,
@@ -1224,11 +1612,13 @@
         do[rows, :] = mm_nt(dz[rows, :], wo[...]).astype(BF)
         return carry
 
+    bg.step(1)
+
     lax.fori_loop(0, total // size, project, 0)
     groups = qw // kw
     tile = 256
     scale = head ** (-0.5)
-    starts = doc_starts(lengths, lax.broadcasted_iota(jnp.int32, (1, total), 1))
+    starts = doc_starts(docs, lengths, lax.broadcasted_iota(jnp.int32, (1, total), 1))
     for first, low_key, high_key in attention_tiles(total, tile):
         keys = pl.ds(low_key, high_key - low_key)
         for kv in range(kw // head):
@@ -1246,7 +1636,11 @@
             dqt = mm(kt[pl.ds(kv * head, head), keys], ds) * scale
             joined = jnp.concatenate([dqt[:, i * tile : (i + 1) * tile] for i in range(groups)], axis=0)
             dq[pl.ds(first, tile), cols] = jnp.transpose(joined)
-    bg.step(1)
+        if first == tile:
+            bg.step(2)
+        if first == 2 * tile:
+            bg.step(3)
+    bg.step(4)
     gq_ref[...] = jnp.zeros_like(gq_ref)
     gk_ref[...] = jnp.zeros_like(gk_ref)
 
@@ -1274,17 +1668,17 @@
         put_rows(gw, t * 256, mm_tn(nf[:, pl.ds(t * 256, 256)], dlow[...]).astype(BF))
     more = pltpu.make_async_copy(gw, gw_hbm, osem.at[1])
     more.start()
-    bg.step(2)
+    bg.step(5)
     close_scatter(scatter, mine, dh_ref, h_ref, gain_ref, out_ref, gg_ref)
     gather.finish()
     scatter.wait_all_sends()
     save.wait()
     more.wait()
-    bg.step(3)
+    bg.finish()
 
 
 def attention_backward(
-    head, lengths, dh, h, gain, qgain, kgain, cosine, sine, wq, wkv, wo, n, raw, ready, o, pieces, ident, tasks=(),
+    head, docs, lengths, dh, h, gain, qgain, kgain, cosine, sine, wq, wkv, wo, n, raw, ready, o, pieces, ident, tasks=(),
     parts=PARTS,
 ):
     size, width = h.shape
@@ -1293,8 +1687,8 @@
     every = qw + 2 * kw
     each = width // pieces
     return hosted(
-        functools.partial(attention_backward_kernel, head), ident, "attention_backward",
-        [lengths, dh, h, gain, qgain, kgain, cosine, sine, wq, wkv, wo, n, raw, ready, o], [SCALARS] + [INV] * 7 + [HBM] * 7,
+        functools.partial(attention_backward_kernel, head, docs), ident, "attention_backward",
+        [lengths, dh, h, gain, qgain, kgain, cosine, sine, wq, wkv, wo, n, raw, ready, o], [INV] * 8 + [HBM] * 7,
         [
             shaped((size, width), F32), shaped((1, width), F32), shaped((1, qw), F32), shaped((1, kw), F32),
             shaped((pieces, each, every), BF), shaped((pieces, qw, each), BF),
@@ -1313,19 +1707,17 @@
     )
 
 
-def tail_kernel(token_ref, done_ref, bg):
+def tail_kernel(bg):
     g = Group(bg.others)
     g.greet()
     g.meet()
-    done_ref[...] = token_ref[...]
     for k in range(4):
         bg.step(k)
-
-
-def tail(token, ident, tasks):
-    return hosted(
-        tail_kernel, ident, "tail", [token], [INV], [shaped(token.shape, token.dtype)], [INV], [], tasks, 0, 2**22
-    )
+    bg.finish()
+
+
+def tail(ident, tasks):
+    return hosted(tail_kernel, ident, "tail", [], [], [], [], [], tasks, 0, 2**22)[1]
 
 
 rope_base = 1000000.0
@@ -1372,16 +1764,9 @@
 ):
     length = tokens.shape[0]
     head_dim = head_gains.shape[1]
-    quarter = lax.axis_index("c") * 2 + lax.axis_index("zl")
-    rows = length // 4
-    lengths = swap(doc_lengths)
-    cosine, sine = rope_tables(doc_positions(lengths[0], length), head_dim)
-    conv_in = swap(conv_in.reshape(conv_in.shape[0], -1))
-    conv_kernel = swap(conv_kernel)
-    conv_out = swap(conv_out)
-    query_w = swap(query_w)
-    kv_w = swap(kv_w.reshape(kv_w.shape[0], -1))
-    out_w = swap(out_w)
+    docs, count = doc_lengths.shape[1], conv_kernel.shape[0]
+    conv_in = conv_in.reshape(conv_in.shape[0], -1)
+    kv_w = kv_w.reshape(kv_w.shape[0], -1)
     own_w = [gate_up[l].reshape(gate_up.shape[1], -1) for l in (0, 1)]
     own_v = [down[l] for l in (0, 1)]
     pieces = 8 if planes else 1
@@ -1389,75 +1774,89 @@
     qgain = jnp.tile(head_gains[0:1], (1, query_w.shape[1] // head_dim))
     kgain = jnp.tile(head_gains[1:2], (1, kv_width // head_dim))
     gain = [norm_gains[i : i + 1] for i in range(4)]
-    ws, vs = [None, None], [None, None]
-
-    def take_w(l, pieces_of):
-        ws[l] = pieces_of.reshape(-1, pieces_of.shape[-1])
-
-    if not planes:
-        for l in (0, 1):
-            take_w(l, gather_dp(own_w[l], 0))
-            vs[l] = gather_dp(own_v[l], 1)[None]
-
-    up_full = lax.all_gather(swap(grad_out), TP, axis=1, tiled=True)
-    (h1, x_block, n0, projected), got = conv_forward(
-        lengths, swap(tokens), gain[0], conv_kernel, conv_in, conv_out, 0, list(([Fetch(own_w[0]), Fetch(own_v[0])] if planes else ()))
+    lens = jnp.pad(doc_lengths.astype(F32), ((0, 7), (0, LANES - docs)))
+    taps = jnp.pad(conv_kernel, ((0, 8 - count), (0, 0)))
+    rows_of = lambda got: got.reshape(-1, got.shape[-1])
+    if planes:
+        first = [Take(conv_in, (0, 0, 1, 2), True), Take(conv_out, (0, 0, 1, 2), True)]
+        first += [Fetch(own_w[0], (0, 1, 3, 3)), Fetch(own_v[0], (0, 1, 3, 3))]
+        second = [Take(x, (0, 0, 1, 2)) for x in (query_w, kv_w, out_w)] + [Fetch(own_v[1], (0, 1, 2, 2))]
+        third = [Fetch(own_w[1], (0, 1, 3, 3)), Spread(grad_out, (1, 2, 3))]
+    else:
+        first, second, third = [], [], [Spread(grad_out, (1, 2, 3))]
+        conv_in, conv_out, query_w, kv_w, out_w = map(swap, (conv_in, conv_out, query_w, kv_w, out_w))
+        w0, w1 = (gather_dp(w, 0) for w in own_w)
+        v0, v1 = (gather_dp(v, 1)[None] for v in own_v)
+
+    (h1, x_block, n0, projected, lens, taps, conv_in, conv_out), got = conv_forward(
+        docs, count, lens, tokens, gain[0], taps, conv_in, conv_out, planes, 0, first
     )
     if planes:
-        take_w(0, got[0])
-        vs[0] = got[1]
-    (h2, n1, hidden0), got = ffn_forward(h1, gain[1], ws[0], vs[0], 1, list(([Fetch(own_v[1])] if planes else ())))
+        w0, v0 = rows_of(got[0]), got[1]
+    (h2, n1, hidden0), got = ffn_forward(h1, gain[1], w0, v0, 1, second)
     if planes:
-        vs[1] = got[0]
+        query_w, kv_w, out_w, v1 = got
+    cosine, sine = rope_tables(doc_positions(lens[0, :docs].astype(jnp.int32), length), head_dim)
     (h3, n2, raw, ready, attended), got = attention_forward(
-        head_dim, lengths, h2, gain[2], qgain, kgain, cosine, sine, query_w, kv_w, out_w, 2, list(([Fetch(own_w[1])] if planes else ()))
+        head_dim, docs, lens, h2, gain[2], qgain, kgain, cosine, sine, query_w, kv_w, out_w, 2, third
     )
     if planes:
-        take_w(1, got[0])
-    (h4, n3, hidden1), _ = ffn_forward(h3, gain[3], ws[1], vs[1], 3)
-    output = swap(lax.all_to_all(h4.astype(BF), TP, 1, 0, tiled=True))
-
-    def halves(grad):
+        w1 = rows_of(got[0])
+    up_full = got[-1]
+    (h4, n3, hidden1), _ = ffn_forward(h3, gain[3], w1, v1, 3)
+
+    def halves(grad, *at):
         half = grad.shape[1] // 2
-        return [Reduce(grad, 0, half), Reduce(grad, half, half)]
-
-    def whole(grad):
-        return [Reduce(grad, 0, grad.shape[1])]
-
-    dh4 = lax.dynamic_slice_in_dim(up_full, quarter * rows, rows, 0).astype(F32)
-    (dh3, gain3, gw1, gv1), _ = ffn_backward(dh4, h3, gain[3], up_full, ws[1], vs[1], n3, hidden1, 4)
-    (dh2, gain2, gq, gk, gqkv, gow), sums_w1 = attention_backward(
-        head_dim, lengths, dh3, h2, gain[2], qgain, kgain, cosine, sine, query_w, kv_w, out_w, n2, raw, ready, attended,
-        pieces, 5, list((halves(gw1) if planes else ())),
+        return [Reduce(grad, i * half, half, at[i], False) for i in (0, 1)] if planes else []
+
+    def whole(grad, at, last=False):
+        return [Reduce(grad, 0, grad.shape[1], at, last)] if planes else []
+
+    def settled(sums):
+        return [Settle(x, (0,)) for x in sums]
+
+    quarter = lax.axis_index("c") * 2 + lax.axis_index("zl")
+    dh4 = lax.dynamic_slice_in_dim(up_full, quarter * h4.shape[0], h4.shape[0], 0).astype(F32)
+    (dh3, gain3, gw1, gv1), (output,) = ffn_backward(
+        dh4, h3, gain[3], up_full, w1, v1, n3, hidden1, 4, [Deliver(h4, (0, 2))]
     )
-    (dh1, gain1, gw0, gv0), sums_v1 = ffn_backward(
-        dh2, h1, gain[1], None, ws[0], vs[0], n1, hidden0, 6, list((whole(gv1) + whole(gqkv) + whole(gow) if planes else ()))
+    (dh2, gain2, gq, gk, gqkv, gow), sums = attention_backward(
+        head_dim, docs, lens, dh3, h2, gain[2], qgain, kgain, cosine, sine, query_w, kv_w, out_w, n2, raw, ready, attended,
+        pieces, 5, halves(gw1, (0, 1, 4), (0, 3, 5)),
     )
-    (dh0, gain0, gtaps, gci, gco), sums_w0 = conv_backward(
-        lengths, dh1, x_block.astype(F32), gain[0], conv_kernel, conv_in, conv_out, n0, projected, pieces, 7,
-        list((halves(gw0) if planes else ())),
+    (dh1, gain1, gw0, gv0), got = ffn_backward(
+        dh2, h1, gain[1], None, w0, v0, n1, hidden0, 6,
+        settled(sums) + whole(gv1, (0, 1, 2)) + whole(gqkv, (0, 2, 3)) + whole(gow, (0, 2, 3)),
     )
-    grad_tokens = swap(lax.all_to_all(dh0, TP, 1, 0, tiled=True))
+    sums_w1, sums = got[:2], got[2:]
+    (dh0, gain0, gtaps, gci, gco), got = conv_backward(
+        docs, count, lens, dh1, x_block.astype(F32), gain[0], taps, conv_in, conv_out, n0, projected, pieces, 7,
+        settled(sums) + halves(gw0, (0, 1, 3), (0, 3, 5)),
+    )
+    others, sums = got[:3], got[3:]
+    grads, totals, *got = tail(
+        8,
+        [Deliver(dh0, (0, 0)), Total([gain0, gain1, gain2, gain3, gtaps, gq, gk], (0, 1, 2, 3), count, ("c", "zl", "s", *(("r",) if planes else ()), "zh"))]
+        + settled(sums) + whole(gv0, (0, 1, 2), True) + whole(gci, (0, 1, 2), True) + whole(gco, (0, 1, 2), True),
+    )
     if planes:
-        _, (gv0, gci, gco) = tail(gain0, 8, whole(gv0) + whole(gci) + whole(gco))
-        gv1, gqkv, gow = sums_v1
-        gw0, gw1 = (jnp.concatenate(sums, axis=0) for sums in (sums_w0, sums_w1))
+        gw1 = jnp.concatenate(sums_w1, axis=0)
+        gv1, gqkv, gow = others
+        gw0 = jnp.concatenate(got[:2], axis=0)
+        gv0, gci, gco = got[2:]
     else:
+        totals = lax.psum(totals, "r")
         gw0, gw1, gci, gqkv = (scatter_dp(g[0], 0) for g in (gw0, gw1, gci, gqkv))
         gv0, gv1, gco, gow = (scatter_dp(g[0], 1) for g in (gv0, gv1, gco, gow))
-    kernel_full = jnp.zeros((conv_kernel.shape[0], norm_gains.shape[1]), F32)
-    kernel_full = lax.dynamic_update_slice_in_dim(kernel_full, gtaps, quarter * conv_kernel.shape[1], 1)
-    head_grads = jnp.stack([jnp.sum(x.reshape(-1, head_dim), axis=0) for x in (gq, gk)])
-    gains, heads, kernels = lax.psum(
-        (jnp.concatenate([gain0, gain1, gain2, gain3]), head_grads, kernel_full), ("r", "s", "c", "zh", "zl")
-    )
+    heads = totals[7, : gq.shape[1] + gk.shape[1]].reshape(-1, head_dim)
+    split = gq.shape[1] // head_dim
     return (
         output,
-        grad_tokens,
-        gains,
-        heads,
+        grads.astype(F32),
+        totals[:4],
+        jnp.stack([jnp.sum(heads[:split], axis=0), jnp.sum(heads[split:], axis=0)]),
         gci.reshape(-1, 3, conv_kernel.shape[1]),
-        kernels,
+        totals[4 : 4 + count],
         gco,
         gqkv[:, : query_w.shape[1]],
         gqkv[:, query_w.shape[1] :].reshape(-1, 2, kv_width),

time: 787 us -> 617 us (0.78)
  waiting for transfers between devices: 57.7 us -> 0 us
  starting transfers between devices: 48 us -> 0 us
  blocking collectives: 36.6 us -> 0 us
  between operations: 14.8 us -> 1.39 us
  Pallas kernels: 577 us -> 569 us
    ppermute x11 -> x0, waiting for transfers between devices: 56.4 us -> none  [swap(): return lax.ppermute(x, ('c', 'zh'), [(0, 0), (1, 2), (2, 1), (3, 3)])]
    ppermute x11 -> x0, starting transfers between devices: 38.3 us -> none  [swap(): return lax.ppermute(x, ('c', 'zh'), [(0, 0), (1, 2), (2, 1), (3, 3)])]
    psum x1 -> x0, blocking collectives: 36.6 us -> none  [local(): lax.psum((jnp.concatenate([gain0, gain1, gain2, gain3]), head_grads, kern...]
    all_to_all x2 -> x0, starting transfers between devices: 9.66 us -> none  [the longest x1 5.28 us: local(): output = swap(lax.all_to_all(h4.astype(BF), TP, 1, 0, tiled=True))]
  transfers between devices with their start and end apart: 14 -> 0, of which waited for: 4 -> 0; matrix products, arithmetic and copies ran while one was open for 5% -> 0% of each run, Pallas kernels for 74% -> 0%
where the time goes in v5:
time: 617 us; the launch traced here: 606 us
  Pallas kernels  569 us (92%)
  local copies, waits for them, and re-layouts  20.7 us (3%)
  other arithmetic  14.4 us (2%)
    pallas_call x9, Pallas kernels, hosted(): pl.pallas_call(body, out_shape=tuple(outs), in_specs=in_specs, out_specs=...  569 us

profile of v5, /device:TPU:1, one launch (start us, length us, event | category | flops | bytes accessed | tf_op | source)
XLA Modules:
  0.0 606.0 jit_solution(11286436661457655902)
XLA Ops:
  0.6 1.5 fusion.3
  2.1 2.1 fusion.1
  4.2 0.9 copy.43
  5.1 0.0 copy-done
  5.1 0.8 slice_bitcast_fusion
  6.0 1.7 copy.37
  7.7 0.0 copy-start.15
  7.7 0.0 copy-start.17
  7.7 1.6 copy.38.refs_4_.refs_6_
  9.3 0.0 copy-done.15
  9.3 0.6 pad.9.refs_3_
  9.9 0.0 copy-done.17
  9.9 0.6 pad.8.refs_0_
  10.5 112.7 %conv_forward.1 = (f32[256,1024]{1,0:T(8,128)}, bf16[256,1024]{1,0:T(8,128)(2,1)}, bf16[1024,1024]{1,0:T(8,128)(2,1)}, bf16[1024,768]{1,0:T(8,128)(2,1)}, f32[8,...) custom-call(f32[8,128]{1,0:T(8,128)} %pad.8.refs_0_, ...), custom_call_target="tpu_custom_call" | custom-call | flops 2147483648 | bytes 16777216 | tf_op jit(solution)/shard_map/conv_forward/pallas_call | solution.py:784
  123.3 0.7 convert_bitcast_fusion
  123.9 0.1 select_reduce_fusion.1
  124.0 0.1 select_reduce_fusion
  124.2 1.9 fusion
  126.1 0.0 copy-start.8
  126.1 1.8 pad_maximum_fusion.4
  127.9 0.0 copy-done.8
  127.9 0.9 copy.47
  128.8 52.4 %ffn_forward.2 = (f32[256,1024]{1,0:T(8,128)}, bf16[1024,1024]{1,0:T(8,128)(2,1)}, bf16[1024,2304]{1,0:T(8,128)(2,1)}, bf16[1024,256]{1,0:T(8,128)(2,1)}, bf16[1...) custom-call(f32[256,1024]{1,0:T(8,128)} %get-tuple-element.79.refs_0_.refs_1_, ...), custom_call_target="tpu_custom_call" | custom-call | flops 7247757312 | bytes 16777216 | tf_op jit(solution)/shard_map/ffn_forward/pallas_call | solution.py:784
  181.3 0.0 copy-done.16
  181.3 0.6 tile.24.refs_3_.refs_4_
  182.0 0.6 tile.27.refs_4_.refs_5_
  182.5 0.9 copy.45
  183.4 96.8 %attention_forward.1 = (f32[256,1024]{1,0:T(8,128)}, bf16[1024,1024]{1,0:T(8,128)(2,1)}, bf16[1024,512]{1,0:T(8,128)(2,1)}, bf16[1024,512]{1,0:T(8,128)(2,1)}, b...) custom-call(f32[8,128]{1,0:T(8,128)} %get-tuple-element.78.refs_0_, ...), custom_call_target="tpu_custom_call" | custom-call | flops 1610612736 | bytes 16777216 | tf_op jit(solution)/shard_map/attention_forward/pallas_call | solution.py:784
  280.2 37.5 %ffn_forward.3 = (f32[256,1024]{1,0:T(8,128)}, bf16[1024,1024]{1,0:T(8,128)(2,1)}, bf16[1024,2304]{1,0:T(8,128)(2,1)}) custom-call(f32[256,1024]{1,0:T(8,128)} %get-tuple-element.87.refs_0_.refs_1_, f32[1,1024]{1,0:T(1,128)} %get-tuple-element.198.refs_1_.refs_2_, bf16[1024,2304]{1,0:T(8,128)(2,1)} %bitcast.42, ...), custom_call_target="tpu_custom_call" | custom-call | flops 7247757312 | bytes 16777216 | tf_op jit(solution)/shard_map/ffn_forward/pallas_call | solution.py:784
  317.7 2.1 dynamic-slice_convert_fusion.refs_0_
  319.8 39.3 %ffn_backward.2 = (f32[256,1024]{1,0:T(8,128)}, f32[1,1024]{1,0:T(1,128)}, bf16[8,128,2304]{2,1,0:T(8,128)(2,1)}, bf16[8,1152,128]{2,1,0:T(8,128)(2,1)}, bf16[1024,256]{1,0:T(8,128)(2,1)}) custom-call(f32[256,1024]{1,0:T(8,128)} %dynamic-slice_convert_fusion.refs_0_, f32[256,1024]{1,0:T(8,128)} %get-tuple-element.87.refs_0_.refs_1_, ...), custom_call_target="tpu_custom_call" | custom-call | flops 14495514624 | bytes 33554432 | tf_op jit(solution)/shard_map/ffn_backward/pallas_call | solution.py:784
  359.1 57.7 %attention_backward.1 = (f32[256,1024]{1,0:T(8,128)}, f32[1,1024]{1,0:T(1,128)}, f32[1,256]{1,0:T(1,128)}, f32[1,128]{1,0:T(1,128)}, bf16[8,128,512]{2,1,0:T(8,1...) custom-call(f32[8,128]{1,0:T(8,128)} %get-tuple-element.78.refs_0_, ...), custom_call_target="tpu_custom_call" | custom-call | flops 3221225472 | bytes 33554432 | tf_op jit(solution)/shard_map/attention_backward/pallas_call | solution.py:784
  416.9 51.3 %ffn_backward.3 = (f32[256,1024]{1,0:T(8,128)}, f32[1,1024]{1,0:T(1,128)}, bf16[8,128,2304]{2,1,0:T(8,128)(2,1)}, bf16[8,1152,128]{2,1,0:T(8,128)(2,1)}, f32[64,...) custom-call(f32[256,1024]{1,0:T(8,128)} %get-tuple-element.100.refs_, ...), custom_call_target="tpu_custom_call" | custom-call | flops 14495514624 | bytes 33554432 | tf_op jit(solution)/shard_map/ffn_backward/pallas_call | solution.py:784
  468.2 1.1 convert_element_type.31.refs_2_
  469.3 52.5 %conv_backward.1 = (f32[256,1024]{1,0:T(8,128)}, f32[1,1024]{1,0:T(1,128)}, f32[8,256]{1,0:T(8,128)}, bf16[8,128,768]{2,1,0:T(8,128)(2,1)}, bf16[8,256,128]{2,1,...) custom-call(f32[8,128]{1,0:T(8,128)} %get-tuple-element.78.refs_0_, ...), custom_call_target="tpu_custom_call" | custom-call | flops 4294967296 | bytes 16777216 | tf_op jit(solution)/shard_map/conv_backward/pallas_call | solution.py:784
  521.8 0.0 copy-start.3
  521.8 69.1 %tail.1 = (bf16[1024,256]{1,0:T(8,128)(2,1)}, f32[8,1024]{1,0:T(8,128)}, f32[64,2304]{1,0:T(8,128)}, f32[64,2304]{1,0:T(8,128)}, f32[1152,128]{1,0:T(8,128)}, /*index=5*/f32[128,768]{1,0:T(8,128)}, f32[256,128]{1,0:T(8,128)}) custom-call(f32[256,1024]{1,0:T(8,128)} %get-tuple-element.119.refs_0_, f32[1,1024]{1,0:T(1,128)} %get-tuple-element.120.refs_1_, ...), custom_call_target="tpu_custom_call" | custom-call | bytes 4194304 | tf_op jit(solution)/shard_map/tail/pallas_call | solution.py:784
  591.0 2.2 pad_maximum_fusion.3
  593.2 0.1 pad_maximum_fusion.1
  593.3 0.0 copy-start.1
  593.3 0.0 copy-start.2
  593.3 0.7 stack.30
  594.0 0.4 copy-done.1
  594.4 0.2 copy-done.2
  594.6 0.1 pad_maximum_fusion.2
  594.6 0.7 stack.31
  595.3 2.5 pad_maximum_fusion
  597.8 0.0 copy-done.14
  597.9 0.1 slice.73
  598.0 0.1 slice.75
  598.1 0.6 pad_maximum_fusion.6
  598.7 0.0 copy-done.7
  598.7 1.0 convert_element_type.32
  599.7 0.2 copy.41
  599.9 0.0 copy-start.12
  599.9 0.9 copy.42
  600.8 0.6 slice.71
  601.4 0.6 slice.76
  602.0 0.0 copy-done.11
  602.0 0.7 fusion.2
  602.7 0.7 reshape.79
  603.4 0.8 copy.51
  604.2 0.7 copy.52
  604.9 0.7 copy.53
  (29 shorter events, 0.1 us)
Async XLA Ops:
  2.1 3.0 copy-start
  7.7 1.6 copy-start.15
  7.7 2.2 copy-start.17
  126.1 1.9 copy-start.8
  128.8 52.5 %copy-start.16 = (f32[2,64]{1,0:T(2,128)S(1)}, f32[2,64]{1,0:T(2,128)}, u32[]{:S(2)}) copy-start(f32[2,64]{1,0:T(2,128)} %param.17) | copy-start | bytes 1540
  416.9 51.4 %copy-start.6 = (bf16[256,1024]{1,0:T(8,128)(2,1)S(1)}, bf16[256,1024]{1,0:T(8,128)(2,1)}, u32[]{:S(2)}) copy-start(bf16[256,1024]{1,0:T(8,128)(2,1)} %get-tuple-element.109) | copy-start | bytes 1572868
  521.8 69.2 %copy-start.3 = (f32[1152,128]{1,0:T(8,128)S(1)}, f32[1152,128]{1,0:T(8,128)}, u32[]{:S(2)}) copy-start(f32[1152,128]{1,0:T(8,128)} %get-tuple-element.143) | copy-start | bytes 1769476
  591.0 2.3 copy-start.4
  591.0 2.3 copy-start.5
  593.3 1.1 copy-start.1
  593.3 1.2 copy-start.2
  595.3 2.5 copy-start.14
  595.3 3.3 copy-start.7
  597.8 1.9 copy-start.10
  598.7 3.4 copy-start.11
  599.7 3.7 copy-start.9
  599.7 4.5 copy-start.13
  599.9 5.0 copy-start.12

commit v6 on v5

--- a/solution.py
+++ b/solution.py
@@ -162,12 +162,16 @@
     return jax.ShapeDtypeStruct(shape, dtype)
 
 
+END = 99
+
+
 class Place:
     def __init__(self):
         self.y, self.x, self.c, self.zh = (lax.axis_index(a) for a in ("r", "s", "c", "zh"))
         self.across_x, self.across_y = {"s": 1 - self.x}, {"r": 1 - self.y}
         self.partner = {"c": 1 - self.c}
         self.plain = self.c == self.zh
+        self.outer = lax.axis_index("zl") == self.zh
 
     def over(self, core):
         return {"c": core, "zh": 1 - self.zh}
@@ -194,204 +198,240 @@
 
 
 class Fetch:
-    def __init__(self, shard, at):
-        rows, cols = shard.shape
-        self.at = at
+    def __init__(self, shard, at, cuts=1, stage=0):
+        rows, cols = shard.shape[-2:]
+        self.at, self.cuts, self.stage, self.step_rows = at, cuts, stage, rows // cuts
         self.ins = [shard]
         self.outs = [jax.ShapeDtypeStruct((8, rows, cols), shard.dtype)]
         self.out_specs = [HBM]
-        self.scratch = [DMA((9,)), DMA((8,)), DMA((1,))]
+        self.in_place = stage == 2
+        self.semaphores()
+        if not self.in_place:
+            self.scratch.append(pltpu.VMEM((rows, cols), BF))
+
+    def semaphores(self):
+        self.scratch = [DMA((9 * self.cuts,)), DMA((8 * self.cuts,)), DMA((2,))]
 
     def bind(self, ins, outs, scratch):
         (self.own,), (self.out,) = ins, outs
-        self.sent, self.come, self.sem = scratch
+        self.sent, self.come, self.sem = scratch[:3]
+        self.bounce = scratch[3] if len(scratch) > 3 else None
         self.p = Place()
 
-    def copy(self, src, piece, sent, come, where):
+    def greets(self):
+        return Place.PLANES if self.stage == 2 else Place.PLANES + Place.ENDS
+
+    def part(self, ref, q):
+        return ref.at[pl.ds(q * self.step_rows, self.step_rows)]
+
+    def given(self, q):
+        return self.part(self.own, q)
+
+    def slot(self, piece, q):
+        return self.part(self.out.at[piece], q)
+
+    def home(self, a, q):
+        return self.slot(self.p.piece(0, 0, a), q)
+
+    def copy(self, src, dst, q, sent, come, where):
         return pltpu.make_async_remote_copy(
-            src_ref=src, dst_ref=self.out.at[piece], send_sem=self.sent.at[sent], recv_sem=self.come.at[come],
+            src_ref=src, dst_ref=dst, send_sem=self.sent.at[9 * q + sent], recv_sem=self.come.at[8 * q + come],
             device_id=where, device_id_type=MESH,
         )
 
-    def to_plane(self):
+    def to_plane(self, q):
         p = self.p
-        return self.copy(self.own, p.piece(0, 0, p.c), 0, p.c, p.over(p.zh))
-
-    def to_partner(self):
+        return self.copy(self.given(q), self.home(p.c, q), q, 0, p.c, p.over(p.zh))
+
+    def to_partner(self, q):
         p = self.p
-        return self.copy(self.own, p.piece(0, 0, p.c), 1, p.c, p.partner)
-
-    def arrived(self, a):
-        return self.copy(self.own, self.p.piece(0, 0, a), 0, a, self.p.partner).wait_recv()
+        return self.copy(self.given(q), self.home(p.c, q), q, 1, p.c, p.partner)
+
+    def arrived(self, a, q):
+        self.copy(self.given(q), self.home(a, q), q, 0, a, self.p.partner).wait_recv()
 
     def keep(self):
-        return pltpu.make_async_copy(self.own, self.out.at[self.p.piece(0, 0, self.p.c)], self.sem.at[0])
-
-    def to_x(self, a, src):
-        return self.copy(src, self.p.piece(0, 0, a), 2 + a, 2 + a, self.p.across_x)
-
-    def to_y(self, a, src):
-        return self.copy(src, self.p.piece(0, 0, a), 4 + a, 4 + a, self.p.across_y)
-
-    def spread(self, a, src):
-        self.to_x(a, src).start()
-        self.to_y(a, src).start()
-
-    def slot(self, a):
-        return self.out.at[self.p.piece(0, 0, a)]
-
-    def on_y(self):
-        piece = self.p.piece(0, 1, 0)
-        return self.copy(self.out.at[piece], piece, 6, 6, self.p.across_y)
-
-    def on_x(self):
-        piece = self.p.piece(1, 0, 1)
-        return self.copy(self.out.at[piece], piece, 7, 7, self.p.across_x)
-
-    def greets(self):
-        return Place.PLANES + Place.ENDS
+        slot = self.out.at[self.p.piece(0, 0, self.p.c)]
+        return [
+            pltpu.make_async_copy(self.own, self.bounce, self.sem.at[0]),
+            pltpu.make_async_copy(self.bounce, slot, self.sem.at[1]),
+        ]
+
+    def kept(self):
+        self.keep()[0].start()
+
+    def land(self):
+        copies = self.keep()
+        for i, copy in enumerate(copies):
+            if i:
+                copy.start()
+            copy.wait()
+
+    def to_x(self, a, q, src=None):
+        dst = self.slot(self.p.piece(0, 0, a), q)
+        return self.copy(dst if src is None else src, dst, q, 2 + a, 2 + a, self.p.across_x)
+
+    def to_y(self, a, q, src=None):
+        dst = self.slot(self.p.piece(0, 0, a), q)
+        return self.copy(dst if src is None else src, dst, q, 4 + a, 4 + a, self.p.across_y)
+
+    def spread(self, a, q, src):
+        self.to_x(a, q, src).start()
+        self.to_y(a, q, src).start()
+
+    def on_y(self, q):
+        there = self.slot(self.p.piece(0, 1, 0), q)
+        return self.copy(there, there, q, 6, 6, self.p.across_y)
+
+    def on_x(self, q):
+        there = self.slot(self.p.piece(1, 0, 1), q)
+        return self.copy(there, there, q, 7, 7, self.p.across_x)
+
+    def forward(self, q):
+        self.to_x(0, q).wait_recv()
+        self.on_y(q).start()
+        self.to_y(1, q).wait_recv()
+        self.on_x(q).start()
+
+    def plain(self, run):
+        pl.when(self.p.plain)(run)
+
+    def other(self, run):
+        pl.when(jnp.logical_not(self.p.plain))(run)
 
     def step(self, k):
-        p = self.p
-        if k == 0:
-
-            @pl.when(p.plain)
-            def _():
-                self.keep().start()
-                self.spread(p.c, self.own)
-
-            @pl.when(jnp.logical_not(p.plain))
-            def _():
-                self.to_partner().start()
-
-        elif k == 1:
-            self.to_plane().start()
-
-            @pl.when(p.plain)
-            def _():
-                self.arrived(1 - p.c)
-                self.spread(1 - p.c, self.slot(1 - p.c))
-
-        elif k == 2:
-
-            @pl.when(jnp.logical_not(p.plain))
-            def _():
+        p, every = self.p, range(self.cuts)
+
+        def own():
+            for q in every:
+                self.spread(p.c, q, self.given(q))
+
+        def partner():
+            for q in every:
+                self.to_partner(q).start()
+
+        def second():
+            for q in every:
+                self.arrived(1 - p.c, q)
+                self.spread(1 - p.c, q, self.home(1 - p.c, q))
+
+        def planes():
+            for q in every:
                 for a in (0, 1):
-                    self.arrived(a)
-                    self.spread(a, self.slot(a))
-
+                    self.spread(a, q, self.home(a, q))
+
+        def there(q):
+            for a in (0, 1):
+                self.arrived(a, q)
+                self.spread(a, q, self.home(a, q))
+
+        if self.stage == 2:
+            if k == 0:
+                self.other(planes)
+            elif k == 1:
+                self.other(lambda: [self.forward(q) for q in every] and None)
+            elif k == END:
+                self.other(self.close)
+        elif k == 0:
+            self.plain(self.kept)
+            self.other(partner)
+            self.plain(own)
+            self.plain(second)
+        elif k == END:
+            for q in every:
+                self.to_plane(q).wait_send()
+            if self.stage:
+                self.plain(self.close)
+                self.other(lambda: [self.arrived(a, q) for q in every for a in (0, 1)] and None)
+            else:
+                self.close()
+            self.plain(self.land)
+            self.other(lambda: [self.to_partner(q).wait_send() for q in every] and None)
+        elif k in (1, 2):
+            self.leave(k == 1)
         elif k == 3:
-            self.to_x(0, self.slot(0)).wait_recv()
-            self.on_y().start()
-            self.to_y(1, self.slot(1)).wait_recv()
-            self.on_x().start()
-        else:
-            self.to_x(1, self.slot(1)).wait_recv()
-            self.to_y(0, self.slot(0)).wait_recv()
-            self.on_y().wait()
-            self.on_x().wait()
-            self.to_plane().wait_send()
+            self.plain(lambda: [self.forward(q) for q in every] and None)
+        elif not self.stage:
+            q = k - 4
+            if q < self.cuts:
+                self.other(functools.partial(there, q))
+            if q:
+                self.other(lambda: self.forward(q - 1))
+
+    def leave(self, outer):
+        @pl.when(self.p.outer if outer else jnp.logical_not(self.p.outer))
+        def _():
+            for q in range(self.cuts):
+                self.to_plane(q).start()
+
+    def close(self):
+        for q in range(self.cuts):
+            self.to_x(1, q).wait_recv()
+            self.to_y(0, q).wait_recv()
+            self.on_y(q).wait()
+            self.on_x(q).wait()
             for a in (0, 1):
-                self.to_x(a, self.slot(a)).wait_send()
-                self.to_y(a, self.slot(a)).wait_send()
-
-            @pl.when(p.plain)
-            def _():
-                self.keep().wait()
-
-            @pl.when(jnp.logical_not(p.plain))
-            def _():
-                self.to_partner().wait_send()
+                self.to_x(a, q).wait_send()
+                self.to_y(a, q).wait_send()
 
 
 class Take(Fetch):
-    def __init__(self, whole, at, inside=None):
+    def __init__(self, whole, at, inside=False):
         rows, cols = whole.shape
-        self.at, self.each = at, rows // 8
+        self.at, self.each, self.cuts, self.stage = at, rows // 8, 1, 0
         self.ins = [whole]
         self.outs = [] if inside else [jax.ShapeDtypeStruct((rows, cols), whole.dtype)]
         self.out_specs = [] if inside else [HBM]
-        self.scratch = [DMA((9,)), DMA((8,)), DMA((1,))]
+        self.in_place = False
+        self.semaphores()
+        if not inside:
+            self.scratch.append(pltpu.VMEM((rows, cols), BF))
 
     def bind(self, ins, outs, scratch):
         (self.own,) = ins
         self.whole = outs[0] if outs else None
-        self.sent, self.come, self.sem = scratch
+        self.sent, self.come, self.sem = scratch[:3]
+        self.bounce = scratch[3] if len(scratch) > 3 else None
         self.p = Place()
 
     def rows(self, piece):
         return pl.ds(pl.multiple_of(piece * self.each, 16), self.each)
 
-    def copy(self, src, piece, sent, come, where):
-        return pltpu.make_async_remote_copy(
-            src_ref=self.own.at[self.rows(piece)] if src is None else src, dst_ref=self.whole.at[self.rows(piece)],
-            send_sem=self.sent.at[sent], recv_sem=self.come.at[come], device_id=where, device_id_type=MESH,
-        )
-
-    def to_plane(self):
-        p = self.p
-        return self.copy(None, p.piece(0, 0, p.c), 0, p.c, p.over(p.zh))
-
-    def arrived(self, a):
-        return self.copy(None, self.p.piece(0, 0, a), 0, a, self.p.partner).wait_recv()
+    def given(self, q):
+        return self.own.at[self.rows(self.p.piece(0, 0, self.p.c))]
+
+    def slot(self, piece, q):
+        return self.whole.at[self.rows(piece)]
 
     def keep(self):
-        return pltpu.make_async_copy(self.own, self.whole, self.sem.at[0])
-
-    def slot(self, a):
-        return self.whole.at[self.rows(self.p.piece(0, 0, a))]
-
-    def on_y(self):
-        piece = self.p.piece(0, 1, 0)
-        return self.copy(self.whole.at[self.rows(piece)], piece, 6, 6, self.p.across_y)
-
-    def on_x(self):
-        piece = self.p.piece(1, 0, 1)
-        return self.copy(self.whole.at[self.rows(piece)], piece, 7, 7, self.p.across_x)
+        if self.bounce is None:
+            return [pltpu.make_async_copy(self.own, self.whole, self.sem.at[0])]
+        return [
+            pltpu.make_async_copy(self.own, self.bounce, self.sem.at[0]),
+            pltpu.make_async_copy(self.bounce, self.whole, self.sem.at[1]),
+        ]
 
     def step(self, k):
-        p = self.p
+        def there():
+            for a in (0, 1):
+                self.arrived(a, 0)
+                self.spread(a, 0, self.home(a, 0))
+
+        def last():
+            self.close()
+
         if k == 0:
-
-            @pl.when(p.plain)
-            def _():
-                self.keep().start()
-
-        elif k == 1:
-            self.to_plane().start()
-        elif k == 2:
-
-            @pl.when(jnp.logical_not(p.plain))
-            def _():
-                for a in (0, 1):
-                    self.arrived(a)
-                    self.spread(a, self.slot(a))
-
+            self.plain(self.kept)
+        elif k in (1, 2):
+            self.leave(k == 1)
         elif k == 3:
-
-            @pl.when(jnp.logical_not(p.plain))
-            def _():
-                self.to_x(0, self.slot(0)).wait_recv()
-                self.on_y().start()
-                self.to_y(1, self.slot(1)).wait_recv()
-                self.on_x().start()
-
-        else:
-            self.to_plane().wait_send()
-
-            @pl.when(p.plain)
-            def _():
-                self.keep().wait()
-
-            @pl.when(jnp.logical_not(p.plain))
-            def _():
-                self.to_x(1, self.slot(1)).wait_recv()
-                self.to_y(0, self.slot(0)).wait_recv()
-                self.on_y().wait()
-                self.on_x().wait()
-                for a in (0, 1):
-                    self.to_x(a, self.slot(a)).wait_send()
-                    self.to_y(a, self.slot(a)).wait_send()
+            self.other(there)
+        elif k == 4:
+            self.other(lambda: self.forward(0))
+        elif k == END:
+            self.to_plane(0).wait_send()
+            self.plain(self.land)
+            self.other(last)
 
 
 class Exchange:
@@ -452,7 +492,7 @@
         elif k == 2:
             for p in range(self.parts):
                 self.gather.wait_part(p)
-        elif k == 4:
+        elif k == END:
             self.gather.wait_beside()
             for p in range(self.parts):
                 self.gather.wait_far(p)
@@ -507,7 +547,7 @@
             for here, stay, leave in self.parts():
                 pl.when(here)(lambda stay=stay: stay.start())
                 pl.when(jnp.logical_not(here))(lambda leave=leave: leave.start())
-        elif k == 4:
+        elif k == END:
             rows, width = self.low.shape
             for here, stay, leave in self.parts():
                 pl.when(here)(lambda stay=stay: stay.wait())
@@ -560,7 +600,8 @@
                 self.sum[0, pl.ds(7, 1), pl.ds(done, head.shape[1])] = head[...]
                 done += head.shape[1]
             self.hop(0).start()
-        elif k < 5:
+        else:
+            k = min(k, 4)
             last = len(self.axes) if k == 4 else k
             for i in range(k - 1, last):
                 self.hop(i).wait()
@@ -662,18 +703,23 @@
                     self.out[i] = (self.held[2 * i].astype(F32) + self.in2[i].astype(F32)).astype(BF)
             if self.last:
                 self.settle()
-        elif k == 4:
+                self.settle(False)
+        elif k == END:
             if self.last:
                 self.close()
             for hop in self.first_hops() + self.second_hops():
                 hop.wait_send()
 
-    def settle(self):
-        @pl.when(self.p.plain)
-        def _():
-            self.to_partner().start()
-
-        @pl.when(jnp.logical_not(self.p.plain))
+    def settle(self, outer=True):
+        if outer:
+
+            @pl.when(self.p.plain)
+            def _():
+                self.to_partner().start()
+
+        now = self.p.outer if outer else jnp.logical_not(self.p.outer)
+
+        @pl.when(now & jnp.logical_not(self.p.plain))
         def _():
             self.to_owner(0).start()
             self.to_owner(1).start()
@@ -728,7 +774,9 @@
         if k == 0:
             self.load().start()
             self.settle()
-        elif k == 4:
+        elif k == 1:
+            self.settle(False)
+        elif k == END:
             self.load().wait()
             self.close()
 
@@ -742,7 +790,7 @@
         self.others = [place.called(name) for name in names]
 
     def step(self, k):
-        for i in range(4):
+        for i in range(max([len(task.at) for task in self.tasks], default=0)):
             for task in self.tasks:
                 if i < len(task.at) and task.at[i] == k:
                     task.step(i)
@@ -750,7 +798,7 @@
     def finish(self, tasks=None):
         for task in self.tasks if tasks is None else tasks:
             if task not in self.done:
-                task.step(4)
+                task.step(END)
                 self.done.append(task)
 
 
@@ -781,12 +829,19 @@
             task.bind(*mine)
         kernel(*parts[0][0], *parts[1][0], *parts[2][0], Background(tasks, greets))
 
+    aliases, at_in, at_out = {}, groups[0][0], groups[1][0]
+    for task in tasks:
+        if getattr(task, "in_place", False):
+            aliases[at_in] = at_out
+        at_in += len(task.ins)
+        at_out += len(task.outs)
     results = pl.pallas_call(
         body,
         out_shape=tuple(outs),
         in_specs=in_specs,
         out_specs=tuple(out_specs),
         scratch_shapes=scratch,
+        input_output_aliases=aliases,
         compiler_params=params(ident),
         cost_estimate=pl.CostEstimate(flops=flops, bytes_accessed=traffic, transcendentals=0),
         name=name,
@@ -906,6 +961,7 @@
         scatter.close(0, p).wait_recv()
         o_over[here, :] = (tpart[...] + i_near[0, here, :].astype(F32)).astype(BF)
         scatter.link(p).start()
+        bg.step(10 + p)
     n_out = pltpu.make_async_copy(nf, n_hbm, osem.at[2 + 2 * parts])
     n_out.start()
     bg.step(2)
@@ -1252,8 +1308,8 @@
         blocks[p].arrive()
         gather.link(p, g.mine).start()
         gather.close(p, g.mine).start()
+    bg.step(1)
     gather.wait_beside()
-    bg.step(1)
     for p in range(parts):
         gather.wait_part(p)
     for p in range(parts):
@@ -1275,6 +1331,7 @@
         return carry
 
     lax.fori_loop(0, total // size, project, 0)
+    bg.step(4)
     saves = start_all([(nf, n_hbm), (low, p_hbm), (win, win_out), (wout, wout_out)], osem)
     places = lax.broadcasted_iota(jnp.int32, (total, LANES), 0)
     within = places - doc_starts(docs, lengths, places)
@@ -1282,6 +1339,7 @@
         b, c, x = (proj[:, pl.ds(i * chans + k * LANES, LANES)] for i in range(3))
         taps = [taps_out[pl.ds(j, 1), pl.ds(k * LANES, LANES)] for j in range(count)]
         mixed[:, pl.ds(k * LANES, LANES)] = (c * conv_taps(b * x, within, taps)).astype(BF)
+    bg.step(5)
     scatter_all(g, scatter, product(mixed, wout, False), mine, tpart)
     bg.step(3)
     block_ref[...] = full[at_rows(g.mine, size, 0, size), :]
@@ -1778,12 +1836,12 @@
     taps = jnp.pad(conv_kernel, ((0, 8 - count), (0, 0)))
     rows_of = lambda got: got.reshape(-1, got.shape[-1])
     if planes:
-        first = [Take(conv_in, (0, 0, 1, 2), True), Take(conv_out, (0, 0, 1, 2), True)]
-        first += [Fetch(own_w[0], (0, 1, 3, 3)), Fetch(own_v[0], (0, 1, 3, 3))]
-        second = [Take(x, (0, 0, 1, 2)) for x in (query_w, kv_w, out_w)] + [Fetch(own_v[1], (0, 1, 2, 2))]
-        third = [Fetch(own_w[1], (0, 1, 3, 3)), Spread(grad_out, (1, 2, 3))]
+        first = [Take(conv_in, (0, 1, 1, 2, 2), True), Take(conv_out, (0, 1, 1, 2, 2), True)]
+        first += [Fetch(own_w[0], (0, 1, 1, 2, 4, 5, 3, 3, 3), 4), Fetch(own_v[0], (0, 1, 1, 2, 3, 3, 3), 2)]
+        first += [Take(x, (0, 3, 3, 3, 3)) for x in (query_w, kv_w, out_w)]
+        second = [Fetch(own_w[1], (0, 0, 0, 2), 1, 1), Fetch(own_v[1], (0, 0, 0, 2), 1, 1)]
     else:
-        first, second, third = [], [], [Spread(grad_out, (1, 2, 3))]
+        first, second, third = [], [], []
         conv_in, conv_out, query_w, kv_w, out_w = map(swap, (conv_in, conv_out, query_w, kv_w, out_w))
         w0, w1 = (gather_dp(w, 0) for w in own_w)
         v0, v1 = (gather_dp(v, 1)[None] for v in own_v)
@@ -1793,17 +1851,17 @@
     )
     if planes:
         w0, v0 = rows_of(got[0]), got[1]
+        query_w, kv_w, out_w = got[2:]
     (h2, n1, hidden0), got = ffn_forward(h1, gain[1], w0, v0, 1, second)
     if planes:
-        query_w, kv_w, out_w, v1 = got
+        third = [Fetch(got[0], (0, 4), 2, 2), Fetch(got[1], (0, 4), 1, 2)]
     cosine, sine = rope_tables(doc_positions(lens[0, :docs].astype(jnp.int32), length), head_dim)
     (h3, n2, raw, ready, attended), got = attention_forward(
         head_dim, docs, lens, h2, gain[2], qgain, kgain, cosine, sine, query_w, kv_w, out_w, 2, third
     )
     if planes:
-        w1 = rows_of(got[0])
-    up_full = got[-1]
-    (h4, n3, hidden1), _ = ffn_forward(h3, gain[3], w1, v1, 3)
+        w1, v1 = rows_of(got[0]), got[1]
+    (h4, n3, hidden1), (up_full,) = ffn_forward(h3, gain[3], w1, v1, 3, [Spread(grad_out, (0, 1, 2))])
 
     def halves(grad, *at):
         half = grad.shape[1] // 2
@@ -1812,8 +1870,8 @@
     def whole(grad, at, last=False):
         return [Reduce(grad, 0, grad.shape[1], at, last)] if planes else []
 
-    def settled(sums):
-        return [Settle(x, (0,)) for x in sums]
+    def settled(sums, at):
+        return [Settle(x, at) for x in sums]
 
     quarter = lax.axis_index("c") * 2 + lax.axis_index("zl")
     dh4 = lax.dynamic_slice_in_dim(up_full, quarter * h4.shape[0], h4.shape[0], 0).astype(F32)
@@ -1826,18 +1884,18 @@
     )
     (dh1, gain1, gw0, gv0), got = ffn_backward(
         dh2, h1, gain[1], None, w0, v0, n1, hidden0, 6,
-        settled(sums) + whole(gv1, (0, 1, 2)) + whole(gqkv, (0, 2, 3)) + whole(gow, (0, 2, 3)),
+        settled(sums, (0, 2)) + whole(gv1, (0, 1, 2)) + whole(gqkv, (0, 2, 3)) + whole(gow, (0, 2, 3)),
     )
     sums_w1, sums = got[:2], got[2:]
     (dh0, gain0, gtaps, gci, gco), got = conv_backward(
         docs, count, lens, dh1, x_block.astype(F32), gain[0], taps, conv_in, conv_out, n0, projected, pieces, 7,
-        settled(sums) + halves(gw0, (0, 1, 3), (0, 3, 5)),
+        settled(sums, (0, 3)) + halves(gw0, (0, 1, 3), (0, 3, 5)),
     )
     others, sums = got[:3], got[3:]
     grads, totals, *got = tail(
         8,
         [Deliver(dh0, (0, 0)), Total([gain0, gain1, gain2, gain3, gtaps, gq, gk], (0, 1, 2, 3), count, ("c", "zl", "s", *(("r",) if planes else ()), "zh"))]
-        + settled(sums) + whole(gv0, (0, 1, 2), True) + whole(gci, (0, 1, 2), True) + whole(gco, (0, 1, 2), True),
+        + settled(sums, (0, 0)) + whole(gv0, (0, 1, 2), True) + whole(gci, (0, 1, 2), True) + whole(gco, (0, 1, 2), True),
     )
     if planes:
         gw1 = jnp.concatenate(sums_w1, axis=0)

time: 617 us -> 575 us (0.932)
  Pallas kernels: 569 us -> 532 us
    pallas_call x9, Pallas kernels: 569 us -> 532 us  [hosted(): pl.pallas_call(body, out_shape=tuple(outs), in_specs=in_specs, out_specs=...]
where the time goes in v6:
time: 575 us; the launch traced here: 569 us
  Pallas kernels  532 us (93%)
  local copies, waits for them, and re-layouts  20.7 us (4%)
  other arithmetic  14.4 us (3%)
    pallas_call x9, Pallas kernels, hosted(): pl.pallas_call(body, out_shape=tuple(outs), in_specs=in_specs, out_specs=...  532 us

profile of v6, /device:TPU:1, one launch (start us, length us, event | category | flops | bytes accessed | tf_op | source)
XLA Modules:
  0.0 568.7 jit_solution(5872686405963091788)
XLA Ops:
  0.6 1.5 fusion.3
  2.1 2.1 fusion.1
  4.2 0.9 copy.45
  5.1 0.0 copy-done
  5.1 0.8 slice_bitcast_fusion
  6.0 1.7 copy.39
  7.7 0.0 copy-start.8
  7.7 0.0 copy-start.15
  7.7 0.0 copy-start.17
  7.7 1.6 copy.40.refs_4_.refs_6_
  9.3 0.0 copy-done.8
  9.3 0.9 copy.49
  10.2 0.0 copy-done.15
  10.2 0.6 pad.9.refs_3_
  10.8 0.0 copy-done.17
  10.8 0.6 pad.8.refs_0_
  11.4 111.9 %conv_forward.1 = (f32[256,1024]{1,0:T(8,128)}, bf16[256,1024]{1,0:T(8,128)(2,1)}, bf16[1024,1024]{1,0:T(8,128)(2,1)}, bf16[1024,768]{1,0:T(8,128)(2,1)}, f32[8,...) custom-call(f32[8,128]{1,0:T(8,128)} %pad.8.refs_0_, ...), custom_call_target="tpu_custom_call" | custom-call | flops 2147483648 | bytes 16777216 | tf_op jit(solution)/shard_map/conv_forward/pallas_call | solution.py:838
  123.3 0.7 convert_bitcast_fusion
  123.9 0.1 select_reduce_fusion.1
  124.1 0.1 select_reduce_fusion
  124.2 1.9 fusion
  126.1 1.8 pad_maximum_fusion.4
  127.9 0.9 copy.47
  128.8 57.4 %ffn_forward.2 = (f32[256,1024]{1,0:T(8,128)}, bf16[1024,1024]{1,0:T(8,128)(2,1)}, bf16[1024,2304]{1,0:T(8,128)(2,1)}, bf16[8,128,2304]{2,1,0:T(8,128)(2,1)}, bf16[8,1152,128]{2,1,0:T(8,128)(2,1)}) custom-call(f32[256,1024]{1,0:T(8,128)} %get-tuple-element.81.refs_0_.refs_1_, f32[1,1024]{1,0:T(1,128)} %get-tuple-element.203.refs_1_.refs_2_, ...), custom_call_target="tpu_custom_call" | custom-call | flops 7247757312 | bytes 16777216 | tf_op jit(solution)/shard_map/ffn_forward/pallas_call | solution.py:838
  186.2 0.0 copy-done.16
  186.3 0.6 tile.24.refs_3_.refs_4_
  186.9 0.6 tile.27.refs_4_.refs_5_
  187.5 46.0 %attention_forward.1 = (f32[256,1024]{1,0:T(8,128)}, bf16[1024,1024]{1,0:T(8,128)(2,1)}, bf16[1024,512]{1,0:T(8,128)(2,1)}, bf16[1024,512]{1,0:T(8,128)(2,1)}, b...) custom-call(f32[8,128]{1,0:T(8,128)} %get-tuple-element.80.refs_0_, ...), custom_call_target="tpu_custom_call", output_to_operand_aliasing={{5}: (10, {}), {6}: (11, {})} | custom-call | flops 1610612736 | bytes 16777216 | tf_op jit(solution)/shard_map/attention_forward/pallas_call | solution.py:838
  233.5 45.5 %ffn_forward.3 = (f32[256,1024]{1,0:T(8,128)}, bf16[1024,1024]{1,0:T(8,128)(2,1)}, bf16[1024,2304]{1,0:T(8,128)(2,1)}, bf16[1024,1024]{1,0:T(8,128)(2,1)}) custom-call(f32[256,1024]{1,0:T(8,128)} %get-tuple-element.90.refs_0_.refs_1_, f32[1,1024]{1,0:T(1,128)} %get-tuple-element.202.refs_1_.refs_2_, bf16[1024,2304]{1,0:T(8,128)(2,1)} %bitcast.29, ...), custom_call_target="tpu_custom_call" | custom-call | flops 7247757312 | bytes 16777216 | tf_op jit(solution)/shard_map/ffn_forward/pallas_call | solution.py:838
  279.0 2.1 dynamic-slice_convert_fusion.refs_0_
  281.2 39.0 %ffn_backward.2 = (f32[256,1024]{1,0:T(8,128)}, f32[1,1024]{1,0:T(1,128)}, bf16[8,128,2304]{2,1,0:T(8,128)(2,1)}, bf16[8,1152,128]{2,1,0:T(8,128)(2,1)}, bf16[1024,256]{1,0:T(8,128)(2,1)}) custom-call(f32[256,1024]{1,0:T(8,128)} %dynamic-slice_convert_fusion.refs_0_, f32[256,1024]{1,0:T(8,128)} %get-tuple-element.90.refs_0_.refs_1_, ...), custom_call_target="tpu_custom_call" | custom-call | flops 14495514624 | bytes 33554432 | tf_op jit(solution)/shard_map/ffn_backward/pallas_call | solution.py:838
  320.2 58.5 %attention_backward.1 = (f32[256,1024]{1,0:T(8,128)}, f32[1,1024]{1,0:T(1,128)}, f32[1,256]{1,0:T(1,128)}, f32[1,128]{1,0:T(1,128)}, bf16[8,128,512]{2,1,0:T(8,1...) custom-call(f32[8,128]{1,0:T(8,128)} %get-tuple-element.80.refs_0_, ...), custom_call_target="tpu_custom_call" | custom-call | flops 3221225472 | bytes 33554432 | tf_op jit(solution)/shard_map/attention_backward/pallas_call | solution.py:838
  378.6 0.0 copy-start.6
  378.6 52.2 %ffn_backward.3 = (f32[256,1024]{1,0:T(8,128)}, f32[1,1024]{1,0:T(1,128)}, bf16[8,128,2304]{2,1,0:T(8,128)(2,1)}, bf16[8,1152,128]{2,1,0:T(8,128)(2,1)}, f32[64,...) custom-call(f32[256,1024]{1,0:T(8,128)} %get-tuple-element.104.refs_, ...), custom_call_target="tpu_custom_call" | custom-call | flops 14495514624 | bytes 33554432 | tf_op jit(solution)/shard_map/ffn_backward/pallas_call | solution.py:838
  430.8 0.0 copy-done.6
  430.8 1.1 convert_element_type.31.refs_2_
  431.9 52.1 %conv_backward.1 = (f32[256,1024]{1,0:T(8,128)}, f32[1,1024]{1,0:T(1,128)}, f32[8,256]{1,0:T(8,128)}, bf16[8,128,768]{2,1,0:T(8,128)(2,1)}, bf16[8,256,128]{2,1,...) custom-call(f32[8,128]{1,0:T(8,128)} %get-tuple-element.80.refs_0_, ...), custom_call_target="tpu_custom_call" | custom-call | flops 4294967296 | bytes 16777216 | tf_op jit(solution)/shard_map/conv_backward/pallas_call | solution.py:838
  484.1 0.0 copy-start.3
  484.1 69.6 %tail.1 = (bf16[1024,256]{1,0:T(8,128)(2,1)}, f32[8,1024]{1,0:T(8,128)}, f32[64,2304]{1,0:T(8,128)}, f32[64,2304]{1,0:T(8,128)}, f32[1152,128]{1,0:T(8,128)}, /*index=5*/f32[128,768]{1,0:T(8,128)}, f32[256,128]{1,0:T(8,128)}) custom-call(f32[256,1024]{1,0:T(8,128)} %get-tuple-element.123.refs_0_, f32[1,1024]{1,0:T(1,128)} %get-tuple-element.124.refs_1_, ...), custom_call_target="tpu_custom_call" | custom-call | bytes 4194304 | tf_op jit(solution)/shard_map/tail/pallas_call | solution.py:838
  553.7 0.0 copy-start.4
  553.7 2.2 pad_maximum_fusion.3
  556.0 0.1 pad_maximum_fusion.1
  556.1 0.0 copy-start.1
  556.1 0.0 copy-start.2
  556.1 0.7 stack.30
  556.8 0.4 copy-done.1
  557.1 0.2 copy-done.2
  557.3 0.1 pad_maximum_fusion.2
  557.4 0.7 stack.31
  558.1 2.5 pad_maximum_fusion
  560.6 0.1 slice.73
  560.8 0.1 slice.75
  560.9 0.6 pad_maximum_fusion.6
  561.4 1.0 convert_element_type.32
  562.5 0.2 copy.43
  562.7 0.9 copy.44
  563.6 0.6 slice.71
  564.2 0.6 slice.76
  564.8 0.0 copy-done.11
  564.8 0.7 fusion.2
  565.5 0.7 reshape.79
  566.2 0.8 copy.55
  567.0 0.7 copy.56
  567.7 0.7 copy.57
  (29 shorter events, 0.1 us)
Async XLA Ops:
  2.1 3.0 copy-start
  7.7 1.6 copy-start.8
  7.7 2.5 copy-start.15
  7.7 3.1 copy-start.17
  128.8 57.4 %copy-start.16 = (f32[2,64]{1,0:T(2,128)S(1)}, f32[2,64]{1,0:T(2,128)}, u32[]{:S(2)}) copy-start(f32[2,64]{1,0:T(2,128)} %param.17) | copy-start | bytes 1540
  378.6 52.2 %copy-start.6 = (bf16[256,1024]{1,0:T(8,128)(2,1)S(1)}, bf16[256,1024]{1,0:T(8,128)(2,1)}, u32[]{:S(2)}) copy-start(bf16[256,1024]{1,0:T(8,128)(2,1)} %get-tuple-element.113) | copy-start | bytes 1572868
  484.1 69.7 %copy-start.3 = (f32[1152,128]{1,0:T(8,128)S(1)}, f32[1152,128]{1,0:T(8,128)}, u32[]{:S(2)}) copy-start(f32[1152,128]{1,0:T(8,128)} %get-tuple-element.147) | copy-start | bytes 1769476
  553.7 2.3 copy-start.4
  553.7 2.3 copy-start.5
  556.1 1.1 copy-start.1
  556.1 1.2 copy-start.2
  558.1 2.5 copy-start.14
  558.1 3.3 copy-start.7
  560.6 1.9 copy-start.10
  561.4 3.4 copy-start.11
  562.5 3.7 copy-start.9
  562.5 4.5 copy-start.13
  562.7 5.0 copy-start.12

commit v7 on v6

--- a/solution.py
+++ b/solution.py
@@ -850,13 +850,13 @@
     return results[0], [r[0] for r in results[1:] if r]
 
 
-def put_rows(scratch, first, value):
+def put_rows(scratch, first, value, cols=slice(None)):
     tall = scratch.shape[1]
     done = 0
     while done < value.shape[0]:
         piece, at = divmod(first + done, tall)
         count = min(tall - at, value.shape[0] - done)
-        scratch[piece, pl.ds(at, count), :] = value[done : done + count]
+        scratch[piece, pl.ds(at, count), cols] = value[done : done + count]
         done += count
 
 
@@ -893,33 +893,30 @@
     bg.step(0)
     wait_all(loads)
 
+    third = hidden // 3
+
     def rows_of(places):
         return jnp.concatenate([nf[r, :] for r, _ in places], axis=0) if len(places) > 1 else nf[places[0][0], :]
 
     def up(places):
         def body(t, carry):
             x = rows_of(places)
-            wt = jnp.concatenate([w[:, lanes(t * LANES, LANES)], w[:, lanes(hidden + t * LANES, LANES)]], axis=1)
-            both = mm(x, wt)
-            gate, upper = both[:, :LANES], both[:, LANES:]
+            cols, more = lanes(t * third, third), lanes(hidden + t * third, third)
+            both = mm(x, jnp.concatenate([w[:, cols], w[:, more]], axis=1))
+            gate, upper = both[:, :third], both[:, third:]
             a = gate * jax.nn.sigmoid(gate) * upper
-            act[:, lanes(t * LANES, LANES)] = a.astype(BF)
+            act[:, cols] = a.astype(BF)
             at = 0
             for r, count in places:
-                u[r, lanes(t * LANES, LANES)] = gate[at : at + count].astype(BF)
-                u[r, lanes(hidden + t * LANES, LANES)] = upper[at : at + count].astype(BF)
+                u[r, cols] = gate[at : at + count].astype(BF)
+                u[r, more] = upper[at : at + count].astype(BF)
                 at += count
             return carry
 
-        lax.fori_loop(0, hidden // LANES, body, 0)
+        lax.fori_loop(0, 3, body, 0)
 
     def down(store):
-        def body(t, carry):
-            cols = lanes(t * 256, 256)
-            store(cols, mm(act[...], v[:, cols]))
-            return carry
-
-        lax.fori_loop(0, width // 256, body, 0)
+        store(slice(None), mm(act[...], v[...]))
 
     def keep(index, r, count):
         return pltpu.make_async_copy(u.at[r], u_hbm.at[r], osem.at[index])
@@ -980,6 +977,7 @@
         keep(2 + 2 * p, at_rows(g.across, size, p * step, step), step).wait()
         keep(3 + 2 * p, at_rows(g.far, size, p * step, step), step).wait()
     n_out.wait()
+    bg.step(6)
     bg.finish()
 
 
@@ -1020,18 +1018,18 @@
         scatter.link(p).wait_recv()
         dn = mine[here, :] + scatter.in_near[1, here, :].astype(F32) + scatter.in_over[here, :].astype(F32)
         term, grad_gain = rms_back(dn, h_ref[here, :], gain_ref[...])
-        out_ref[here, :] = dh_ref[here, :] + term
+        out_ref[here, :] = dh_ref[here, :].astype(F32) + term
         gg_ref[...] += grad_gain
 
 
 def ffn_backward_kernel(
     known, dh_ref, h_ref, gain_ref, df_hbm, w_hbm, v_hbm, n_hbm, u_hbm, out_ref, gg_ref, gw_hbm, gv_hbm,
-    w, v, nf, u, act, df, tpart, mine, gtile, gv, n_near, n_over, n_on, o_near, i_near, o_over, i_over, s_near, s_over,
+    w, v, nf, u, act, df, tpart, mine, gw, gv, n_near, n_over, n_on, o_near, i_near, o_over, i_over, s_near, s_over,
     wsem, osem, bg,
 ):
     g = Group(bg.others)
     g.greet()
-    size, width = dh_ref.shape
+    size, width = h_ref.shape
     hidden = v.shape[0]
     loads = column_loads(v_hbm, v) + [(u_hbm, u), (w_hbm, w), (n_hbm, nf)]
     loads = start_all(loads + [(df_hbm, df)] if known else loads, wsem)
@@ -1074,11 +1072,11 @@
 
     def second(places, store):
         def body(t, carry):
-            cols = lanes(t * 256, 256)
+            cols = lanes(t * 512, 512)
             store(cols, mm_nt(cat(u, places, slice(None)), w[cols, :]))
             return carry
 
-        lax.fori_loop(0, width // 256, body, 0)
+        lax.fori_loop(0, width // 512, body, 0)
 
     whole = lambda block: [(at_rows(block, size, 0, size), size)]
 
@@ -1124,40 +1122,25 @@
     if known:
         beside()
         own()
-    flush = []
-    count = 0
-
-    def emit(value, dst):
-        nonlocal count
-        slot = count % 2
-        if count >= 2:
-            flush[count - 2].wait()
-        gtile[slot, :, : value.shape[1]] = value.astype(BF)
-        copy = pltpu.make_async_copy(gtile.at[slot, :, : value.shape[1]], dst, osem.at[slot])
-        copy.start()
-        flush.append(copy)
-        count += 1
-
-    tall = gtile.shape[1]
     for t in range(3):
         put_columns(gv, t * third, mm_tn(act[:, t * third : (t + 1) * third], df[...]).astype(BF))
     save = pltpu.make_async_copy(gv, gv_hbm, osem.at[2])
     save.start()
     bg.step(3)
-    each = gw_hbm.shape[1]
-    for t in range(width // tall):
-        piece, at = divmod(t * tall, each)
+    for t in range(width // 512):
         for k in range(2):
             cols = slice(k * hidden, (k + 1) * hidden)
-            emit(mm_tn(nf[:, t * tall : (t + 1) * tall], u[:, cols]), gw_hbm.at[piece, pl.ds(at, tall), cols])
+            put_rows(gw, t * 512, mm_tn(nf[:, t * 512 : (t + 1) * 512], u[:, cols]).astype(BF), cols)
+    more = pltpu.make_async_copy(gw, gw_hbm, osem.at[0])
+    more.start()
     bg.step(4)
-    close_scatter(scatter, mine, dh_ref, h_ref, gain_ref, out_ref, gg_ref)
+    close_scatter(scatter, mine, df.at[at_rows(g.mine, size, 0, size)] if known else dh_ref, h_ref, gain_ref, out_ref, gg_ref)
     if not known:
         gather.finish()
     scatter.wait_all_sends()
-    for copy in flush[-2:]:
-        copy.wait()
+    more.wait()
     save.wait()
+    bg.step(6)
     bg.finish()
 
 
@@ -1166,7 +1149,9 @@
     pieces, hidden = v.shape[:2]
     total = 4 * size
     known = df is not None
-    if not known:
+    if known:
+        dh = gain
+    else:
         df = n
     return hosted(
         functools.partial(ffn_backward_kernel, known), ident, "ffn_backward", [dh, h, gain, df, w, v, n, u],
@@ -1180,7 +1165,7 @@
             pltpu.VMEM((width, 2 * hidden), BF), pltpu.VMEM((hidden, width), BF), pltpu.VMEM((total, width), BF),
             pltpu.VMEM((total, 2 * hidden), BF), pltpu.VMEM((total, hidden), BF), pltpu.VMEM((total, width), BF),
             pltpu.VMEM((size // parts, width), F32), pltpu.VMEM((size, width), F32),
-            pltpu.VMEM((2, 128, hidden), BF), pltpu.VMEM((pieces, hidden, width // pieces), BF),
+            pltpu.VMEM((pieces, width // pieces, 2 * hidden), BF), pltpu.VMEM((pieces, hidden, width // pieces), BF),
             *gather_scratch(parts), *scatter_scratch(size, width, parts), DMA((4 + pieces,)), DMA((3,)),
         ],
         tasks, 12 * total * width * hidden, 2**25,
@@ -1204,7 +1189,7 @@
     return found[0] if len(found) == 1 else jnp.concatenate(found, axis=0)
 
 
-def product(src, weight, turned, tile=256):
+def product(src, weight, turned, tile=512):
     def run(places, store):
         width = weight.shape[0] if turned else weight.shape[1]
 
@@ -1355,6 +1340,7 @@
     gather.finish()
     scatter.wait_all_sends()
     wait_all(saves)
+    bg.step(6)
     bg.finish()
 
 
@@ -1444,6 +1430,7 @@
     save.wait()
     more.wait()
     bg.step(5)
+    bg.step(6)
     bg.finish()
 
 
@@ -1609,6 +1596,7 @@
     scatter.wait_all_sends()
     wait_all(saves)
     save_o.wait()
+    bg.step(6)
     bg.finish()
 
 
@@ -1732,6 +1720,7 @@
     scatter.wait_all_sends()
     save.wait()
     more.wait()
+    bg.step(6)
     bg.finish()
 
 
@@ -1771,6 +1760,7 @@
     g.meet()
     for k in range(4):
         bg.step(k)
+    bg.step(6)
     bg.finish()
 
 
@@ -1863,9 +1853,9 @@
         w1, v1 = rows_of(got[0]), got[1]
     (h4, n3, hidden1), (up_full,) = ffn_forward(h3, gain[3], w1, v1, 3, [Spread(grad_out, (0, 1, 2))])
 
-    def halves(grad, *at):
+    def halves(grad, first, second, last=False):
         half = grad.shape[1] // 2
-        return [Reduce(grad, i * half, half, at[i], False) for i in (0, 1)] if planes else []
+        return [Reduce(grad, 0, half, first, last), Reduce(grad, half, half, second, False)] if planes else []
 
     def whole(grad, at, last=False):
         return [Reduce(grad, 0, grad.shape[1], at, last)] if planes else []
@@ -1873,14 +1863,12 @@
     def settled(sums, at):
         return [Settle(x, at) for x in sums]
 
-    quarter = lax.axis_index("c") * 2 + lax.axis_index("zl")
-    dh4 = lax.dynamic_slice_in_dim(up_full, quarter * h4.shape[0], h4.shape[0], 0).astype(F32)
     (dh3, gain3, gw1, gv1), (output,) = ffn_backward(
-        dh4, h3, gain[3], up_full, w1, v1, n3, hidden1, 4, [Deliver(h4, (0, 2))]
+        None, h3, gain[3], up_full, w1, v1, n3, hidden1, 4, [Deliver(h4, (0, 2))]
     )
     (dh2, gain2, gq, gk, gqkv, gow), sums = attention_backward(
         head_dim, docs, lens, dh3, h2, gain[2], qgain, kgain, cosine, sine, query_w, kv_w, out_w, n2, raw, ready, attended,
-        pieces, 5, halves(gw1, (0, 1, 4), (0, 3, 5)),
+        pieces, 5, halves(gw1, (0, 2, 5), (0, 4, 6)),
     )
     (dh1, gain1, gw0, gv0), got = ffn_backward(
         dh2, h1, gain[1], None, w0, v0, n1, hidden0, 6,
@@ -1889,19 +1877,19 @@
     sums_w1, sums = got[:2], got[2:]
     (dh0, gain0, gtaps, gci, gco), got = conv_backward(
         docs, count, lens, dh1, x_block.astype(F32), gain[0], taps, conv_in, conv_out, n0, projected, pieces, 7,
-        settled(sums, (0, 3)) + halves(gw0, (0, 1, 3), (0, 3, 5)),
+        settled(sums, (0, 3)) + halves(gw0, (0, 1, 4), (0, 3, 6), True),
     )
-    others, sums = got[:3], got[3:]
-    grads, totals, *got = tail(
+    others, first_w0, sums = got[:3], got[3:4], got[4:]
+    totals, grads, *got = tail(
         8,
-        [Deliver(dh0, (0, 0)), Total([gain0, gain1, gain2, gain3, gtaps, gq, gk], (0, 1, 2, 3), count, ("c", "zl", "s", *(("r",) if planes else ()), "zh"))]
-        + settled(sums, (0, 0)) + whole(gv0, (0, 1, 2), True) + whole(gci, (0, 1, 2), True) + whole(gco, (0, 1, 2), True),
+        [Total([gain0, gain1, gain2, gain3, gtaps, gq, gk], (0, 1, 2, 3), count, ("zh", "s", *(("r",) if planes else ()), "zl", "c")), Deliver(dh0, (0, 0))]
+        + settled(sums, (0, 0)) + whole(gv0, (0, 0, 1), True) + whole(gci, (1, 2, 3), True) + whole(gco, (1, 2, 3), True),
     )
     if planes:
         gw1 = jnp.concatenate(sums_w1, axis=0)
         gv1, gqkv, gow = others
-        gw0 = jnp.concatenate(got[:2], axis=0)
-        gv0, gci, gco = got[2:]
+        gw0 = jnp.concatenate([first_w0[0], got[0]], axis=0)
+        gv0, gci, gco = got[1:]
     else:
         totals = lax.psum(totals, "r")
         gw0, gw1, gci, gqkv = (scatter_dp(g[0], 0) for g in (gw0, gw1, gci, gqkv))

time: 575 us -> 550 us (0.957)
  Pallas kernels: 532 us -> 511 us
    pallas_call x9, Pallas kernels: 532 us -> 511 us  [hosted(): pl.pallas_call(body, out_shape=tuple(outs), in_specs=in_specs, out_specs=...]
where the time goes in v7:
time: 550 us; the launch traced here: 545 us
  Pallas kernels  511 us (93%)
  local copies, waits for them, and re-layouts  20.7 us (4%)
  other arithmetic  12.3 us (2%)
    pallas_call x9, Pallas kernels, hosted(): pl.pallas_call(body, out_shape=tuple(outs), in_specs=in_specs, out_specs=...  511 us

profile of v7, /device:TPU:1, one launch (start us, length us, event | category | flops | bytes accessed | tf_op | source)
XLA Modules:
  0.0 545.2 jit_solution(17302747031540157913)
XLA Ops:
  0.6 1.5 fusion.3
  2.1 2.1 fusion.1
  4.2 0.9 copy.45
  5.1 0.0 copy-done
  5.1 0.8 slice_bitcast_fusion
  6.0 1.7 copy.39
  7.7 0.0 copy-start.8
  7.7 0.0 copy-start.15
  7.7 0.0 copy-start.17
  7.7 1.6 copy.40.refs_4_.refs_6_
  9.3 0.0 copy-done.8
  9.3 0.9 copy.49
  10.2 0.0 copy-done.15
  10.2 0.6 pad.9.refs_3_
  10.8 0.0 copy-done.17
  10.8 0.6 pad.8.refs_0_
  11.4 110.6 %conv_forward.1 = (f32[256,1024]{1,0:T(8,128)}, bf16[256,1024]{1,0:T(8,128)(2,1)}, bf16[1024,1024]{1,0:T(8,128)(2,1)}, bf16[1024,768]{1,0:T(8,128)(2,1)}, f32[8,...) custom-call(f32[8,128]{1,0:T(8,128)} %pad.8.refs_0_, ...), custom_call_target="tpu_custom_call" | custom-call | flops 2147483648 | bytes 16777216 | tf_op jit(solution)/shard_map/conv_forward/pallas_call | solution.py:838
  122.0 0.7 convert_bitcast_fusion
  122.7 0.1 select_reduce_fusion.1
  122.8 0.1 select_reduce_fusion
  122.9 1.9 fusion
  124.8 1.8 pad_maximum_fusion.4
  126.7 0.9 copy.47
  127.5 58.4 %ffn_forward.2 = (f32[256,1024]{1,0:T(8,128)}, bf16[1024,1024]{1,0:T(8,128)(2,1)}, bf16[1024,2304]{1,0:T(8,128)(2,1)}, bf16[8,128,2304]{2,1,0:T(8,128)(2,1)}, bf16[8,1152,128]{2,1,0:T(8,128)(2,1)}) custom-call(f32[256,1024]{1,0:T(8,128)} %get-tuple-element.80.refs_0_.refs_1_, f32[1,1024]{1,0:T(1,128)} %get-tuple-element.203.refs_1_.refs_2_, ...), custom_call_target="tpu_custom_call" | custom-call | flops 7247757312 | bytes 16777216 | tf_op jit(solution)/shard_map/ffn_forward/pallas_call | solution.py:838
  185.9 0.0 copy-done.16
  186.0 0.6 tile.24.refs_3_.refs_4_
  186.6 0.6 tile.27.refs_4_.refs_5_
  187.2 44.7 %attention_forward.1 = (f32[256,1024]{1,0:T(8,128)}, bf16[1024,1024]{1,0:T(8,128)(2,1)}, bf16[1024,512]{1,0:T(8,128)(2,1)}, bf16[1024,512]{1,0:T(8,128)(2,1)}, b...) custom-call(f32[8,128]{1,0:T(8,128)} %get-tuple-element.79.refs_0_, ...), custom_call_target="tpu_custom_call", output_to_operand_aliasing={{5}: (10, {}), {6}: (11, {})} | custom-call | flops 1610612736 | bytes 16777216 | tf_op jit(solution)/shard_map/attention_forward/pallas_call | solution.py:838
  231.9 45.5 %ffn_forward.3 = (f32[256,1024]{1,0:T(8,128)}, bf16[1024,1024]{1,0:T(8,128)(2,1)}, bf16[1024,2304]{1,0:T(8,128)(2,1)}, bf16[1024,1024]{1,0:T(8,128)(2,1)}) custom-call(f32[256,1024]{1,0:T(8,128)} %get-tuple-element.89.refs_0_.refs_1_, f32[1,1024]{1,0:T(1,128)} %get-tuple-element.202.refs_1_.refs_0_.refs_2_, bf16[1024,2304]{1,0:T(8,128)(2,1)} %bitcast.29, ...), custom_call_target="tpu_custom_call" | custom-call | flops 7247757312 | bytes 16777216 | tf_op jit(solution)/shard_map/ffn_forward/pallas_call | solution.py:838
  277.4 34.7 %ffn_backward.2 = (f32[256,1024]{1,0:T(8,128)}, f32[1,1024]{1,0:T(1,128)}, bf16[8,128,2304]{2,1,0:T(8,128)(2,1)}, bf16[8,1152,128]{2,1,0:T(8,128)(2,1)}, bf16[1024,256]{1,0:T(8,128)(2,1)}) custom-call(f32[1,1024]{1,0:T(1,128)} %get-tuple-element.202.refs_1_.refs_0_.refs_2_, f32[256,1024]{1,0:T(8,128)} %get-tuple-element.89.refs_0_.refs_1_, ...), custom_call_target="tpu_custom_call" | custom-call | flops 14495514624 | bytes 33554432 | tf_op jit(solution)/shard_map/ffn_backward/pallas_call | solution.py:838
  312.1 50.4 %attention_backward.1 = (f32[256,1024]{1,0:T(8,128)}, f32[1,1024]{1,0:T(1,128)}, f32[1,256]{1,0:T(1,128)}, f32[1,128]{1,0:T(1,128)}, bf16[8,128,512]{2,1,0:T(8,1...) custom-call(f32[8,128]{1,0:T(8,128)} %get-tuple-element.79.refs_0_, ...), custom_call_target="tpu_custom_call" | custom-call | flops 3221225472 | bytes 33554432 | tf_op jit(solution)/shard_map/attention_backward/pallas_call | solution.py:838
  362.5 0.0 copy-start.6
  362.5 52.4 %ffn_backward.3 = (f32[256,1024]{1,0:T(8,128)}, f32[1,1024]{1,0:T(1,128)}, bf16[8,128,2304]{2,1,0:T(8,128)(2,1)}, bf16[8,1152,128]{2,1,0:T(8,128)(2,1)}, f32[64,...) custom-call(f32[256,1024]{1,0:T(8,128)} %get-tuple-element.103.refs_, ...), custom_call_target="tpu_custom_call" | custom-call | flops 14495514624 | bytes 33554432 | tf_op jit(solution)/shard_map/ffn_backward/pallas_call | solution.py:838
  414.9 0.0 copy-done.6
  414.9 1.1 convert_element_type.27.refs_2_
  416.0 58.5 %conv_backward.1 = (f32[256,1024]{1,0:T(8,128)}, f32[1,1024]{1,0:T(1,128)}, f32[8,256]{1,0:T(8,128)}, bf16[8,128,768]{2,1,0:T(8,128)(2,1)}, bf16[8,256,128]{2,1,...) custom-call(f32[8,128]{1,0:T(8,128)} %get-tuple-element.79.refs_0_, ...), custom_call_target="tpu_custom_call" | custom-call | flops 4294967296 | bytes 16777216 | tf_op jit(solution)/shard_map/conv_backward/pallas_call | solution.py:838
  474.5 0.0 copy-start.4
  474.5 55.9 %tail.1 = (f32[8,1024]{1,0:T(8,128)}, bf16[1024,256]{1,0:T(8,128)(2,1)}, f32[64,2304]{1,0:T(8,128)}, f32[1152,128]{1,0:T(8,128)}, f32[128,768]{1,0:T(8,128)}, /*index=5*/f32[256,128]{1,0:T(8,128)}) custom-call(f32[1,1024]{1,0:T(1,128)} %get-tuple-element.122.refs_0_, f32[1,1024]{1,0:T(1,128)} %get-tuple-element.123.refs_1_, ...), custom_call_target="tpu_custom_call" | custom-call | bytes 4194304 | tf_op jit(solution)/shard_map/tail/pallas_call | solution.py:838
  530.4 0.0 copy-start.3
  530.4 0.0 copy-start.5
  530.4 0.0 copy-done.4
  530.4 2.2 pad_maximum_fusion.3
  532.7 0.1 pad_maximum_fusion.1
  532.8 0.7 stack.30
  533.5 0.4 copy-done.1
  533.8 0.2 copy-done.2
  534.0 0.1 pad_maximum_fusion.2
  534.1 0.7 stack.31
  534.8 2.5 pad_maximum_fusion
  537.3 0.1 slice.73
  537.4 0.1 slice.75
  537.6 0.6 pad_maximum_fusion.6
  538.1 1.0 convert_element_type.28
  539.2 0.2 copy.43
  539.4 0.9 copy.44
  540.3 0.6 slice.71
  540.9 0.6 slice.76
  541.5 0.7 fusion.2
  542.2 0.7 reshape.79
  542.9 0.8 copy.55
  543.7 0.0 copy-done.13
  543.7 0.7 copy.56
  544.3 0.0 copy-done.12
  544.3 0.7 copy.57
  (28 shorter events, 0.1 us)
Async XLA Ops:
  2.1 3.0 copy-start
  7.7 1.6 copy-start.8
  7.7 2.5 copy-start.15
  7.7 3.1 copy-start.17
  127.5 58.4 %copy-start.16 = (f32[2,64]{1,0:T(2,128)S(1)}, f32[2,64]{1,0:T(2,128)}, u32[]{:S(2)}) copy-start(f32[2,64]{1,0:T(2,128)} %param.17) | copy-start | bytes 1540
  362.5 52.4 %copy-start.6 = (bf16[256,1024]{1,0:T(8,128)(2,1)S(1)}, bf16[256,1024]{1,0:T(8,128)(2,1)}, u32[]{:S(2)}) copy-start(bf16[256,1024]{1,0:T(8,128)(2,1)} %get-tuple-element.112) | copy-start | bytes 1572868
  474.5 55.9 %copy-start.4 = (f32[1152,128]{1,0:T(8,128)S(1)}, f32[1152,128]{1,0:T(8,128)}, u32[]{:S(2)}) copy-start(f32[1152,128]{1,0:T(8,128)} %get-tuple-element.145) | copy-start | bytes 1769476
  530.4 2.3 copy-start.3
  530.4 2.3 copy-start.5
  532.8 1.1 copy-start.1
  532.8 1.2 copy-start.2
  534.8 2.5 copy-start.14
  534.8 3.3 copy-start.7
  537.3 1.9 copy-start.10
  538.1 3.4 copy-start.11
  539.2 3.7 copy-start.9
  539.2 4.5 copy-start.13
  539.3 5.0 copy-start.12

commit v8 on v7

--- a/solution.py
+++ b/solution.py
@@ -1520,8 +1520,8 @@
 
 
 def attention_forward_kernel(
-    head, docs, lengths, h_ref, gain_ref, qgain_ref, kgain_ref, cos_ref, sin_ref, wq_hbm, wkv_hbm, wo_hbm,
-    out_ref, n_hbm, raw_hbm, ready_hbm, o_hbm,
+    head, docs, lengths, h_ref, gain_ref, qgain_ref, kgain_ref, speed_ref, wq_hbm, wkv_hbm, wo_hbm,
+    out_ref, n_hbm, raw_hbm, ready_hbm, o_hbm, cos_ref, sin_ref,
     w, wo, nf, low, ready, vt, o, tpart, mine, n_near, n_over, n_on, o_near, i_near, o_over, i_over,
     s_near, s_over, wsem, osem, bg,
 ):
@@ -1538,6 +1538,12 @@
     g.meet()
     gather.start()
     bg.step(0)
+    places = lax.broadcasted_iota(jnp.int32, (total, LANES), 0)
+    angles = (places - doc_starts(docs, lengths, places)).astype(F32) * speed_ref[...]
+    lane = lax.broadcasted_iota(jnp.int32, (total, LANES), 1)
+    sine = jnp.sin(angles)
+    cos_ref[...] = jnp.cos(angles)
+    sin_ref[...] = jnp.where(lane % head < head // 2, -sine, sine)
     wait_all(loads)
 
     def project(block):
@@ -1600,19 +1606,19 @@
     bg.finish()
 
 
-def attention_forward(head, docs, lengths, h, gain, qgain, kgain, cosine, sine, wq, wkv, wo, ident, tasks=(), parts=PARTS):
+def attention_forward(head, docs, lengths, h, gain, qgain, kgain, speed, wq, wkv, wo, ident, tasks=(), parts=PARTS):
     size, width = h.shape
     total, qw = 4 * size, wo.shape[0]
     kw = wkv.shape[1] // 2
     every = qw + 2 * kw
     return hosted(
         functools.partial(attention_forward_kernel, head, docs), ident, "attention_forward",
-        [lengths, h, gain, qgain, kgain, cosine, sine, wq, wkv, wo], [INV] * 7 + [HBM] * 3,
+        [lengths, h, gain, qgain, kgain, speed, wq, wkv, wo], [INV] * 6 + [HBM] * 3,
         [
             shaped((size, width), F32), shaped((total, width), BF), shaped((total, every), BF), shaped((total, every), BF),
-            shaped((total, qw), BF),
+            shaped((total, qw), BF), shaped((total, LANES), F32), shaped((total, LANES), F32),
         ],
-        [INV] + [HBM] * 4,
+        [INV] + [HBM] * 4 + [INV] * 2,
         [
             pltpu.VMEM((width, every), BF), pltpu.VMEM((qw, width), BF), pltpu.VMEM((total, width), BF),
             pltpu.VMEM((total, every), BF), pltpu.VMEM((total, every), BF),
@@ -1773,25 +1779,10 @@
 DP = ("r", "s", "zh")
 
 
-def doc_positions(lengths_row, length):
-    count = lengths_row.shape[0]
-    upto = jnp.arange(count)[:, None] >= jnp.arange(count)[None, :]
-    doc_ends = jnp.sum(jnp.where(upto, lengths_row[None, :], 0), axis=1)
-    places = jnp.arange(length, dtype=jnp.int32)
-    passed = places[:, None] >= doc_ends[None, :]
-    return places - jnp.max(jnp.where(passed, doc_ends[None, :], 0), axis=1)
-
-
-def rope_tables(position, head_dim):
+def rope_speeds(head_dim):
     half_dim = head_dim // 2
     inverse = rope_base ** (-2.0 * jnp.arange(half_dim, dtype=F32) / head_dim)
-    angles = position.astype(F32)[:, None] * inverse[None, :]
-    cosine, sine = jnp.cos(angles), jnp.sin(angles)
-    copies = LANES // head_dim
-    return (
-        jnp.concatenate([cosine, cosine] * copies, axis=1),
-        jnp.concatenate([-sine, sine] * copies, axis=1),
-    )
+    return jnp.tile(inverse, LANES // half_dim)[None]
 
 
 def swap(x):
@@ -1826,10 +1817,10 @@
     taps = jnp.pad(conv_kernel, ((0, 8 - count), (0, 0)))
     rows_of = lambda got: got.reshape(-1, got.shape[-1])
     if planes:
-        first = [Take(conv_in, (0, 1, 1, 2, 2), True), Take(conv_out, (0, 1, 1, 2, 2), True)]
-        first += [Fetch(own_w[0], (0, 1, 1, 2, 4, 5, 3, 3, 3), 4), Fetch(own_v[0], (0, 1, 1, 2, 3, 3, 3), 2)]
-        first += [Take(x, (0, 3, 3, 3, 3)) for x in (query_w, kv_w, out_w)]
-        second = [Fetch(own_w[1], (0, 0, 0, 2), 1, 1), Fetch(own_v[1], (0, 0, 0, 2), 1, 1)]
+        first = [Take(conv_in, (0, 0, 0, 2, 2), True), Take(conv_out, (0, 0, 0, 2, 2), True)]
+        first += [Fetch(own_w[0], (0, 1, 1, 2, 2, 2, 4, 5, 3), 4), Fetch(own_v[0], (0, 1, 1, 2, 4, 5, 3), 2)]
+        second = [Take(x, (0, 0, 0, 2, 2)) for x in (query_w, kv_w, out_w)]
+        second += [Fetch(own_w[1], (0, 0, 0, 2), 1, 1), Fetch(own_v[1], (0, 0, 0, 2), 1, 1)]
     else:
         first, second, third = [], [], []
         conv_in, conv_out, query_w, kv_w, out_w = map(swap, (conv_in, conv_out, query_w, kv_w, out_w))
@@ -1841,13 +1832,12 @@
     )
     if planes:
         w0, v0 = rows_of(got[0]), got[1]
-        query_w, kv_w, out_w = got[2:]
     (h2, n1, hidden0), got = ffn_forward(h1, gain[1], w0, v0, 1, second)
     if planes:
-        third = [Fetch(got[0], (0, 4), 2, 2), Fetch(got[1], (0, 4), 1, 2)]
-    cosine, sine = rope_tables(doc_positions(lens[0, :docs].astype(jnp.int32), length), head_dim)
-    (h3, n2, raw, ready, attended), got = attention_forward(
-        head_dim, docs, lens, h2, gain[2], qgain, kgain, cosine, sine, query_w, kv_w, out_w, 2, third
+        query_w, kv_w, out_w = got[:3]
+        third = [Fetch(got[3], (0, 4), 2, 2), Fetch(got[4], (0, 4), 1, 2)]
+    (h3, n2, raw, ready, attended, cosine, sine), got = attention_forward(
+        head_dim, docs, lens, h2, gain[2], qgain, kgain, rope_speeds(head_dim), query_w, kv_w, out_w, 2, third
     )
     if planes:
         w1, v1 = rows_of(got[0]), got[1]
@@ -1872,12 +1862,12 @@
     )
     (dh1, gain1, gw0, gv0), got = ffn_backward(
         dh2, h1, gain[1], None, w0, v0, n1, hidden0, 6,
-        settled(sums, (0, 2)) + whole(gv1, (0, 1, 2)) + whole(gqkv, (0, 2, 3)) + whole(gow, (0, 2, 3)),
+        settled(sums, (0, 0)) + whole(gv1, (0, 1, 2)) + whole(gqkv, (0, 2, 3)) + whole(gow, (0, 2, 3)),
     )
     sums_w1, sums = got[:2], got[2:]
     (dh0, gain0, gtaps, gci, gco), got = conv_backward(
         docs, count, lens, dh1, x_block.astype(F32), gain[0], taps, conv_in, conv_out, n0, projected, pieces, 7,
-        settled(sums, (0, 3)) + halves(gw0, (0, 1, 4), (0, 3, 6), True),
+        settled(sums, (0, 0)) + halves(gw0, (0, 1, 4), (0, 3, 6), True),
     )
     others, first_w0, sums = got[:3], got[3:4], got[4:]
     totals, grads, *got = tail(

time: 550 us -> 530 us (0.964)
  Pallas kernels: 511 us -> 491 us
    pallas_call x9, Pallas kernels: 511 us -> 491 us  [hosted(): pl.pallas_call(body, out_shape=tuple(outs), in_specs=in_specs, out_specs=...]
where the time goes in v8:
time: 530 us; the launch traced here: 521 us
  Pallas kernels  491 us (93%)
  local copies, waits for them, and re-layouts  21.4 us (4%)
  other arithmetic  7.66 us (1%)
    pallas_call x9, Pallas kernels, hosted(): pl.pallas_call(body, out_shape=tuple(outs), in_specs=in_specs, out_specs=...  491 us

profile of v8, /device:TPU:1, one launch (start us, length us, event | category | flops | bytes accessed | tf_op | source)
XLA Modules:
  0.0 521.0 jit_solution(17397735102586578606)
XLA Ops:
  0.6 1.5 fusion.2
  2.1 2.1 fusion
  4.2 0.9 copy.34
  5.1 0.0 copy-done
  5.1 0.8 slice_bitcast_fusion
  6.0 1.7 copy.29
  7.7 0.0 copy-start.15
  7.7 0.0 copy-start.17
  7.7 1.6 copy.30.refs_4_.refs_6_
  9.3 0.0 copy-done.15
  9.3 0.6 pad.9.refs_3_
  9.9 0.0 copy-done.17
  9.9 0.6 pad.8.refs_0_
  10.5 94.2 %conv_forward.1 = (f32[256,1024]{1,0:T(8,128)}, bf16[256,1024]{1,0:T(8,128)(2,1)}, bf16[1024,1024]{1,0:T(8,128)(2,1)}, bf16[1024,768]{1,0:T(8,128)(2,1)}, f32[8,...) custom-call(f32[8,128]{1,0:T(8,128)} %pad.8.refs_0_, ...), custom_call_target="tpu_custom_call" | custom-call | flops 2147483648 | bytes 16777216 | tf_op jit(solution)/shard_map/conv_forward/pallas_call | solution.py:838
  104.7 0.9 copy.36
  105.6 0.0 copy-done.8
  105.6 0.9 copy.38
  106.4 56.9 %ffn_forward.2 = (f32[256,1024]{1,0:T(8,128)}, bf16[1024,1024]{1,0:T(8,128)(2,1)}, bf16[1024,2304]{1,0:T(8,128)(2,1)}, bf16[1024,256]{1,0:T(8,128)(2,1)}, bf16[1...) custom-call(f32[256,1024]{1,0:T(8,128)} %get-tuple-element.82.refs_0, ...), custom_call_target="tpu_custom_call" | custom-call | flops 7247757312 | bytes 16777216 | tf_op jit(solution)/shard_map/ffn_forward/pallas_call | solution.py:838
  163.3 0.0 copy-done.16
  163.4 0.6 tile.30.refs_3_.refs_4_
  164.0 0.6 tile.33.refs_4_.refs_5_
  164.6 0.6 broadcast_in_dim_tile.3.refs_5_
  165.2 44.6 %attention_forward.1 = (f32[256,1024]{1,0:T(8,128)}, bf16[1024,1024]{1,0:T(8,128)(2,1)}, bf16[1024,512]{1,0:T(8,128)(2,1)}, bf16[1024,512]{1,0:T(8,128)(2,1)}, b...) custom-call(f32[8,128]{1,0:T(8,128)} %get-tuple-element.81.refs_0_, ...), custom_call_target="tpu_custom_call", output_to_operand_aliasing={{7}: (9, {}), {8}: (10, {})} | custom-call | flops 1610612736 | bytes 16777216 | tf_op jit(solution)/shard_map/attention_forward/pallas_call | solution.py:838
  209.8 46.8 %ffn_forward.3 = (f32[256,1024]{1,0:T(8,128)}, bf16[1024,1024]{1,0:T(8,128)(2,1)}, bf16[1024,2304]{1,0:T(8,128)(2,1)}, bf16[1024,1024]{1,0:T(8,128)(2,1)}) custom-call(f32[256,1024]{1,0:T(8,128)} %get-tuple-element.91.refs_0_.refs_1_, f32[1,1024]{1,0:T(1,128)} %get-tuple-element.182.refs_1_.refs_0_.refs_2_, bf16[1024,2304]{1,0:T(8,128)(2,1)} %bitcast.27, ...), custom_call_target="tpu_custom_call" | custom-call | flops 7247757312 | bytes 16777216 | tf_op jit(solution)/shard_map/ffn_forward/pallas_call | solution.py:838
  256.6 34.3 %ffn_backward.2 = (f32[256,1024]{1,0:T(8,128)}, f32[1,1024]{1,0:T(1,128)}, bf16[8,128,2304]{2,1,0:T(8,128)(2,1)}, bf16[8,1152,128]{2,1,0:T(8,128)(2,1)}, bf16[1024,256]{1,0:T(8,128)(2,1)}) custom-call(f32[1,1024]{1,0:T(1,128)} %get-tuple-element.182.refs_1_.refs_0_.refs_2_, f32[256,1024]{1,0:T(8,128)} %get-tuple-element.91.refs_0_.refs_1_, ...), custom_call_target="tpu_custom_call" | custom-call | flops 14495514624 | bytes 33554432 | tf_op jit(solution)/shard_map/ffn_backward/pallas_call | solution.py:838
  290.8 50.0 %attention_backward.1 = (f32[256,1024]{1,0:T(8,128)}, f32[1,1024]{1,0:T(1,128)}, f32[1,256]{1,0:T(1,128)}, f32[1,128]{1,0:T(1,128)}, bf16[8,128,512]{2,1,0:T(8,1...) custom-call(f32[8,128]{1,0:T(8,128)} %get-tuple-element.81.refs_0_, ...), custom_call_target="tpu_custom_call" | custom-call | flops 3221225472 | bytes 33554432 | tf_op jit(solution)/shard_map/attention_backward/pallas_call | solution.py:838
  340.9 0.0 copy-start.6
  340.9 49.5 %ffn_backward.3 = (f32[256,1024]{1,0:T(8,128)}, f32[1,1024]{1,0:T(1,128)}, bf16[8,128,2304]{2,1,0:T(8,128)(2,1)}, bf16[8,1152,128]{2,1,0:T(8,128)(2,1)}, f32[64,...) custom-call(f32[256,1024]{1,0:T(8,128)} %get-tuple-element.107.refs_, ...), custom_call_target="tpu_custom_call" | custom-call | flops 14495514624 | bytes 33554432 | tf_op jit(solution)/shard_map/ffn_backward/pallas_call | solution.py:838
  390.4 0.0 copy-done.6
  390.4 1.1 convert_element_type.14.refs_2_
  391.5 58.2 %conv_backward.1 = (f32[256,1024]{1,0:T(8,128)}, f32[1,1024]{1,0:T(1,128)}, f32[8,256]{1,0:T(8,128)}, bf16[8,128,768]{2,1,0:T(8,128)(2,1)}, bf16[8,256,128]{2,1,...) custom-call(f32[8,128]{1,0:T(8,128)} %get-tuple-element.81.refs_0_, ...), custom_call_target="tpu_custom_call" | custom-call | flops 4294967296 | bytes 16777216 | tf_op jit(solution)/shard_map/conv_backward/pallas_call | solution.py:838
  449.8 0.0 copy-start.4
  449.8 56.4 %tail.1 = (f32[8,1024]{1,0:T(8,128)}, bf16[1024,256]{1,0:T(8,128)(2,1)}, f32[64,2304]{1,0:T(8,128)}, f32[1152,128]{1,0:T(8,128)}, f32[128,768]{1,0:T(8,128)}, /*index=5*/f32[256,128]{1,0:T(8,128)}) custom-call(f32[1,1024]{1,0:T(1,128)} %get-tuple-element.126.refs_0_, f32[1,1024]{1,0:T(1,128)} %get-tuple-element.127.refs_1_, ...), custom_call_target="tpu_custom_call" | custom-call | bytes 4194304 | tf_op jit(solution)/shard_map/tail/pallas_call | solution.py:838
  506.2 0.0 copy-start.3
  506.2 0.0 copy-start.5
  506.2 0.0 copy-done.4
  506.2 2.2 pad_maximum_fusion.3
  508.5 0.0 copy-done.3
  508.5 0.1 pad_maximum_fusion.1
  508.6 0.0 copy-start.1
  508.6 0.0 copy-start.2
  508.6 0.7 stack.30
  509.3 0.4 copy-done.1
  509.6 0.2 copy-done.2
  509.8 0.1 pad_maximum_fusion.2
  509.9 0.7 stack.31
  510.6 2.5 pad_maximum_fusion
  513.1 0.0 copy-done.14
  513.1 0.1 slice.69
  513.2 0.1 slice.71
  513.3 0.6 pad_maximum_fusion.4
  513.9 0.0 copy-done.7
  513.9 1.0 convert_element_type.15
  515.0 0.2 copy.32
  515.1 0.0 copy-start.12
  515.1 0.9 copy.33
  516.1 0.6 slice.67
  516.7 0.6 slice.72
  517.3 0.0 copy-done.11
  517.3 0.7 fusion.1
  517.9 0.7 reshape.71
  518.7 0.8 copy.44
  519.5 0.7 copy.45
  520.1 0.7 copy.46
  (24 shorter events, 0.1 us)
Async XLA Ops:
  2.1 3.0 copy-start
  7.7 1.6 copy-start.15
  7.7 2.2 copy-start.17
  10.5 95.1 %copy-start.8 = (bf16[1024,2,128]{2,1,0:T(2,128)(2,1)S(1)}, bf16[1024,2,128]{2,1,0:T(2,128)(2,1)}, u32[]{:S(2)}) copy-start(bf16[1024,2,128]{2,1,0:T(2,128)(2,1)} %param.22) | copy-start | bytes 1572868
  106.4 56.9 %copy-start.16 = (f32[2,64]{1,0:T(2,128)S(1)}, f32[2,64]{1,0:T(2,128)}, u32[]{:S(2)}) copy-start(f32[2,64]{1,0:T(2,128)} %param.17) | copy-start | bytes 1540
  340.9 49.5 %copy-start.6 = (bf16[256,1024]{1,0:T(8,128)(2,1)S(1)}, bf16[256,1024]{1,0:T(8,128)(2,1)}, u32[]{:S(2)}) copy-start(bf16[256,1024]{1,0:T(8,128)(2,1)} %get-tuple-element.116) | copy-start | bytes 1572868
  449.8 56.5 %copy-start.4 = (f32[1152,128]{1,0:T(8,128)S(1)}, f32[1152,128]{1,0:T(8,128)}, u32[]{:S(2)}) copy-start(f32[1152,128]{1,0:T(8,128)} %get-tuple-element.149) | copy-start | bytes 1769476
  506.2 2.3 copy-start.3
  506.2 2.3 copy-start.5
  508.6 1.1 copy-start.1
  508.6 1.2 copy-start.2
  510.6 2.5 copy-start.14
  510.6 3.3 copy-start.7
  513.1 1.9 copy-start.10
  513.9 3.4 copy-start.11
  515.0 3.7 copy-start.9
  515.0 4.5 copy-start.13
  515.1 5.0 copy-start.12

commit v9 on v8

--- a/solution.py
+++ b/solution.py
@@ -198,8 +198,9 @@
 
 
 class Fetch:
-    def __init__(self, shard, at, cuts=1, stage=0):
+    def __init__(self, shard, at, cuts=1, stage=0, layer=None):
         rows, cols = shard.shape[-2:]
+        self.layer = layer
         self.at, self.cuts, self.stage, self.step_rows = at, cuts, stage, rows // cuts
         self.ins = [shard]
         self.outs = [jax.ShapeDtypeStruct((8, rows, cols), shard.dtype)]
@@ -214,6 +215,8 @@
 
     def bind(self, ins, outs, scratch):
         (self.own,), (self.out,) = ins, outs
+        if self.layer is not None:
+            self.own = self.own.at[self.layer]
         self.sent, self.come, self.sem = scratch[:3]
         self.bounce = scratch[3] if len(scratch) > 3 else None
         self.p = Place()
@@ -1189,7 +1192,7 @@
     return found[0] if len(found) == 1 else jnp.concatenate(found, axis=0)
 
 
-def product(src, weight, turned, tile=512):
+def product(src, weight, turned, tile=1024):
     def run(places, store):
         width = weight.shape[0] if turned else weight.shape[1]
 
@@ -1806,8 +1809,7 @@
     docs, count = doc_lengths.shape[1], conv_kernel.shape[0]
     conv_in = conv_in.reshape(conv_in.shape[0], -1)
     kv_w = kv_w.reshape(kv_w.shape[0], -1)
-    own_w = [gate_up[l].reshape(gate_up.shape[1], -1) for l in (0, 1)]
-    own_v = [down[l] for l in (0, 1)]
+    own_w = gate_up.reshape(*gate_up.shape[:2], -1)
     pieces = 8 if planes else 1
     kv_width = kv_w.shape[1] // 2
     qgain = jnp.tile(head_gains[0:1], (1, query_w.shape[1] // head_dim))
@@ -1818,14 +1820,14 @@
     rows_of = lambda got: got.reshape(-1, got.shape[-1])
     if planes:
         first = [Take(conv_in, (0, 0, 0, 2, 2), True), Take(conv_out, (0, 0, 0, 2, 2), True)]
-        first += [Fetch(own_w[0], (0, 1, 1, 2, 2, 2, 4, 5, 3), 4), Fetch(own_v[0], (0, 1, 1, 2, 4, 5, 3), 2)]
+        first += [Fetch(own_w, (0, 1, 1, 2, 2, 2, 4, 5, 3), 4, 0, 0), Fetch(down, (0, 1, 1, 2, 4, 5, 3), 2, 0, 0)]
         second = [Take(x, (0, 0, 0, 2, 2)) for x in (query_w, kv_w, out_w)]
-        second += [Fetch(own_w[1], (0, 0, 0, 2), 1, 1), Fetch(own_v[1], (0, 0, 0, 2), 1, 1)]
+        second += [Fetch(own_w, (0, 0, 0, 2), 1, 1, 1), Fetch(down, (0, 0, 0, 2), 1, 1, 1)]
     else:
         first, second, third = [], [], []
         conv_in, conv_out, query_w, kv_w, out_w = map(swap, (conv_in, conv_out, query_w, kv_w, out_w))
         w0, w1 = (gather_dp(w, 0) for w in own_w)
-        v0, v1 = (gather_dp(v, 1)[None] for v in own_v)
+        v0, v1 = (gather_dp(v, 1)[None] for v in down)
 
     (h1, x_block, n0, projected, lens, taps, conv_in, conv_out), got = conv_forward(
         docs, count, lens, tokens, gain[0], taps, conv_in, conv_out, planes, 0, first
@@ -1876,14 +1878,14 @@
         + settled(sums, (0, 0)) + whole(gv0, (0, 0, 1), True) + whole(gci, (1, 2, 3), True) + whole(gco, (1, 2, 3), True),
     )
     if planes:
-        gw1 = jnp.concatenate(sums_w1, axis=0)
         gv1, gqkv, gow = others
-        gw0 = jnp.concatenate([first_w0[0], got[0]], axis=0)
+        gate_ups = [*first_w0, got[0], *sums_w1]
         gv0, gci, gco = got[1:]
     else:
         totals = lax.psum(totals, "r")
         gw0, gw1, gci, gqkv = (scatter_dp(g[0], 0) for g in (gw0, gw1, gci, gqkv))
         gv0, gv1, gco, gow = (scatter_dp(g[0], 1) for g in (gv0, gv1, gco, gow))
+        gate_ups = [gw0, gw1]
     heads = totals[7, : gq.shape[1] + gk.shape[1]].reshape(-1, head_dim)
     split = gq.shape[1] // head_dim
     return (
@@ -1897,7 +1899,7 @@
         gqkv[:, : query_w.shape[1]],
         gqkv[:, query_w.shape[1] :].reshape(-1, 2, kv_width),
         gow,
-        jnp.stack([gw0, gw1]).reshape(2, gate_up.shape[1], 2, -1),
+        jnp.concatenate(gate_ups, axis=0).reshape(2, gate_up.shape[1], 2, -1),
         jnp.stack([gv0, gv1]),
     )
 

time: 530 us -> 523 us (0.987)
    reshape x0 -> x2, local copies, waits for them, and re-layouts: none -> 6.19 us  [the longest x1 3.8 us: local(): own_w = gate_up.reshape(*gate_up.shape[:2], -1)]
where the time goes in v9:
time: 523 us; the launch traced here: 517 us
  Pallas kernels  490 us (94%)
  local copies, waits for them, and re-layouts  20.1 us (4%)
    pallas_call x9, Pallas kernels, hosted(): pl.pallas_call(body, out_shape=tuple(outs), in_specs=in_specs, out_specs=...  490 us

profile of v9, /device:TPU:1, one launch (start us, length us, event | category | flops | bytes accessed | tf_op | source)
XLA Modules:
  0.0 516.6 jit_solution(12787458450000594873)
XLA Ops:
  0.6 0.0 copy-start
  0.7 1.5 fusion.1
  2.2 3.8 reshape.68.refs_8_.refs_7_
  6.0 0.0 copy-done
  6.0 0.9 copy.29
  6.8 0.0 copy-start.15
  6.8 0.0 copy-start.17
  6.8 1.6 copy.30.refs_4_.refs_6_
  8.4 0.0 copy-done.15
  8.4 0.6 pad.9.refs_3_
  9.0 0.0 copy-done.17
  9.0 0.6 pad.8.refs_0_
  9.6 94.2 %conv_forward.1 = (f32[256,1024]{1,0:T(8,128)}, bf16[256,1024]{1,0:T(8,128)(2,1)}, bf16[1024,1024]{1,0:T(8,128)(2,1)}, bf16[1024,768]{1,0:T(8,128)(2,1)}, f32[8,...) custom-call(f32[8,128]{1,0:T(8,128)} %pad.8.refs_0_, ...), custom_call_target="tpu_custom_call" | custom-call | flops 2147483648 | bytes 16777216 | tf_op jit(solution)/shard_map/conv_forward/pallas_call | solution.py:841
  103.9 0.0 copy-done.8
  103.9 0.9 copy.36
  104.7 57.5 %ffn_forward.2 = (f32[256,1024]{1,0:T(8,128)}, bf16[1024,1024]{1,0:T(8,128)(2,1)}, bf16[1024,2304]{1,0:T(8,128)(2,1)}, bf16[1024,256]{1,0:T(8,128)(2,1)}, bf16[1...) custom-call(f32[256,1024]{1,0:T(8,128)} %get-tuple-element.82.refs_0, ...), custom_call_target="tpu_custom_call" | custom-call | flops 7247757312 | bytes 16777216 | tf_op jit(solution)/shard_map/ffn_forward/pallas_call | solution.py:841
  162.3 0.0 copy-done.16
  162.3 0.6 tile.30.refs_3_.refs_4_
  162.9 0.6 tile.33.refs_4_.refs_5_
  163.5 0.6 broadcast_in_dim_tile.3.refs_5_
  164.1 43.3 %attention_forward.1 = (f32[256,1024]{1,0:T(8,128)}, bf16[1024,1024]{1,0:T(8,128)(2,1)}, bf16[1024,512]{1,0:T(8,128)(2,1)}, bf16[1024,512]{1,0:T(8,128)(2,1)}, b...) custom-call(f32[8,128]{1,0:T(8,128)} %get-tuple-element.81.refs_0_, ...), custom_call_target="tpu_custom_call", output_to_operand_aliasing={{7}: (9, {}), {8}: (10, {})} | custom-call | flops 1610612736 | bytes 16777216 | tf_op jit(solution)/shard_map/attention_forward/pallas_call | solution.py:841
  207.4 46.9 %ffn_forward.3 = (f32[256,1024]{1,0:T(8,128)}, bf16[1024,1024]{1,0:T(8,128)(2,1)}, bf16[1024,2304]{1,0:T(8,128)(2,1)}, bf16[1024,1024]{1,0:T(8,128)(2,1)}) custom-call(f32[256,1024]{1,0:T(8,128)} %get-tuple-element.91.refs_0_.refs_1_, f32[1,1024]{1,0:T(1,128)} %get-tuple-element.178.refs_1_.refs_0_.refs_2_, bf16[1024,2304]{1,0:T(8,128)(2,1)} %bitcast.17, ...), custom_call_target="tpu_custom_call" | custom-call | flops 7247757312 | bytes 16777216 | tf_op jit(solution)/shard_map/ffn_forward/pallas_call | solution.py:841
  254.3 34.7 %ffn_backward.2 = (f32[256,1024]{1,0:T(8,128)}, f32[1,1024]{1,0:T(1,128)}, bf16[8,128,2304]{2,1,0:T(8,128)(2,1)}, bf16[8,1152,128]{2,1,0:T(8,128)(2,1)}, bf16[1024,256]{1,0:T(8,128)(2,1)}) custom-call(f32[1,1024]{1,0:T(1,128)} %get-tuple-element.178.refs_1_.refs_0_.refs_2_, f32[256,1024]{1,0:T(8,128)} %get-tuple-element.91.refs_0_.refs_1_, ...), custom_call_target="tpu_custom_call" | custom-call | flops 14495514624 | bytes 33554432 | tf_op jit(solution)/shard_map/ffn_backward/pallas_call | solution.py:841
  289.0 50.0 %attention_backward.1 = (f32[256,1024]{1,0:T(8,128)}, f32[1,1024]{1,0:T(1,128)}, f32[1,256]{1,0:T(1,128)}, f32[1,128]{1,0:T(1,128)}, bf16[8,128,512]{2,1,0:T(8,1...) custom-call(f32[8,128]{1,0:T(8,128)} %get-tuple-element.81.refs_0_, ...), custom_call_target="tpu_custom_call" | custom-call | flops 3221225472 | bytes 33554432 | tf_op jit(solution)/shard_map/attention_backward/pallas_call | solution.py:841
  339.0 0.0 copy-start.6
  339.0 49.5 %ffn_backward.3 = (f32[256,1024]{1,0:T(8,128)}, f32[1,1024]{1,0:T(1,128)}, bf16[8,128,2304]{2,1,0:T(8,128)(2,1)}, bf16[8,1152,128]{2,1,0:T(8,128)(2,1)}, f32[64,...) custom-call(f32[256,1024]{1,0:T(8,128)} %get-tuple-element.107.refs_, ...), custom_call_target="tpu_custom_call" | custom-call | flops 14495514624 | bytes 33554432 | tf_op jit(solution)/shard_map/ffn_backward/pallas_call | solution.py:841
  388.5 0.0 copy-done.6
  388.5 1.1 convert_element_type.14.refs_2_
  389.6 57.9 %conv_backward.1 = (f32[256,1024]{1,0:T(8,128)}, f32[1,1024]{1,0:T(1,128)}, f32[8,256]{1,0:T(8,128)}, bf16[8,128,768]{2,1,0:T(8,128)(2,1)}, bf16[8,256,128]{2,1,...) custom-call(f32[8,128]{1,0:T(8,128)} %get-tuple-element.81.refs_0_, ...), custom_call_target="tpu_custom_call" | custom-call | flops 4294967296 | bytes 16777216 | tf_op jit(solution)/shard_map/conv_backward/pallas_call | solution.py:841
  447.5 0.0 copy-start.5
  447.5 56.3 %tail.1 = (f32[8,1024]{1,0:T(8,128)}, bf16[1024,256]{1,0:T(8,128)(2,1)}, f32[64,2304]{1,0:T(8,128)}, f32[1152,128]{1,0:T(8,128)}, f32[128,768]{1,0:T(8,128)}, /*index=5*/f32[256,128]{1,0:T(8,128)}) custom-call(f32[1,1024]{1,0:T(1,128)} %get-tuple-element.126.refs_0_, f32[1,1024]{1,0:T(1,128)} %get-tuple-element.127.refs_1_, ...), custom_call_target="tpu_custom_call" | custom-call | bytes 4194304 | tf_op jit(solution)/shard_map/tail/pallas_call | solution.py:841
  503.8 0.0 copy-start.1
  503.8 0.0 copy-start.2
  503.8 0.0 copy-start.3
  503.8 0.0 copy-start.4
  503.8 0.0 copy-done.5
  503.8 2.3 pad_maximum_fusion.1
  506.2 0.0 copy-done.1
  506.2 0.0 copy-done.2
  506.2 0.0 copy-done.3
  506.2 0.0 copy-done.4
  506.2 0.2 pad_maximum_fusion
  506.3 0.0 copy-start.14
  506.3 0.0 copy-start.7
  506.4 0.0 copy-start.10
  506.4 2.4 reshape.74
  508.8 0.0 copy-done.14
  508.8 0.1 slice.53
  508.9 0.1 slice.55
  509.0 0.6 pad_maximum_fusion.2
  509.6 0.0 copy-done.7
  509.6 1.0 convert_element_type.15
  510.6 0.0 copy-done.10
  510.6 0.2 copy.32
  510.8 0.9 copy.33
  511.7 0.6 slice.51
  512.3 0.6 slice.56
  513.0 0.0 copy-done.11
  513.0 0.7 fusion
  513.6 0.7 reshape.73
  514.3 0.0 copy-done.9
  514.3 0.8 copy.42
  515.1 0.7 copy.43
  515.8 0.7 copy.44
  (18 shorter events, 0.1 us)
Async XLA Ops:
  0.6 5.3 %copy-start = (bf16[1024,3,256]{2,0,1:T(8,128)(2,1)S(1)}, bf16[1024,3,256]{2,0,1:T(8,128)(2,1)}, u32[]{:S(2)}) copy-start(bf16[1024,3,256]{2,0,1:T(8,128)(2,1)} %param.18) | copy-start | bytes 4718596
  6.8 1.6 copy-start.15
  6.8 2.2 copy-start.17
  9.6 94.2 %copy-start.8 = (bf16[1024,2,128]{2,1,0:T(2,128)(2,1)S(1)}, bf16[1024,2,128]{2,1,0:T(2,128)(2,1)}, u32[]{:S(2)}) copy-start(bf16[1024,2,128]{2,1,0:T(2,128)(2,1)} %param.22) | copy-start | bytes 1572868
  104.7 57.5 %copy-start.16 = (f32[2,64]{1,0:T(2,128)S(1)}, f32[2,64]{1,0:T(2,128)}, u32[]{:S(2)}) copy-start(f32[2,64]{1,0:T(2,128)} %param.17) | copy-start | bytes 1540
  339.0 49.5 %copy-start.6 = (bf16[256,1024]{1,0:T(8,128)(2,1)S(1)}, bf16[256,1024]{1,0:T(8,128)(2,1)}, u32[]{:S(2)}) copy-start(bf16[256,1024]{1,0:T(8,128)(2,1)} %get-tuple-element.116) | copy-start | bytes 1572868
  447.5 56.3 %copy-start.5 = (f32[1152,128]{1,0:T(8,128)S(1)}, f32[1152,128]{1,0:T(8,128)}, u32[]{:S(2)}) copy-start(f32[1152,128]{1,0:T(8,128)} %get-tuple-element.149) | copy-start | bytes 1769476
  503.8 2.4 copy-start.1
  503.8 2.4 copy-start.2
  503.8 2.3 copy-start.3
  503.8 2.3 copy-start.4
  506.3 2.4 copy-start.14
  506.3 3.2 copy-start.7
  506.4 4.3 copy-start.10
  508.8 4.2 copy-start.11
  508.8 5.6 %copy-start.9 = (bf16[1024,256]{1,0:T(8,128)(2,1)S(1)}, bf16[1024,256]{1,0:T(8,128)(2,1)}, u32[]{:S(2)}) copy-start(bf16[1024,256]{1,0:T(8,128)(2,1)} %get-tuple-element.194) | copy-start | bytes 1572868
  509.6 5.5 %copy-start.13 = (f32[256,128]{1,0:T(8,128)S(1)}, f32[256,128]{1,0:T(8,128)}, u32[]{:S(2)}) copy-start(f32[256,128]{1,0:T(8,128)} %get-tuple-element.200) | copy-start | bytes 393220
  509.6 6.2 %copy-start.12 = (f32[256,128]{1,0:T(8,128)S(1)}, f32[256,128]{1,0:T(8,128)}, u32[]{:S(2)}) copy-start(f32[256,128]{1,0:T(8,128)} %get-tuple-element.203) | copy-start | bytes 393220

commit v10 on v9

--- a/solution.py
+++ b/solution.py
@@ -472,7 +472,7 @@
         self.ins = [block]
         self.outs = [jax.ShapeDtypeStruct((rows, 4 * cols), block.dtype)]
         self.out_specs = [HBM]
-        self.scratch = [*gather_scratch(parts), DMA((2, 1)), DMA((1,))]
+        self.scratch = [*gather_scratch(parts), DMA((2, parts)), DMA((parts,))]
 
     def bind(self, ins, outs, scratch):
         (self.block,), (self.full,) = ins, outs
@@ -480,18 +480,24 @@
         self.p, self.g = Place(), Group(calls=False)
         self.gather = Columns(self.g, self.full, near, over, onward)
         cols = self.block.shape[1]
-        mine, there = (self.full.at[:, lanes(b * cols, cols)] for b in (self.g.mine, self.g.beside))
-        self.exchange = Exchange(self.block, mine, there, sems, sem)
+        self.exchanges = []
+        for p in range(self.parts):
+            rows = pl.ds(p * self.gather.step, self.gather.step)
+            mine, there = (self.full.at[rows, lanes(b * cols, cols)] for b in (self.g.mine, self.g.beside))
+            self.exchanges.append(Exchange(self.block.at[rows], mine, there, sems, sem, p))
 
     def greets(self):
         return Place.ENDS
 
     def step(self, k):
         if k == 0:
-            self.exchange.start()
+            for exchange in self.exchanges:
+                exchange.start()
         elif k == 1:
-            self.exchange.arrive()
-            self.gather.start()
+            for p, exchange in enumerate(self.exchanges):
+                exchange.arrive()
+                self.gather.link(p, self.g.mine).start()
+                self.gather.close(p, self.g.mine).start()
         elif k == 2:
             for p in range(self.parts):
                 self.gather.wait_part(p)
@@ -500,7 +506,8 @@
             for p in range(self.parts):
                 self.gather.wait_far(p)
             self.gather.finish()
-            self.exchange.finish()
+            for exchange in self.exchanges:
+                exchange.finish()
 
 
 class Deliver:
@@ -1820,7 +1827,7 @@
     rows_of = lambda got: got.reshape(-1, got.shape[-1])
     if planes:
         first = [Take(conv_in, (0, 0, 0, 2, 2), True), Take(conv_out, (0, 0, 0, 2, 2), True)]
-        first += [Fetch(own_w, (0, 1, 1, 2, 2, 2, 4, 5, 3), 4, 0, 0), Fetch(down, (0, 1, 1, 2, 4, 5, 3), 2, 0, 0)]
+        first += [Fetch(own_w, (0, 1, 1, 2, 2, 4, 5), 2, 0, 0), Fetch(down, (0, 1, 1, 2, 5, 3), 1, 0, 0)]
         second = [Take(x, (0, 0, 0, 2, 2)) for x in (query_w, kv_w, out_w)]
         second += [Fetch(own_w, (0, 0, 0, 2), 1, 1, 1), Fetch(down, (0, 0, 0, 2), 1, 1, 1)]
     else:

time: 523 us -> 521 us (level)
  no operation moved by 1% of the time
where the time goes in v10:
time: 521 us; the launch traced here: 513 us
  Pallas kernels  486 us (93%)
  local copies, waits for them, and re-layouts  20.1 us (4%)
  other arithmetic  5.22 us (1%)
    pallas_call x9, Pallas kernels, hosted(): pl.pallas_call(body, out_shape=tuple(outs), in_specs=in_specs, out_specs=...  486 us

profile of v10, /device:TPU:1, one launch (start us, length us, event | category | flops | bytes accessed | tf_op | source)
XLA Modules:
  0.0 512.6 jit_solution(1904245874132274602)
XLA Ops:
  0.6 0.0 copy-start
  0.7 1.5 fusion.1
  2.2 3.8 reshape.68.refs_8_.refs_7_
  6.0 0.0 copy-done
  6.0 0.9 copy.29
  6.8 0.0 copy-start.15
  6.8 0.0 copy-start.17
  6.8 1.6 copy.30.refs_4_.refs_6_
  8.4 0.0 copy-done.15
  8.4 0.6 pad.9.refs_3_
  9.0 0.0 copy-done.17
  9.0 0.6 pad.8.refs_0_
  9.6 94.3 %conv_forward.1 = (f32[256,1024]{1,0:T(8,128)}, bf16[256,1024]{1,0:T(8,128)(2,1)}, bf16[1024,1024]{1,0:T(8,128)(2,1)}, bf16[1024,768]{1,0:T(8,128)(2,1)}, f32[8,...) custom-call(f32[8,128]{1,0:T(8,128)} %pad.8.refs_0_, ...), custom_call_target="tpu_custom_call" | custom-call | flops 2147483648 | bytes 16777216 | tf_op jit(solution)/shard_map/conv_forward/pallas_call | solution.py:848
  104.0 0.0 copy-done.8
  104.0 0.9 copy.36
  104.8 55.7 %ffn_forward.2 = (f32[256,1024]{1,0:T(8,128)}, bf16[1024,1024]{1,0:T(8,128)(2,1)}, bf16[1024,2304]{1,0:T(8,128)(2,1)}, bf16[1024,256]{1,0:T(8,128)(2,1)}, bf16[1...) custom-call(f32[256,1024]{1,0:T(8,128)} %get-tuple-element.82.refs_0, ...), custom_call_target="tpu_custom_call" | custom-call | flops 7247757312 | bytes 16777216 | tf_op jit(solution)/shard_map/ffn_forward/pallas_call | solution.py:848
  160.5 0.0 copy-done.16
  160.5 0.6 tile.30.refs_3_.refs_4_
  161.2 0.6 tile.33.refs_4_.refs_5_
  161.8 0.6 broadcast_in_dim_tile.3.refs_5_
  162.4 43.7 %attention_forward.1 = (f32[256,1024]{1,0:T(8,128)}, bf16[1024,1024]{1,0:T(8,128)(2,1)}, bf16[1024,512]{1,0:T(8,128)(2,1)}, bf16[1024,512]{1,0:T(8,128)(2,1)}, b...) custom-call(f32[8,128]{1,0:T(8,128)} %get-tuple-element.81.refs_0_, ...), custom_call_target="tpu_custom_call", output_to_operand_aliasing={{7}: (9, {}), {8}: (10, {})} | custom-call | flops 1610612736 | bytes 16777216 | tf_op jit(solution)/shard_map/attention_forward/pallas_call | solution.py:848
  206.1 44.6 %ffn_forward.3 = (f32[256,1024]{1,0:T(8,128)}, bf16[1024,1024]{1,0:T(8,128)(2,1)}, bf16[1024,2304]{1,0:T(8,128)(2,1)}, bf16[1024,1024]{1,0:T(8,128)(2,1)}) custom-call(f32[256,1024]{1,0:T(8,128)} %get-tuple-element.91.refs_0_.refs_1_, f32[1,1024]{1,0:T(1,128)} %get-tuple-element.178.refs_1_.refs_0_.refs_2_, bf16[1024,2304]{1,0:T(8,128)(2,1)} %bitcast.17, ...), custom_call_target="tpu_custom_call" | custom-call | flops 7247757312 | bytes 16777216 | tf_op jit(solution)/shard_map/ffn_forward/pallas_call | solution.py:848
  250.7 34.7 %ffn_backward.2 = (f32[256,1024]{1,0:T(8,128)}, f32[1,1024]{1,0:T(1,128)}, bf16[8,128,2304]{2,1,0:T(8,128)(2,1)}, bf16[8,1152,128]{2,1,0:T(8,128)(2,1)}, bf16[1024,256]{1,0:T(8,128)(2,1)}) custom-call(f32[1,1024]{1,0:T(1,128)} %get-tuple-element.178.refs_1_.refs_0_.refs_2_, f32[256,1024]{1,0:T(8,128)} %get-tuple-element.91.refs_0_.refs_1_, ...), custom_call_target="tpu_custom_call" | custom-call | flops 14495514624 | bytes 33554432 | tf_op jit(solution)/shard_map/ffn_backward/pallas_call | solution.py:848
  285.4 50.4 %attention_backward.1 = (f32[256,1024]{1,0:T(8,128)}, f32[1,1024]{1,0:T(1,128)}, f32[1,256]{1,0:T(1,128)}, f32[1,128]{1,0:T(1,128)}, bf16[8,128,512]{2,1,0:T(8,1...) custom-call(f32[8,128]{1,0:T(8,128)} %get-tuple-element.81.refs_0_, ...), custom_call_target="tpu_custom_call" | custom-call | flops 3221225472 | bytes 33554432 | tf_op jit(solution)/shard_map/attention_backward/pallas_call | solution.py:848
  335.8 0.0 copy-start.6
  335.8 50.3 %ffn_backward.3 = (f32[256,1024]{1,0:T(8,128)}, f32[1,1024]{1,0:T(1,128)}, bf16[8,128,2304]{2,1,0:T(8,128)(2,1)}, bf16[8,1152,128]{2,1,0:T(8,128)(2,1)}, f32[64,...) custom-call(f32[256,1024]{1,0:T(8,128)} %get-tuple-element.107.refs_, ...), custom_call_target="tpu_custom_call" | custom-call | flops 14495514624 | bytes 33554432 | tf_op jit(solution)/shard_map/ffn_backward/pallas_call | solution.py:848
  386.1 0.0 copy-done.6
  386.1 1.1 convert_element_type.14.refs_2_
  387.2 54.4 %conv_backward.1 = (f32[256,1024]{1,0:T(8,128)}, f32[1,1024]{1,0:T(1,128)}, f32[8,256]{1,0:T(8,128)}, bf16[8,128,768]{2,1,0:T(8,128)(2,1)}, bf16[8,256,128]{2,1,...) custom-call(f32[8,128]{1,0:T(8,128)} %get-tuple-element.81.refs_0_, ...), custom_call_target="tpu_custom_call" | custom-call | flops 4294967296 | bytes 16777216 | tf_op jit(solution)/shard_map/conv_backward/pallas_call | solution.py:848
  441.6 0.0 copy-start.5
  441.6 58.2 %tail.1 = (f32[8,1024]{1,0:T(8,128)}, bf16[1024,256]{1,0:T(8,128)(2,1)}, f32[64,2304]{1,0:T(8,128)}, f32[1152,128]{1,0:T(8,128)}, f32[128,768]{1,0:T(8,128)}, /*index=5*/f32[256,128]{1,0:T(8,128)}) custom-call(f32[1,1024]{1,0:T(1,128)} %get-tuple-element.126.refs_0_, f32[1,1024]{1,0:T(1,128)} %get-tuple-element.127.refs_1_, ...), custom_call_target="tpu_custom_call" | custom-call | bytes 4194304 | tf_op jit(solution)/shard_map/tail/pallas_call | solution.py:848
  499.8 0.0 copy-start.1
  499.8 0.0 copy-start.2
  499.8 0.0 copy-start.3
  499.8 0.0 copy-start.4
  499.8 0.0 copy-done.5
  499.8 2.3 pad_maximum_fusion.1
  502.1 0.0 copy-done.1
  502.1 0.0 copy-done.2
  502.1 0.0 copy-done.3
  502.1 0.0 copy-done.4
  502.1 0.2 pad_maximum_fusion
  502.3 0.0 copy-start.14
  502.3 0.0 copy-start.7
  502.3 0.0 copy-start.10
  502.3 2.4 reshape.74
  504.7 0.0 copy-done.14
  504.7 0.1 slice.53
  504.9 0.1 slice.55
  505.0 0.6 pad_maximum_fusion.2
  505.6 0.0 copy-done.7
  505.6 1.0 convert_element_type.15
  506.6 0.0 copy-done.10
  506.6 0.2 copy.32
  506.8 0.9 copy.33
  507.7 0.6 slice.51
  508.3 0.6 slice.56
  508.9 0.0 copy-done.11
  508.9 0.7 fusion
  509.6 0.7 reshape.73
  510.3 0.0 copy-done.9
  510.3 0.8 copy.42
  511.1 0.7 copy.43
  511.8 0.7 copy.44
  (18 shorter events, 0.1 us)
Async XLA Ops:
  0.6 5.3 %copy-start = (bf16[1024,3,256]{2,0,1:T(8,128)(2,1)S(1)}, bf16[1024,3,256]{2,0,1:T(8,128)(2,1)}, u32[]{:S(2)}) copy-start(bf16[1024,3,256]{2,0,1:T(8,128)(2,1)} %param.18) | copy-start | bytes 4718596
  6.8 1.6 copy-start.15
  6.8 2.2 copy-start.17
  9.6 94.3 %copy-start.8 = (bf16[1024,2,128]{2,1,0:T(2,128)(2,1)S(1)}, bf16[1024,2,128]{2,1,0:T(2,128)(2,1)}, u32[]{:S(2)}) copy-start(bf16[1024,2,128]{2,1,0:T(2,128)(2,1)} %param.22) | copy-start | bytes 1572868
  104.8 55.7 %copy-start.16 = (f32[2,64]{1,0:T(2,128)S(1)}, f32[2,64]{1,0:T(2,128)}, u32[]{:S(2)}) copy-start(f32[2,64]{1,0:T(2,128)} %param.17) | copy-start | bytes 1540
  335.8 50.3 %copy-start.6 = (bf16[256,1024]{1,0:T(8,128)(2,1)S(1)}, bf16[256,1024]{1,0:T(8,128)(2,1)}, u32[]{:S(2)}) copy-start(bf16[256,1024]{1,0:T(8,128)(2,1)} %get-tuple-element.116) | copy-start | bytes 1572868
  441.6 58.2 %copy-start.5 = (f32[1152,128]{1,0:T(8,128)S(1)}, f32[1152,128]{1,0:T(8,128)}, u32[]{:S(2)}) copy-start(f32[1152,128]{1,0:T(8,128)} %get-tuple-element.149) | copy-start | bytes 1769476
  499.8 2.4 copy-start.1
  499.8 2.4 copy-start.2
  499.8 2.3 copy-start.3
  499.8 2.3 copy-start.4
  502.3 2.4 copy-start.14
  502.3 3.2 copy-start.7
  502.3 4.3 copy-start.10
  504.7 4.2 copy-start.11
  504.7 5.6 %copy-start.9 = (bf16[1024,256]{1,0:T(8,128)(2,1)S(1)}, bf16[1024,256]{1,0:T(8,128)(2,1)}, u32[]{:S(2)}) copy-start(bf16[1024,256]{1,0:T(8,128)(2,1)} %get-tuple-element.194) | copy-start | bytes 1572868
  505.6 5.5 %copy-start.13 = (f32[256,128]{1,0:T(8,128)S(1)}, f32[256,128]{1,0:T(8,128)}, u32[]{:S(2)}) copy-start(f32[256,128]{1,0:T(8,128)} %get-tuple-element.200) | copy-start | bytes 393220
  505.6 6.2 %copy-start.12 = (f32[256,128]{1,0:T(8,128)S(1)}, f32[256,128]{1,0:T(8,128)}, u32[]{:S(2)}) copy-start(f32[256,128]{1,0:T(8,128)} %get-tuple-element.203) | copy-start | bytes 393220

commit v11 on v10

--- a/solution.py
+++ b/solution.py
@@ -1871,7 +1871,7 @@
     )
     (dh1, gain1, gw0, gv0), got = ffn_backward(
         dh2, h1, gain[1], None, w0, v0, n1, hidden0, 6,
-        settled(sums, (0, 0)) + whole(gv1, (0, 1, 2)) + whole(gqkv, (0, 2, 3)) + whole(gow, (0, 2, 3)),
+        settled(sums, (0, 0)) + whole(gv1, (0, 2, 4)) + whole(gqkv, (0, 2, 4)) + whole(gow, (0, 2, 4)),
     )
     sums_w1, sums = got[:2], got[2:]
     (dh0, gain0, gtaps, gci, gco), got = conv_backward(

time: 521 us -> 521 us (level)
  no operation moved by 1% of the time
where the time goes in v11:
time: 521 us; the launch traced here: 512 us
  Pallas kernels  485 us (93%)
  local copies, waits for them, and re-layouts  20.1 us (4%)
  other arithmetic  5.22 us (1%)
    pallas_call x9, Pallas kernels, hosted(): pl.pallas_call(body, out_shape=tuple(outs), in_specs=in_specs, out_specs=...  485 us

profile of v11, /device:TPU:1, one launch (start us, length us, event | category | flops | bytes accessed | tf_op | source)
XLA Modules:
  0.0 511.8 jit_solution(2995194712247261877)
XLA Ops:
  0.6 0.0 copy-start
  0.7 1.5 fusion.1
  2.2 3.8 reshape.68.refs_8_.refs_7_
  6.0 0.0 copy-done
  6.0 0.9 copy.29
  6.8 0.0 copy-start.15
  6.8 0.0 copy-start.17
  6.8 1.6 copy.30.refs_4_.refs_6_
  8.4 0.0 copy-done.15
  8.4 0.6 pad.9.refs_3_
  9.0 0.0 copy-done.17
  9.0 0.6 pad.8.refs_0_
  9.6 94.3 %conv_forward.1 = (f32[256,1024]{1,0:T(8,128)}, bf16[256,1024]{1,0:T(8,128)(2,1)}, bf16[1024,1024]{1,0:T(8,128)(2,1)}, bf16[1024,768]{1,0:T(8,128)(2,1)}, f32[8,...) custom-call(f32[8,128]{1,0:T(8,128)} %pad.8.refs_0_, ...), custom_call_target="tpu_custom_call" | custom-call | flops 2147483648 | bytes 16777216 | tf_op jit(solution)/shard_map/conv_forward/pallas_call | solution.py:848
  104.0 0.0 copy-done.8
  104.0 0.9 copy.36
  104.8 55.7 %ffn_forward.2 = (f32[256,1024]{1,0:T(8,128)}, bf16[1024,1024]{1,0:T(8,128)(2,1)}, bf16[1024,2304]{1,0:T(8,128)(2,1)}, bf16[1024,256]{1,0:T(8,128)(2,1)}, bf16[1...) custom-call(f32[256,1024]{1,0:T(8,128)} %get-tuple-element.82.refs_0, ...), custom_call_target="tpu_custom_call" | custom-call | flops 7247757312 | bytes 16777216 | tf_op jit(solution)/shard_map/ffn_forward/pallas_call | solution.py:848
  160.5 0.0 copy-done.16
  160.5 0.6 tile.30.refs_3_.refs_4_
  161.2 0.6 tile.33.refs_4_.refs_5_
  161.8 0.6 broadcast_in_dim_tile.3.refs_5_
  162.4 43.7 %attention_forward.1 = (f32[256,1024]{1,0:T(8,128)}, bf16[1024,1024]{1,0:T(8,128)(2,1)}, bf16[1024,512]{1,0:T(8,128)(2,1)}, bf16[1024,512]{1,0:T(8,128)(2,1)}, b...) custom-call(f32[8,128]{1,0:T(8,128)} %get-tuple-element.81.refs_0_, ...), custom_call_target="tpu_custom_call", output_to_operand_aliasing={{7}: (9, {}), {8}: (10, {})} | custom-call | flops 1610612736 | bytes 16777216 | tf_op jit(solution)/shard_map/attention_forward/pallas_call | solution.py:848
  206.1 44.6 %ffn_forward.3 = (f32[256,1024]{1,0:T(8,128)}, bf16[1024,1024]{1,0:T(8,128)(2,1)}, bf16[1024,2304]{1,0:T(8,128)(2,1)}, bf16[1024,1024]{1,0:T(8,128)(2,1)}) custom-call(f32[256,1024]{1,0:T(8,128)} %get-tuple-element.91.refs_0_.refs_1_, f32[1,1024]{1,0:T(1,128)} %get-tuple-element.178.refs_1_.refs_0_.refs_2_, bf16[1024,2304]{1,0:T(8,128)(2,1)} %bitcast.17, ...), custom_call_target="tpu_custom_call" | custom-call | flops 7247757312 | bytes 16777216 | tf_op jit(solution)/shard_map/ffn_forward/pallas_call | solution.py:848
  250.7 34.7 %ffn_backward.2 = (f32[256,1024]{1,0:T(8,128)}, f32[1,1024]{1,0:T(1,128)}, bf16[8,128,2304]{2,1,0:T(8,128)(2,1)}, bf16[8,1152,128]{2,1,0:T(8,128)(2,1)}, bf16[1024,256]{1,0:T(8,128)(2,1)}) custom-call(f32[1,1024]{1,0:T(1,128)} %get-tuple-element.178.refs_1_.refs_0_.refs_2_, f32[256,1024]{1,0:T(8,128)} %get-tuple-element.91.refs_0_.refs_1_, ...), custom_call_target="tpu_custom_call" | custom-call | flops 14495514624 | bytes 33554432 | tf_op jit(solution)/shard_map/ffn_backward/pallas_call | solution.py:848
  285.4 50.4 %attention_backward.1 = (f32[256,1024]{1,0:T(8,128)}, f32[1,1024]{1,0:T(1,128)}, f32[1,256]{1,0:T(1,128)}, f32[1,128]{1,0:T(1,128)}, bf16[8,128,512]{2,1,0:T(8,1...) custom-call(f32[8,128]{1,0:T(8,128)} %get-tuple-element.81.refs_0_, ...), custom_call_target="tpu_custom_call" | custom-call | flops 3221225472 | bytes 33554432 | tf_op jit(solution)/shard_map/attention_backward/pallas_call | solution.py:848
  335.8 0.0 copy-start.6
  335.8 49.5 %ffn_backward.3 = (f32[256,1024]{1,0:T(8,128)}, f32[1,1024]{1,0:T(1,128)}, bf16[8,128,2304]{2,1,0:T(8,128)(2,1)}, bf16[8,1152,128]{2,1,0:T(8,128)(2,1)}, f32[64,...) custom-call(f32[256,1024]{1,0:T(8,128)} %get-tuple-element.107.refs_, ...), custom_call_target="tpu_custom_call" | custom-call | flops 14495514624 | bytes 33554432 | tf_op jit(solution)/shard_map/ffn_backward/pallas_call | solution.py:848
  385.3 0.0 copy-done.6
  385.3 1.1 convert_element_type.14.refs_2_
  386.4 54.4 %conv_backward.1 = (f32[256,1024]{1,0:T(8,128)}, f32[1,1024]{1,0:T(1,128)}, f32[8,256]{1,0:T(8,128)}, bf16[8,128,768]{2,1,0:T(8,128)(2,1)}, bf16[8,256,128]{2,1,...) custom-call(f32[8,128]{1,0:T(8,128)} %get-tuple-element.81.refs_0_, ...), custom_call_target="tpu_custom_call" | custom-call | flops 4294967296 | bytes 16777216 | tf_op jit(solution)/shard_map/conv_backward/pallas_call | solution.py:848
  440.8 0.0 copy-start.5
  440.8 58.1 %tail.1 = (f32[8,1024]{1,0:T(8,128)}, bf16[1024,256]{1,0:T(8,128)(2,1)}, f32[64,2304]{1,0:T(8,128)}, f32[1152,128]{1,0:T(8,128)}, f32[128,768]{1,0:T(8,128)}, /*index=5*/f32[256,128]{1,0:T(8,128)}) custom-call(f32[1,1024]{1,0:T(1,128)} %get-tuple-element.126.refs_0_, f32[1,1024]{1,0:T(1,128)} %get-tuple-element.127.refs_1_, ...), custom_call_target="tpu_custom_call" | custom-call | bytes 4194304 | tf_op jit(solution)/shard_map/tail/pallas_call | solution.py:848
  498.9 0.0 copy-start.1
  498.9 0.0 copy-start.2
  498.9 0.0 copy-start.3
  498.9 0.0 copy-start.4
  499.0 0.0 copy-done.5
  499.0 2.3 pad_maximum_fusion.1
  501.3 0.0 copy-done.1
  501.3 0.0 copy-done.2
  501.3 0.0 copy-done.3
  501.3 0.0 copy-done.4
  501.3 0.2 pad_maximum_fusion
  501.5 0.0 copy-start.14
  501.5 0.0 copy-start.7
  501.5 0.0 copy-start.10
  501.5 2.4 reshape.74
  503.9 0.0 copy-done.14
  503.9 0.1 slice.53
  504.0 0.1 slice.55
  504.1 0.6 pad_maximum_fusion.2
  504.7 1.0 convert_element_type.15
  505.8 0.0 copy-done.10
  505.8 0.2 copy.32
  505.9 0.9 copy.33
  506.9 0.6 slice.51
  507.5 0.6 slice.56
  508.1 0.7 fusion
  508.7 0.7 reshape.73
  509.5 0.0 copy-done.9
  509.5 0.8 copy.42
  510.3 0.0 copy-done.13
  510.3 0.7 copy.43
  510.9 0.0 copy-done.12
  510.9 0.7 copy.44
  (18 shorter events, 0.1 us)
Async XLA Ops:
  0.6 5.3 %copy-start = (bf16[1024,3,256]{2,0,1:T(8,128)(2,1)S(1)}, bf16[1024,3,256]{2,0,1:T(8,128)(2,1)}, u32[]{:S(2)}) copy-start(bf16[1024,3,256]{2,0,1:T(8,128)(2,1)} %param.18) | copy-start | bytes 4718596
  6.8 1.6 copy-start.15
  6.8 2.2 copy-start.17
  9.6 94.3 %copy-start.8 = (bf16[1024,2,128]{2,1,0:T(2,128)(2,1)S(1)}, bf16[1024,2,128]{2,1,0:T(2,128)(2,1)}, u32[]{:S(2)}) copy-start(bf16[1024,2,128]{2,1,0:T(2,128)(2,1)} %param.22) | copy-start | bytes 1572868
  104.8 55.7 %copy-start.16 = (f32[2,64]{1,0:T(2,128)S(1)}, f32[2,64]{1,0:T(2,128)}, u32[]{:S(2)}) copy-start(f32[2,64]{1,0:T(2,128)} %param.17) | copy-start | bytes 1540
  335.8 49.5 %copy-start.6 = (bf16[256,1024]{1,0:T(8,128)(2,1)S(1)}, bf16[256,1024]{1,0:T(8,128)(2,1)}, u32[]{:S(2)}) copy-start(bf16[256,1024]{1,0:T(8,128)(2,1)} %get-tuple-element.116) | copy-start | bytes 1572868
  440.8 58.2 %copy-start.5 = (f32[1152,128]{1,0:T(8,128)S(1)}, f32[1152,128]{1,0:T(8,128)}, u32[]{:S(2)}) copy-start(f32[1152,128]{1,0:T(8,128)} %get-tuple-element.149) | copy-start | bytes 1769476
  498.9 2.4 copy-start.1
  498.9 2.4 copy-start.2
  498.9 2.3 copy-start.3
  498.9 2.3 copy-start.4
  501.5 2.4 copy-start.14
  501.5 3.2 copy-start.7
  501.5 4.3 copy-start.10
  503.9 4.2 copy-start.11
  503.9 5.6 %copy-start.9 = (bf16[1024,256]{1,0:T(8,128)(2,1)S(1)}, bf16[1024,256]{1,0:T(8,128)(2,1)}, u32[]{:S(2)}) copy-start(bf16[1024,256]{1,0:T(8,128)(2,1)} %get-tuple-element.194) | copy-start | bytes 1572868
  504.7 5.5 %copy-start.13 = (f32[256,128]{1,0:T(8,128)S(1)}, f32[256,128]{1,0:T(8,128)}, u32[]{:S(2)}) copy-start(f32[256,128]{1,0:T(8,128)} %get-tuple-element.200) | copy-start | bytes 393220
  504.7 6.2 %copy-start.12 = (f32[256,128]{1,0:T(8,128)S(1)}, f32[256,128]{1,0:T(8,128)}, u32[]{:S(2)}) copy-start(f32[256,128]{1,0:T(8,128)} %get-tuple-element.203) | copy-start | bytes 393220
